TPU v7x, 32 devices: a whole 2x2x4 slice. The times are simulated.
32 devices in a mesh: dp: 4 (over x, core), tensor: 8 (over z, y).
Axes of the slice: x: 2, y: 2, z: 4, core: 2. Of those that a mesh axis runs over, the one named last changes fastest.
Arguments:
- inputs: bfloat16 [2, 8192, 1024], P(None, ('dp', 'tensor')), may hold values from -6 to 6
- resets: int32 [2, 8192], P(None, ('dp', 'tensor')), may hold values 0 or 1
- cotangent: bfloat16 [2, 8192, 1024], P(None, ('dp', 'tensor')), may hold values from -6 to 6
- norm_gain: float32 [1024], replicated, may hold values from 0.5 to 1.5
- ema_alpha: float32 [1024, 16], replicated, may hold values from 0.02 to 0.2
- ema_damp: float32 [1024, 16], replicated, may hold values from 9.765625e-05 to 0.5
- ema_beta: float32 [1024, 16], replicated, may hold values from -4 to 4
- ema_eta: float32 [1024, 16], replicated, may hold values from -1.5 to 1.5
- ema_omega: float32 [1024], replicated, may hold values from -4 to 4
- w_gates: bfloat16 [1024, 2176], replicated, may hold values from -0.1875 to 0.1875
- b_gates: float32 [2176], replicated, may hold values from -3 to 3
- qk_gain: float32 [2, 128], replicated, may hold values from -4 to 4
- q_bias: float32 [128], replicated, may hold values from -3 to 3
- w_value: bfloat16 [1024, 2048], P(None, 'tensor'), may hold values from -0.1875 to 0.1875
- b_value: bfloat16 [2048], P('tensor'), may hold values from -3 to 3
- w_reset: bfloat16 [1024, 2048], P(None, 'tensor'), may hold values from -0.1875 to 0.1875
- b_reset: bfloat16 [2048], P('tensor'), may hold values from -3 to 3
- w_branch: bfloat16 [2048, 1024], P('tensor'), may hold values from -0.25 to 0.25
- ffn_gain: float32 [1024], replicated, may hold values from 0.5 to 1.5
- w_in: bfloat16 [1024, 4096], P(None, 'tensor'), may hold values from -0.1875 to 0.1875
- b_in: bfloat16 [4096], P('tensor'), may hold values from -3 to 3
- w_out: bfloat16 [4096, 1024], P('tensor'), may hold values from -0.09375 to 0.09375
- b_out: float32 [1024], replicated, may hold values from -3 to 3
Outputs:
- output: bfloat16 [2, 8192, 1024], P(None, ('dp', 'tensor'))
- grad_inputs: float32 [2, 8192, 1024], P(None, ('dp', 'tensor'))
- grad_norm_gain: float32 [1024], replicated
- grad_ema_alpha: float32 [1024, 16], replicated
- grad_ema_damp: float32 [1024, 16], replicated
- grad_ema_beta: float32 [1024, 16], replicated
- grad_ema_eta: float32 [1024, 16], replicated
- grad_ema_omega: float32 [1024], replicated
- grad_w_gates: float32 [1024, 2176], replicated
- grad_b_gates: float32 [2176], replicated
- grad_qk_gain: float32 [2, 128], replicated
- grad_q_bias: float32 [128], replicated
- grad_w_value: float32 [1024, 2048], P(None, 'tensor')
- grad_b_value: float32 [2048], P('tensor')
- grad_w_reset: float32 [1024, 2048], P(None, 'tensor')
- grad_b_reset: float32 [2048], P('tensor')
- grad_w_branch: float32 [2048, 1024], P('tensor')
- grad_ffn_gain: float32 [1024], replicated
- grad_w_in: float32 [1024, 4096], P(None, 'tensor')
- grad_b_in: float32 [4096], P('tensor')
- grad_w_out: float32 [4096, 1024], P('tensor')
- grad_b_out: float32 [1024], replicated
Inputs may be any that keep to these rules, and one draw needn't show every extreme that they name: `resets`: 1 marks the first token of a document; the first token of every 2048-token segment starts a document whatever the mask says.
All inputs are finite; a program needn't handle non-finite values. No bound on the sum of `resets` on one device may be relied on, other than what follows from the above.
Results may differ from a plain program's by a relative error of at most 0.012.
The roundings to bfloat16 on the way count: a program that leaves them out, or rounds other values in their place, can miss the bound.
Values may be sent and summed in bfloat16 or wider, within the bound.
No kernel may reach another device: no remote copies, remote signals or barrier semaphores. Data moves between devices by JAX's collectives and lax.ppermute only.
A program may use at most 576 MiB of HBM per device.

v0:
```python
from functools import partial

import jax
import jax.numpy as jnp
from jax import lax
from jax.sharding import PartitionSpec as P

BLOCK = 128
EMA_BLOCK = 32


HIGHEST = lax.Precision.HIGHEST
EPSILON = 1e-06


def carried_in(value, axis, combine, identity, reverse):
    size, mine = (lax.axis_size(axis), lax.axis_index(axis))
    everything = jax.tree.map(lambda part: lax.all_gather(part, axis), value)
    start = jax.tree.map(
        lambda part, zero: jnp.broadcast_to(jnp.asarray(zero, part.dtype), part.shape),
        value,
        identity,
    )

    def step(k, before):
        at = size - 1 - k if reverse else k
        reached = at > mine if reverse else at < mine
        new = combine(before, jax.tree.map(lambda part: part[at], everything))
        return jax.tree.map(lambda a, b: jnp.where(reached, a, b), new, before)

    return lax.fori_loop(0, size, step, start)


def dot_plain(left_side, right_side):
    return jnp.dot(left_side, right_side, preferred_element_type=jnp.float32)


def dot_against(left_side, right_side):
    return lax.dot_general(
        left_side, right_side, (((1,), (1,)), ((), ())), preferred_element_type=jnp.float32
    )


def dot_over_rows(left_side, right_side):
    return lax.dot_general(
        left_side, right_side, (((0,), (0,)), ((), ())), preferred_element_type=jnp.float32
    )


def silu_slope(values):
    sigmoid_v = jax.nn.sigmoid(values)
    return sigmoid_v * (1.0 + values * (1.0 - sigmoid_v))


def rms_scale(values, gain_row):
    return (
        values * lax.rsqrt(jnp.mean(values * values, axis=-1, keepdims=True) + EPSILON) * gain_row
    )


def ema_tables(rate_alpha, rate_damp, beta_in, eta_out, block_rows):
    log_decay = jnp.log(1.0 - rate_alpha * rate_damp)
    lag_steps = jnp.arange(block_rows).astype(jnp.float32)
    powers = jnp.exp(lag_steps[:, None, None] * log_decay[None])
    kernel = jnp.sum(powers * (rate_alpha * beta_in * eta_out)[None], axis=-1)
    offsets = jnp.arange(block_rows)
    lag_index = offsets[:, None] - offsets[None, :]
    lower_mask = (lag_index >= 0).astype(jnp.float32)
    toeplitz = jnp.take(kernel, jnp.maximum(lag_index, 0), axis=0) * lower_mask[:, :, None]
    decay_rate = jnp.exp(log_decay)
    enter_table = powers * (decay_rate * eta_out)[None]
    leave_table = powers[::-1] * (rate_alpha * beta_in)[None]
    through = powers[-1] * decay_rate
    return (toeplitz, enter_table, leave_table, through)


def ema_block(tables, state_in, block_inputs):
    toeplitz, enter_table, leave_table, through = tables
    row_block, flag_block = block_inputs
    doc_index = jnp.cumsum(flag_block)
    offsets = jnp.arange(flag_block.shape[0])
    same_doc = (
        (doc_index[:, None] == doc_index[None, :]) & (offsets[:, None] >= offsets[None, :])
    ).astype(jnp.float32)
    before_reset = (doc_index == 0).astype(jnp.float32)
    inner_sum = jnp.sum(toeplitz * same_doc[:, :, None] * row_block[None, :, :], axis=1)
    outer_sum = before_reset[:, None] * jnp.sum(enter_table * state_in[None], axis=-1)
    last_doc = (doc_index == doc_index[-1]).astype(jnp.float32)
    keep_state = (doc_index[-1] == 0).astype(jnp.float32)
    fresh_state = keep_state * through * state_in + jnp.sum(
        leave_table * (row_block * last_doc[:, None])[:, :, None], axis=0
    )
    return (fresh_state, inner_sum + outer_sum)


def ema_local(normed, doc_flags, rate_alpha, rate_damp, beta_in, eta_out):
    tables = ema_tables(rate_alpha, rate_damp, beta_in, eta_out, EMA_BLOCK)
    start_state = jnp.zeros(rate_alpha.shape, jnp.float32)
    row_count = normed.shape[0]
    block_count = row_count // EMA_BLOCK
    final_state, smoothed = lax.scan(
        partial(ema_block, tables),
        start_state,
        (normed.reshape(block_count, EMA_BLOCK, -1), doc_flags.reshape(block_count, EMA_BLOCK)),
    )
    clear_rows = (jnp.sum(doc_flags) == 0).astype(jnp.float32)
    carry_factor = clear_rows * jnp.exp(row_count * jnp.log(1.0 - rate_alpha * rate_damp))
    return (smoothed.reshape(row_count, -1), carry_factor, final_state)


def ema_entry(state_in, doc_flags, rate_alpha, rate_damp, eta_out):
    row_count = doc_flags.shape[0]
    before_reset = (jnp.cumsum(doc_flags) == 0).astype(jnp.float32)
    step_index = jnp.arange(1, row_count + 1).astype(jnp.float32)
    powers = jnp.exp(step_index[:, None, None] * jnp.log(1.0 - rate_alpha * rate_damp)[None])
    return before_reset[:, None] * jnp.sum(powers * (eta_out * state_in)[None], axis=-1)


def carry_combine(earlier, later):
    return (earlier[0] * later[0], earlier[1] * later[0] + later[1])


def back_combine(earlier, later):
    return (later[0] * earlier[0], later[1] + later[0] * earlier[1])


def block_mask(flag_rows):
    block_count = flag_rows.shape[0] // BLOCK
    doc_index = jnp.cumsum(flag_rows.astype(jnp.int32).reshape(block_count, BLOCK), axis=1)
    offsets = jnp.arange(BLOCK)
    return (doc_index[:, :, None] == doc_index[:, None, :]) & (
        offsets[:, None] >= offsets[None, :]
    )[None]


def block_scores(query_low, key_low, allowed):
    block_count = allowed.shape[0]
    score_scale = query_low.shape[-1] ** (-0.5)
    scores = (
        jnp.einsum(
            "cik,cjk->cij",
            query_low.reshape(block_count, BLOCK, -1),
            key_low.reshape(block_count, BLOCK, -1),
            preferred_element_type=jnp.float32,
        )
        * score_scale
    )
    return jnp.where(allowed, scores, -1000000000.0)


def local(
    inputs,
    resets,
    cotangent,
    norm_gain,
    ema_alpha,
    ema_damp,
    ema_beta,
    ema_eta,
    ema_omega,
    w_gates,
    b_gates,
    qk_gain,
    q_bias,
    w_value,
    b_value,
    w_reset,
    b_reset,
    w_branch,
    ffn_gain,
    w_in,
    b_in,
    w_out,
    b_out,
):
    micros, row_count, model_width = inputs.shape
    tensor_rank = lax.axis_index("tensor")
    offsets = tensor_rank * row_count + jnp.arange(row_count)
    leading = offsets == 0
    (
        value_weight,
        value_bias,
        reset_weight,
        reset_bias,
        branch_weight,
        inner_weight,
        inner_bias,
        outer_weight,
    ) = (w_value, b_value, w_reset, b_reset, w_branch, w_in, b_in, w_out)
    totals = {}
    for entry_name, template in (
        ("norm_gain", norm_gain),
        ("ema_alpha", ema_alpha),
        ("ema_damp", ema_damp),
        ("ema_beta", ema_beta),
        ("ema_eta", ema_eta),
        ("ema_omega", ema_omega),
        ("w_gates", w_gates),
        ("b_gates", b_gates),
        ("qk_gain", qk_gain),
        ("q_bias", q_bias),
        ("w_value", value_weight),
        ("b_value", value_bias),
        ("w_reset", reset_weight),
        ("b_reset", reset_bias),
        ("w_branch", branch_weight),
        ("ffn_gain", ffn_gain),
        ("w_in", inner_weight),
        ("b_in", inner_bias),
        ("w_out", outer_weight),
        ("b_out", b_out),
    ):
        totals[entry_name] = jnp.zeros(template.shape, jnp.float32)
    results = []
    input_grads = []
    for micro_index in range(micros):
        source = inputs[micro_index].astype(jnp.float32)
        doc_flags = jnp.where(leading, 1, resets[micro_index])
        normed, norm_pull = jax.vjp(rms_scale, source, norm_gain)

        def local_ema(values, rate_alpha, rate_damp, beta_in, eta_out):
            return ema_local(values, doc_flags, rate_alpha, rate_damp, beta_in, eta_out)

        (smoothed, carry_factor, final_state), ema_pull = jax.vjp(
            local_ema, normed, ema_alpha, ema_damp, ema_beta, ema_eta
        )
        incoming = carried_in(
            (carry_factor, final_state),
            "tensor",
            carry_combine,
            (jnp.ones_like(final_state), jnp.zeros_like(final_state)),
            False,
        )
        incoming_state = incoming[1]

        def entry_term(state_in, rate_alpha, rate_damp, eta_out):
            return ema_entry(state_in, doc_flags, rate_alpha, rate_damp, eta_out)

        correction, entry_pull = jax.vjp(entry_term, incoming_state, ema_alpha, ema_damp, ema_eta)
        blended = smoothed + correction + ema_omega * normed
        mixed_low = jax.nn.silu(blended).astype(jnp.bfloat16)
        normed_low = normed.astype(jnp.bfloat16)
        gate_pre = dot_plain(mixed_low, w_gates) + b_gates
        update = jax.nn.sigmoid(gate_pre[:, :model_width])
        direct = gate_pre[:, model_width : 2 * model_width]
        shared_pre = gate_pre[:, 2 * model_width :]
        shared_low = jax.nn.silu(shared_pre).astype(jnp.bfloat16)
        flag_low = doc_flags.astype(jnp.bfloat16)
        row_normed, row_mixed, row_shared, row_flags = (
            lax.all_gather(normed_low, "tensor", axis=0, tiled=True),
            lax.all_gather(mixed_low, "tensor", axis=0, tiled=True),
            lax.all_gather(shared_low, "tensor", axis=0, tiled=True),
            lax.all_gather(flag_low, "tensor", axis=0, tiled=True),
        )
        total_rows = row_normed.shape[0]
        block_count = total_rows // BLOCK
        value_pre = dot_plain(row_normed, value_weight) + value_bias
        value_low = jax.nn.silu(value_pre).astype(jnp.bfloat16)
        reset_pre = dot_plain(row_mixed, reset_weight) + reset_bias
        reset_gate = jax.nn.silu(reset_pre)
        shared_all = row_shared.astype(jnp.float32)
        query_low = (shared_all * qk_gain[0] + q_bias).astype(jnp.bfloat16)
        key_low = (shared_all * qk_gain[1]).astype(jnp.bfloat16)
        allowed = block_mask(row_flags)
        scores = block_scores(query_low, key_low, allowed)
        log_total = jax.nn.logsumexp(scores, axis=-1, keepdims=True)
        weights_soft = jnp.exp(scores - log_total)
        value_blocks = value_low.reshape(block_count, BLOCK, -1)
        attended = jnp.einsum(
            "cij,cjv->civ",
            weights_soft.astype(jnp.bfloat16),
            value_blocks,
            preferred_element_type=jnp.float32,
        ).reshape(total_rows, -1)
        gated_low = (reset_gate * attended).astype(jnp.bfloat16)
        branch = lax.psum_scatter(
            dot_plain(gated_low, branch_weight), "tensor", scatter_dimension=0, tiled=True
        )
        pre_hidden = direct + branch
        hidden = jax.nn.silu(pre_hidden)
        mixed_out = update * hidden + (1.0 - update) * source
        ffn_normed, ffn_pull = jax.vjp(rms_scale, mixed_out, ffn_gain)
        ffn_low = ffn_normed.astype(jnp.bfloat16)
        ffn_rows = lax.all_gather(ffn_low, "tensor", axis=0, tiled=True)
        pre_act = dot_plain(ffn_rows, inner_weight) + inner_bias
        activ_low = jax.nn.silu(pre_act).astype(jnp.bfloat16)
        feed_out = lax.psum_scatter(
            dot_plain(activ_low, outer_weight), "tensor", scatter_dimension=0, tiled=True
        )
        results.append((mixed_out + feed_out + b_out).astype(jnp.bfloat16))
        grad_out = cotangent[micro_index].astype(jnp.float32)
        totals["b_out"] = totals["b_out"] + jnp.sum(grad_out, axis=0)
        grad_rows = lax.all_gather(cotangent[micro_index], "tensor", axis=0, tiled=True)
        grad_act = dot_against(grad_rows, outer_weight)
        totals["w_out"] = totals["w_out"] + dot_over_rows(activ_low, grad_rows)
        grad_pre_low = (grad_act * silu_slope(pre_act)).astype(jnp.bfloat16)
        totals["w_in"] = totals["w_in"] + dot_over_rows(ffn_rows, grad_pre_low)
        totals["b_in"] = totals["b_in"] + jnp.sum(grad_pre_low.astype(jnp.float32), axis=0)
        grad_ffn_part = dot_against(grad_pre_low, inner_weight)
        grad_ffn = lax.psum_scatter(grad_ffn_part, "tensor", scatter_dimension=0, tiled=True)
        grad_mixed, grad_ffn_gain = ffn_pull(grad_ffn)
        grad_mixed = grad_mixed + grad_out
        totals["ffn_gain"] = totals["ffn_gain"] + grad_ffn_gain
        grad_source = grad_mixed * (1.0 - update)
        grad_update_pre = grad_mixed * (hidden - source) * update * (1.0 - update)
        grad_hidden_pre = grad_mixed * update * silu_slope(pre_hidden)
        grad_hidden_low = grad_hidden_pre.astype(jnp.bfloat16)
        hidden_rows = lax.all_gather(grad_hidden_low, "tensor", axis=0, tiled=True)
        grad_gated = dot_against(hidden_rows, branch_weight)
        totals["w_branch"] = totals["w_branch"] + dot_over_rows(gated_low, hidden_rows)
        grad_attended_low = (grad_gated * reset_gate).astype(jnp.bfloat16)
        grad_reset_low = (grad_gated * attended * silu_slope(reset_pre)).astype(jnp.bfloat16)
        totals["w_reset"] = totals["w_reset"] + dot_over_rows(row_mixed, grad_reset_low)
        totals["b_reset"] = totals["b_reset"] + jnp.sum(grad_reset_low.astype(jnp.float32), axis=0)
        again_scores = block_scores(query_low, key_low, allowed)
        again_soft = jnp.exp(again_scores - log_total)
        grad_blocks = grad_attended_low.reshape(block_count, BLOCK, -1)
        grad_soft = jnp.einsum(
            "civ,cjv->cij", grad_blocks, value_blocks, preferred_element_type=jnp.float32
        )
        grad_value = jnp.einsum(
            "cij,civ->cjv",
            again_soft.astype(jnp.bfloat16),
            grad_blocks,
            preferred_element_type=jnp.float32,
        ).reshape(total_rows, -1)
        score_scale = query_low.shape[-1] ** (-0.5)
        grad_scores = (
            again_soft
            * (grad_soft - jnp.sum(grad_soft * again_soft, axis=-1, keepdims=True))
            * score_scale
        )
        query_blocks = query_low.astype(jnp.float32).reshape(block_count, BLOCK, -1)
        key_blocks = key_low.astype(jnp.float32).reshape(block_count, BLOCK, -1)
        grad_query = jnp.einsum("cij,cjk->cik", grad_scores, key_blocks, precision=HIGHEST).reshape(
            total_rows, -1
        )
        grad_key = jnp.einsum("cij,cik->cjk", grad_scores, query_blocks, precision=HIGHEST).reshape(
            total_rows, -1
        )
        totals["qk_gain"] = totals["qk_gain"] + jnp.stack(
            [jnp.sum(grad_query * shared_all, axis=0), jnp.sum(grad_key * shared_all, axis=0)]
        )
        totals["q_bias"] = totals["q_bias"] + jnp.sum(grad_query, axis=0)
        grad_shared_part = grad_query * qk_gain[0] + grad_key * qk_gain[1]
        grad_value_low = (grad_value * silu_slope(value_pre)).astype(jnp.bfloat16)
        totals["w_value"] = totals["w_value"] + dot_over_rows(row_normed, grad_value_low)
        totals["b_value"] = totals["b_value"] + jnp.sum(grad_value_low.astype(jnp.float32), axis=0)
        grad_normed_part = dot_against(grad_value_low, value_weight)
        grad_mixed_part = dot_against(grad_reset_low, reset_weight)
        grad_normed_sum, grad_mixed_sum, grad_shared = (
            lax.psum_scatter(grad_normed_part, "tensor", scatter_dimension=0, tiled=True),
            lax.psum_scatter(grad_mixed_part, "tensor", scatter_dimension=0, tiled=True),
            lax.psum_scatter(grad_shared_part, "tensor", scatter_dimension=0, tiled=True),
        )
        grad_shared_pre = grad_shared * silu_slope(shared_pre)
        grad_gates_low = jnp.concatenate(
            [grad_update_pre, grad_hidden_pre, grad_shared_pre], axis=1
        ).astype(jnp.bfloat16)
        totals["w_gates"] = totals["w_gates"] + dot_over_rows(mixed_low, grad_gates_low)
        totals["b_gates"] = totals["b_gates"] + jnp.sum(grad_gates_low.astype(jnp.float32), axis=0)
        grad_mixed_in = grad_mixed_sum + dot_against(grad_gates_low, w_gates)
        grad_blended = grad_mixed_in * silu_slope(blended)
        totals["ema_omega"] = totals["ema_omega"] + jnp.sum(grad_blended * normed, axis=0)
        grad_state_in, grad_alpha_entry, grad_damp_entry, grad_eta_entry = entry_pull(grad_blended)
        later_sum = carried_in(
            (carry_factor, grad_state_in),
            "tensor",
            back_combine,
            (jnp.ones_like(grad_state_in), jnp.zeros_like(grad_state_in)),
            True,
        )
        grad_final = later_sum[1]
        grad_normed_ema, grad_alpha_local, grad_damp_local, grad_beta_local, grad_eta_local = (
            ema_pull((grad_blended, incoming_state * grad_final, grad_final))
        )
        totals["ema_alpha"] = totals["ema_alpha"] + grad_alpha_entry + grad_alpha_local
        totals["ema_damp"] = totals["ema_damp"] + grad_damp_entry + grad_damp_local
        totals["ema_beta"] = totals["ema_beta"] + grad_beta_local
        totals["ema_eta"] = totals["ema_eta"] + grad_eta_entry + grad_eta_local
        grad_normed = grad_normed_sum + grad_blended * ema_omega + grad_normed_ema
        grad_source_norm, grad_norm_gain = norm_pull(grad_normed)
        totals["norm_gain"] = totals["norm_gain"] + grad_norm_gain
        input_grads.append(grad_source + grad_source_norm)
    reduced = (
        totals["w_value"],
        totals["b_value"],
        totals["w_reset"],
        totals["b_reset"],
        totals["w_branch"],
        totals["w_in"],
        totals["b_in"],
        totals["w_out"],
    )
    (
        grad_w_value,
        grad_b_value,
        grad_w_reset,
        grad_b_reset,
        grad_w_branch,
        grad_w_in,
        grad_b_in,
        grad_w_out,
    ) = lax.psum(
        (
            reduced[0],
            reduced[1],
            reduced[2],
            reduced[3],
            reduced[4],
            reduced[5],
            reduced[6],
            reduced[7],
        ),
        "dp",
    )
    (
        grad_norm_gain,
        grad_ema_alpha,
        grad_ema_damp,
        grad_ema_beta,
        grad_ema_eta,
        grad_ema_omega,
        grad_w_gates,
        grad_b_gates,
        grad_qk_gain,
        grad_q_bias,
        grad_ffn_gain,
        grad_b_out,
    ) = lax.psum(
        (
            totals["norm_gain"],
            totals["ema_alpha"],
            totals["ema_damp"],
            totals["ema_beta"],
            totals["ema_eta"],
            totals["ema_omega"],
            totals["w_gates"],
            totals["b_gates"],
            totals["qk_gain"],
            totals["q_bias"],
            totals["ffn_gain"],
            totals["b_out"],
        ),
        ("dp", "tensor"),
    )
    return (
        jnp.stack(results),
        jnp.stack(input_grads),
        grad_norm_gain,
        grad_ema_alpha,
        grad_ema_damp,
        grad_ema_beta,
        grad_ema_eta,
        grad_ema_omega,
        grad_w_gates,
        grad_b_gates,
        grad_qk_gain,
        grad_q_bias,
        grad_w_value,
        grad_b_value,
        grad_w_reset,
        grad_b_reset,
        grad_w_branch,
        grad_ffn_gain,
        grad_w_in,
        grad_b_in,
        grad_w_out,
        grad_b_out,
    )


def solution(mesh):
    return jax.shard_map(
        local,
        mesh=mesh,
        in_specs=(
            P(None, ("dp", "tensor"), None),
            P(None, ("dp", "tensor")),
            P(None, ("dp", "tensor"), None),
            P(),
            P(),
            P(),
            P(),
            P(),
            P(),
            P(),
            P(),
            P(),
            P(),
            P(None, "tensor"),
            P("tensor"),
            P(None, "tensor"),
            P("tensor"),
            P("tensor", None),
            P(),
            P(None, "tensor"),
            P("tensor"),
            P("tensor", None),
            P(),
        ),
        out_specs=(
            P(None, ("dp", "tensor"), None),
            P(None, ("dp", "tensor"), None),
            P(),
            P(),
            P(),
            P(),
            P(),
            P(),
            P(),
            P(),
            P(),
            P(),
            P(None, "tensor"),
            P("tensor"),
            P(None, "tensor"),
            P("tensor"),
            P("tensor", None),
            P(),
            P(None, "tensor"),
            P("tensor"),
            P("tensor", None),
            P(),
        ),
        check_vma=False,
    )
```

profile of v0, /device:TPU:0, one launch (start us, length us, event | category | flops | bytes accessed | tf_op | source)
XLA Modules:
  0.0 3584.2 jit_solution(14982911749464623647)
XLA Ops:
  23.3 8.7 copy.159
  47.2 11.3 broadcast.682.clone.1
  65.2 218.7 %while.184 = (s32[]{:T(128)}, f32[1024,16]{1,0:T(8,128)}, f32[8,32,1024]{2,1,0:T(8,128)}, f32[8,32,32,1]{2,1,3,0:T(8,128)}, f32[8,1,32,1024]{3,2,1,0:T(8,128)}, ...) while((s32[]{:T(128)}, f32[1024,16]{1,0:T(8,128)}, ...), condition=%wide.region_7.9_spmd.clone.clone, body=%wide.region_2.8_spmd.clone.clone.sunk | while | flops 7464165 | bytes 26514640 | solution.py:101
  67.5 7.6 multiply_reduce_fusion.33
  93.8 7.6 multiply_reduce_fusion.33
  121.3 7.6 multiply_reduce_fusion.33
  148.8 7.6 multiply_reduce_fusion.33
  176.3 7.6 multiply_reduce_fusion.33
  203.7 7.6 multiply_reduce_fusion.33
  231.2 7.6 multiply_reduce_fusion.33
  258.7 7.6 multiply_reduce_fusion.33
  283.9 86.1 %all-gather.1 = f32[8192,16]{1,0:T(8,128)} all-gather(f32[1024,16]{1,0:T(8,128)} %get-tuple-element.1494), channel_id=3, replica_groups=mesh['dp'=4,'tensor'=8] {'tensor'}, dimensions={0}, use_global_device_ids=true | all-gather | bytes 589824 | tf_op jit(solution)/shard_map/all_gather | solution.py:18
  372.9 31.9 all-gather
  405.3 11.3 broadcast.682.clone
  423.1 232.3 %while.185 = (s32[]{:T(128)}, f32[1024,16]{1,0:T(8,128)}, f32[8,32,1024]{2,1,0:T(8,128)}, f32[8,32,32,1]{2,1,3,0:T(8,128)}, f32[8,1,32,1024]{3,2,1,0:T(8,128)}, ...) while((s32[]{:T(128)}, f32[1024,16]{1,0:T(8,128)}, ...), condition=%wide.region_26.28_spmd.clone.clone, body=%wide.region_21.27_spmd.clone.clone.sunk | while | flops 7464165 | bytes 18125976 | solution.py:101
  426.2 7.6 multiply_reduce_fusion.35
  454.4 7.6 multiply_reduce_fusion.35
  483.5 7.6 multiply_reduce_fusion.35
  512.7 7.6 multiply_reduce_fusion.35
  541.8 7.6 multiply_reduce_fusion.35
  571.0 7.6 multiply_reduce_fusion.35
  600.1 7.6 multiply_reduce_fusion.35
  655.4 75.1 %all-gather.3 = f32[8192,16]{1,0:T(8,128)} all-gather(f32[1024,16]{1,0:T(8,128)} %get-tuple-element.1497), channel_id=5, replica_groups=mesh['dp'=4,'tensor'=8] {'tensor'}, dimensions={0}, use_global_device_ids=true | all-gather | bytes 589824 | tf_op jit(solution)/shard_map/all_gather | solution.py:18
  733.4 31.6 all-gather.2
  766.9 8.1 multiply_reduce_fusion.11
  778.7 19.3 all-gather.8
  807.4 33.4 all_gather.88
  840.8 32.1 all_gather.97
  883.4 54.5 %all-gather.21.cloned.1.call-done = bf16[2048,1024]{1,0:T(8,128)(2,1)} async-done(((bf16[256,1024]{1,0:T(8,128)(2,1)}), bf16[2048,1024]{1,0:T(8,128)(2,1)}) %all-gather.21.cloned.1.call-update) | async-done | bytes 4194320 | tf_op jit(solution)/shard_map/all_gather | solution.py:251
  949.5 147.4 %reduce-scatter.13.cloned.1.call-done = f32[256,1024]{1,0:T(8,128)} async-done(((f32[2048,1024]{1,0:T(8,128)}), f32[256,1024]{1,0:T(8,128)}) %reduce-scatter.13.cloned.1.call-update) | async-done | bytes 1048592 | tf_op jit(solution)/shard_map/reduce_scatter | solution.py:276
  1105.4 68.6 %all-gather.25.cloned.1.call-done = bf16[2048,1024]{1,0:T(8,128)(2,1)} async-done(((bf16[256,1024]{1,0:T(8,128)(2,1)}), bf16[2048,1024]{1,0:T(8,128)(2,1)}) %all-gather.25.cloned.1.call-update) | async-done | bytes 4194320 | tf_op jit(solution)/shard_map/all_gather | solution.py:284
  1181.0 67.5 %all-gather.37.cloned.1.call-done = bf16[1,2048,1024]{2,1,0:T(8,128)(2,1)} async-done(((bf16[1,256,1024]{2,1,0:T(8,128)(2,1)}), bf16[1,2048,1024]{2,1,0:T(8,128)(2,1)}) %all-gather.37.cloned.1.call-update) | async-done | bytes 4194320 | tf_op jit(solution)/shard_map/all_gather | solution.py:293
  1248.5 7.8 convert_reduce_fusion.5
  1264.0 18.2 all-gather.9
  1286.0 37.0 %all-gather.29.cloned.1.call-done = bf16[2048,1024]{1,0:T(8,128)(2,1)} async-done(((bf16[256,1024]{1,0:T(8,128)(2,1)}), bf16[2048,1024]{1,0:T(8,128)(2,1)}) %all-gather.29.cloned.1.call-update) | async-done | bytes 4194320 | tf_op jit(solution)/shard_map/all_gather | solution.py:250
  1330.9 66.2 %all-gather.27.cloned.1.call-done = bf16[2048,1024]{1,0:T(8,128)(2,1)} async-done(((bf16[256,1024]{1,0:T(8,128)(2,1)}), bf16[2048,1024]{1,0:T(8,128)(2,1)}) %all-gather.27.cloned.1.call-update) | async-done | bytes 4194320 | tf_op jit(solution)/shard_map/all_gather | solution.py:251
  1408.8 140.2 %reduce-scatter.21.cloned.1.call-done = f32[256,1024]{1,0:T(8,128)} async-done(((f32[2048,1024]{1,0:T(8,128)}), f32[256,1024]{1,0:T(8,128)}) %reduce-scatter.21.cloned.1.call-update) | async-done | bytes 1048592 | tf_op jit(solution)/shard_map/reduce_scatter | solution.py:300
  1551.4 149.3 %reduce-scatter.17.cloned.1.call-done = f32[256,1024]{1,0:T(8,128)} async-done(((f32[2048,1024]{1,0:T(8,128)}), f32[256,1024]{1,0:T(8,128)}) %reduce-scatter.17.cloned.1.call-update) | async-done | bytes 1048592 | tf_op jit(solution)/shard_map/reduce_scatter | solution.py:276
  1709.2 71.3 %all-gather.31.cloned.1.call-done = bf16[2048,1024]{1,0:T(8,128)(2,1)} async-done(((bf16[256,1024]{1,0:T(8,128)(2,1)}), bf16[2048,1024]{1,0:T(8,128)(2,1)}) %all-gather.31.cloned.1.call-update) | async-done | bytes 4194320 | tf_op jit(solution)/shard_map/all_gather | solution.py:284
  1787.3 67.3 %all-gather.39.cloned.1.call-done = bf16[1,2048,1024]{2,1,0:T(8,128)(2,1)} async-done(((bf16[1,256,1024]{2,1,0:T(8,128)(2,1)}), bf16[1,2048,1024]{2,1,0:T(8,128)(2,1)}) %all-gather.39.cloned.1.call-update) | async-done | bytes 4194320 | tf_op jit(solution)/shard_map/all_gather | solution.py:293
  1854.6 7.8 convert_reduce_fusion.4
  1870.3 146.6 %reduce-scatter.29.cloned.1.call-done = f32[256,1024]{1,0:T(8,128)} async-done(((f32[2048,1024]{1,0:T(8,128)}), f32[256,1024]{1,0:T(8,128)}) %reduce-scatter.29.cloned.1.call-update) | async-done | bytes 1048592 | tf_op jit(solution)/shard_map/reduce_scatter | solution.py:300
  2024.0 67.5 %all-gather.33.cloned.1.call-done = bf16[2048,1024]{1,0:T(8,128)(2,1)} async-done(((bf16[256,1024]{1,0:T(8,128)(2,1)}), bf16[2048,1024]{1,0:T(8,128)(2,1)}) %all-gather.33.cloned.1.call-update) | async-done | bytes 4194320 | tf_op jit(solution)/shard_map/all_gather | solution.py:308
  2110.5 54.7 %all-gather.35.cloned.1.call-done = bf16[2048,1024]{1,0:T(8,128)(2,1)} async-done(((bf16[256,1024]{1,0:T(8,128)(2,1)}), bf16[2048,1024]{1,0:T(8,128)(2,1)}) %all-gather.35.cloned.1.call-update) | async-done | bytes 4194320 | tf_op jit(solution)/shard_map/all_gather | solution.py:308
  2202.5 8.0 fusion.187
  2210.6 8.0 fusion.188
  2253.4 128.8 %reduce-scatter.25.cloned.1.call-done = f32[256,1024]{1,0:T(8,128)} async-done(((f32[2048,1024]{1,0:T(8,128)}), f32[256,1024]{1,0:T(8,128)}) %reduce-scatter.25.cloned.1.call-update) | async-done | bytes 1048592 | tf_op jit(solution)/shard_map/reduce_scatter | solution.py:353
  2396.6 51.2 %reduce-scatter.35.cloned.1.call-done = f32[256,128]{1,0:T(8,128)} async-done(((f32[2048,128]{1,0:T(8,128)}), f32[256,128]{1,0:T(8,128)}) %reduce-scatter.35.cloned.1.call-update) | async-done | bytes 131088 | tf_op jit(solution)/shard_map/reduce_scatter | solution.py:354
  2448.9 8.5 convolution_add_fusion
  2457.4 142.4 %reduce-scatter.33.cloned.1.call-done = f32[256,1024]{1,0:T(8,128)} async-done(((f32[2048,1024]{1,0:T(8,128)}), f32[256,1024]{1,0:T(8,128)}) %reduce-scatter.33.cloned.1.call-update) | async-done | bytes 1048592 | tf_op jit(solution)/shard_map/reduce_scatter | solution.py:353
  2605.3 10.6 multiply_reduce_fusion.6
  2616.6 34.5 all-gather.7
  2652.2 16.3 while.182
  2670.2 176.3 %while.183 = (s32[]{:T(128)}, f32[32,32,1024]{2,1,0:T(8,128)}, f32[32,1024,16]{1,2,0:T(8,128)}, f32[1024,16]{0,1:T(8,128)}, f32[32,1024,16]{1,2,0:T(8,128)}, /*i...) while((s32[]{:T(128)}, f32[32,32,1024]{2,1,0:T(8,128)}, ...), condition=%wide.region_67.69_spmd.clone, body=%wide.region_63.68_spmd.clone.sunk | while | flops 12697604 | bytes 27145500 | solution.py:101
  2846.5 31.9 all-gather.5
  2879.5 21.1 while.180
  2903.2 174.8 %while.181 = (s32[]{:T(128)}, f32[32,32,1024]{2,1,0:T(8,128)}, f32[32,1024,16]{1,2,0:T(8,128)}, f32[1024,16]{0,1:T(8,128)}, f32[32,1024,16]{1,2,0:T(8,128)}, /*i...) while((s32[]{:T(128)}, f32[32,32,1024]{2,1,0:T(8,128)}, ...), condition=%wide.region_52.54_spmd.clone, body=%wide.region_48.53_spmd.clone.sunk | while | flops 12697604 | bytes 27145656 | solution.py:101
  3085.6 10.6 scatter_custom_fusion
  3096.2 10.9 scatter_custom_fusion.1
  3133.1 39.3 %all-reduce.2 = (f32[1024]{0:T(1024)}, f32[1024]{0:T(1024)}, f32[2176]{0:T(1024)}, f32[2,128]{1,0:T(2,128)}, f32[128]{0:T(128)}, /*index=5*/f32[1024]{0:T(1024)}, f32[1024]{0:T(1024)}) all-reduce(f32[1024]{0:T(1024)S(1)} %add.776, f32[1024]{0:T(1024)S(1)} %add.787, ...), channel_id=1, replica_groups=mesh['dp'=4,'tensor'=8] {'dp','tensor'}, use_global_device_ids=true, to_apply=%region_71.73 | all-reduce | flops 6656 | bytes 53248 | tf_op jit(solution)/shard_map/psum | solution.py:430
  3176.6 42.3 %reduce-scatter.19.cloned.1.call-done = f32[256,1024]{1,0:T(8,128)} async-done(((f32[2048,1024]{1,0:T(8,128)}), f32[256,1024]{1,0:T(8,128)}) %reduce-scatter.19.cloned.1.call-update) | async-done | bytes 1048592 | tf_op jit(solution)/shard_map/reduce_scatter | solution.py:287
  3225.6 132.5 %all-reduce.11.cloned.1.call-done = (f32[1024,256]{1,0:T(8,128)}, f32[1024,256]{1,0:T(8,128)}, f32[256,1024]{1,0:T(8,128)}, f32[1024,512]{1,0:T(8,128)}, f32[512,1024]{1,0:T(8,128)}) async-done(((f32[1024,256]{1,0:T(8,128)}, f32[1024,256]{1,0:T(8,128)}, f32[256,1024]{1,0:T(8,128)}, f32[1024,512]{1,0:T(8,128)}, f32[512,1024]{1,0:T(8,128)}), (f32[1024,256]{1,0:T(8,128)}, f32[1024,256]{1,0:T(8,128)}, ...) | async-done | bytes 7340048 | tf_op jit(solution)/shard_map/psum | solution.py:404
  3358.1 197.8 %all-reduce.9.cloned.1.call-done = (f32[1024,16]{0,1:T(8,128)}, f32[1024,16]{0,1:T(8,128)}, f32[1024,16]{0,1:T(8,128)}, f32[1024,16]{0,1:T(8,128)}, f32[1024,2176]{1,0:T(8,128)}) async-done(((f32[1024,16]{0,1:T(8,128)}, f32[1024,16]{0,1:T(8,128)}, f32[1024,16]{0,1:T(8,128)}, f32[1024,16]{0,1:T(8,128)}, f32[1024,2176]{1,0:T(8,128)}), (f32[1024,16]{0,1:T(8,128)}, f32[1024,16]{0,1:T(8,128)}, ...) | async-done | bytes 9175056 | tf_op jit(solution)/shard_map/psum | solution.py:430
  3561.8 7.8 copy.475
  (1497 shorter events, 1053.2 us)
Async XLA Ops:
  7.2 1241.3 %copy-start = (bf16[512,1024]{1,0:T(8,128)(2,1)S(1)}, bf16[512,1024]{1,0:T(8,128)(2,1)}, u32[]{:S(2)}) copy-start(bf16[512,1024]{1,0:T(8,128)(2,1)} %param.62) | copy-start | bytes 3145732
  7.3 868.3 %all-gather.23.cloned.1.call-start = ((), (), s32[]{:S(2)}) async-start(), calls=%async_computation.13 | async-start | bytes 4718592 | tf_op jit(solution)/shard_map/all_gather | solution.py:250
  283.9 86.1 %copy-start.172 = (f32[8,32,1]{1,2,0:T(1,128)}, f32[8,32,1]{1,2,0:T(1,128)S(1)}, u32[]{:S(2)}) copy-start(f32[8,32,1]{1,2,0:T(1,128)S(1)} %get-tuple-element.3850) | copy-start | bytes 3076
  283.9 86.1 %copy-start.173 = (f32[8,32,1]{1,2,0:T(1,128)}, f32[8,32,1]{1,2,0:T(1,128)S(1)}, u32[]{:S(2)}) copy-start(f32[8,32,1]{1,2,0:T(1,128)S(1)} %get-tuple-element.3857) | copy-start | bytes 3076
  283.9 86.1 %copy-start.208 = (f32[8]{0:T(128)}, f32[8]{0:T(128)S(1)}, u32[]{:S(2)}) copy-start(f32[8]{0:T(128)S(1)} %get-tuple-element.3852) | copy-start | bytes 100
  405.3 361.5 %copy-start.52 = (f32[1024,16]{0,1:T(8,128)}, f32[1024,16]{0,1:T(8,128)S(1)}, u32[]{:S(2)}) copy-start(f32[1024,16]{0,1:T(8,128)S(1)} %get-tuple-element.1495) | copy-start | bytes 196612
  655.4 75.1 %copy-start.24 = (f32[1024,16]{0,1:T(8,128)}, f32[1024,16]{0,1:T(8,128)S(1)}, u32[]{:S(2)}) copy-start(f32[1024,16]{0,1:T(8,128)S(1)} %get-tuple-element.4104) | copy-start | bytes 196612
  655.4 75.1 %copy-start.135 = (f32[32]{0:T(128)}, f32[32]{0:T(128)S(1)}, u32[]{:S(2)}) copy-start(f32[32]{0:T(128)S(1)} %get-tuple-element.4173) | copy-start | bytes 388
  655.4 75.1 %copy-start.174 = (f32[8,32,1]{1,2,0:T(1,128)}, f32[8,32,1]{1,2,0:T(1,128)S(1)}, u32[]{:S(2)}) copy-start(f32[8,32,1]{1,2,0:T(1,128)S(1)} %get-tuple-element.3952) | copy-start | bytes 3076
  655.4 75.1 %copy-start.175 = (f32[8,32,1]{1,2,0:T(1,128)}, f32[8,32,1]{1,2,0:T(1,128)S(1)}, u32[]{:S(2)}) copy-start(f32[8,32,1]{1,2,0:T(1,128)S(1)} %get-tuple-element.3959) | copy-start | bytes 3076
  655.4 75.1 %copy-start.210 = (f32[8]{0:T(128)}, f32[8]{0:T(128)S(1)}, u32[]{:S(2)}) copy-start(f32[8]{0:T(128)S(1)} %get-tuple-element.3954) | copy-start | bytes 100
  655.4 111.4 %copy-start.21 = (f32[1024,16]{0,1:T(8,128)}, f32[1024,16]{0,1:T(8,128)S(1)}, u32[]{:S(2)}) copy-start(f32[1024,16]{0,1:T(8,128)S(1)} %get-tuple-element.4100) | copy-start | bytes 196612
  730.5 34.6 copy-start.49
  733.4 33.4 copy-start.75
  733.4 33.4 copy-start.212
  777.9 160.0 %all-gather.21.cloned.1.call-start = ((), (), s32[]{:S(2)}) async-start(), calls=%async_computation.12 | async-start | bytes 4718592 | tf_op jit(solution)/shard_map/all_gather | solution.py:251
  778.6 318.3 %reduce-scatter.13.cloned.1.call-start = ((), (), s32[]{:S(2)}) async-start(), calls=%async_computation.14 | async-start | bytes 9437184 | tf_op jit(solution)/shard_map/reduce_scatter | solution.py:276
  803.7 69.2 %copy-start.189 = (f32[128]{0:T(128)S(1)}, f32[128]{0:T(128)}, u32[]{:S(2)}) copy-start(f32[128]{0:T(128)} %param.53) | copy-start | bytes 1540
  807.4 66.9 %copy-start.20 = (f32[256,2176]{1,0:T(8,128)}, f32[256,2176]{1,0:T(8,128)S(1)}, u32[]{:S(2)}) copy-start(f32[256,2176]{1,0:T(8,128)S(1)} %convolution_add_fusion.1) | copy-start | bytes 6684676
  840.8 34.0 copy-start.42
  949.5 151.0 %copy-start.115 = (f32[1024]{0:T(1024)S(1)}, f32[1024]{0:T(1024)}, u32[]{:S(2)}) copy-start(f32[1024]{0:T(1024)} %param.59) | copy-start | bytes 12292
  949.5 224.5 %all-gather.25.cloned.1.call-start = ((), (), s32[]{:S(2)}) async-start(), calls=%async_computation.15 | async-start | bytes 4718592 | tf_op jit(solution)/shard_map/all_gather | solution.py:284
  1099.5 601.3 %copy-start.142 = (f32[256]{0:T(256)}, f32[256]{0:T(256)S(1)}, u32[]{:S(2)}) copy-start(f32[256]{0:T(256)S(1)} %fusion.175) | copy-start | bytes 3076
  1101.5 147.0 %all-gather.37.cloned.1.call-start = ((), (), s32[]{:S(2)}) async-start(), calls=%async_computation.32 | async-start | bytes 4718592 | tf_op jit(solution)/shard_map/all_gather | solution.py:293
  1103.8 219.3 %all-gather.29.cloned.1.call-start = ((), (), s32[]{:S(2)}) async-start(), calls=%async_computation.18 | async-start | bytes 4718592 | tf_op jit(solution)/shard_map/all_gather | solution.py:250
  1104.4 292.7 %all-gather.27.cloned.1.call-start = ((), (), s32[]{:S(2)}) async-start(), calls=%async_computation.17 | async-start | bytes 4718592 | tf_op jit(solution)/shard_map/all_gather | solution.py:251
  1105.1 443.9 %reduce-scatter.21.cloned.1.call-start = ((), (), s32[]{:S(2)}) async-start(), calls=%async_computation.22 | async-start | bytes 9437184 | tf_op jit(solution)/shard_map/reduce_scatter | solution.py:300
  1263.4 437.4 %reduce-scatter.17.cloned.1.call-start = ((), (), s32[]{:S(2)}) async-start(), calls=%async_computation.19 | async-start | bytes 9437184 | tf_op jit(solution)/shard_map/reduce_scatter | solution.py:276
  1408.8 371.8 %all-gather.31.cloned.1.call-start = ((), (), s32[]{:S(2)}) async-start(), calls=%async_computation.20 | async-start | bytes 4718592 | tf_op jit(solution)/shard_map/all_gather | solution.py:284
  1551.4 154.6 %copy-start.164 = (f32[256]{0:T(256)}, f32[256]{0:T(256)S(1)}, u32[]{:S(2)}) copy-start(f32[256]{0:T(256)S(1)} %multiply_multiply_fusion.15) | copy-start | bytes 3076
  1706.1 313.4 %copy-start.150 = (f32[256]{0:T(256)}, f32[256]{0:T(256)S(1)}, u32[]{:S(2)}) copy-start(f32[256]{0:T(256)S(1)} %fusion.177) | copy-start | bytes 3076
  1708.0 146.6 %all-gather.39.cloned.1.call-start = ((), (), s32[]{:S(2)}) async-start(), calls=%async_computation.33 | async-start | bytes 4718592 | tf_op jit(solution)/shard_map/all_gather | solution.py:293
  1708.7 308.2 %reduce-scatter.29.cloned.1.call-start = ((), (), s32[]{:S(2)}) async-start(), calls=%async_computation.27 | async-start | bytes 9437184 | tf_op jit(solution)/shard_map/reduce_scatter | solution.py:300
  1869.5 222.0 %all-gather.33.cloned.1.call-start = ((), (), s32[]{:S(2)}) async-start(), calls=%async_computation.23 | async-start | bytes 4718592 | tf_op jit(solution)/shard_map/all_gather | solution.py:308
  1870.2 294.9 %all-gather.35.cloned.1.call-start = ((), (), s32[]{:S(2)}) async-start(), calls=%async_computation.28 | async-start | bytes 4718592 | tf_op jit(solution)/shard_map/all_gather | solution.py:308
  2023.8 222.2 %reduce-scatter.27.cloned.1.call-start = ((), (), s32[]{:S(2)}) async-start(), calls=%async_computation.26 | async-start | bytes 1179648 | tf_op jit(solution)/shard_map/reduce_scatter | solution.py:354
  2104.5 277.6 %reduce-scatter.25.cloned.1.call-start = ((), (), s32[]{:S(2)}) async-start(), calls=%async_computation.25 | async-start | bytes 9437184 | tf_op jit(solution)/shard_map/reduce_scatter | solution.py:353
  2110.4 337.4 %reduce-scatter.35.cloned.1.call-start = ((), (), s32[]{:S(2)}) async-start(), calls=%async_computation.31 | async-start | bytes 1179648 | tf_op jit(solution)/shard_map/reduce_scatter | solution.py:354
  2178.2 421.6 %reduce-scatter.33.cloned.1.call-start = ((), (), s32[]{:S(2)}) async-start(), calls=%async_computation.30 | async-start | bytes 9437184 | tf_op jit(solution)/shard_map/reduce_scatter | solution.py:353
  2184.3 943.5 %reduce-scatter.23.cloned.1.call-start = ((), (), s32[]{:S(2)}) async-start(), calls=%async_computation.24 | async-start | bytes 9437184 | tf_op jit(solution)/shard_map/reduce_scatter | solution.py:352
  2193.6 934.3 %reduce-scatter.31.cloned.1.call-start = ((), (), s32[]{:S(2)}) async-start(), calls=%async_computation.29 | async-start | bytes 9437184 | tf_op jit(solution)/shard_map/reduce_scatter | solution.py:352
  2202.4 969.9 %reduce-scatter.15.cloned.1.call-start = ((), (), s32[]{:S(2)}) async-start(), calls=%async_computation.16 | async-start | bytes 9437184 | tf_op jit(solution)/shard_map/reduce_scatter | solution.py:287
  2210.5 1008.4 %reduce-scatter.19.cloned.1.call-start = ((), (), s32[]{:S(2)}) async-start(), calls=%async_computation.21 | async-start | bytes 9437184 | tf_op jit(solution)/shard_map/reduce_scatter | solution.py:287
  2218.6 1139.5 %all-reduce.11.cloned.1.call-start = ((), (), s32[]{:S(2)}) async-start(), calls=%async_computation.35 | async-start | bytes 14680064 | tf_op jit(solution)/shard_map/psum | solution.py:404
  2247.1 135.1 %copy-start.108 = (bf16[256,128]{1,0:T(8,128)(2,1)}, bf16[256,128]{1,0:T(8,128)(2,1)S(1)}, u32[]{:S(2)}) copy-start(bf16[256,128]{1,0:T(8,128)(2,1)S(1)} %multiply_convert_fusion.15) | copy-start | bytes 196612
  2247.1 135.0 %copy-start.171 = (f32[256]{0:T(256)S(1)}, f32[256]{0:T(256)}, u32[]{:S(2)}) copy-start(f32[256]{0:T(256)} %copy-done.170) | copy-start | bytes 3076
  2396.5 52.3 %copy-start.28 = (bf16[256,1024]{1,0:T(8,128)(2,1)S(1)}, bf16[256,1024]{1,0:T(8,128)(2,1)}, u32[]{:S(2)}) copy-start(bf16[256,1024]{1,0:T(8,128)(2,1)} %get-tuple-element.2805) | copy-start | bytes 1572868
  2396.5 52.3 %copy-start.35 = (bf16[256,1024]{1,0:T(8,128)(2,1)S(1)}, bf16[256,1024]{1,0:T(8,128)(2,1)}, u32[]{:S(2)}) copy-start(bf16[256,1024]{1,0:T(8,128)(2,1)} %copy-done.34) | copy-start | bytes 1572868
  2396.5 52.3 %copy-start.39 = (bf16[256,1024]{1,0:T(8,128)(2,1)S(1)}, bf16[256,1024]{1,0:T(8,128)(2,1)}, u32[]{:S(2)}) copy-start(bf16[256,1024]{1,0:T(8,128)(2,1)} %get-tuple-element.2804) | copy-start | bytes 1572868
  2396.6 1159.3 %all-reduce.9.cloned.1.call-start = ((), (), s32[]{:S(2)}) async-start(), calls=%async_computation.34 | async-start | bytes 18350080 | tf_op jit(solution)/shard_map/psum | solution.py:430
  2448.8 151.0 %copy-start.110 = (bf16[256,128]{1,0:T(8,128)(2,1)}, bf16[256,128]{1,0:T(8,128)(2,1)S(1)}, u32[]{:S(2)}) copy-start(bf16[256,128]{1,0:T(8,128)(2,1)S(1)} %multiply_convert_fusion.14) | copy-start | bytes 196612
  2448.9 150.9 %copy-start.169 = (f32[256]{0:T(256)S(1)}, f32[256]{0:T(256)}, u32[]{:S(2)}) copy-start(f32[256]{0:T(256)} %copy-done.168) | copy-start | bytes 3076
  2615.9 36.3 %copy-start.125 = (f32[1024,16]{0,1:T(8,128)}, f32[1024,16]{0,1:T(8,128)S(1)}, u32[]{:S(2)}) copy-start(f32[1024,16]{0,1:T(8,128)S(1)} %get-tuple-element.2471) | copy-start | bytes 196612
  2615.9 36.3 %copy-start.127 = (f32[1024,16]{0,1:T(8,128)}, f32[1024,16]{0,1:T(8,128)S(1)}, u32[]{:S(2)}) copy-start(f32[1024,16]{0,1:T(8,128)S(1)} %get-tuple-element.2491) | copy-start | bytes 196612
  2903.2 174.8 %copy-start.130 = (f32[32,32]{1,0:T(8,128)S(1)}, f32[32,32]{1,0:T(8,128)}, u32[]{:S(2)}) copy-start(f32[32,32]{1,0:T(8,128)} %copy-done.129) | copy-start | bytes 12292
  3127.9 44.4 %copy-start.163 = (f32[256]{0:T(256)S(1)}, f32[256]{0:T(256)}, u32[]{:S(2)}) copy-start(f32[256]{0:T(256)} %get-tuple-element.2481) | copy-start | bytes 3076
  3127.9 44.4 %copy-start.162 = (f32[256]{0:T(256)S(1)}, f32[256]{0:T(256)}, u32[]{:S(2)}) copy-start(f32[256]{0:T(256)} %get-tuple-element.2482) | copy-start | bytes 3076
  3127.9 44.5 %copy-start.13 = (f32[256,1024]{1,0:T(8,128)S(1)}, f32[256,1024]{1,0:T(8,128)}, u32[]{:S(2)}) copy-start(f32[256,1024]{1,0:T(8,128)} %copy-done.12) | copy-start | bytes 3145732
  3127.9 44.5 %copy-start.116 = (f32[1024]{0:T(1024)S(1)}, f32[1024]{0:T(1024)}, u32[]{:S(2)}) copy-start(f32[1024]{0:T(1024)} %param.59) | copy-start | bytes 12292
  3127.9 44.5 %copy-start.143 = (f32[256]{0:T(256)S(1)}, f32[256]{0:T(256)}, u32[]{:S(2)}) copy-start(f32[256]{0:T(256)} %copy-done.142) | copy-start | bytes 3076
  3127.9 44.5 %copy-start.154 = (f32[1024]{0:T(1024)S(1)}, f32[1024]{0:T(1024)}, u32[]{:S(2)}) copy-start(f32[1024]{0:T(1024)} %param.63) | copy-start | bytes 12292
  3128.0 44.5 %copy-start.165 = (f32[256]{0:T(256)S(1)}, f32[256]{0:T(256)}, u32[]{:S(2)}) copy-start(f32[256]{0:T(256)} %copy-done.164) | copy-start | bytes 3076
  3172.5 46.5 %copy-start.151 = (f32[256]{0:T(256)S(1)}, f32[256]{0:T(256)}, u32[]{:S(2)}) copy-start(f32[256]{0:T(256)} %copy-done.150) | copy-start | bytes 3076
  3172.5 46.5 %copy-start.167 = (f32[256]{0:T(256)S(1)}, f32[256]{0:T(256)}, u32[]{:S(2)}) copy-start(f32[256]{0:T(256)} %copy-done.166) | copy-start | bytes 3076
  (259 other events, 1507.5 us)
Sparse Core Ops, SparseCore 0:
  778.0 85.3 all-gather.22
  865.5 72.3 all-gather.20
  949.6 147.2 reduce-scatter.12
  1101.6 72.3 all-gather.24
  1176.8 71.6 all-gather.36
  1251.3 71.7 all-gather.28
  1325.4 71.6 all-gather.26
  1401.7 147.2 reduce-scatter.20
  1552.7 148.0 reduce-scatter.16
  1708.1 72.3 all-gather.30
  1782.9 71.6 all-gather.38
  1869.6 147.2 reduce-scatter.28
  2019.1 72.3 all-gather.32
  2093.5 71.6 all-gather.34
  2168.4 61.6 reduce-scatter.26
  2234.1 148.0 reduce-scatter.24
  2385.4 62.3 reduce-scatter.34
  2451.7 148.0 reduce-scatter.32
  2603.4 152.6 reduce-scatter.22
  2760.1 154.3 reduce-scatter.30
  2918.0 148.0 reduce-scatter.14
  3070.2 148.6 reduce-scatter.18
  3221.7 136.3 all-reduce.10
  3366.1 189.7 all-reduce.8
where the time goes:
time: 3600 us; the launch traced here: 3580 us
  waiting for transfers between devices  1840 us (51%)
  other arithmetic  760 us (21%)
  blocking collectives  440 us (12%)
  local copies, waits for them, and re-layouts  312 us (9%)
  matrix products  201 us (6%)
    reduce_scatter x2, waiting for transfers between devices, local(): lax.psum_scatter(dot_plain(gated_low, branch_weight), 'tensor', scatter_d...  297 us
    all_gather x6, blocking collectives, carried_in(): everything = jax.tree.map(lambda part: lax.all_gather(part, axis), value)  291 us
    reduce_scatter x2, waiting for transfers between devices, local(): lax.psum_scatter(grad_ffn_part, 'tensor', scatter_dimension=0, tiled=True)  287 us
    reduce_scatter x2, waiting for transfers between devices, local(): lax.psum_scatter(grad_mixed_part, 'tensor', scatter_dimension=0, tiled=True)  271 us
    psum x1, waiting for transfers between devices, local(): lax.psum((totals['norm_gain'], totals['ema_alpha'], totals['ema_damp'], t...  198 us
    all_gather x2, waiting for transfers between devices, local(): ffn_rows = lax.all_gather(ffn_low, 'tensor', axis=0, tiled=True)  140 us
    all_gather x2, waiting for transfers between devices, local(): lax.all_gather(cotangent[micro_index], 'tensor', axis=0, tiled=True)  135 us
    dynamic_update_slice x80, other arithmetic, ema_local(): lax.scan(partial(ema_block, tables), start_state, (normed.reshape(block_c...  134 us
  transfers between devices with their start and end apart: 24, of which 19 were waited for; matrix products, arithmetic and copies ran while one was open for 18% of the time, Pallas kernels for 0%

commit v1 on v0

v1 whole, which is shorter than its diff:
```python
from functools import partial

import jax
import jax.numpy as jnp
from jax import lax
from jax.experimental import pallas as pl
from jax.experimental.pallas import tpu as pltpu
from jax.sharding import PartitionSpec as P

BLOCK = 128
HIGHEST = lax.Precision.HIGHEST
EPSILON = 1e-06
AXES = ("dp", "tensor")
F32 = jnp.float32
BF16 = jnp.bfloat16


def dot_plain(a, b):
    return jnp.dot(a, b, preferred_element_type=F32)


def dot_against(a, b):
    return lax.dot_general(a, b, (((1,), (1,)), ((), ())), preferred_element_type=F32)


def dot_over_rows(a, b):
    return lax.dot_general(a, b, (((0,), (0,)), ((), ())), preferred_element_type=F32)


def rounded(v):
    return lax.reduce_precision(v, exponent_bits=8, mantissa_bits=7)


def silu_slope(v):
    s = jax.nn.sigmoid(v)
    return s * (1.0 + v * (1.0 - s))


class Grid:
    def __init__(self):
        dp, tensor = lax.axis_size("dp"), lax.axis_size("tensor")
        self.size = {"x": dp // 2, "c": 2, "z": 4, "y": tensor // 4}
        d, t = lax.axis_index("dp"), lax.axis_index("tensor")
        self.at = {"x": d // 2, "c": d % 2, "z": t // self.size["y"], "y": t % self.size["y"]}

    def send(self, value, digit, shift, wrap=True):
        n = self.size
        pairs = []
        for x in range(n["x"]):
            for c in range(n["c"]):
                for z in range(n["z"]):
                    for y in range(n["y"]):
                        here = {"x": x, "c": c, "z": z, "y": y}
                        there = dict(here)
                        there[digit] = here[digit] + shift
                        if not wrap and not 0 <= there[digit] < n[digit]:
                            continue
                        there[digit] %= n[digit]
                        pairs.append(tuple(
                            ((k["x"] * n["c"] + k["c"]) * n["z"] + k["z"]) * n["y"] + k["y"]
                            for k in (here, there)
                        ))
        return lax.ppermute(value, AXES, pairs)


def ema_step(state, row, keep, decay, feed):
    return [(s * keep) * q + f * row for s, q, f in zip(state, decay, feed)]


def row_of(ref, base, r):
    return ref[pl.ds(base + r, 8, stride=8), :]


def spread(ref, block, values):
    for j in range(8):
        ref[pl.ds(pl.multiple_of(block * 64, 64) + 8 * j, 8), :] = values[:, j * 128 : (j + 1) * 128]


def collect(ref, block):
    return jnp.concatenate(
        [ref[pl.ds(pl.multiple_of(block * 64, 64) + 8 * j, 8), :] for j in range(8)], axis=1
    )


def norm_kernel(flags, x_ref, gain_ref, decay_ref, feed_ref, normed_ref, low_ref, final_ref):
    micros, rows = flags.shape
    heads = decay_ref.shape[0]

    def norm_block(b, carry):
        at = pl.ds(pl.multiple_of(b * 16, 16), 16)
        x = x_ref[at, :].astype(F32)
        n = x * lax.rsqrt(jnp.mean(x * x, axis=-1, keepdims=True) + EPSILON) * gain_ref[...]
        low_ref[at, :] = n.astype(BF16)
        spread(normed_ref, 2 * b, n[:8])
        spread(normed_ref, 2 * b + 1, n[8:])
        return carry

    lax.fori_loop(0, micros * rows // 16, norm_block, 0)
    for m in range(micros):
        for h0 in range(0, heads, 8):
            decay = [decay_ref[h0 + h] for h in range(8)]
            feed = [feed_ref[h0 + h] for h in range(8)]

            def block(b, state, m=m, decay=decay, feed=feed):
                base = pl.multiple_of((m * (rows // 8) + b) * 64, 64)
                for r in range(8):
                    keep = (1 - flags[m, b * 8 + r]).astype(F32)
                    state = ema_step(state, row_of(normed_ref, base, r), keep, decay, feed)
                return state

            state = lax.fori_loop(0, rows // 8, block, [jnp.zeros((8, 128), F32)] * 8)
            for h in range(8):
                final_ref[m, h0 + h] = state[h]


def blend_kernel(
    flags, normed_ref, start_ref, decay_ref, feed_ref, out_ref, omega_ref, blended_ref, low_ref, acc_ref
):
    micros, rows = flags.shape
    heads = decay_ref.shape[0]
    omega = omega_ref[...]
    for m in range(micros):
        for h0 in range(0, heads, 8):
            decay = [decay_ref[h0 + h] for h in range(8)]
            feed = [feed_ref[h0 + h] for h in range(8)]
            tell = [out_ref[h0 + h] for h in range(8)]

            def block(b, state, m=m, h0=h0, decay=decay, feed=feed, tell=tell):
                base = pl.multiple_of((m * (rows // 8) + b) * 64, 64)
                for r in range(8):
                    keep = (1 - flags[m, b * 8 + r]).astype(F32)
                    row = row_of(normed_ref, base, r)
                    state = ema_step(state, row, keep, decay, feed)
                    told = [s * t for s, t in zip(state, tell)]
                    while len(told) > 1:
                        told = [told[i] + told[i + 1] for i in range(0, len(told), 2)]
                    at = pl.ds(base + r, 8, stride=8)
                    if h0 == 0:
                        acc_ref[at, :] = told[0] + omega * row
                    else:
                        acc_ref[at, :] = acc_ref[at, :] + told[0]
                return state

            lax.fori_loop(0, rows // 8, block, [start_ref[m, h0 + h] for h in range(8)])

    def finish(b, carry):
        at = pl.ds(pl.multiple_of(b * 16, 16), 16)
        v = jnp.concatenate([collect(acc_ref, 2 * b), collect(acc_ref, 2 * b + 1)], axis=0)
        blended_ref[at, :] = v
        low_ref[at, :] = (v / (1.0 + jnp.exp(-v))).astype(BF16)
        return carry

    lax.fori_loop(0, micros * rows // 16, finish, 0)


def back_first_kernel(flags, grad_ref, decay_ref, tell_ref, left_ref, rows_ref):
    micros, rows = flags.shape
    heads = decay_ref.shape[0]

    def lay(b, carry):
        spread(rows_ref, b, grad_ref[pl.ds(pl.multiple_of(b * 8, 8), 8), :])
        return carry

    lax.fori_loop(0, micros * rows // 8, lay, 0)
    for m in range(micros):
        for h0 in range(0, heads, 8):
            decay = [decay_ref[h0 + h] for h in range(8)]
            tell = [tell_ref[h0 + h] for h in range(8)]

            def block(i, left, m=m, decay=decay, tell=tell):
                b = rows // 8 - 1 - i
                base = pl.multiple_of((m * (rows // 8) + b) * 64, 64)
                for r in reversed(range(8)):
                    keep = (1 - flags[m, b * 8 + r]).astype(F32)
                    row = row_of(rows_ref, base, r)
                    left = [((t * row + k) * keep) * q for k, q, t in zip(left, decay, tell)]
                return left

            left = lax.fori_loop(0, rows // 8, block, [jnp.zeros((8, 128), F32)] * 8)
            for h in range(8):
                left_ref[m, h0 + h] = left[h]


def back_kernel(
    flags, normed_ref, rows_ref, start_ref, right_ref, decay_ref, feed_ref, tell_ref,
    grad_ref, eta_ref, one_ref, two_ref, states, acc_ref,
):
    micros, rows = flags.shape
    heads = decay_ref.shape[0]
    group = 4
    for m in range(micros):
        for h0 in range(0, heads, group):
            decay = [decay_ref[h0 + h] for h in range(group)]
            feed = [feed_ref[h0 + h] for h in range(group)]
            tell = [tell_ref[h0 + h] for h in range(group)]

            def ahead(b, state, m=m, decay=decay, feed=feed):
                base = pl.multiple_of((m * (rows // 8) + b) * 64, 64)
                for r in range(8):
                    keep = (1 - flags[m, b * 8 + r]).astype(F32)
                    for h in range(group):
                        states[b * 8 + r, h] = state[h]
                    state = ema_step(state, row_of(normed_ref, base, r), keep, decay, feed)
                return state

            last = lax.fori_loop(0, rows // 8, ahead, [start_ref[m, h0 + h] for h in range(group)])

            def back(i, carry, m=m, h0=h0, decay=decay, feed=feed, tell=tell):
                left, after, eta, one, two = carry
                b = rows // 8 - 1 - i
                base = pl.multiple_of((m * (rows // 8) + b) * 64, 64)
                for r in reversed(range(8)):
                    keep = (1 - flags[m, b * 8 + r]).astype(F32)
                    g = row_of(rows_ref, base, r)
                    x = row_of(normed_ref, base, r)
                    before = [states[b * 8 + r, h] for h in range(group)]
                    eta = [e + s * g for e, s in zip(eta, after)]
                    now = [t * g + k for t, k in zip(tell, left)]
                    one = [o + n * x for o, n in zip(one, now)]
                    kept = [n * keep for n in now]
                    two = [w + k * s for w, k, s in zip(two, kept, before)]
                    left = [k * q for k, q in zip(kept, decay)]
                    gn = [n * f for n, f in zip(now, feed)]
                    while len(gn) > 1:
                        gn = [gn[i] + gn[i + 1] for i in range(0, len(gn), 2)]
                    at = pl.ds(base + r, 8, stride=8)
                    if h0 == 0:
                        acc_ref[at, :] = gn[0]
                    else:
                        acc_ref[at, :] = acc_ref[at, :] + gn[0]
                    after = before
                return left, after, eta, one, two

            zero = [jnp.zeros((8, 128), F32)] * group
            if m == 0:
                sums = (zero, zero, zero)
            else:
                sums = tuple([ref[h0 + h] for h in range(group)] for ref in (eta_ref, one_ref, two_ref))
            right = [right_ref[m, h0 + h] for h in range(group)]
            _, _, eta, one, two = lax.fori_loop(0, rows // 8, back, (right, last, *sums))
            for h in range(group):
                eta_ref[h0 + h] = eta[h]
                one_ref[h0 + h] = one[h]
                two_ref[h0 + h] = two[h]

    def finish(b, carry):
        grad_ref[pl.ds(pl.multiple_of(b * 8, 8), 8), :] = collect(acc_ref, b)
        return carry

    lax.fori_loop(0, micros * rows // 8, finish, 0)


def call(kernel, outs, scratch, smem, *arrays):
    return pl.pallas_call(
        kernel,
        out_shape=outs,
        in_specs=[pl.BlockSpec(memory_space=pltpu.SMEM)] * smem
        + [pl.BlockSpec(memory_space=pltpu.VMEM)] * (len(arrays) - smem),
        out_specs=jax.tree.map(lambda _: pl.BlockSpec(memory_space=pltpu.VMEM), outs),
        scratch_shapes=scratch,
    )(*arrays)


def scan_carry(grid, local, clear, whole, reverse):
    sign = -1 if reverse else 1
    micros, heads = local.shape[:2]
    flag = jnp.broadcast_to(clear[:, None, None, None], (micros, 1, 8, 128))
    pack = jnp.concatenate([local, flag], axis=1)
    n = grid.size["y"]
    near = [pack] + [grid.send(pack, "y", sign * r) for r in range(1, n)]
    stack = jnp.stack(near)
    at = grid.at["y"] if not reverse else n - 1 - grid.at["y"]
    ordered = [lax.dynamic_index_in_dim(stack, (at - a) % n, 0, False) for a in range(n)]
    inner = jnp.zeros_like(local)
    through = jnp.ones((micros, 1, 8, 128), F32)
    mine, reach = inner, through
    power = jnp.ones_like(whole)
    mine_power = power
    for a in range(n):
        mine = jnp.where(at == a, inner, mine)
        reach = jnp.where(at == a, through, reach)
        mine_power = jnp.where(at == a, power, mine_power)
        inner = ordered[a][:, :heads] + ordered[a][:, heads:] * whole * inner
        through = through * ordered[a][:, heads:]
        power = power * whole
    pack = jnp.concatenate([inner, through], axis=1)
    entering = jnp.zeros_like(local)
    factor = jnp.ones((micros, 1, 8, 128), F32)
    scale = jnp.ones_like(whole)
    for k in range(1, grid.size["z"]):
        got = grid.send(pack, "z", sign * k, wrap=False)
        entering = entering + factor * scale * got[:, :heads]
        factor = factor * got[:, heads:]
        scale = scale * power
    return mine + reach * mine_power * entering


def gather_units(grid, seed, split_x):
    parts = {(0, 0): {(0, 0): seed}}
    for k in range(1, grid.size["z"]):
        parts[k, 0] = {(0, 0): grid.send(seed, "z", k)}
    for kz in range(grid.size["z"]):
        for k in range(1, grid.size["y"]):
            parts[kz, k] = {(0, 0): grid.send(parts[kz, 0][0, 0], "y", k)}
    if split_x:
        for key in parts:
            parts[key][0, 1] = grid.send(parts[key][0, 0], "x", 1)
    for key in parts:
        for kx in range(2 if split_x else 1):
            parts[key][1, kx] = grid.send(parts[key][0, kx], "c", 1)
    return parts


def in_order(parts):
    return [parts[key][sub] for key in sorted(parts) for sub in sorted(parts[key])]


def scatter_sum(grid, value, stages):
    for digit, axis, relative in stages:
        n = grid.size[digit]
        at = grid.at[digit]

        def part(r, value=value, axis=axis, relative=relative, n=n, at=at):
            if relative:
                return lax.index_in_dim(value, r, axis, True)
            return lax.dynamic_slice_in_dim(value, (at - r) % n, 1, axis)

        total = part(0).astype(F32)
        for r in range(1, n):
            total = total + grid.send(part(r), digit, -r).astype(F32)
        value = total.astype(BF16)
    return value


def local(
    inputs, resets, cotangent, norm_gain, ema_alpha, ema_damp, ema_beta, ema_eta, ema_omega,
    w_gates, b_gates, qk_gain, q_bias, w_value, b_value, w_reset, b_reset, w_branch, ffn_gain,
    w_in, b_in, w_out, b_out,
):
    grid = Grid()
    size, at = grid.size, grid.at
    micros, rows, width = inputs.shape
    total = micros * rows
    heads = ema_alpha.shape[1]
    rank = lax.axis_index("tensor")
    units_v, units_f = w_value.shape[1], w_in.shape[1]
    n_tensor = lax.axis_size("tensor")
    split_x = size["x"] == 2

    half_v = units_v // 2
    part_f = units_f // (4 if split_x else 2)
    off_v = at["c"] * half_v
    off_f = (at["c"] * 2 + at["x"] if split_x else at["c"]) * part_f
    cols = lambda w, o, n: lax.dynamic_slice_in_dim(w, o, n, 1)
    rws = lambda w, o, n: lax.dynamic_slice_in_dim(w, o, n, 0)
    seed_vr = jnp.concatenate([cols(w_value, off_v, half_v), cols(w_reset, off_v, half_v)], axis=0)
    got_vr = in_order(gather_units(grid, seed_vr, False))
    got_b = in_order(gather_units(grid, rws(w_branch, off_v, half_v), False))
    got_i = in_order(gather_units(grid, cols(w_in, off_f, part_f), split_x))
    got_o = in_order(gather_units(grid, rws(w_out, off_f, part_f), split_x))
    all_value = jnp.concatenate([p[:width] for p in got_vr], axis=1)
    all_reset = jnp.concatenate([p[width:] for p in got_vr], axis=1)
    all_branch = jnp.concatenate(got_b, axis=0)
    all_in = jnp.concatenate(got_i, axis=1)
    all_out = jnp.concatenate(got_o, axis=0)

    table = lax.all_gather(
        jnp.concatenate([b_value, b_reset, b_in])[None], "tensor", axis=0, tiled=True
    ).astype(F32)
    zs = [(at["z"] - k) % size["z"] for k in range(size["z"])]
    ys = [(at["y"] - k) % size["y"] for k in range(size["y"])]
    owners = jnp.stack([z * size["y"] + y for z in zs for y in ys])
    subs_v = jnp.stack([at["c"], 1 - at["c"]])
    subs_f = (
        jnp.stack([c * 2 + x for c in (at["c"], 1 - at["c"]) for x in (at["x"], 1 - at["x"])])
        if split_x
        else subs_v
    )
    place_v = (owners[:, None] * 2 + subs_v[None]).reshape(-1)
    n_f = 4 if split_x else 2
    place_f = (owners[:, None] * n_f + subs_f[None]).reshape(-1)
    bias_v = jnp.take(table[:, :units_v].reshape(-1, half_v), place_v, axis=0).reshape(1, -1)
    bias_r = jnp.take(table[:, units_v : 2 * units_v].reshape(-1, half_v), place_v, axis=0).reshape(1, -1)
    bias_i = jnp.take(table[:, 2 * units_v :].reshape(-1, part_f), place_f, axis=0).reshape(1, -1)

    offsets = rank * rows + jnp.arange(rows)
    flags = jnp.where(offsets[None] == 0, 1, resets).astype(jnp.int32)
    tile = lambda a: a.T.reshape(heads, 8, 128)
    decay = tile(1.0 - ema_alpha * ema_damp)
    feed = tile(ema_alpha * ema_beta)
    tell = tile(ema_eta)
    whole = jnp.exp(rows * jnp.log(decay))[None]
    clear = (jnp.sum(flags, axis=1) == 0).astype(F32)
    source_low = inputs.reshape(total, width)
    laid = jax.ShapeDtypeStruct((total * 8, 128), F32)
    wide = jax.ShapeDtypeStruct((total, width), F32)
    wide_low = jax.ShapeDtypeStruct((total, width), BF16)
    states = jax.ShapeDtypeStruct((micros, heads, 8, 128), F32)
    sums = jax.ShapeDtypeStruct((heads, 8, 128), F32)
    normed_laid, normed_low, final = call(
        norm_kernel, (laid, wide_low, states), [], 1,
        flags, source_low, norm_gain[None], decay, feed,
    )
    start = scan_carry(grid, final, clear, whole, False)
    blended, mixed_low = call(
        blend_kernel, (wide, wide_low), [pltpu.VMEM((total * 8, 128), F32)], 1,
        flags, normed_laid, start, decay, feed, tell, ema_omega.reshape(8, 128),
    )

    source = source_low.astype(F32)
    scale_in = lax.rsqrt(jnp.mean(source * source, axis=-1, keepdims=True) + EPSILON)
    gate_pre = dot_plain(mixed_low, w_gates) + b_gates
    update = jax.nn.sigmoid(gate_pre[:, :width])
    direct = gate_pre[:, width : 2 * width]
    shared_pre = gate_pre[:, 2 * width :]
    shared = rounded(jax.nn.silu(shared_pre))
    query = (shared * qk_gain[0] + q_bias).astype(BF16)
    key = (shared * qk_gain[1]).astype(BF16)
    blocks = total // BLOCK
    doc = jnp.cumsum(flags.reshape(blocks, BLOCK), axis=1)
    order = jnp.arange(BLOCK)
    allowed = (doc[:, :, None] == doc[:, None, :]) & (order[:, None] >= order[None, :])[None]
    score_scale = query.shape[-1] ** (-0.5)
    query_b, key_b = query.reshape(blocks, BLOCK, -1), key.reshape(blocks, BLOCK, -1)
    scores = jnp.einsum("cik,cjk->cij", query_b, key_b, preferred_element_type=F32) * score_scale
    scores = jnp.where(allowed, scores, -1000000000.0)
    probs = jax.nn.softmax(scores, axis=-1)
    probs_low = probs.astype(BF16)

    value_pre = dot_plain(normed_low, all_value) + bias_v
    value_low = jax.nn.silu(value_pre).astype(BF16)
    reset_pre = dot_plain(mixed_low, all_reset) + bias_r
    reset_gate = jax.nn.silu(reset_pre)
    value_b = value_low.reshape(blocks, BLOCK, -1)
    attended = jnp.einsum(
        "cij,cjv->civ", probs_low, value_b, preferred_element_type=F32
    ).reshape(total, -1)
    gated_low = (reset_gate * attended).astype(BF16)
    branch = dot_plain(gated_low, all_branch)
    pre_hidden = direct + branch
    hidden = jax.nn.silu(pre_hidden)
    mixed_out = update * hidden + (1.0 - update) * source
    scale_mid = lax.rsqrt(jnp.mean(mixed_out * mixed_out, axis=-1, keepdims=True) + EPSILON)
    ffn_low = (mixed_out * scale_mid * ffn_gain).astype(BF16)
    pre_act = dot_plain(ffn_low, all_in) + bias_i
    activ_low = jax.nn.silu(pre_act).astype(BF16)
    grad_low = cotangent.reshape(total, width)
    grad_out = grad_low.astype(F32)
    feed_out = dot_plain(activ_low, all_out)
    output = (mixed_out + feed_out + b_out).astype(BF16)

    n_z, n_y, n_x = size["z"], size["y"], size["x"]

    def sum_f(d, order):
        if split_x:
            d = d.reshape(n_z, n_y, 2, 2, part_f, width)
        else:
            d = d.reshape(n_z, n_y, 2, n_x, part_f // n_x, width)
        kinds = {"c": ("c", 2, True), "x": ("x", 3, split_x), "y": ("y", 1, True), "z": ("z", 0, True)}
        d = scatter_sum(grid, d, [kinds[k] for k in order])
        d = d.reshape(-1, width)
        everyone = lax.all_gather(d, "dp", axis=0, tiled=False)
        everyone = everyone.reshape(n_x, 2, -1, width).transpose(1, 0, 2, 3)
        return everyone.reshape(units_f, width).astype(F32)

    def sum_v(d, order):
        d = d.reshape(n_z, n_y, 2, n_x, half_v // n_x, width)
        kinds = {"c": ("c", 2, True), "x": ("x", 3, False), "y": ("y", 1, True), "z": ("z", 0, True)}
        d = scatter_sum(grid, d, [kinds[k] for k in order])
        d = d.reshape(-1, width)
        everyone = lax.all_gather(d, "dp", axis=0, tiled=False)
        everyone = everyone.reshape(n_x, 2, -1, width).transpose(1, 0, 2, 3)
        return everyone.reshape(units_v, width).astype(F32)

    grad_w_out = sum_f(dot_over_rows(activ_low, grad_low).astype(BF16), "cxyz")
    grad_act = dot_against(grad_low, all_out)
    grad_pre_low = (grad_act * silu_slope(pre_act)).astype(BF16)
    grad_w_in = sum_f(dot_over_rows(grad_pre_low, ffn_low).astype(BF16), "cyxz").T
    sum_b_in = jnp.sum(rounded(grad_act * silu_slope(pre_act)), axis=0)
    grad_ffn = dot_against(grad_pre_low, all_in)

    scaled = mixed_out * scale_mid
    sum_ffn_gain = jnp.sum(grad_ffn * scaled, axis=0)
    inner = grad_ffn * ffn_gain
    grad_mixed = (
        grad_out + scale_mid * (inner - scaled * jnp.mean(inner * scaled, axis=-1, keepdims=True))
    )
    grad_source = grad_mixed * (1.0 - update)
    grad_update_pre = grad_mixed * (hidden - source) * update * (1.0 - update)
    grad_hidden_pre = grad_mixed * update * silu_slope(pre_hidden)
    grad_hidden_low = grad_hidden_pre.astype(BF16)
    grad_gated = dot_against(grad_hidden_low, all_branch)
    grad_w_branch = sum_v(dot_over_rows(gated_low, grad_hidden_low).astype(BF16), "cxyz")
    grad_attended_low = (grad_gated * reset_gate).astype(BF16)
    grad_reset_low = (grad_gated * attended * silu_slope(reset_pre)).astype(BF16)
    grad_w_reset = sum_v(dot_over_rows(grad_reset_low, mixed_low).astype(BF16), "cyxz").T
    sum_b_reset = jnp.sum(rounded(grad_gated * attended * silu_slope(reset_pre)), axis=0)
    grad_b = grad_attended_low.reshape(blocks, BLOCK, -1)
    grad_probs = jnp.einsum("civ,cjv->cij", grad_b, value_b, preferred_element_type=F32)
    grad_value = jnp.einsum(
        "cij,civ->cjv", probs_low, grad_b, preferred_element_type=F32
    ).reshape(total, -1)
    grad_value_low = (grad_value * silu_slope(value_pre)).astype(BF16)
    grad_w_value = sum_v(dot_over_rows(grad_value_low, normed_low).astype(BF16), "cxyz").T
    sum_b_value = jnp.sum(rounded(grad_value * silu_slope(value_pre)), axis=0)
    grad_scores = (
        probs * (grad_probs - jnp.sum(grad_probs * probs, axis=-1, keepdims=True)) * score_scale
    )
    grad_query = jnp.einsum(
        "cij,cjk->cik", grad_scores, key_b.astype(F32), precision=HIGHEST
    ).reshape(total, -1)
    grad_key = jnp.einsum(
        "cij,cik->cjk", grad_scores, query_b.astype(F32), precision=HIGHEST
    ).reshape(total, -1)
    sum_qk = jnp.stack([jnp.sum(grad_query * shared, axis=0), jnp.sum(grad_key * shared, axis=0)])
    sum_q_bias = jnp.sum(grad_query, axis=0)
    grad_shared_pre = (grad_query * qk_gain[0] + grad_key * qk_gain[1]) * silu_slope(shared_pre)
    grad_gates = rounded(
        jnp.concatenate([grad_update_pre, grad_hidden_pre, grad_shared_pre], axis=1)
    )
    grad_gates_low = grad_gates.astype(BF16)
    sum_b_gates = jnp.sum(grad_gates, axis=0)
    d_gates = dot_over_rows(mixed_low, grad_gates_low).astype(BF16)
    n_all = n_x * 2 * n_tensor
    d_gates = d_gates.reshape(n_x, 2, n_z, n_y, width // n_all, -1)
    d_gates = scatter_sum(
        grid, d_gates, [("c", 1, False), ("y", 3, False), ("x", 0, False), ("z", 2, False)]
    ).reshape(width // n_all, -1)
    grad_w_gates = lax.all_gather(d_gates, AXES, axis=0, tiled=True).astype(F32)
    grad_mixed_in = dot_against(grad_reset_low, all_reset) + dot_against(grad_gates_low, w_gates)
    grad_blended = grad_mixed_in * silu_slope(blended)
    left, grad_laid = call(
        back_first_kernel, (states, laid), [], 1, flags, grad_blended, decay, tell
    )
    right = scan_carry(grid, left, clear, whole, True)
    grad_normed_ema, sum_eta, sum_one, sum_two = call(
        back_kernel, (wide, sums, sums, sums),
        [pltpu.VMEM((rows, 4, 8, 128), F32), pltpu.VMEM((total * 8, 128), F32)], 1,
        flags, normed_laid, grad_laid, start, right, decay, feed, tell,
    )
    grad_normed = (
        dot_against(grad_value_low, all_value) + grad_blended * ema_omega + grad_normed_ema
    )
    scaled_in = source * scale_in
    normed = scaled_in * norm_gain
    sum_omega = jnp.sum(grad_blended * normed, axis=0)
    sum_norm_gain = jnp.sum(grad_normed * scaled_in, axis=0)
    inner = grad_normed * norm_gain
    grad_inputs = grad_source + scale_in * (
        inner - scaled_in * jnp.mean(inner * scaled_in, axis=-1, keepdims=True)
    )

    put = lambda v, place: jnp.zeros((place.size, v.size // place.size), F32).at[place].set(
        v.reshape(place.size, -1)
    ).reshape(-1)
    pieces = [
        sum_eta.reshape(-1), sum_one.reshape(-1), sum_two.reshape(-1),
        sum_norm_gain, sum_omega, sum_b_gates, sum_qk.reshape(-1), sum_q_bias, sum_ffn_gain,
        jnp.sum(grad_out, axis=0),
        put(sum_b_value, place_v), put(sum_b_reset, place_v), put(sum_b_in, place_f),
    ]
    packed = lax.psum(jnp.concatenate(pieces).reshape(-1, 128), AXES).reshape(-1)
    cut, at_piece = [], 0
    for p in pieces:
        cut.append(packed[at_piece : at_piece + p.size])
        at_piece += p.size
    untile = lambda v: v.reshape(heads, width).T
    eta, one, two = (untile(v) for v in cut[:3])
    own = lambda v, n: lax.dynamic_slice_in_dim(v, rank * n, n, 0)
    return (
        output.reshape(inputs.shape),
        grad_inputs.reshape(inputs.shape),
        cut[3],
        ema_beta * one - ema_damp * two,
        -ema_alpha * two,
        ema_alpha * one,
        eta,
        cut[4],
        grad_w_gates,
        cut[5],
        cut[6].reshape(2, -1),
        cut[7],
        grad_w_value,
        own(cut[10], units_v),
        grad_w_reset,
        own(cut[11], units_v),
        grad_w_branch,
        cut[8],
        grad_w_in,
        own(cut[12], units_f),
        grad_w_out,
        cut[9],
    )


def solution(mesh):
    rows = P(None, AXES, None)
    col, row, vec, rep = P(None, "tensor"), P("tensor", None), P("tensor"), P()
    return jax.shard_map(
        local,
        mesh=mesh,
        in_specs=(
            rows, P(None, AXES), rows, rep, rep, rep, rep, rep, rep, rep, rep, rep, rep,
            col, vec, col, vec, row, rep, col, vec, row, rep,
        ),
        out_specs=(
            rows, rows, rep, rep, rep, rep, rep, rep, rep, rep, rep, rep,
            col, vec, col, vec, row, rep, col, vec, row, rep,
        ),
        check_vma=False,
    )
```

time: 3600 us -> 907 us (0.25)
  waiting for transfers between devices: 1840 us -> 284 us
  other arithmetic: 760 us -> 77.5 us
  blocking collectives: 440 us -> 48 us
  local copies, waits for them, and re-layouts: 312 us -> 138 us
  starting transfers between devices: 2.45 us -> 137 us
  matrix products: 201 us -> 132 us
  Pallas kernels: 0 us -> 62 us
    reduce_scatter x12 -> x0, waiting for transfers between devices: 948 us -> none  [the longest x2 297 us: local(): lax.psum_scatter(dot_plain(gated_low, branch_weight), 'tensor', scatter_d...]
    all_gather x10 -> x3, waiting for transfers between devices: 555 us -> 0.01 us  [the longest x2 0.01 us: sum_f(): everyone = lax.all_gather(d, 'dp', axis=0, tiled=False)]
    reduce_sum x99 -> x6, other arithmetic: 423 us -> 7.16 us  [the longest x1 3.18 us: local(): sum_b_value = jnp.sum(rounded(grad_value * silu_slope(value_pre)), axis=0)]
    all_gather x10 -> x4, blocking collectives: 394 us -> 48 us  [the longest x1 26.3 us: local(): lax.all_gather(jnp.concatenate([b_value, b_reset, b_in])[None], 'tensor',...]
    psum x2 -> x1, waiting for transfers between devices: 330 us -> 43.9 us  [local(): lax.psum(jnp.concatenate(pieces).reshape(-1, 128), AXES).reshape(-1)]
    ppermute x0 -> x136, waiting for transfers between devices: none -> 240 us  [send(): return lax.ppermute(value, AXES, pairs)]
    ppermute x0 -> x136, starting transfers between devices: none -> 136 us  [send(): return lax.ppermute(value, AXES, pairs)]
    dynamic_update_slice x80 -> x0, other arithmetic: 134 us -> none  [ema_local(): lax.scan(partial(ema_block, tables), start_state, (normed.reshape(block_c...]
  transfers between devices with their start and end apart: 24 -> 140, of which waited for: 19 -> 50; matrix products, arithmetic and copies ran while one was open for 18% -> 24% of each run, Pallas kernels for 0% -> 6%
where the time goes in v1:
time: 907 us; the launch traced here: 897 us
  waiting for transfers between devices  284 us (31%)
  local copies, waits for them, and re-layouts  138 us (15%)
  starting transfers between devices  137 us (15%)
  matrix products  132 us (15%)
  other arithmetic  77.5 us (9%)
  Pallas kernels  62 us (7%)
  blocking collectives  48 us (5%)
  between operations  18.5 us (2%)
    ppermute x136, waiting for transfers between devices, send(): return lax.ppermute(value, AXES, pairs)  240 us
    ppermute x136, starting transfers between devices, send(): return lax.ppermute(value, AXES, pairs)  136 us
    unnamed x319, local copies, waits for them, and re-layouts  85.8 us
    pallas_call x4, Pallas kernels, call(): pl.pallas_call(kernel, out_shape=outs, in_specs=[pl.BlockSpec(memory_spac...  62 us
    dot_general x6, matrix products, dot_against(): lax.dot_general(a, b, (((1,), (1,)), ((), ())), preferred_element_type=F32)  49.6 us
    psum x1, waiting for transfers between devices, local(): lax.psum(jnp.concatenate(pieces).reshape(-1, 128), AXES).reshape(-1)  43.9 us
    convert_element_type x24, other arithmetic, scatter_sum(): value = total.astype(BF16)  40.8 us
    dot_general x6, matrix products, dot_plain(): return jnp.dot(a, b, preferred_element_type=F32)  39.2 us
  transfers between devices with their start and end apart: 140, of which 50 were waited for; matrix products, arithmetic and copies ran while one was open for 24% of the time, Pallas kernels for 6%

profile of v1, /device:TPU:0, one launch (start us, length us, event | category | flops | bytes accessed | tf_op | source)
XLA Modules:
  0.0 897.3 jit_solution(2346282180063863216)
XLA Ops:
  19.4 11.7 %shard_map.390 = (f32[4096,128]{1,0:T(8,128)}, bf16[512,1024]{1,0:T(8,128)(2,1)}, f32[2,16,8,128]{3,2,1,0:T(8,128)}) custom-call(s32[2,256]{1,0:T(2,128)} %get-tuple-element.135.flags, bf16[512,1024]{1,0:T(8,128)(2,1)} %bitcast.274, f32[1,1024]{1,0:T(1,128)} %bitcast.331, f32[16,8,128]{2,1,0:T(8,128)} %bitcast.299, f32[16,8,128]{2,1,0:T(8,128)} %bitcast.313), custom_call_target="tpu_custom_call" | custom-call | tf_op jit(solution)/shard_map/pallas_call | solution.py:254
  35.3 26.3 %all-gather = bf16[8192]{0:T(1024)(128)(2,1)S(1)} all-gather(bf16[1024]{0:T(1024)(128)(2,1)S(1)} %pad_maximum_fusion.5), channel_id=2, replica_groups=mesh['dp'=4,'tensor'=8] {'tensor'}, dimensions={0}, use_global_device_ids=true | all-gather | bytes 18432 | tf_op jit(solution)/shard_map/all_gather | solution.py:367
  92.6 5.4 collective-permute-start.3
  98.0 7.7 collective-permute-done.3
  105.7 4.3 collective-permute-start.30
  110.7 12.5 %shard_map.391 = (f32[512,1024]{1,0:T(8,128)}, bf16[512,1024]{1,0:T(8,128)(2,1)}) custom-call(s32[2,256]{1,0:T(2,128)} %get-tuple-element.135.flags, f32[4096,128]{1,0:T(8,128)} %get-tuple-element.34.normed_ref, f32[2,16,8,128]{3,2,1,0:T(8,128)} %fusion.56.start_ref, f32[16,8,128]{2,1,0:T(8,128)} %bitcast.300, f32[16,8,128]{2,1,0:T(8,128)} %bitcast.314, ...), custom_call_target="tpu_custom_call" | custom-call | tf_op jit(solution)/shard_map/pallas_call | solution.py:254
  123.3 5.3 convolution_add_fusion
  147.3 4.5 collective-permute-done.24
  156.9 3.5 collective-permute-done.38
  200.0 4.6 collective-permute-done.77
  228.6 3.5 collective-permute-start.11
  232.2 17.4 %collective-permute-done.49 = bf16[1024,128]{1,0:T(8,128)(2,1)S(1)} collective-permute-done((bf16[1024,128]{1,0:T(8,128)(2,1)S(1)}, bf16[1024,128]{1,0:T(8,128)(2,1)S(1)}, u32[]{:S(2)}, u32[]{:S(2)}) %collective-permute-start.49) | collective-permute-done | bytes 262176 | tf_op jit(solution)/shard_map/ppermute | solution.py:63
  254.7 8.8 collective-permute-done.50
  282.9 3.9 collective-permute-start.15
  292.5 4.6 collective-permute-done.93
  301.8 4.4 collective-permute-done.61
  312.6 4.9 collective-permute-done.9
  319.7 9.0 %collective-permute-done.13 = bf16[2048,128]{1,0:T(8,128)(2,1)S(1)} collective-permute-done((bf16[2048,128]{1,0:T(8,128)(2,1)S(1)}, bf16[2048,128]{1,0:T(8,128)(2,1)S(1)}, u32[]{:S(2)}, u32[]{:S(2)}) %collective-permute-start.13) | collective-permute-done | bytes 524320 | tf_op jit(solution)/shard_map/ppermute | solution.py:63
  328.7 10.0 %collective-permute-done.17 = bf16[2048,128]{1,0:T(8,128)(2,1)S(1)} collective-permute-done((bf16[2048,128]{1,0:T(8,128)(2,1)S(1)}, bf16[2048,128]{1,0:T(8,128)(2,1)S(1)}, u32[]{:S(2)}, u32[]{:S(2)}) %collective-permute-start.17) | collective-permute-done | bytes 524320 | tf_op jit(solution)/shard_map/ppermute | solution.py:63
  341.7 5.4 multiply_convert_fusion.2
  347.1 4.5 fusion.63
  351.6 8.7 fusion.1
  363.7 7.2 fusion.83
  371.0 11.3 %reduce-precision_reduce_fusion = (f32[4096]{0:T(1024)S(1)}, bf16[512,4096]{1,0:T(8,128)(2,1)S(1)}) fusion(f32[512,4096]{1,0:T(8,128)} %fusion.83, f32[4096]{0:T(1024)S(1)} %select_bitcast_fusion, bf16[4096,1024]{1,0:T(8,128)(2,1)} %constant_dynamic-update-slice_fusion.50, bf16[512,1024]{1,0:T(8,128)(2,1)S(1)} %bitcast.275), kind=kOutput, calls=%fused_computation.10 | convolution fusion | flops 4320129024 | bytes 22052864 | tf_op jit(solution)/shard_map/dot_general | solution.py:23
  382.3 9.2 %multiply_reduce_fusion = (f32[1024]{0:T(1024)S(1)}, f32[512]{0:T(512)S(1)}, f32[512,1024]{1,0:T(8,128)S(1)}) fusion(f32[512,1024]{1,0:T(8,128)S(1)} %get-tuple-element.123, f32[512]{0:T(512)S(1)} %add_rsqrt_fusion, f32[1024]{0:T(1024)S(1)} %copy-done.63, bf16[1024,4096]{1,0:T(8,128)(2,1)} %constant_dynamic-update-slice_fusion.18, ...), kind=kOutput, calls=%fused_computation.74 | convolution fusion | flops 4298111488 | bytes 16789504 | tf_op jit(solution)/shard_map/dot_general | solution.py:23
  391.6 3.6 fusion.20
  395.2 9.0 %reduce-precision_reduce_fusion.1 = (f32[2048]{0:T(1024)S(1)}, bf16[512,2048]{1,0:T(8,128)(2,1)}, bf16[512,2048]{1,0:T(8,128)(2,1)S(1)}) fusion(f32[512,2048]{1,0:T(8,128)} %get-tuple-element.242, f32[2048]{0:T(1024)S(1)} %get-tuple-element.235, f32[4,128,2048]{2,1,0:T(8,128)S(1)} %copy-done.28, bf16[2048,1024]{1,0:T(8,128)(2,1)} %constant_dynamic-update-slice_fusion.2, ...), kind=kOutput, calls=%fused_computation.30 | convolution fusion | flops 2164783104 | bytes 18890752 | tf_op jit(solution)/shard_map/dot_general | solution.py:23
  406.3 4.4 fusion.61
  411.9 7.6 fusion.85
  419.5 4.4 convolution_convert_fusion.2
  423.9 7.1 convolution_convert_fusion.1
  431.1 11.8 %convolution_convert_fusion = bf16[4096,1024]{1,0:T(8,128)(2,1)} fusion(bf16[512,1024]{1,0:T(8,128)(2,1)S(1)} %bitcast.276, f32[512,4096]{1,0:T(8,128)} %fusion.83, f32[4096]{0:T(1024)S(1)} %select_bitcast_fusion), kind=kOutput, calls=%fused_computation.13 | convolution fusion | flops 4311744512 | bytes 17842176 | tf_op jit(solution)/shard_map/dot_general | solution.py:27
  442.9 9.2 %add_convert_fusion.14 = bf16[512,1024]{1,0:T(8,128)(2,1)} fusion(f32[512,1024]{1,0:T(8,128)S(1)} %copy-done.19, bf16[4096,1024]{1,0:T(8,128)(2,1)S(1)} %bitcast.335, f32[1024]{0:T(1024)S(1)} %copy-done.86, f32[512,4096]{1,0:T(8,128)} %fusion.83, f32[4096]{0:T(1024)S(1)} %select_bitcast_fusion), kind=kOutput, calls=%fused_computation.84 | convolution fusion | flops 4309123072 | bytes 19943424 | tf_op jit(solution)/shard_map/dot_general | solution.py:19
  452.1 4.1 multiply_multiply_fusion.grad_ref
  456.2 8.7 shard_map.392
  467.7 5.1 slice.594
  480.5 4.5 convolution_convert_fusion.4
  496.7 6.4 collective-permute-done.98
  507.4 7.7 collective-permute-done.99
  515.8 29.1 %shard_map.393 = (f32[512,1024]{1,0:T(8,128)}, f32[16,8,128]{2,1,0:T(8,128)}, f32[16,8,128]{2,1,0:T(8,128)}, f32[16,8,128]{2,1,0:T(8,128)}) custom-call(s32[2,256]{1,0:T(2,128)} %get-tuple-element.135.flags, f32[4096,128]{1,0:T(8,128)} %get-tuple-element.34.normed_ref, f32[4096,128]{1,0:T(8,128)} %get-tuple-element.39.rows_ref, ...), custom_call_target="tpu_custom_call" | custom-call | tf_op jit(solution)/shard_map/pallas_call | solution.py:254
  546.6 8.3 fusion.14
  555.0 5.6 add_convert_fusion.1
  561.6 5.6 add_convert_fusion
  570.4 37.1 %collective-permute-done.125 = bf16[4,1,1,2,128,1024]{5,4,3,2,1,0:T(8,128)(2,1)S(1)} collective-permute-done((bf16[4,1,1,2,128,1024]{5,4,3,2,1,0:T(8,128)(2,1)S(1)}, bf16[4,1,1,2,128,1024]{5,4,3,2,1,0:T(8,128)(2,1)S(1)}, u32[]{:S(2)}, u32[]{:S(2)}) %collective-permute-start.125) | collective-permute-done | bytes 2097184 | tf_op jit(solution)/shard_map/ppermute | solution.py:63
  623.7 15.2 %collective-permute-done.126 = bf16[4,1,1,1,128,1024]{5,4,3,2,1,0:T(8,128)(2,1)} collective-permute-done((bf16[4,1,1,1,128,1024]{5,4,3,2,1,0:T(8,128)(2,1)}, bf16[4,1,1,1,128,1024]{5,4,3,2,1,0:T(8,128)(2,1)}, u32[]{:S(2)}, u32[]{:S(2)}) %collective-permute-start.126) | collective-permute-done | bytes 1048608 | tf_op jit(solution)/shard_map/ppermute | solution.py:63
  646.1 5.8 collective-permute-done.129
  651.9 8.8 collective-permute-done.128
  665.5 5.4 collective-permute-start.135
  679.2 6.2 collective-permute-done.134
  689.2 6.1 collective-permute-start.105
  699.0 3.9 collective-permute-done.105
  702.9 3.8 collective-permute-done.104
  707.7 5.3 fusion.13
  712.9 43.9 %all-reduce.2.cloned.1.call-done = f32[500,128]{1,0:T(8,128)} async-done(((f32[500,128]{1,0:T(8,128)}), f32[500,128]{1,0:T(8,128)}) %all-reduce.2.cloned.1.call-update) | async-done | bytes 256016 | tf_op jit(solution)/shard_map/psum | solution.py:562
  788.3 5.2 collective-permute-done.107
  799.6 16.4 %collective-permute-done.119 = bf16[4,2,1,1,64,1024]{5,4,3,2,1,0:T(8,128)(2,1)} collective-permute-done((bf16[4,2,1,1,64,1024]{5,4,3,2,1,0:T(8,128)(2,1)}, bf16[4,2,1,1,64,1024]{5,4,3,2,1,0:T(8,128)(2,1)}, u32[]{:S(2)}, u32[]{:S(2)}) %collective-permute-start.119) | collective-permute-done | bytes 1048608 | tf_op jit(solution)/shard_map/ppermute | solution.py:63
  832.4 4.7 collective-permute-done.110
  837.1 4.4 collective-permute-start.122
  841.6 7.1 all-gather.2
  848.7 3.5 collective-permute-start.121
  852.3 7.0 all-gather.3
  863.3 7.6 all-gather.4
  875.9 3.9 reshape.583
  882.8 6.4 bitcast_convert_fusion
  (726 shorter events, 330.2 us)
Async XLA Ops:
  8.1 748.7 %all-reduce.2.cloned.1.call-start = ((), (), s32[]{:S(2)}) async-start(), calls=%async_computation | async-start | bytes 516096 | tf_op jit(solution)/shard_map/psum | solution.py:562
  10.4 119.5 %collective-permute-start.4 = (bf16[2048,128]{1,0:T(8,128)(2,1)S(1)}, bf16[2048,128]{1,0:T(8,128)(2,1)}, u32[]{:S(2)}, u32[]{:S(2)}) collective-permute-start(bf16[2048,128]{1,0:T(8,128)(2,1)S(1)} %pad_maximum_fusion), channel_id=1, source_target_pairs={{0,8},{1,9},{2,10},{3,11},{4,12},{5,13},{6,14},{7,15},{8,0},{9,1},... | collective-permute-start | bytes 1572872 | tf_op jit(solution)/shard_map/ppermute | solution.py:63
  10.9 121.6 %collective-permute-start.5 = (bf16[2048,128]{1,0:T(8,128)(2,1)S(1)}, bf16[2048,128]{1,0:T(8,128)(2,1)}, u32[]{:S(2)}, u32[]{:S(2)}) collective-permute-start(bf16[2048,128]{1,0:T(8,128)(2,1)S(1)} %pad_maximum_fusion), channel_id=1, source_target_pairs={{0,1},{1,0},{2,3},{3,2},{4,5},{5,4},{6,7},{7,6},{8,9},{9,8},{10,11... | collective-permute-start | bytes 1572872 | tf_op jit(solution)/shard_map/ppermute | solution.py:63
  15.3 60.5 %collective-permute-start.19 = (bf16[128,1024]{1,0:T(8,128)(2,1)}, bf16[128,1024]{1,0:T(8,128)(2,1)}, u32[]{:S(2)}, u32[]{:S(2)}) collective-permute-start(bf16[128,1024]{1,0:T(8,128)(2,1)} %get-tuple-element.129), channel_id=1, source_target_pairs={{0,8},{1,9},{2,10},{3,11},{4,12},{5,13},{6,14},{7,15},{8,0},{9,1},... | collective-permute-start | bytes 786440 | tf_op jit(solution)/shard_map/ppermute | solution.py:63
  15.5 62.1 %collective-permute-start.20 = (bf16[128,1024]{1,0:T(8,128)(2,1)}, bf16[128,1024]{1,0:T(8,128)(2,1)S(1)}, u32[]{:S(2)}, u32[]{:S(2)}) collective-permute-start(bf16[128,1024]{1,0:T(8,128)(2,1)} %get-tuple-element.129), channel_id=1, source_target_pairs={{0,1},{1,0},{2,3},{3,2},{4,5},{5,4},{6,7},{7,6},{8,9},{9,8},{10,11... | collective-permute-start | bytes 786440 | tf_op jit(solution)/shard_map/ppermute | solution.py:63
  32.7 41.5 %collective-permute-start = (f32[2,17,8,128]{3,2,1,0:T(8,128)}, f32[2,17,8,128]{3,2,1,0:T(8,128)S(1)}, u32[]{:S(2)}, u32[]{:S(2)}) collective-permute-start(f32[2,17,8,128]{3,2,1,0:T(8,128)} %get-tuple-element.217), channel_id=1, source_target_pairs={{0,1},{1,0},{2,3},{3,2},{4,5},{5,4},{6,7},{7,6},{8,9},{9,8},{10,11... | collective-permute-start | bytes 417800 | tf_op jit(solution)/shard_map/ppermute | solution.py:63
  89.3 42.2 %collective-permute-start.22 = (bf16[128,1024]{1,0:T(8,128)(2,1)}, bf16[128,1024]{1,0:T(8,128)(2,1)}, u32[]{:S(2)}, u32[]{:S(2)}) collective-permute-start(bf16[128,1024]{1,0:T(8,128)(2,1)} %get-tuple-element.129), channel_id=1, source_target_pairs={{0,2},{1,3},{2,4},{3,5},{4,6},{5,7},{6,0},{7,1},{8,10},{9,11},{10,... | collective-permute-start | bytes 786440 | tf_op jit(solution)/shard_map/ppermute | solution.py:63
  90.4 64.5 %collective-permute-start.26 = (bf16[128,1024]{1,0:T(8,128)(2,1)}, bf16[128,1024]{1,0:T(8,128)(2,1)}, u32[]{:S(2)}, u32[]{:S(2)}) collective-permute-start(bf16[128,1024]{1,0:T(8,128)(2,1)} %get-tuple-element.129), channel_id=1, source_target_pairs={{0,4},{1,5},{2,6},{3,7},{4,0},{5,1},{6,2},{7,3},{8,12},{9,13},{10,... | collective-permute-start | bytes 786440 | tf_op jit(solution)/shard_map/ppermute | solution.py:63
  92.6 13.1 %collective-permute-start.3 = (f32[2,17,8,128]{3,2,1,0:T(8,128)S(1)}, f32[2,17,8,128]{3,2,1,0:T(8,128)S(1)}, u32[]{:S(2)}, u32[]{:S(2)}) collective-permute-start(f32[2,17,8,128]{3,2,1,0:T(8,128)S(1)} %pad_maximum_fusion.3), channel_id=1, source_target_pairs={{0,6},{1,7},{8,14},{9,15},{16,22},{17,23},{24,30},{25,31}} | collective-permute-start | bytes 417800 | tf_op jit(solution)/shard_map/ppermute | solution.py:63
  105.7 62.5 %collective-permute-start.30 = (bf16[128,1024]{1,0:T(8,128)(2,1)}, bf16[128,1024]{1,0:T(8,128)(2,1)}, u32[]{:S(2)}, u32[]{:S(2)}) collective-permute-start(bf16[128,1024]{1,0:T(8,128)(2,1)} %get-tuple-element.129), channel_id=1, source_target_pairs={{0,6},{1,7},{2,0},{3,1},{4,2},{5,3},{6,4},{7,5},{8,14},{9,15},{10,... | collective-permute-start | bytes 786440 | tf_op jit(solution)/shard_map/ppermute | solution.py:63
  141.5 13.4 %collective-permute-start.69 = (bf16[128,1024]{1,0:T(8,128)(2,1)S(1)}, bf16[128,1024]{1,0:T(8,128)(2,1)S(1)}, u32[]{:S(2)}, u32[]{:S(2)}) collective-permute-start(bf16[128,1024]{1,0:T(8,128)(2,1)S(1)} %collective-permute-done.68), channel_id=1, source_target_pairs={{0,16},{1,17},{2,18},{3,19},{4,20},{5,21},{6,22},{7,23},{8,24},{9,... | collective-permute-start | bytes 786440 | tf_op jit(solution)/shard_map/ppermute | solution.py:63
  160.3 13.9 %collective-permute-start.72 = (bf16[128,1024]{1,0:T(8,128)(2,1)S(1)}, bf16[128,1024]{1,0:T(8,128)(2,1)S(1)}, u32[]{:S(2)}, u32[]{:S(2)}) collective-permute-start(bf16[128,1024]{1,0:T(8,128)(2,1)S(1)} %copy-done.48), channel_id=1, source_target_pairs={{0,2},{1,3},{2,4},{3,5},{4,6},{5,7},{6,0},{7,1},{8,10},{9,11},{10,... | collective-permute-start | bytes 786440 | tf_op jit(solution)/shard_map/ppermute | solution.py:63
  163.8 41.5 %collective-permute-start.80 = (bf16[128,1024]{1,0:T(8,128)(2,1)S(1)}, bf16[128,1024]{1,0:T(8,128)(2,1)S(1)}, u32[]{:S(2)}, u32[]{:S(2)}) collective-permute-start(bf16[128,1024]{1,0:T(8,128)(2,1)S(1)} %copy-done.48), channel_id=1, source_target_pairs={{0,4},{1,5},{2,6},{3,7},{4,0},{5,1},{6,2},{7,3},{8,12},{9,13},{10,... | collective-permute-start | bytes 786440 | tf_op jit(solution)/shard_map/ppermute | solution.py:63
  193.5 18.5 %collective-permute-start.6 = (bf16[2048,128]{1,0:T(8,128)(2,1)}, bf16[2048,128]{1,0:T(8,128)(2,1)S(1)}, u32[]{:S(2)}, u32[]{:S(2)}) collective-permute-start(bf16[2048,128]{1,0:T(8,128)(2,1)} %collective-permute-done.5), channel_id=1, source_target_pairs={{0,8},{1,9},{2,10},{3,11},{4,12},{5,13},{6,14},{7,15},{8,0},{9,1},... | collective-permute-start | bytes 1572872 | tf_op jit(solution)/shard_map/ppermute | solution.py:63
  205.3 46.1 %collective-permute-start.7 = (bf16[2048,128]{1,0:T(8,128)(2,1)S(1)}, bf16[2048,128]{1,0:T(8,128)(2,1)S(1)}, u32[]{:S(2)}, u32[]{:S(2)}) collective-permute-start(bf16[2048,128]{1,0:T(8,128)(2,1)S(1)} %pad_maximum_fusion), channel_id=1, source_target_pairs={{0,2},{1,3},{2,4},{3,5},{4,6},{5,7},{6,0},{7,1},{8,10},{9,11},{10,... | collective-permute-start | bytes 1572872 | tf_op jit(solution)/shard_map/ppermute | solution.py:63
  212.0 16.7 %collective-permute-start.88 = (bf16[128,1024]{1,0:T(8,128)(2,1)S(1)}, bf16[128,1024]{1,0:T(8,128)(2,1)S(1)}, u32[]{:S(2)}, u32[]{:S(2)}) collective-permute-start(bf16[128,1024]{1,0:T(8,128)(2,1)S(1)} %copy-done.48), channel_id=1, source_target_pairs={{0,6},{1,7},{2,0},{3,1},{4,2},{5,3},{6,4},{7,5},{8,14},{9,15},{10,... | collective-permute-start | bytes 786440 | tf_op jit(solution)/shard_map/ppermute | solution.py:63
  221.7 27.9 %collective-permute-start.49 = (bf16[1024,128]{1,0:T(8,128)(2,1)S(1)}, bf16[1024,128]{1,0:T(8,128)(2,1)S(1)}, u32[]{:S(2)}, u32[]{:S(2)}) collective-permute-start(bf16[1024,128]{1,0:T(8,128)(2,1)S(1)} %copy-done.50), channel_id=1, source_target_pairs={{0,4},{1,5},{2,6},{3,7},{4,0},{5,1},{6,2},{7,3},{8,12},{9,13},{10,... | collective-permute-start | bytes 786440 | tf_op jit(solution)/shard_map/ppermute | solution.py:63
  225.6 26.0 %collective-permute-start.86 = (bf16[128,1024]{1,0:T(8,128)(2,1)S(1)}, bf16[128,1024]{1,0:T(8,128)(2,1)S(1)}, u32[]{:S(2)}, u32[]{:S(2)}) collective-permute-start(bf16[128,1024]{1,0:T(8,128)(2,1)S(1)} %collective-permute-done.84), channel_id=1, source_target_pairs={{0,8},{1,9},{2,10},{3,11},{4,12},{5,13},{6,14},{7,15},{8,0},{9,1},... | collective-permute-start | bytes 786440 | tf_op jit(solution)/shard_map/ppermute | solution.py:63
  226.5 25.9 %collective-permute-start.87 = (bf16[128,1024]{1,0:T(8,128)(2,1)S(1)}, bf16[128,1024]{1,0:T(8,128)(2,1)S(1)}, u32[]{:S(2)}, u32[]{:S(2)}) collective-permute-start(bf16[128,1024]{1,0:T(8,128)(2,1)S(1)} %collective-permute-done.85), channel_id=1, source_target_pairs={{0,8},{1,9},{2,10},{3,11},{4,12},{5,13},{6,14},{7,15},{8,0},{9,1},... | collective-permute-start | bytes 786440 | tf_op jit(solution)/shard_map/ppermute | solution.py:63
  228.6 70.8 %collective-permute-start.11 = (bf16[2048,128]{1,0:T(8,128)(2,1)S(1)}, bf16[2048,128]{1,0:T(8,128)(2,1)S(1)}, u32[]{:S(2)}, u32[]{:S(2)}) collective-permute-start(bf16[2048,128]{1,0:T(8,128)(2,1)S(1)} %pad_maximum_fusion), channel_id=1, source_target_pairs={{0,4},{1,5},{2,6},{3,7},{4,0},{5,1},{6,2},{7,3},{8,12},{9,13},{10,... | collective-permute-start | bytes 1572872 | tf_op jit(solution)/shard_map/ppermute | solution.py:63
  249.6 16.7 %collective-permute-start.89 = (bf16[128,1024]{1,0:T(8,128)(2,1)S(1)}, bf16[128,1024]{1,0:T(8,128)(2,1)S(1)}, u32[]{:S(2)}, u32[]{:S(2)}) collective-permute-start(bf16[128,1024]{1,0:T(8,128)(2,1)S(1)} %collective-permute-done.88), channel_id=1, source_target_pairs={{0,16},{1,17},{2,18},{3,19},{4,20},{5,21},{6,22},{7,23},{8,24},{9,... | collective-permute-start | bytes 786440 | tf_op jit(solution)/shard_map/ppermute | solution.py:63
  254.5 14.7 %collective-permute-start.51 = (bf16[1024,128]{1,0:T(8,128)(2,1)S(1)}, bf16[1024,128]{1,0:T(8,128)(2,1)S(1)}, u32[]{:S(2)}, u32[]{:S(2)}) collective-permute-start(bf16[1024,128]{1,0:T(8,128)(2,1)S(1)} %collective-permute-done.49), channel_id=1, source_target_pairs={{0,8},{1,9},{2,10},{3,11},{4,12},{5,13},{6,14},{7,15},{8,0},{9,1},... | collective-permute-start | bytes 786440 | tf_op jit(solution)/shard_map/ppermute | solution.py:63
  282.9 26.4 %collective-permute-start.15 = (bf16[2048,128]{1,0:T(8,128)(2,1)S(1)}, bf16[2048,128]{1,0:T(8,128)(2,1)S(1)}, u32[]{:S(2)}, u32[]{:S(2)}) collective-permute-start(bf16[2048,128]{1,0:T(8,128)(2,1)S(1)} %pad_maximum_fusion), channel_id=1, source_target_pairs={{0,6},{1,7},{2,0},{3,1},{4,2},{5,3},{6,4},{7,5},{8,14},{9,15},{10,... | collective-permute-start | bytes 1572872 | tf_op jit(solution)/shard_map/ppermute | solution.py:63
  299.4 18.1 %collective-permute-start.9 = (bf16[2048,128]{1,0:T(8,128)(2,1)S(1)}, bf16[2048,128]{1,0:T(8,128)(2,1)S(1)}, u32[]{:S(2)}, u32[]{:S(2)}) collective-permute-start(bf16[2048,128]{1,0:T(8,128)(2,1)S(1)} %collective-permute-done.7), channel_id=1, source_target_pairs={{0,1},{1,0},{2,3},{3,2},{4,5},{5,4},{6,7},{7,6},{8,9},{9,8},{10,11... | collective-permute-start | bytes 1572872 | tf_op jit(solution)/shard_map/ppermute | solution.py:63
  309.4 19.4 %collective-permute-start.13 = (bf16[2048,128]{1,0:T(8,128)(2,1)S(1)}, bf16[2048,128]{1,0:T(8,128)(2,1)S(1)}, u32[]{:S(2)}, u32[]{:S(2)}) collective-permute-start(bf16[2048,128]{1,0:T(8,128)(2,1)S(1)} %collective-permute-done.11), channel_id=1, source_target_pairs={{0,1},{1,0},{2,3},{3,2},{4,5},{5,4},{6,7},{7,6},{8,9},{9,8},{10,11... | collective-permute-start | bytes 1572872 | tf_op jit(solution)/shard_map/ppermute | solution.py:63
  310.8 27.9 %collective-permute-start.17 = (bf16[2048,128]{1,0:T(8,128)(2,1)S(1)}, bf16[2048,128]{1,0:T(8,128)(2,1)S(1)}, u32[]{:S(2)}, u32[]{:S(2)}) collective-permute-start(bf16[2048,128]{1,0:T(8,128)(2,1)S(1)} %collective-permute-done.15), channel_id=1, source_target_pairs={{0,1},{1,0},{2,3},{3,2},{4,5},{5,4},{6,7},{7,6},{8,9},{9,8},{10,11... | collective-permute-start | bytes 1572872 | tf_op jit(solution)/shard_map/ppermute | solution.py:63
  312.6 27.7 %collective-permute-start.12 = (bf16[2048,128]{1,0:T(8,128)(2,1)S(1)}, bf16[2048,128]{1,0:T(8,128)(2,1)S(1)}, u32[]{:S(2)}, u32[]{:S(2)}) collective-permute-start(bf16[2048,128]{1,0:T(8,128)(2,1)S(1)} %collective-permute-done.11), channel_id=1, source_target_pairs={{0,8},{1,9},{2,10},{3,11},{4,12},{5,13},{6,14},{7,15},{8,0},{9,1},... | collective-permute-start | bytes 1572872 | tf_op jit(solution)/shard_map/ppermute | solution.py:63
  317.5 22.5 %collective-permute-start.10 = (bf16[2048,128]{1,0:T(8,128)(2,1)S(1)}, bf16[2048,128]{1,0:T(8,128)(2,1)S(1)}, u32[]{:S(2)}, u32[]{:S(2)}) collective-permute-start(bf16[2048,128]{1,0:T(8,128)(2,1)S(1)} %collective-permute-done.9), channel_id=1, source_target_pairs={{0,8},{1,9},{2,10},{3,11},{4,12},{5,13},{6,14},{7,15},{8,0},{9,1},... | collective-permute-start | bytes 1572872 | tf_op jit(solution)/shard_map/ppermute | solution.py:63
  318.3 20.4 %collective-permute-start.64 = (bf16[1024,128]{1,0:T(8,128)(2,1)S(1)}, bf16[1024,128]{1,0:T(8,128)(2,1)S(1)}, u32[]{:S(2)}, u32[]{:S(2)}) collective-permute-start(bf16[1024,128]{1,0:T(8,128)(2,1)S(1)} %collective-permute-done.62), channel_id=1, source_target_pairs={{0,8},{1,9},{2,10},{3,11},{4,12},{5,13},{6,14},{7,15},{8,0},{9,1},... | collective-permute-start | bytes 786440 | tf_op jit(solution)/shard_map/ppermute | solution.py:63
  466.0 27.3 %collective-permute-start.96 = (f32[2,17,8,128]{3,2,1,0:T(8,128)S(1)}, f32[2,17,8,128]{3,2,1,0:T(8,128)S(1)}, u32[]{:S(2)}, u32[]{:S(2)}) collective-permute-start(f32[2,17,8,128]{3,2,1,0:T(8,128)S(1)} %get-tuple-element.209), channel_id=1, source_target_pairs={{0,1},{1,0},{2,3},{3,2},{4,5},{5,4},{6,7},{7,6},{8,9},{9,8},{10,11... | collective-permute-start | bytes 417800 | tf_op jit(solution)/shard_map/ppermute | solution.py:63
  472.8 82.2 %collective-permute-start.124 = (bf16[4,2,1,2,128,1024]{5,4,3,2,1,0:T(8,128)(2,1)}, bf16[4,2,1,2,128,1024]{5,4,3,2,1,0:T(8,128)(2,1)}, u32[]{:S(2)}, u32[]{:S(2)}) collective-permute-start(bf16[4,2,1,2,128,1024]{5,4,3,2,1,0:T(8,128)(2,1)} %slice.594), channel_id=1, source_target_pairs={{0,8},{1,9},{2,10},{3,11},{4,12},{5,13},{6,14},{7,15},{8,0},{9,1},... | collective-permute-start | bytes 12582920 | tf_op jit(solution)/shard_map/ppermute | solution.py:63
  479.9 131.0 %collective-permute-start.100 = (bf16[2,1,4,2,32,2176]{5,4,3,2,1,0:T(8,128)(2,1)}, bf16[2,1,4,2,32,2176]{5,4,3,2,1,0:T(8,128)(2,1)}, u32[]{:S(2)}, u32[]{:S(2)}) collective-permute-start(bf16[2,1,4,2,32,2176]{5,4,3,2,1,0:T(8,128)(2,1)} %constant_dynamic-slice_fusion.8), channel_id=1, source_target_pairs={{0,8},{1,9},{2,10},{3,11},{4,12},{5,13},{6,14},{7,15},{8,0},{9,1},... | collective-permute-start | bytes 6684680 | tf_op jit(solution)/shard_map/ppermute | solution.py:63
  493.4 68.2 %collective-permute-start.130 = (bf16[4,2,1,2,128,1024]{5,4,3,2,1,0:T(8,128)(2,1)}, bf16[4,2,1,2,128,1024]{5,4,3,2,1,0:T(8,128)(2,1)}, u32[]{:S(2)}, u32[]{:S(2)}) collective-permute-start(bf16[4,2,1,2,128,1024]{5,4,3,2,1,0:T(8,128)(2,1)} %slice.605), channel_id=1, source_target_pairs={{0,8},{1,9},{2,10},{3,11},{4,12},{5,13},{6,14},{7,15},{8,0},{9,1},... | collective-permute-start | bytes 12582920 | tf_op jit(solution)/shard_map/ppermute | solution.py:63
  503.1 259.5 %collective-permute-start.106 = (bf16[4,2,1,2,64,1024]{5,4,3,2,1,0:T(8,128)(2,1)}, bf16[4,2,1,2,64,1024]{5,4,3,2,1,0:T(8,128)(2,1)}, u32[]{:S(2)}, u32[]{:S(2)}) collective-permute-start(bf16[4,2,1,2,64,1024]{5,4,3,2,1,0:T(8,128)(2,1)} %slice.567), channel_id=1, source_target_pairs={{0,8},{1,9},{2,10},{3,11},{4,12},{5,13},{6,14},{7,15},{8,0},{9,1},... | collective-permute-start | bytes 6291464 | tf_op jit(solution)/shard_map/ppermute | solution.py:63
  560.8 46.7 %collective-permute-start.125 = (bf16[4,1,1,2,128,1024]{5,4,3,2,1,0:T(8,128)(2,1)S(1)}, bf16[4,1,1,2,128,1024]{5,4,3,2,1,0:T(8,128)(2,1)S(1)}, u32[]{:S(2)}, u32[]{:S(2)}) collective-permute-start(bf16[4,1,1,2,128,1024]{5,4,3,2,1,0:T(8,128)(2,1)S(1)} %slice.596), channel_id=1, source_target_pairs={{0,1},{1,0},{2,3},{3,2},{4,5},{5,4},{6,7},{7,6},{8,9},{9,8},{10,11... | collective-permute-start | bytes 6291464 | tf_op jit(solution)/shard_map/ppermute | solution.py:63
  569.0 48.9 %collective-permute-start.131 = (bf16[4,2,1,1,128,1024]{5,4,3,2,1,0:T(8,128)(2,1)}, bf16[4,2,1,1,128,1024]{5,4,3,2,1,0:T(8,128)(2,1)}, u32[]{:S(2)}, u32[]{:S(2)}) collective-permute-start(bf16[4,2,1,1,128,1024]{5,4,3,2,1,0:T(8,128)(2,1)} %slice.607), channel_id=1, source_target_pairs={{0,16},{1,17},{2,18},{3,19},{4,20},{5,21},{6,22},{7,23},{8,24},{9,... | collective-permute-start | bytes 6291464 | tf_op jit(solution)/shard_map/ppermute | solution.py:63
  609.7 29.2 %collective-permute-start.126 = (bf16[4,1,1,1,128,1024]{5,4,3,2,1,0:T(8,128)(2,1)}, bf16[4,1,1,1,128,1024]{5,4,3,2,1,0:T(8,128)(2,1)}, u32[]{:S(2)}, u32[]{:S(2)}) collective-permute-start(bf16[4,1,1,1,128,1024]{5,4,3,2,1,0:T(8,128)(2,1)} %slice.598), channel_id=1, source_target_pairs={{0,16},{1,17},{2,18},{3,19},{4,20},{5,21},{6,22},{7,23},{8,24},{9,... | collective-permute-start | bytes 3145736 | tf_op jit(solution)/shard_map/ppermute | solution.py:63
  614.5 28.2 %collective-permute-start.101 = (bf16[2,1,4,1,32,2176]{5,4,3,2,1,0:T(8,128)(2,1)S(1)}, bf16[2,1,4,1,32,2176]{5,4,3,2,1,0:T(8,128)(2,1)}, u32[]{:S(2)}, u32[]{:S(2)}) collective-permute-start(bf16[2,1,4,1,32,2176]{5,4,3,2,1,0:T(8,128)(2,1)S(1)} %constant_dynamic-slice_fusion.7), channel_id=1, source_target_pairs={{0,1},{1,0},{2,3},{3,2},{4,5},{5,4},{6,7},{7,6},{8,9},{9,8},{10,11... | collective-permute-start | bytes 3342344 | tf_op jit(solution)/shard_map/ppermute | solution.py:63
  616.1 256.1 %all-gather.13.cloned.1.call-start = ((), (), s32[]{:S(2)}) async-start(), calls=%async_computation.2 | async-start | bytes 1310720 | tf_op jit(solution)/shard_map/all_gather | solution.py:462
  622.2 41.2 %collective-permute-start.132 = (bf16[4,1,1,1,128,1024]{5,4,3,2,1,0:T(8,128)(2,1)}, bf16[4,1,1,1,128,1024]{5,4,3,2,1,0:T(8,128)(2,1)}, u32[]{:S(2)}, u32[]{:S(2)}) collective-permute-start(bf16[4,1,1,1,128,1024]{5,4,3,2,1,0:T(8,128)(2,1)} %slice.609), channel_id=1, source_target_pairs={{0,1},{1,0},{2,3},{3,2},{4,5},{5,4},{6,7},{7,6},{8,9},{9,8},{10,11... | collective-permute-start | bytes 3145736 | tf_op jit(solution)/shard_map/ppermute | solution.py:63
  640.7 20.0 %collective-permute-start.128 = (bf16[1,1,1,1,128,1024]{5,4,3,2,1,0:T(8,128)(2,1)S(1)}, bf16[1,1,1,1,128,1024]{5,4,3,2,1,0:T(8,128)(2,1)S(1)}, u32[]{:S(2)}, u32[]{:S(2)}) collective-permute-start(bf16[1,1,1,1,128,1024]{5,4,3,2,1,0:T(8,128)(2,1)S(1)} %get-tuple-element.147), channel_id=1, source_target_pairs={{0,4},{1,5},{2,6},{3,7},{4,0},{5,1},{6,2},{7,3},{8,12},{9,13},{10,... | collective-permute-start | bytes 786440 | tf_op jit(solution)/shard_map/ppermute | solution.py:63
  642.7 18.0 %collective-permute-start.127 = (bf16[1,1,1,1,128,1024]{5,4,3,2,1,0:T(8,128)(2,1)S(1)}, bf16[1,1,1,1,128,1024]{5,4,3,2,1,0:T(8,128)(2,1)S(1)}, u32[]{:S(2)}, u32[]{:S(2)}) collective-permute-start(bf16[1,1,1,1,128,1024]{5,4,3,2,1,0:T(8,128)(2,1)S(1)} %get-tuple-element.145), channel_id=1, source_target_pairs={{0,6},{1,7},{2,0},{3,1},{4,2},{5,3},{6,4},{7,5},{8,14},{9,15},{10,... | collective-permute-start | bytes 786440 | tf_op jit(solution)/shard_map/ppermute | solution.py:63
  661.6 218.2 %all-gather.15.cloned.1.call-start = ((), (), s32[]{:S(2)}) async-start(), calls=%async_computation.3 | async-start | bytes 1310720 | tf_op jit(solution)/shard_map/all_gather | solution.py:462
  662.5 25.5 %collective-permute-start.102 = (bf16[1,1,4,1,32,2176]{5,4,3,2,1,0:T(8,128)(2,1)}, bf16[1,1,4,1,32,2176]{5,4,3,2,1,0:T(8,128)(2,1)}, u32[]{:S(2)}, u32[]{:S(2)}) collective-permute-start(bf16[1,1,4,1,32,2176]{5,4,3,2,1,0:T(8,128)(2,1)} %constant_dynamic-slice_fusion.6), channel_id=1, source_target_pairs={{0,16},{1,17},{2,18},{3,19},{4,20},{5,21},{6,22},{7,23},{8,24},{9,... | collective-permute-start | bytes 1671176 | tf_op jit(solution)/shard_map/ppermute | solution.py:63
  665.5 13.7 %collective-permute-start.135 = (bf16[1,1,1,1,128,1024]{5,4,3,2,1,0:T(8,128)(2,1)S(1)}, bf16[1,1,1,1,128,1024]{5,4,3,2,1,0:T(8,128)(2,1)S(1)}, u32[]{:S(2)}, u32[]{:S(2)}) collective-permute-start(bf16[1,1,1,1,128,1024]{5,4,3,2,1,0:T(8,128)(2,1)S(1)} %get-tuple-element.143), channel_id=1, source_target_pairs={{0,2},{1,3},{2,4},{3,5},{4,6},{5,7},{6,0},{7,1},{8,10},{9,11},{10,... | collective-permute-start | bytes 786440 | tf_op jit(solution)/shard_map/ppermute | solution.py:63
  670.8 14.6 %collective-permute-start.134 = (bf16[1,1,1,1,128,1024]{5,4,3,2,1,0:T(8,128)(2,1)S(1)}, bf16[1,1,1,1,128,1024]{5,4,3,2,1,0:T(8,128)(2,1)S(1)}, u32[]{:S(2)}, u32[]{:S(2)}) collective-permute-start(bf16[1,1,1,1,128,1024]{5,4,3,2,1,0:T(8,128)(2,1)S(1)} %get-tuple-element.144), channel_id=1, source_target_pairs={{0,4},{1,5},{2,6},{3,7},{4,0},{5,1},{6,2},{7,3},{8,12},{9,13},{10,... | collective-permute-start | bytes 786440 | tf_op jit(solution)/shard_map/ppermute | solution.py:63
  670.8 16.2 %collective-permute-start.133 = (bf16[1,1,1,1,128,1024]{5,4,3,2,1,0:T(8,128)(2,1)S(1)}, bf16[1,1,1,1,128,1024]{5,4,3,2,1,0:T(8,128)(2,1)S(1)}, u32[]{:S(2)}, u32[]{:S(2)}) collective-permute-start(bf16[1,1,1,1,128,1024]{5,4,3,2,1,0:T(8,128)(2,1)S(1)} %get-tuple-element.142), channel_id=1, source_target_pairs={{0,6},{1,7},{2,0},{3,1},{4,2},{5,3},{6,4},{7,5},{8,14},{9,15},{10,... | collective-permute-start | bytes 786440 | tf_op jit(solution)/shard_map/ppermute | solution.py:63
  679.2 89.5 %collective-permute-start.112 = (bf16[4,2,1,2,64,1024]{5,4,3,2,1,0:T(8,128)(2,1)}, bf16[4,2,1,2,64,1024]{5,4,3,2,1,0:T(8,128)(2,1)}, u32[]{:S(2)}, u32[]{:S(2)}) collective-permute-start(bf16[4,2,1,2,64,1024]{5,4,3,2,1,0:T(8,128)(2,1)} %slice.576), channel_id=1, source_target_pairs={{0,8},{1,9},{2,10},{3,11},{4,12},{5,13},{6,14},{7,15},{8,0},{9,1},... | collective-permute-start | bytes 6291464 | tf_op jit(solution)/shard_map/ppermute | solution.py:63
  687.9 194.9 %all-gather.11.cloned.1.call-start = ((), (), s32[]{:S(2)}) async-start(), calls=%async_computation.1 | async-start | bytes 4595712 | tf_op jit(solution)/shard_map/all_gather | solution.py:529
  689.2 13.7 %collective-permute-start.105 = (bf16[1,1,1,1,32,2176]{5,4,3,2,1,0:T(8,128)(2,1)S(1)}, bf16[1,1,1,1,32,2176]{5,4,3,2,1,0:T(8,128)(2,1)S(1)}, u32[]{:S(2)}, u32[]{:S(2)}) collective-permute-start(bf16[1,1,1,1,32,2176]{5,4,3,2,1,0:T(8,128)(2,1)S(1)} %get-tuple-element.149), channel_id=1, source_target_pairs={{0,2},{1,3},{2,4},{3,5},{4,6},{5,7},{6,0},{7,1},{8,10},{9,11},{10,... | collective-permute-start | bytes 417800 | tf_op jit(solution)/shard_map/ppermute | solution.py:63
  702.9 70.8 %collective-permute-start.118 = (bf16[4,2,1,2,64,1024]{5,4,3,2,1,0:T(8,128)(2,1)}, bf16[4,2,1,2,64,1024]{5,4,3,2,1,0:T(8,128)(2,1)}, u32[]{:S(2)}, u32[]{:S(2)}) collective-permute-start(bf16[4,2,1,2,64,1024]{5,4,3,2,1,0:T(8,128)(2,1)} %slice.585), channel_id=1, source_target_pairs={{0,8},{1,9},{2,10},{3,11},{4,12},{5,13},{6,14},{7,15},{8,0},{9,1},... | collective-permute-start | bytes 6291464 | tf_op jit(solution)/shard_map/ppermute | solution.py:63
  767.1 26.4 %collective-permute-start.107 = (bf16[4,2,1,1,64,1024]{5,4,3,2,1,0:T(8,128)(2,1)}, bf16[4,2,1,1,64,1024]{5,4,3,2,1,0:T(8,128)(2,1)}, u32[]{:S(2)}, u32[]{:S(2)}) collective-permute-start(bf16[4,2,1,1,64,1024]{5,4,3,2,1,0:T(8,128)(2,1)} %constant_dynamic-slice_fusion.2), channel_id=1, source_target_pairs={{0,16},{1,17},{2,18},{3,19},{4,20},{5,21},{6,22},{7,23},{8,24},{9,... | collective-permute-start | bytes 3145736 | tf_op jit(solution)/shard_map/ppermute | solution.py:63
  772.3 26.2 %collective-permute-start.113 = (bf16[4,1,1,2,64,1024]{5,4,3,2,1,0:T(8,128)(2,1)}, bf16[4,1,1,2,64,1024]{5,4,3,2,1,0:T(8,128)(2,1)S(1)}, u32[]{:S(2)}, u32[]{:S(2)}) collective-permute-start(bf16[4,1,1,2,64,1024]{5,4,3,2,1,0:T(8,128)(2,1)} %slice.578), channel_id=1, source_target_pairs={{0,1},{1,0},{2,3},{3,2},{4,5},{5,4},{6,7},{7,6},{8,9},{9,8},{10,11... | collective-permute-start | bytes 3145736 | tf_op jit(solution)/shard_map/ppermute | solution.py:63
  778.7 37.3 %collective-permute-start.119 = (bf16[4,2,1,1,64,1024]{5,4,3,2,1,0:T(8,128)(2,1)}, bf16[4,2,1,1,64,1024]{5,4,3,2,1,0:T(8,128)(2,1)}, u32[]{:S(2)}, u32[]{:S(2)}) collective-permute-start(bf16[4,2,1,1,64,1024]{5,4,3,2,1,0:T(8,128)(2,1)} %constant_dynamic-slice_fusion), channel_id=1, source_target_pairs={{0,16},{1,17},{2,18},{3,19},{4,20},{5,21},{6,22},{7,23},{8,24},{9,... | collective-permute-start | bytes 3145736 | tf_op jit(solution)/shard_map/ppermute | solution.py:63
  795.5 23.8 %collective-permute-start.108 = (bf16[4,1,1,1,64,1024]{5,4,3,2,1,0:T(8,128)(2,1)S(1)}, bf16[4,1,1,1,64,1024]{5,4,3,2,1,0:T(8,128)(2,1)S(1)}, u32[]{:S(2)}, u32[]{:S(2)}) collective-permute-start(bf16[4,1,1,1,64,1024]{5,4,3,2,1,0:T(8,128)(2,1)S(1)} %slice.569), channel_id=1, source_target_pairs={{0,1},{1,0},{2,3},{3,2},{4,5},{5,4},{6,7},{7,6},{8,9},{9,8},{10,11... | collective-permute-start | bytes 1572872 | tf_op jit(solution)/shard_map/ppermute | solution.py:63
  799.0 26.5 %collective-permute-start.114 = (bf16[4,1,1,1,64,1024]{5,4,3,2,1,0:T(8,128)(2,1)S(1)}, bf16[4,1,1,1,64,1024]{5,4,3,2,1,0:T(8,128)(2,1)S(1)}, u32[]{:S(2)}, u32[]{:S(2)}) collective-permute-start(bf16[4,1,1,1,64,1024]{5,4,3,2,1,0:T(8,128)(2,1)S(1)} %constant_dynamic-slice_fusion.1), channel_id=1, source_target_pairs={{0,16},{1,17},{2,18},{3,19},{4,20},{5,21},{6,22},{7,23},{8,24},{9,... | collective-permute-start | bytes 1572872 | tf_op jit(solution)/shard_map/ppermute | solution.py:63
  820.8 16.3 %collective-permute-start.110 = (bf16[1,1,1,1,64,1024]{5,4,3,2,1,0:T(8,128)(2,1)S(1)}, bf16[1,1,1,1,64,1024]{5,4,3,2,1,0:T(8,128)(2,1)S(1)}, u32[]{:S(2)}, u32[]{:S(2)}) collective-permute-start(bf16[1,1,1,1,64,1024]{5,4,3,2,1,0:T(8,128)(2,1)S(1)} %get-tuple-element.159), channel_id=1, source_target_pairs={{0,4},{1,5},{2,6},{3,7},{4,0},{5,1},{6,2},{7,3},{8,12},{9,13},{10,... | collective-permute-start | bytes 393224 | tf_op jit(solution)/shard_map/ppermute | solution.py:63
  822.3 14.8 %collective-permute-start.109 = (bf16[1,1,1,1,64,1024]{5,4,3,2,1,0:T(8,128)(2,1)S(1)}, bf16[1,1,1,1,64,1024]{5,4,3,2,1,0:T(8,128)(2,1)S(1)}, u32[]{:S(2)}, u32[]{:S(2)}) collective-permute-start(bf16[1,1,1,1,64,1024]{5,4,3,2,1,0:T(8,128)(2,1)S(1)} %get-tuple-element.157), channel_id=1, source_target_pairs={{0,6},{1,7},{2,0},{3,1},{4,2},{5,3},{6,4},{7,5},{8,14},{9,15},{10,... | collective-permute-start | bytes 393224 | tf_op jit(solution)/shard_map/ppermute | solution.py:63
  825.8 22.9 %collective-permute-start.117 = (bf16[1,1,1,1,64,1024]{5,4,3,2,1,0:T(8,128)(2,1)S(1)}, bf16[1,1,1,1,64,1024]{5,4,3,2,1,0:T(8,128)(2,1)S(1)}, u32[]{:S(2)}, u32[]{:S(2)}) collective-permute-start(bf16[1,1,1,1,64,1024]{5,4,3,2,1,0:T(8,128)(2,1)S(1)} %get-tuple-element.155), channel_id=1, source_target_pairs={{0,2},{1,3},{2,4},{3,5},{4,6},{5,7},{6,0},{7,1},{8,10},{9,11},{10,... | collective-permute-start | bytes 393224 | tf_op jit(solution)/shard_map/ppermute | solution.py:63
  828.4 23.8 %collective-permute-start.116 = (bf16[1,1,1,1,64,1024]{5,4,3,2,1,0:T(8,128)(2,1)S(1)}, bf16[1,1,1,1,64,1024]{5,4,3,2,1,0:T(8,128)(2,1)S(1)}, u32[]{:S(2)}, u32[]{:S(2)}) collective-permute-start(bf16[1,1,1,1,64,1024]{5,4,3,2,1,0:T(8,128)(2,1)S(1)} %get-tuple-element.156), channel_id=1, source_target_pairs={{0,4},{1,5},{2,6},{3,7},{4,0},{5,1},{6,2},{7,3},{8,12},{9,13},{10,... | collective-permute-start | bytes 393224 | tf_op jit(solution)/shard_map/ppermute | solution.py:63
  830.8 21.4 %collective-permute-start.115 = (bf16[1,1,1,1,64,1024]{5,4,3,2,1,0:T(8,128)(2,1)S(1)}, bf16[1,1,1,1,64,1024]{5,4,3,2,1,0:T(8,128)(2,1)S(1)}, u32[]{:S(2)}, u32[]{:S(2)}) collective-permute-start(bf16[1,1,1,1,64,1024]{5,4,3,2,1,0:T(8,128)(2,1)S(1)} %get-tuple-element.154), channel_id=1, source_target_pairs={{0,6},{1,7},{2,0},{3,1},{4,2},{5,3},{6,4},{7,5},{8,14},{9,15},{10,... | collective-permute-start | bytes 393224 | tf_op jit(solution)/shard_map/ppermute | solution.py:63
  837.1 25.2 %collective-permute-start.123 = (bf16[1,1,1,1,64,1024]{5,4,3,2,1,0:T(8,128)(2,1)}, bf16[1,1,1,1,64,1024]{5,4,3,2,1,0:T(8,128)(2,1)S(1)}, u32[]{:S(2)}, u32[]{:S(2)}) collective-permute-start(bf16[1,1,1,1,64,1024]{5,4,3,2,1,0:T(8,128)(2,1)} %get-tuple-element.152), channel_id=1, source_target_pairs={{0,2},{1,3},{2,4},{3,5},{4,6},{5,7},{6,0},{7,1},{8,10},{9,11},{10,... | collective-permute-start | bytes 393224 | tf_op jit(solution)/shard_map/ppermute | solution.py:63
  837.1 25.2 %collective-permute-start.122 = (bf16[1,1,1,1,64,1024]{5,4,3,2,1,0:T(8,128)(2,1)}, bf16[1,1,1,1,64,1024]{5,4,3,2,1,0:T(8,128)(2,1)S(1)}, u32[]{:S(2)}, u32[]{:S(2)}) collective-permute-start(bf16[1,1,1,1,64,1024]{5,4,3,2,1,0:T(8,128)(2,1)} %get-tuple-element.153), channel_id=1, source_target_pairs={{0,4},{1,5},{2,6},{3,7},{4,0},{5,1},{6,2},{7,3},{8,12},{9,13},{10,... | collective-permute-start | bytes 393224 | tf_op jit(solution)/shard_map/ppermute | solution.py:63
  848.7 13.7 %collective-permute-start.121 = (bf16[1,1,1,1,64,1024]{5,4,3,2,1,0:T(8,128)(2,1)}, bf16[1,1,1,1,64,1024]{5,4,3,2,1,0:T(8,128)(2,1)S(1)}, u32[]{:S(2)}, u32[]{:S(2)}) collective-permute-start(bf16[1,1,1,1,64,1024]{5,4,3,2,1,0:T(8,128)(2,1)} %get-tuple-element.151), channel_id=1, source_target_pairs={{0,6},{1,7},{2,0},{3,1},{4,2},{5,3},{6,4},{7,5},{8,14},{9,15},{10,... | collective-permute-start | bytes 393224 | tf_op jit(solution)/shard_map/ppermute | solution.py:63
  (181 other events, 2626.4 us)
Sparse Core Ops, SparseCore 0:
  616.2 140.5 all-reduce.1
Sparse Core Ops, SparseCore 1:
  661.7 21.9 all-gather.12
  688.0 22.0 all-gather.14
  712.8 62.8 all-gather.10

commit v2 on v1

v2 whole, which is shorter than its diff:
```python
from functools import partial

import jax
import jax.numpy as jnp
from jax import lax
from jax.experimental import pallas as pl
from jax.experimental.pallas import tpu as pltpu
from jax.sharding import PartitionSpec as P

BLOCK = 128
HIGHEST = lax.Precision.HIGHEST
EPSILON = 1e-06
AXES = ("dp", "tensor")
F32 = jnp.float32
BF16 = jnp.bfloat16


def dot_plain(a, b):
    return jnp.dot(a, b, preferred_element_type=F32)


def dot_against(a, b):
    return lax.dot_general(a, b, (((1,), (1,)), ((), ())), preferred_element_type=F32)


def dot_over_rows(a, b):
    return lax.dot_general(a, b, (((0,), (0,)), ((), ())), preferred_element_type=F32)


def rounded(v):
    return lax.reduce_precision(v, exponent_bits=8, mantissa_bits=7)


def silu_slope(v):
    s = jax.nn.sigmoid(v)
    return s * (1.0 + v * (1.0 - s))


class Grid:
    def __init__(self):
        dp, tensor = lax.axis_size("dp"), lax.axis_size("tensor")
        self.count = dp * tensor
        self.index = lax.axis_index("dp") * tensor + lax.axis_index("tensor")
        masks = lambda n, first: [first << k for k in range(n.bit_length() - 1)]
        self.tensor = masks(tensor, 1)
        self.core, *self.xs = masks(dp, tensor)

    def bit(self, mask):
        return (self.index // mask) % 2

    def swap(self, value, mask):
        return lax.ppermute(value, AXES, [(i, i ^ mask) for i in range(self.count)])


def ema_step(state, row, keep, decay, feed):
    return [(s * keep) * q + f * row for s, q, f in zip(state, decay, feed)]


def row_of(ref, base, r):
    return ref[pl.ds(base + r, 8, stride=8), :]


def spread(ref, block, values):
    for j in range(8):
        ref[pl.ds(pl.multiple_of(block * 64, 64) + 8 * j, 8), :] = values[:, j * 128 : (j + 1) * 128]


def collect(ref, block):
    return jnp.concatenate(
        [ref[pl.ds(pl.multiple_of(block * 64, 64) + 8 * j, 8), :] for j in range(8)], axis=1
    )


def norm_kernel(flags, x_ref, gain_ref, decay_ref, feed_ref, normed_ref, low_ref, final_ref):
    micros, rows = flags.shape
    heads = decay_ref.shape[0]

    def norm_block(b, carry):
        at = pl.ds(pl.multiple_of(b * 16, 16), 16)
        x = x_ref[at, :].astype(F32)
        n = x * lax.rsqrt(jnp.mean(x * x, axis=-1, keepdims=True) + EPSILON) * gain_ref[...]
        low_ref[at, :] = n.astype(BF16)
        spread(normed_ref, 2 * b, n[:8])
        spread(normed_ref, 2 * b + 1, n[8:])
        return carry

    lax.fori_loop(0, micros * rows // 16, norm_block, 0)
    for m in range(micros):
        for h0 in range(0, heads, 8):
            decay = [decay_ref[h0 + h] for h in range(8)]
            feed = [feed_ref[h0 + h] for h in range(8)]

            def block(b, state, m=m, decay=decay, feed=feed):
                base = pl.multiple_of((m * (rows // 8) + b) * 64, 64)
                for r in range(8):
                    keep = (1 - flags[m, b * 8 + r]).astype(F32)
                    state = ema_step(state, row_of(normed_ref, base, r), keep, decay, feed)
                return state

            state = lax.fori_loop(0, rows // 8, block, [jnp.zeros((8, 128), F32)] * 8)
            for h in range(8):
                final_ref[m, h0 + h] = state[h]


def blend_kernel(
    flags, normed_ref, start_ref, decay_ref, feed_ref, out_ref, omega_ref, blended_ref, low_ref, acc_ref
):
    micros, rows = flags.shape
    heads = decay_ref.shape[0]
    omega = omega_ref[...]
    for m in range(micros):
        for h0 in range(0, heads, 8):
            decay = [decay_ref[h0 + h] for h in range(8)]
            feed = [feed_ref[h0 + h] for h in range(8)]
            tell = [out_ref[h0 + h] for h in range(8)]

            def block(b, state, m=m, h0=h0, decay=decay, feed=feed, tell=tell):
                base = pl.multiple_of((m * (rows // 8) + b) * 64, 64)
                for r in range(8):
                    keep = (1 - flags[m, b * 8 + r]).astype(F32)
                    row = row_of(normed_ref, base, r)
                    state = ema_step(state, row, keep, decay, feed)
                    told = [s * t for s, t in zip(state, tell)]
                    while len(told) > 1:
                        told = [told[i] + told[i + 1] for i in range(0, len(told), 2)]
                    at = pl.ds(base + r, 8, stride=8)
                    if h0 == 0:
                        acc_ref[at, :] = told[0] + omega * row
                    else:
                        acc_ref[at, :] = acc_ref[at, :] + told[0]
                return state

            lax.fori_loop(0, rows // 8, block, [start_ref[m, h0 + h] for h in range(8)])

    def finish(b, carry):
        at = pl.ds(pl.multiple_of(b * 16, 16), 16)
        v = jnp.concatenate([collect(acc_ref, 2 * b), collect(acc_ref, 2 * b + 1)], axis=0)
        blended_ref[at, :] = v
        low_ref[at, :] = (v / (1.0 + jnp.exp(-v))).astype(BF16)
        return carry

    lax.fori_loop(0, micros * rows // 16, finish, 0)


def shared_kernel(
    before, flags, gp0_ref, gp1_ref, probs_ref, query_ref, key_ref, shared_ref, pre_ref, gain_ref, gates_ref, weight_ref,
    mix0_ref, mix1_ref, blended_ref, decay_ref, tell_ref,
    rows_ref, left_ref, low_ref, sums_ref,
):
    b = pl.program_id(0)
    width = mix0_ref.shape[-1]
    probs = probs_ref[0]
    grad_probs = gp0_ref[0] + gp1_ref[0]
    scale = query_ref.shape[-1] ** (-0.5)
    grad_scores = probs * (grad_probs - jnp.sum(grad_probs * probs, axis=-1, keepdims=True)) * scale
    exact = partial(lax.dot_general, precision=HIGHEST, preferred_element_type=F32)
    grad_query = exact(grad_scores, key_ref[...].astype(F32), (((1,), (0,)), ((), ())))
    grad_key = exact(grad_scores, query_ref[...].astype(F32), (((0,), (0,)), ((), ())))
    shared = shared_ref[...]
    pre = pre_ref[...]
    grad_pre = (grad_query * gain_ref[0:1] + grad_key * gain_ref[1:2]) * slope(pre, sigmoid(pre))
    low = grad_pre.astype(BF16)
    low_ref[...] = low
    total = lambda v: jnp.sum(v, axis=0, keepdims=True)
    part = jnp.concatenate(
        [
            total(grad_query * shared), total(grad_key * shared), total(grad_query), total(low.astype(F32)),
            jnp.zeros((4, low.shape[-1]), F32),
        ]
    )
    add_to(sums_ref, part)
    mixed = (
        mix0_ref[...]
        + mix1_ref[...]
        + dot_nt(gates_ref[...], weight_ref[:, : 2 * width])
        + dot_nt(low, weight_ref[:, 2 * width :])
    )
    v = blended_ref[...]
    grad = mixed * slope(v, sigmoid(v))
    for i in range(BLOCK // 8):
        spread(rows_ref, b * (BLOCK // 8) + i, grad[8 * i : 8 * i + 8])

    @pl.when(b == pl.num_programs(0) - 1)
    def _():
        micros, rows = flags.shape
        heads = decay_ref.shape[0]
        for m in range(micros):
            for h0 in range(0, heads, 8):
                decay = [decay_ref[h0 + h] for h in range(8)]
                tell = [tell_ref[h0 + h] for h in range(8)]

                def block(i, left, m=m, decay=decay, tell=tell):
                    b = rows // 8 - 1 - i
                    base = pl.multiple_of((m * (rows // 8) + b) * 64, 64)
                    for r in reversed(range(8)):
                        keep = (1 - flags[m, b * 8 + r]).astype(F32)
                        row = row_of(rows_ref, base, r)
                        left = [((t * row + k) * keep) * q for k, q, t in zip(left, decay, tell)]
                    return left

                left = lax.fori_loop(0, rows // 8, block, [jnp.zeros((8, 128), F32)] * 8)
                for h in range(8):
                    left_ref[m, h0 + h] = left[h]


def run_shared(token, flags, gp0, gp1, probs, query, key, shared, pre, gain, gates, weight, mix0, mix1, blended, decay, tell):
    total, width = mix0.shape
    z = query.shape[1]
    rows = lambda n: pl.BlockSpec((BLOCK, n), lambda b: (b, 0))
    pair = pl.BlockSpec((1, BLOCK, BLOCK), lambda b: (b, 0, 0))
    whole = lambda a: pl.BlockSpec(a.shape, lambda b: (0,) * a.ndim)
    micros, heads = flags.shape[0], decay.shape[0]
    return pl.pallas_call(
        shared_kernel,
        grid=(total // BLOCK,),
        in_specs=[
            pl.BlockSpec(memory_space=pl.ANY), pl.BlockSpec(memory_space=pltpu.SMEM), pair, pair, pair, rows(z), rows(z), rows(z), rows(z), whole(gain),
            rows(2 * width), whole(weight), rows(width), rows(width), rows(width), whole(decay), whole(tell),
        ],
        out_specs=[
            pl.BlockSpec((total * 8, 128), lambda b: (0, 0)),
            pl.BlockSpec((micros, heads, 8, 128), lambda b: (0, 0, 0, 0)),
            rows(z),
            pl.BlockSpec((8, z), lambda b: (0, 0)),
        ],
        out_shape=[
            shape_of(total * 8, 128), shape_of(micros, heads, 8, 128), shape_of(total, z, dtype=BF16), shape_of(8, z),
        ],
        cost_estimate=cost(200),
    )(token, flags, gp0, gp1, probs, query, key, shared, pre, gain, gates, weight, mix0, mix1, blended, decay, tell)


def back_kernel(
    m, before, flags, normed_ref, rows_ref, start_ref, right_ref, decay_ref, feed_ref, tell_ref, omega_ref,
    add0_ref, add1_ref, source_ref, base_ref, gain_ref,
    grad_ref, eta_ref, one_ref, two_ref, omega_out, gain_out, token_ref, states, acc_ref,
):
    rows = flags.shape[1]
    heads = decay_ref.shape[0]
    group = 4
    omega = omega_ref[...]
    zero = jnp.zeros((8, 128), F32)
    token_ref[...] = zero
    for h0 in range(0, heads, group):
        decay = [decay_ref[h0 + h] for h in range(group)]
        feed = [feed_ref[h0 + h] for h in range(group)]
        tell = [tell_ref[h0 + h] for h in range(group)]

        def ahead(b, state, decay=decay, feed=feed):
            base = pl.multiple_of(b * 64, 64)
            for r in range(8):
                keep = (1 - flags[m, b * 8 + r]).astype(F32)
                for h in range(group):
                    states[b * 8 + r, h] = state[h]
                state = ema_step(state, row_of(normed_ref, base, r), keep, decay, feed)
            return state

        last = lax.fori_loop(0, rows // 8, ahead, [start_ref[0, h0 + h] for h in range(group)])

        def back(i, carry, h0=h0, decay=decay, feed=feed, tell=tell):
            left, after_state, eta, one, two, with_omega = carry
            b = rows // 8 - 1 - i
            base = pl.multiple_of(b * 64, 64)
            for r in reversed(range(8)):
                keep = (1 - flags[m, b * 8 + r]).astype(F32)
                g = row_of(rows_ref, base, r)
                x = row_of(normed_ref, base, r)
                earlier = [states[b * 8 + r, h] for h in range(group)]
                eta = [e + s * g for e, s in zip(eta, after_state)]
                now = [t * g + k for t, k in zip(tell, left)]
                one = [o + n * x for o, n in zip(one, now)]
                kept = [n * keep for n in now]
                two = [w + k * s for w, k, s in zip(two, kept, earlier)]
                left = [k * q for k, q in zip(kept, decay)]
                gn = [n * f for n, f in zip(now, feed)]
                while len(gn) > 1:
                    gn = [gn[i] + gn[i + 1] for i in range(0, len(gn), 2)]
                at = pl.ds(base + r, 8, stride=8)
                if h0 == 0:
                    acc_ref[at, :] = gn[0] + omega * g
                    with_omega = with_omega + g * x
                else:
                    acc_ref[at, :] = acc_ref[at, :] + gn[0]
                after_state = earlier
            return left, after_state, eta, one, two, with_omega

        right = [right_ref[0, h0 + h] for h in range(group)]
        nothing = [zero] * group
        _, _, eta, one, two, with_omega = lax.fori_loop(
            0, rows // 8, back, (right, last, nothing, nothing, nothing, zero)
        )
        if h0 == 0:
            omega_out[...] = with_omega
        for h in range(group):
            eta_ref[h0 + h] = eta[h]
            one_ref[h0 + h] = one[h]
            two_ref[h0 + h] = two[h]

    def finish(b, gained):
        at = pl.ds(pl.multiple_of(b * 16, 16), 16)
        x = source_ref[at, :].astype(F32)
        scale = lax.rsqrt(jnp.mean(x * x, axis=-1, keepdims=True) + EPSILON)
        scaled = x * scale
        grad = jnp.concatenate([collect(acc_ref, 2 * b), collect(acc_ref, 2 * b + 1)], axis=0)
        grad = grad + add0_ref[at, :] + add1_ref[at, :]
        own = grad * scaled
        gained = gained + own[:8] + own[8:]
        inner = grad * gain_ref[...]
        mean = jnp.mean(inner * scaled, axis=-1, keepdims=True)
        grad_ref[at, :] = base_ref[at, :] + scale * (inner - scaled * mean)
        return gained

    width = source_ref.shape[-1]
    gain_out[...] = lax.fori_loop(0, rows // 16, finish, jnp.zeros((8, width), F32))


def run_back(m, token, flags, laid, grads, start, right, decay, feed, tell, omega, add0, add1, source, base, gain):
    rows, heads = flags.shape[1], decay.shape[0]
    width = source.shape[1]
    whole = lambda a: pl.BlockSpec(a.shape, lambda i: (0,) * a.ndim)
    tall = pl.BlockSpec((rows * 8, 128), lambda i: (m, 0))
    carry = pl.BlockSpec((1, heads, 8, 128), lambda i: (m, 0, 0, 0))
    wide = pl.BlockSpec((rows, width), lambda i: (m, 0))
    sums = pl.BlockSpec((heads, 8, 128), lambda i: (0, 0, 0))
    return pl.pallas_call(
        partial(back_kernel, m),
        grid=(1,),
        in_specs=[
            pl.BlockSpec(memory_space=pl.ANY), pl.BlockSpec(memory_space=pltpu.SMEM), tall, tall, carry, carry,
            whole(decay), whole(feed), whole(tell), whole(omega), wide, wide, wide, wide, whole(gain),
        ],
        out_specs=[
            pl.BlockSpec((rows, width), lambda i: (0, 0)), sums, sums, sums,
            pl.BlockSpec((8, 128), lambda i: (0, 0)), pl.BlockSpec((8, width), lambda i: (0, 0)),
            pl.BlockSpec((8, 128), lambda i: (0, 0)),
        ],
        out_shape=[
            jax.ShapeDtypeStruct((rows, width), F32),
            *[jax.ShapeDtypeStruct((heads, 8, 128), F32)] * 3,
            jax.ShapeDtypeStruct((8, 128), F32),
            jax.ShapeDtypeStruct((8, width), F32),
            jax.ShapeDtypeStruct((8, 128), F32),
        ],
        scratch_shapes=[pltpu.VMEM((rows, 4, 8, 128), F32), pltpu.VMEM((rows * 8, 128), F32)],
        cost_estimate=cost(200),
    )(token, flags, laid, grads, start, right, decay, feed, tell, omega, add0, add1, source, base, gain)


def dot_tn(a, b):
    return lax.dot_general(a, b, (((0,), (0,)), ((), ())), preferred_element_type=F32)


def dot_nt(a, b):
    return lax.dot_general(a, b, (((1,), (1,)), ((), ())), preferred_element_type=F32)


def dot_nn(a, b):
    return lax.dot_general(a, b, (((1,), (0,)), ((), ())), preferred_element_type=F32)


def sigmoid(v):
    return 1.0 / (1.0 + jnp.exp(-v))


def slope(v, s):
    return s * (1.0 + v * (1.0 - s))


def add_to(ref, value, first_ref=None):
    first = pl.program_id(0) == 0

    @pl.when(first)
    def _():
        ref[...] = value if first_ref is None else first_ref[...] + value

    @pl.when(jnp.logical_not(first))
    def _():
        ref[...] = ref[...] + value


def put_sides(ref, lead, v):
    half = v.shape[-1] // 2
    v = v.astype(BF16)
    ref[0, lead] = v[:, :half]
    ref[1, lead] = v[:, half:]


def value_kernel(
    piece, normed_ref, mixed_ref, probs_ref, wv_ref, wr_ref, wb_ref, bv_ref, br_ref, sum_ref,
    value_ref, reset_ref, attended_ref, gated_ref, out_ref,
):
    value_pre = dot_nt(normed_ref[...], flat(wv_ref)) + bv_ref[...]
    value_ref[...] = value_pre
    value = (value_pre * sigmoid(value_pre)).astype(BF16)
    blocks = probs_ref.shape[0]
    attended = jnp.concatenate(
        [dot_nn(probs_ref[b], value[b * BLOCK : (b + 1) * BLOCK]) for b in range(blocks)], axis=0
    )
    attended_ref[...] = attended
    reset_pre = dot_nt(mixed_ref[...], flat(wr_ref)) + br_ref[...]
    reset_ref[...] = reset_pre
    gated = (reset_pre * sigmoid(reset_pre) * attended).astype(BF16)
    gated_ref[...] = gated
    add_to(out_ref, dot_nn(gated, flat(wb_ref)), sum_ref)


def value_back_kernel(
    piece, grad_ref, normed_ref, mixed_ref, probs_ref, wv_ref, wr_ref, wb_ref,
    value_ref, reset_ref, attended_ref, gated_ref,
    d_ref, sum_r_ref, sum_v_ref, mixed_out, normed_out, probs_out,
):
    grad = grad_ref[...]
    grad_gated = dot_nt(grad, flat(wb_ref))
    put_sides(d_ref, 0, dot_tn(gated_ref[...], grad))
    reset_pre = reset_ref[...]
    s = sigmoid(reset_pre)
    grad_attended = (grad_gated * (reset_pre * s)).astype(BF16)
    grad_reset = (grad_gated * attended_ref[...] * slope(reset_pre, s)).astype(BF16)
    sum_r_ref[...] = jnp.sum(grad_reset.astype(F32), axis=0, keepdims=True)
    mixed = mixed_ref[...]
    put_sides(d_ref, 1, dot_tn(grad_reset, mixed))
    add_to(mixed_out, dot_nn(grad_reset, flat(wr_ref)))
    value_pre = value_ref[...]
    s = sigmoid(value_pre)
    value = (value_pre * s).astype(BF16)
    blocks = probs_ref.shape[0]
    grad_value, grad_probs = [], []
    for b in range(blocks):
        rows = slice(b * BLOCK, (b + 1) * BLOCK)
        grad_probs.append(dot_nt(grad_attended[rows], value[rows])[None])
        grad_value.append(dot_tn(probs_ref[b], grad_attended[rows]))
    add_to(probs_out, jnp.concatenate(grad_probs, axis=0))
    grad_value = (jnp.concatenate(grad_value, axis=0) * slope(value_pre, s)).astype(BF16)
    sum_v_ref[...] = jnp.sum(grad_value.astype(F32), axis=0, keepdims=True)
    put_sides(d_ref, 2, dot_tn(grad_value, normed_ref[...]))
    add_to(normed_out, dot_nn(grad_value, flat(wv_ref)))


def inner_kernel(piece, ffn_ref, grad_ref, wi_ref, bi_ref, pre_ref, activ_ref, do_ref):
    wi = flat(wi_ref)
    pre = dot_nt(ffn_ref[...], wi) + bi_ref[...]
    pre_ref[...] = pre
    activ = (pre * sigmoid(pre)).astype(BF16)
    activ_ref[...] = activ
    put_sides(do_ref, 0, dot_tn(activ, grad_ref[...]))


def outer_kernel(
    piece, ffn_ref, grad_ref, wi_ref, wo_ref, pre_ref, activ_ref, sum_o_ref, sum_f_ref,
    di_ref, sum_i_ref, out_ref, ffn_out,
):
    wi = flat(wi_ref)
    wo = flat(wo_ref)
    add_to(out_ref, dot_nn(activ_ref[...], wo), sum_o_ref)
    pre = pre_ref[...]
    grad = (dot_nt(grad_ref[...], wo) * slope(pre, sigmoid(pre))).astype(BF16)
    sum_i_ref[...] = jnp.sum(grad.astype(F32), axis=0, keepdims=True)
    put_sides(di_ref, 0, dot_tn(grad, ffn_ref[...]))
    add_to(ffn_out, dot_nn(grad, wi), sum_f_ref)


UNITS = 512


def cost(micros):
    return pl.CostEstimate(flops=int(micros * SCALE * 1.15e9), bytes_accessed=int(micros * SCALE * 3.3e6), transcendentals=0)


SCALE = 1.0


def shape_of(*dims, dtype=F32):
    return jax.ShapeDtypeStruct(dims, dtype)


def middle(gate_ref, branch_ref, source_ref):
    width = source_ref.shape[-1]
    update = sigmoid(gate_ref[:, :width])
    pre = gate_ref[:, width : 2 * width] + branch_ref[...]
    s = sigmoid(pre)
    return source_ref[...].astype(F32), update, pre, s


def middle_kernel(gate_ref, branch_ref, source_ref, gain_ref, mixed_ref, ffn_ref):
    source, update, pre, s = middle(gate_ref, branch_ref, source_ref)
    mixed = update * (pre * s) + (1.0 - update) * source
    mixed_ref[...] = mixed
    scale = lax.rsqrt(jnp.mean(mixed * mixed, axis=-1, keepdims=True) + EPSILON)
    ffn_ref[...] = (mixed * scale * gain_ref[...]).astype(BF16)


def column_sums(v):
    return jnp.sum(v.reshape(-1, 8, v.shape[-1]), axis=0)


def middle_back_kernel(
    before, gate_ref, branch_ref, source_ref, gain_ref, bias_ref, mixed_ref, feed_ref, grad_ref, ffn_ref,
    out_ref, base_ref, gates_ref, sum_gain_ref, sum_out_ref, sum_gates_ref,
):
    width = source_ref.shape[-1]
    source, update, pre, s = middle(gate_ref, branch_ref, source_ref)
    mixed = mixed_ref[...]
    out_ref[...] = (mixed + feed_ref[...] + bias_ref[...]).astype(BF16)
    scale = lax.rsqrt(jnp.mean(mixed * mixed, axis=-1, keepdims=True) + EPSILON)
    scaled = mixed * scale
    grad_out = grad_ref[...].astype(F32)
    grad_ffn = ffn_ref[...]
    add_to(sum_out_ref, column_sums(grad_out))
    add_to(sum_gain_ref, column_sums(grad_ffn * scaled))
    gained = grad_ffn * gain_ref[...]
    grad = grad_out + scale * (gained - scaled * jnp.mean(gained * scaled, axis=-1, keepdims=True))
    base_ref[...] = grad * (1.0 - update)
    grad_update = (grad * (pre * s - source) * update * (1.0 - update)).astype(BF16)
    grad_hidden = (grad * update * slope(pre, s)).astype(BF16)
    gates_ref[:, :width] = grad_update
    gates_ref[:, width:] = grad_hidden
    add_to(
        sum_gates_ref,
        jnp.concatenate([column_sums(grad_update.astype(F32)), column_sums(grad_hidden.astype(F32))], axis=1),
    )


def run_middle(gate, branch, source, gain):
    total, width = source.shape
    rows = lambda n: pl.BlockSpec((BLOCK, n), lambda i: (i, 0))
    line = pl.BlockSpec((1, width), lambda i: (0, 0))
    return pl.pallas_call(
        middle_kernel,
        grid=(total // BLOCK,),
        in_specs=[rows(gate.shape[1]), rows(width), rows(width), line],
        out_specs=[rows(width), rows(width)],
        out_shape=[shape_of(total, width), shape_of(total, width, dtype=BF16)],
        cost_estimate=cost(5),
    )(gate, branch, source, gain[None])


def run_middle_back(token, gate, branch, source, gain, bias, mixed, feed, grad, ffn):
    total, width = source.shape
    rows = lambda n: pl.BlockSpec((BLOCK, n), lambda i: (i, 0))
    line = pl.BlockSpec((1, width), lambda i: (0, 0))
    few = lambda n: pl.BlockSpec((8, n), lambda i: (0, 0))
    wide = rows(width)
    return pl.pallas_call(
        middle_back_kernel,
        grid=(total // BLOCK,),
        in_specs=[
            pl.BlockSpec(memory_space=pl.ANY), rows(gate.shape[1]), wide, wide, line, line, wide, wide, wide, wide
        ],
        out_specs=[wide, wide, rows(2 * width), few(width), few(width), few(2 * width)],
        out_shape=[
            shape_of(total, width, dtype=BF16), shape_of(total, width), shape_of(total, 2 * width, dtype=BF16),
            shape_of(8, width), shape_of(8, width), shape_of(8, 2 * width),
        ],
        cost_estimate=cost(1),
    )(token, gate, branch, source, gain[None], bias[None], mixed, feed, grad, ffn)


def gates_kernel(piece, before, mixed_ref, gates_ref, d_ref):
    grad = dot_tn(mixed_ref[...], gates_ref[...]).astype(BF16)
    half = grad.shape[-1] // 2
    d_ref[0] = grad[:, :half].reshape(d_ref.shape[1:])
    d_ref[1] = grad[:, half:].reshape(d_ref.shape[1:])


def run_gates(which, token, mixed, gates):
    total, width = mixed.shape
    n = which.shape[0]
    block = width // (2 * n)
    return pl.pallas_call(
        gates_kernel,
        grid_spec=pltpu.PrefetchScalarGridSpec(
            num_scalar_prefetch=1,
            grid=(n,),
            in_specs=[
                pl.BlockSpec(memory_space=pl.ANY),
                pl.BlockSpec((total, block), lambda i, p: (0, p[i])),
                pl.BlockSpec(gates.shape, lambda i, p: (0, 0)),
            ],
            out_specs=pl.BlockSpec((2, 1, block, width), lambda i, p: (0, 0, i, 0)),
        ),
        out_shape=shape_of(2, 1, n * block, width, dtype=BF16),
        cost_estimate=cost(1),
    )(which, token, mixed, gates)


class Pieces:
    def __init__(self, gathered, which, tensor, part_f, part_v):
        self.gathered, self.which, self.tensor = gathered, which, tensor
        self.part_f, self.part_v = part_f, part_v
        self.width = gathered.shape[-1]

    def units(self, part):
        return self.which.shape[0] * self.tensor * part

    def block(self, part):
        return min(UNITS, self.tensor * part)

    def spec(self, part, row):
        step = self.block(part) // part
        per = self.tensor // step
        return pl.BlockSpec(
            (step, part, self.width), lambda i, p: (p[i // per] * per + i % per, row // part, 0)
        )

    @property
    def w_in(self):
        return self.spec(self.part_f, 0)

    @property
    def w_out(self):
        return self.spec(self.part_f, self.part_f)

    def v(self, k):
        return self.spec(self.part_v, 2 * self.part_f + k * self.part_v)


def flat(ref):
    return ref[...].reshape(-1, ref.shape[-1])


def blocked(kernel, micros, pieces, steps, token, in_specs, out_specs, out_shape, *arrays):
    def body(piece, before, *refs):
        kernel(piece, *refs)

    return pl.pallas_call(
        body,
        grid_spec=pltpu.PrefetchScalarGridSpec(
            num_scalar_prefetch=1,
            grid=(steps,),
            in_specs=[pl.BlockSpec(memory_space=pl.ANY), *in_specs],
            out_specs=out_specs,
        ),
        out_shape=out_shape,
        cost_estimate=cost(micros),
    )(pieces.which, token, *arrays)


def block_specs(total, width, block, lead):
    full = pl.BlockSpec((total, width), lambda i, p: (0, 0))
    cols = pl.BlockSpec((total, block), lambda i, p: (0, i))
    line = pl.BlockSpec((1, block), lambda i, p: (0, i))
    grads = pl.BlockSpec((2, lead, block, width // 2), lambda i, p: (0, 0, i, 0))
    return full, cols, line, grads


def run_value(pieces, token, normed, mixed, probs, bv, br, before):
    total, width = normed.shape
    units, block = pieces.units(pieces.part_v), pieces.block(pieces.part_v)
    full, cols, line, grads = block_specs(total, width, block, 3)
    pairs = pl.BlockSpec(probs.shape, lambda i, p: (0, 0, 0))
    g = pieces.gathered
    return blocked(
        value_kernel, 200, pieces, units // block, token,
        [full, full, pairs, pieces.v(0), pieces.v(1), pieces.v(2), line, line, full],
        [cols, cols, cols, cols, full],
        [shape_of(total, units)] * 3 + [shape_of(total, units, dtype=BF16), shape_of(total, width)],
        normed, mixed, probs, g, g, g, bv, br, before,
    )


def run_value_back(pieces, micros, token, grad, normed, mixed, probs, kept):
    total, width = normed.shape
    units, block = pieces.units(pieces.part_v), pieces.block(pieces.part_v)
    full, cols, line, grads = block_specs(total, width, block, 3)
    pairs = pl.BlockSpec(probs.shape, lambda i, p: (0, 0, 0))
    g = pieces.gathered
    return blocked(
        value_back_kernel, micros, pieces, units // block, token,
        [
            pl.BlockSpec((total, width), lambda i, p: (0, 1)), full, full, pairs,
            pieces.v(0), pieces.v(1), pieces.v(2), cols, cols, cols, cols,
        ],
        [grads, line, line, full, full, pairs],
        [shape_of(2, 3, units, width // 2, dtype=BF16)]
        + [shape_of(1, units)] * 2
        + [shape_of(total, width)] * 2
        + [shape_of(*probs.shape)],
        grad, normed, mixed, probs, g, g, g, *kept,
    )


def run_inner(pieces, token, ffn, grad, bias):
    total, width = ffn.shape
    units, block = pieces.units(pieces.part_f), pieces.block(pieces.part_f)
    full, cols, line, grads = block_specs(total, width, block, 1)
    return blocked(
        inner_kernel, 200, pieces, units // block, token,
        [full, full, pieces.w_in, line],
        [cols, cols, grads],
        [shape_of(total, units), shape_of(total, units, dtype=BF16), shape_of(2, 1, units, width // 2, dtype=BF16)],
        ffn, grad, pieces.gathered, bias,
    )


def run_outer(pieces, token, ffn, grad, pre, activ, before_out, before_ffn):
    total, width = ffn.shape
    units, block = pieces.units(pieces.part_f), pieces.block(pieces.part_f)
    full, cols, line, grads = block_specs(total, width, block, 1)
    return blocked(
        outer_kernel, 200, pieces, units // block, token,
        [full, full, pieces.w_in, pieces.w_out, cols, cols, full, full],
        [grads, line, full, full],
        [shape_of(2, 1, units, width // 2, dtype=BF16), shape_of(1, units), shape_of(total, width), shape_of(total, width)],
        ffn, grad, pieces.gathered, pieces.gathered, pre, activ, before_out, before_ffn,
    )


def call(kernel, outs, scratch, smem, *arrays):
    return pl.pallas_call(
        kernel,
        out_shape=outs,
        in_specs=[pl.BlockSpec(memory_space=pltpu.SMEM)] * smem
        + [pl.BlockSpec(memory_space=pltpu.VMEM)] * (len(arrays) - smem),
        out_specs=jax.tree.map(lambda _: pl.BlockSpec(memory_space=pltpu.VMEM), outs),
        scratch_shapes=scratch,
        cost_estimate=cost(12),
    )(*arrays)


def scan_carry(grid, local, clear, whole, reverse):
    micros, heads = local.shape[:2]
    clear = jnp.broadcast_to(clear[:, None, None, None], (micros, 1, 8, 128))
    entering = jnp.zeros_like(local)
    reach = jnp.ones_like(local)
    total = local
    for mask in grid.tensor:
        got = grid.swap(jnp.concatenate([total, clear], axis=1), mask)
        got_total, got_clear = got[:, :heads], got[:, heads:]
        later = grid.bit(mask) == (0 if reverse else 1)
        entering = jnp.where(later, entering + reach * got_total, entering)
        reach = jnp.where(later, reach * got_clear * whole, reach)
        total = jnp.where(
            later, total + clear * whole * got_total, got_total + got_clear * whole * total
        )
        clear = clear * got_clear
        whole = whole * whole
    return entering


def after(values, *others):
    return lax.optimization_barrier((values, others))[0]


class Term:
    def __init__(self, array, labels, fixed):
        self.array, self.labels, self.fixed = array, labels, fixed


class Reduce:
    def __init__(self, grid, high, dims, still=()):
        self.grid, self.dims, self.still = grid, list(dims), still
        self.labels = ["side", "lead", *self.dims, "u", "h"]
        xs, (lo, *hi) = grid.xs[::-1], grid.tensor
        self.orders = [[*xs, lo], [lo, *xs]], hi[::-1]
        self.step = -1
        self.high = self.view(high)
        self.raw = [grid.swap(self.high, grid.core)]

    def view(self, v):
        n = len(self.dims)
        return v.reshape(*v.shape[:2], *[2] * n, v.shape[2] >> n, v.shape[3])

    @property
    def steps(self):
        return len(self.orders[0][0]) + len(self.orders[1])

    def add_low(self, low):
        self.low = self.view(low)

    def take(self):
        if self.step < 0:
            self.sides = [[Term(a, self.labels, {"side": s}) for a in (self.low, self.raw[0])] for s in (0, 1)]
            self.left = [list(self.dims), list(self.dims)]
        else:
            for s in (0, 1):
                for t in self.sides[s]:
                    if self.masks[s] in t.labels:
                        t.fixed[self.masks[s]] = 0
                self.left[s] = [d for d in self.left[s] if d != self.masks[s]]
                if len(self.raw) == 2:
                    self.sides[s].append(Term(self.raw[s], ["lead", *self.left[s], "u", "h"], {}))
                else:
                    self.sides[s].append(Term(self.raw[0], ["lead", *self.left[s], "u", "hh"], {"hh": s}))
        self.step += 1

    def wanted(self):
        (first, second), hi = self.orders
        k = self.step
        if k == self.steps:
            return [(self.sides[s], {}, self.left[s]) for s in (0, 1)], True
        self.masks = [first[k], second[k]] if k < len(first) else [hi[k - len(first)]] * 2
        return [
            (self.sides[s], {self.masks[s]: 1}, [d for d in self.left[s] if d != self.masks[s]]) for s in (0, 1)
        ], k >= len(first)

    def start(self, sends):
        if len(sends) == 2:
            self.raw = [self.grid.swap(v, m) for v, m in zip(sends, self.masks)]
        else:
            self.raw = [self.grid.swap(sends[0], self.masks[0])]


def place_of(grid, still, fixed, name, sel):
    if name in still:
        masks = [*grid.tensor, *grid.xs]
        return sel[2 * masks.index(name) + fixed[name]]
    return fixed[name]


def picked(grid, still, term, extra, sel):
    v = term.array
    fixed = {**term.fixed, **extra}
    for axis in reversed(range(len(term.labels))):
        name = term.labels[axis]
        if name == "hh":
            half = v.shape[-1] // 2
            v = v[..., fixed[name] * half : (fixed[name] + 1) * half]
        elif name in fixed:
            v = lax.dynamic_index_in_dim(v, place_of(grid, still, fixed, name, sel), axis, False)
    return v.astype(F32)


def point(grid, gates, *sums):
    for r in sums:
        r.take()
    outs, tasks = [], []
    for r in sums:
        sides, joined = r.wanted()
        for terms, fixed, left in sides:
            tasks.append((r, terms, fixed, left))
        shapes = []
        for terms, fixed, left in sides:
            low = r.low.shape
            shapes.append((low[1], *[2] * len(left), *low[-2:]))
        if joined:
            outs.append((*shapes[0][:-1], 2 * shapes[0][-1]))
        else:
            outs.extend(shapes)
    sel = grid.sel
    fits = all(len(r.dims) <= 4 and r.low.shape[-2] % 32 == 0 for r in sums)
    if fits:
        *values, token = run_point(grid, gates, tasks, outs, sel)
    else:
        values = []
        sides = [
            sum(picked(grid, r.still, t, {k: v for k, v in fixed.items() if k in t.labels}, sel) for t in terms).astype(BF16)
            for r, terms, fixed, left in tasks
        ]
        for shape in outs:
            v = sides.pop(0)
            values.append(v if v.shape == shape else jnp.concatenate([v, sides.pop(0)], axis=-1))
        token = after(jnp.zeros((8, 128), F32), [g[(0,) * g.ndim] for g in gates])
    done = []
    for r in sums:
        if r.step == r.steps:
            done.append(values.pop(0))
        else:
            n = 2 if r.step < len(r.orders[0][0]) else 1
            r.start(values[:n])
            values = values[n:]
    return (token, *done) if done else token


def run_point(grid, gates, tasks, outs, sel):
    parts = 2
    arrays, specs, layout = [], [], []
    for r, terms, extra, left in tasks:
        mine = []
        for t in terms:
            fixed = {**t.fixed, **{k: v for k, v in extra.items() if k in t.labels}}
            block = []
            for name, size in zip(t.labels, t.array.shape):
                if name == "hh":
                    block.append(size // 2)
                elif name == "u":
                    block.append(size // parts)
                else:
                    block.append(None if name in fixed else size)

            def index(i, p, t=t, fixed=fixed, r=r):
                return tuple(
                    i if name == "u" else place_of(grid, r.still, fixed, name, p) if name in fixed else 0
                    for name in t.labels
                )

            mine.append(len(arrays))
            arrays.append(t.array)
            specs.append(pl.BlockSpec(tuple(block), index))
        layout.append(mine)
    out_specs = []
    for shape in outs:
        block = (*shape[:-2], shape[-2] // parts, shape[-1])
        out_specs.append(pl.BlockSpec(block, lambda i, p, n=len(shape): (*[0] * (n - 2), i, 0)))
    out_specs.append(pl.BlockSpec((8, 128), lambda i, p: (0, 0)))

    def body(p, *refs):
        refs = refs[len(gates) :]
        ins, results = refs[: len(arrays)], refs[len(arrays) :]
        queue = list(layout)
        for ref in results[:-1]:
            first = 0
            while first < ref.shape[-1]:
                mine = queue.pop(0)
                total = ins[mine[0]][...].astype(F32)
                for k in mine[1:]:
                    total = total + ins[k][...].astype(F32)
                ref[..., first : first + total.shape[-1]] = total.astype(BF16)
                first += total.shape[-1]
        results[-1][...] = jnp.zeros((8, 128), F32)

    return pl.pallas_call(
        body,
        grid_spec=pltpu.PrefetchScalarGridSpec(
            num_scalar_prefetch=1,
            grid=(parts,),
            in_specs=[pl.BlockSpec(memory_space=pl.ANY)] * len(gates) + specs,
            out_specs=out_specs,
        ),
        out_shape=[shape_of(*shape, dtype=BF16) for shape in outs] + [shape_of(8, 128)],
        cost_estimate=cost(1),
    )(sel, *gates, *arrays)


def ends(result):
    return result if isinstance(result, tuple) else (result,)


def finish(grid, gates, r, value=None):
    while value is None:
        out = point(grid, gates, r)
        value = out[1] if isinstance(out, tuple) else None
    return value


def share_units(grid, part):
    held = part[None]
    masks = [*grid.xs, grid.core]
    for mask in masks:
        held = jnp.concatenate([held, grid.swap(held, mask)], axis=0)
    n = held.shape[0]
    held = held.astype(F32)
    for k, mask in enumerate(masks):
        held = held.reshape(n >> (k + 1), 2, -1, *part.shape)
        held = jnp.where(grid.bit(mask) == 1, held[:, ::-1], held)
    held = held.reshape(n, *part.shape).transpose(1, 0, 2, 3)
    return held.reshape(part.shape[0], -1, part.shape[-1])


def place_kernel(turned, bits, own_ref, x_ref, c_ref, *outs):
    swap_c, swap_x = bits[0] == 1, bits[1] == 1
    for k, turn in enumerate(turned):
        rows = []
        for own, other in ((own_ref[k], x_ref[k]), (c_ref[0, k], c_ref[1, k])):
            own, other = own.astype(F32), other.astype(F32)
            rows.append(jnp.concatenate([jnp.where(swap_x, other, own), jnp.where(swap_x, own, other)], axis=0))
        v = jnp.concatenate(
            [jnp.where(swap_c, rows[1], rows[0]), jnp.where(swap_c, rows[0], rows[1])], axis=0
        )
        outs[k][...] = v.T if turn else v


def share_and_place(grid, parts, turned, zero):
    results = []
    for part, turns in zip(parts, turned):
        if zero is not None:
            part = part + zero
        lead, units, width = part.shape
        if len(grid.xs) > 1 or units % 16:
            rows = share_units(grid, part)
            results.append([r.T if t else r for r, t in zip(rows, turns)])
            continue
        from_x = grid.swap(part, grid.xs[0])
        from_c = grid.swap(jnp.stack([part, from_x]), grid.core)
        results.append(
            pl.pallas_call(
                partial(place_kernel, turns),
                in_specs=[pl.BlockSpec(memory_space=pltpu.SMEM)] + [pl.BlockSpec(memory_space=pltpu.VMEM)] * 3,
                out_specs=[pl.BlockSpec(memory_space=pltpu.VMEM)] * lead,
                out_shape=[shape_of(*((width, 4 * units) if t else (4 * units, width))) for t in turns],
                cost_estimate=cost(5),
            )(jnp.stack([grid.bit(grid.core), grid.bit(grid.xs[0])]).astype(jnp.int32), part, from_x, from_c)
        )
    return results


def join_kernel(left_ref, right_ref, out_ref):
    n = left_ref.shape[1]
    out_ref[:, :n] = left_ref[...].astype(F32)
    out_ref[:, n:] = right_ref[...].astype(F32)


def join(left, right):
    rows, n = left.shape
    block = 256
    return pl.pallas_call(
        join_kernel,
        grid=(rows // block,),
        in_specs=[pl.BlockSpec((block, n), lambda i: (i, 0)), pl.BlockSpec((block, right.shape[1]), lambda i: (i, 0))],
        out_specs=pl.BlockSpec((block, n + right.shape[1]), lambda i: (i, 0)),
        out_shape=shape_of(rows, n + right.shape[1]),
        cost_estimate=cost(5),
    )(left, right)


def sum_flat(grid, v, part):
    held = v.reshape(-1, 128)
    n = held.shape[0]
    parts = part.astype(BF16)
    masks = [grid.core, *grid.xs, *grid.tensor]
    for mask in masks:
        low = held.astype(BF16)
        got = grid.swap(jnp.concatenate([low, parts]), mask)
        held = low.astype(F32) + got[:n].astype(F32)
        parts = jnp.concatenate([parts, got[n:]])
    parts = parts.reshape(*[2] * len(masks), *part.shape)
    order = masks[::-1]
    for axis, mask in enumerate(order):
        parts = jnp.where(grid.bit(mask) == 1, jnp.flip(parts, axis), parts)
    want = [*grid.xs[::-1], grid.core, *grid.tensor[::-1]]
    parts = parts.transpose(*[order.index(m) for m in want], len(order), len(order) + 1)
    return held.reshape(-1), parts.reshape(-1, part.shape[-1])


def padded(v, size):
    return jnp.concatenate([v, jnp.zeros(-v.size % size, F32)])


def local(
    inputs, resets, cotangent, norm_gain, ema_alpha, ema_damp, ema_beta, ema_eta, ema_omega,
    w_gates, b_gates, qk_gain, q_bias, w_value, b_value, w_reset, b_reset, w_branch, ffn_gain,
    w_in, b_in, w_out, b_out,
):
    grid = Grid()
    micros, rows, width = inputs.shape
    total = micros * rows
    heads = ema_alpha.shape[1]
    rank = lax.axis_index("tensor")
    units_v, units_f = w_value.shape[1], w_in.shape[1]
    n_x = 1 << len(grid.xs)
    split_x = n_x == 2
    core, x_at = grid.bit(grid.core), lax.axis_index("dp") // 2

    half_v, half_f = units_v // 2, units_f // 2

    def chunks(w, half, axis, whole):
        size = half // n_x
        picks = range(n_x) if whole else range(1)
        return jnp.concatenate(
            [lax.dynamic_slice_in_dim(w, core * half + (x_at ^ r) * size, size, axis) for r in picks],
            axis=axis,
        )

    n_tensor = lax.axis_size("tensor")
    part_f, part_v = half_f // n_x, half_v // n_x
    own = lambda w, half, axis: chunks(w, half, axis, False)
    bias = jnp.concatenate([own(b_value, half_v, 0), own(b_reset, half_v, 0), own(b_in, half_f, 0)])
    bias = jnp.zeros((8, width), BF16).at[0, : bias.size].set(bias)
    seed = jnp.concatenate(
        [
            own(w_in, half_f, 1).T, own(w_out, half_f, 0), own(w_value, half_v, 1).T,
            own(w_reset, half_v, 1).T, own(w_branch, half_v, 0), bias,
        ]
    )
    gathered = lax.all_gather(seed, AXES, axis=0)
    which = [
        jnp.stack([(x_at ^ r) * 2 + c for r in range(n_x)]).astype(jnp.int32) for c in (core, 1 - core)
    ]
    pieces = [Pieces(gathered, w, n_tensor, part_f, part_v) for w in which]
    table = gathered[:, 2 * part_f + 3 * part_v].astype(F32).reshape(2 * n_x, n_tensor, width)
    tables = [jnp.stack([lax.dynamic_index_in_dim(table, w[r], 0, False) for r in range(n_x)]) for w in which]
    bias_v = [t[..., :part_v].reshape(1, -1) for t in tables]
    bias_r = [t[..., part_v : 2 * part_v].reshape(1, -1) for t in tables]
    bias_i = [t[..., 2 * part_v : 2 * part_v + part_f].reshape(1, -1) for t in tables]
    dims = [*grid.xs[::-1], *grid.tensor[::-1]]
    still = grid.tensor

    def in_place(low, high):
        d = [grid.core, *dims]
        v = jnp.stack([low, high]).reshape(*[2] * len(d), -1)
        for axis, mask in enumerate(d):
            if mask not in still:
                v = jnp.where(grid.bit(mask) == 1, jnp.flip(v, axis), v)
        want = [*grid.tensor[::-1], grid.core, *grid.xs[::-1]]
        return v.transpose(*[d.index(m) for m in want], len(d)).reshape(-1)

    offsets = rank * rows + jnp.arange(rows)
    flags = jnp.where(offsets[None] == 0, 1, resets).astype(jnp.int32)
    sel = jnp.stack([grid.bit(m) ^ i for m in [*grid.tensor, *grid.xs] for i in (0, 1)]).astype(jnp.int32)
    places = [jnp.stack([2 * x + c for x in range(n_x)]).astype(jnp.int32) for c in (core, 1 - core)]
    flags, grid.sel, places, which = lax.optimization_barrier((flags, sel, places, which))
    for p, w in zip(pieces, which):
        p.which = w
    tile = lambda a: a.T.reshape(heads, 8, 128)
    decay = tile(1.0 - ema_alpha * ema_damp)
    feed = tile(ema_alpha * ema_beta)
    tell = tile(ema_eta)
    whole = jnp.exp(rows * jnp.log(decay))[None]
    clear = (jnp.sum(flags, axis=1) == 0).astype(F32)
    source_low = inputs.reshape(total, width)
    laid = jax.ShapeDtypeStruct((total * 8, 128), F32)
    wide = jax.ShapeDtypeStruct((total, width), F32)
    wide_low = jax.ShapeDtypeStruct((total, width), BF16)
    states = jax.ShapeDtypeStruct((micros, heads, 8, 128), F32)
    sums = jax.ShapeDtypeStruct((heads, 8, 128), F32)
    normed_laid, normed_low, final = call(
        norm_kernel, (laid, wide_low, states), [], 1,
        flags, source_low, norm_gain[None], decay, feed,
    )
    start = scan_carry(grid, final, clear, whole, False)
    blended, mixed_low = call(
        blend_kernel, (wide, wide_low), [pltpu.VMEM((total * 8, 128), F32)], 1,
        flags, normed_laid, start, decay, feed, tell, ema_omega.reshape(8, 128),
    )

    source = source_low.astype(F32)
    gate_pre = dot_plain(mixed_low, w_gates) + b_gates
    update = jax.nn.sigmoid(gate_pre[:, :width])
    direct = gate_pre[:, width : 2 * width]
    shared_pre = gate_pre[:, 2 * width :]
    shared = rounded(jax.nn.silu(shared_pre))
    query = (shared * qk_gain[0] + q_bias).astype(BF16)
    key = (shared * qk_gain[1]).astype(BF16)
    blocks = total // BLOCK
    doc = jnp.cumsum(flags.reshape(blocks, BLOCK), axis=1)
    order = jnp.arange(BLOCK)
    allowed = (doc[:, :, None] == doc[:, None, :]) & (order[:, None] >= order[None, :])[None]
    score_scale = query.shape[-1] ** (-0.5)
    query_b, key_b = query.reshape(blocks, BLOCK, -1), key.reshape(blocks, BLOCK, -1)
    scores = jnp.einsum("cik,cjk->cij", query_b, key_b, preferred_element_type=F32) * score_scale
    scores = jnp.where(allowed, scores, -1000000000.0)
    probs = jax.nn.softmax(scores, axis=-1)
    probs_low = probs.astype(BF16)

    sums_b = jnp.zeros((total, width), F32)
    kept = [None, None]
    for k in (0, 1):
        *kept[k], sums_b = run_value(pieces[k], bias_v[k], normed_low, mixed_low, probs_low, bias_v[k], bias_r[k], sums_b)
    branch = sums_b
    mixed_out, ffn_low = run_middle(gate_pre, branch, source_low, ffn_gain)
    grad_low = cotangent.reshape(total, width)

    inner = [None, None]
    inner[1] = run_inner(pieces[1], bias_i[1], ffn_low, grad_low, bias_i[1])
    r_out = Reduce(grid, inner[1][2], dims, still)
    inner[0] = run_inner(pieces[0], inner[1][1], ffn_low, grad_low, bias_i[0])
    r_out.add_low(inner[0][2])
    token = point(grid, [], r_out)
    feed_out = jnp.zeros((total, width), F32)
    sum_in = [None, None]
    d_high, sum_in[1], feed_out, grad_ffn = run_outer(
        pieces[1], token, ffn_low, grad_low, inner[1][0], inner[1][1], feed_out, feed_out
    )
    r_in = Reduce(grid, d_high, dims, still)
    token = point(grid, [sum_in[1]], r_out)
    d_low, sum_in[0], feed_out, grad_ffn = run_outer(
        pieces[0], token, ffn_low, grad_low, inner[0][0], inner[0][1], feed_out, grad_ffn
    )
    r_in.add_low(d_low)
    token = point(grid, [], r_out, r_in)
    output, grad_source, grad_gates_low, sum_ffn_gain, sum_out, sum_gates = run_middle_back(
        token, gate_pre, branch, source_low, ffn_gain, b_out, mixed_out, feed_out, grad_low, grad_ffn
    )
    bits = [*grid.xs[::-1], grid.core, *grid.tensor[::-1]]
    dims_g = [m for m in bits if m != grid.core]
    if width // (2 * n_x) % 128 == 0:
        d_gates = [None, None]
        d_gates[1] = run_gates(places[1], sum_gates, mixed_low, grad_gates_low)
        r_gates = Reduce(grid, d_gates[1], dims_g, dims_g)
        d_gates[0] = run_gates(places[0], d_gates[1], mixed_low, grad_gates_low)
        r_gates.add_low(d_gates[0])
        token = d_gates[0]
    else:
        c_axis = bits.index(grid.core)
        d_gates = [
            dot_over_rows(mixed_low, side).astype(BF16).reshape(*[2] * len(bits), -1, width)
            for side in (grad_gates_low[:, :width], grad_gates_low[:, width:])
        ]
        half_of = lambda i: jnp.stack(
            [lax.dynamic_index_in_dim(d, i, c_axis, False).reshape(1, width // 2, width) for d in d_gates]
        )
        r_gates = Reduce(grid, half_of(1 - core), dims_g, dims_g)
        r_gates.add_low(half_of(core))
        token = sum_gates

    def run_vb(k, token):
        return run_value_back(pieces[k], 200 if k == 0 else 1, token, grad_gates_low, normed_low, mixed_low, probs_low, kept[k])

    back = [None, None]
    back[1] = run_vb(1, token)
    r_v = Reduce(grid, back[1][0], dims, still)
    token = point(grid, [back[1][1]], r_out, r_in, r_gates)
    back[0] = run_vb(0, token)
    r_v.add_low(back[0][0])
    token = point(grid, [back[0][1]], r_v, r_gates, r_in)
    grad_laid, left, grad_shared_low, sums_shared = run_shared(
        token, flags, back[0][5], back[1][5], probs, query, key, shared, shared_pre, qk_gain, grad_gates_low, w_gates,
        back[0][3], back[1][3], blended, decay, tell,
    )
    token = point(grid, [left], r_gates, r_in)
    left = left + token[0, 0]
    d_shared = dot_over_rows(mixed_low, grad_shared_low + token[0, 0].astype(BF16))
    d_shared = d_shared.reshape(*[2] * len(bits), -1, d_shared.shape[-1])

    def fold(v, mask):
        axis, here = bits.index(mask), grid.bit(mask)
        got = grid.swap(lax.dynamic_slice_in_dim(v, 1 - here, 1, axis).astype(BF16), mask)
        return lax.dynamic_slice_in_dim(v, here, 1, axis) + got.astype(F32)

    right = scan_carry(grid, left, clear, whole, True)
    t_first, *t_rest = grid.tensor
    for mask in [grid.core, *grid.xs, t_first]:
        d_shared = fold(d_shared, mask)
    token = point(grid, [right], r_v, r_gates)
    d_shared = fold(d_shared + token[0, 0], t_rest[0])
    column = shape_of(8, 128)
    results = []
    for m in range(micros):
        part = slice(m * rows, (m + 1) * rows)
        laid_part = slice(m * rows * 8, (m + 1) * rows * 8)
        results.append(
            run_back(
                m, token, flags, normed_laid, grad_laid, start, right, decay, feed, tell, ema_omega.reshape(8, 128),
                back[0][4], back[1][4], source_low, grad_source, norm_gain[None],
            )
        )
        if m == 0:
            token, *done = ends(point(grid, [results[0][1]], r_gates, r_in, r_out, r_v))
            d_shared = d_shared + token[0, 0]
            for mask in t_rest[1:]:
                d_shared = fold(d_shared, mask)
    done_gates = finish(grid, [token], r_gates, *done[:1])
    done_in = finish(grid, [token], r_in, *done[1:2])
    done_out = finish(grid, [token], r_out, *done[2:])
    token_v = point(grid, [results[-1][1]], r_v)
    done_v = finish(grid, [token_v], r_v)
    grad_w_out, grad_w_in = share_and_place(grid, [done_out, done_in], [(False,), (True,)], None)
    (grad_w_out,), (grad_w_in,) = grad_w_out, grad_w_in
    grad_w_gates = lax.all_gather(
        done_gates.reshape(width // grid.count, 2 * width), AXES, axis=0, tiled=True
    )

    z = token_v[0, 0]
    spread_in = lambda k: in_place(back[0][k] + z, back[1][k] + z)
    early = [
        jnp.concatenate([jnp.sum(sum_gates + z, axis=0), sums_shared[3] + z]), sums_shared[:2].reshape(-1) + z,
        sums_shared[2] + z, jnp.sum(sum_ffn_gain + z, axis=0), jnp.sum(sum_out + z, axis=0),
        spread_in(2), spread_in(1), in_place(sum_in[0] + z, sum_in[1] + z),
    ]
    sum_eta, sum_one, sum_two, sum_omega, sum_norm_gain = (
        sum(r[k] + z for r in results) for k in range(1, 6)
    )
    late = [
        sum_eta.reshape(-1), sum_one.reshape(-1), sum_two.reshape(-1), jnp.sum(sum_norm_gain, axis=0), sum_omega.reshape(-1)
    ]

    def cut_like(v, parts):
        out, first = [], 0
        for p in parts:
            out.append(v[first : first + p.size])
            first += p.size
        return out

    small = padded(jnp.concatenate(early), 128)
    summed, d_shared = sum_flat(
        grid, padded(jnp.concatenate([jnp.concatenate(late), small]), 2048), d_shared.reshape(width // grid.count, -1)
    )
    grad_w_gates = join(grad_w_gates, d_shared)
    last = cut_like(summed, late)
    cut = cut_like(summed[sum(p.size for p in late) :], early)
    ((grad_w_branch, grad_w_reset, grad_w_value),) = share_and_place(grid, [done_v], [(False, True, True)], None)
    untile = lambda v: v.reshape(heads, width).T
    eta, one, two = (untile(v) for v in last[:3])
    mine = lambda v, n: lax.dynamic_slice_in_dim(v, rank * n, n, 0)
    return (
        output.reshape(inputs.shape),
        jnp.stack([r[0] + z for r in results]),
        last[3],
        ema_beta * one - ema_damp * two,
        -ema_alpha * two,
        ema_alpha * one,
        eta,
        last[4],
        grad_w_gates,
        cut[0],
        cut[1].reshape(2, -1),
        cut[2],
        grad_w_value,
        mine(cut[5], units_v),
        grad_w_reset,
        mine(cut[6], units_v),
        grad_w_branch,
        cut[3],
        grad_w_in,
        mine(cut[7], units_f),
        grad_w_out,
        cut[4],
    )


def solution(mesh):
    rows = P(None, AXES, None)
    col, row, vec, rep = P(None, "tensor"), P("tensor", None), P("tensor"), P()
    return jax.shard_map(
        local,
        mesh=mesh,
        in_specs=(
            rows, P(None, AXES), rows, rep, rep, rep, rep, rep, rep, rep, rep, rep, rep,
            col, vec, col, vec, row, rep, col, vec, row, rep,
        ),
        out_specs=(
            rows, rows, rep, rep, rep, rep, rep, rep, rep, rep, rep, rep,
            col, vec, col, vec, row, rep, col, vec, row, rep,
        ),
        check_vma=False,
    )
```

time: 907 us -> 653 us (0.72)
  Pallas kernels: 62 us -> 289 us
  matrix products: 132 us -> 6.84 us
  local copies, waits for them, and re-layouts: 138 us -> 37.7 us
  starting transfers between devices: 137 us -> 42.5 us
  waiting for transfers between devices: 284 us -> 219 us
  blocking collectives: 48 us -> 0 us
  other arithmetic: 77.5 us -> 31 us
    pallas_call x0 -> x29, Pallas kernels: none -> 265 us  [the longest x8 120 us: blocked(): pl.pallas_call(body, grid_spec=pltpu.PrefetchScalarGridSpec(num_scalar_pr...]
    ppermute x136 -> x50, waiting for transfers between devices: 240 us -> 106 us  [swap(): return lax.ppermute(value, AXES, [(i, i ^ mask) for i in range(self.count)])]
    all_gather x3 -> x2, waiting for transfers between devices: 0.01 us -> 113 us  [the longest x1 113 us: local(): gathered = lax.all_gather(seed, AXES, axis=0)]
    ppermute x136 -> x50, starting transfers between devices: 136 us -> 42.4 us  [swap(): return lax.ppermute(value, AXES, [(i, i ^ mask) for i in range(self.count)])]
    unnamed x319 -> x179, local copies, waits for them, and re-layouts: 85.8 us -> 17.6 us
    dot_general x12 -> x0, matrix products: 60.1 us -> none  [the longest x6 49.6 us: dot_against(): lax.dot_general(a, b, (((1,), (1,)), ((), ())), preferred_element_type=F32)]
    all_gather x4 -> x0, blocking collectives: 48 us -> none  [the longest x1 26.3 us: local(): lax.all_gather(jnp.concatenate([b_value, b_reset, b_in])[None], 'tensor',...]
    convert_element_type x27 -> x4, other arithmetic: 48.8 us -> 1.24 us  [the longest x1 1.11 us: local(): gathered[:, 2 * part_f + 3 * part_v].astype(F32)]
  transfers between devices with their start and end apart: 140 -> 52, of which waited for: 50 -> 21; matrix products, arithmetic and copies ran while one was open for 24% -> 9% of each run, Pallas kernels for 6% -> 34%
where the time goes in v2:
time: 653 us; the launch traced here: 643 us
  Pallas kernels  289 us (44%)
  waiting for transfers between devices  219 us (34%)
  starting transfers between devices  42.5 us (7%)
  local copies, waits for them, and re-layouts  37.7 us (6%)
  other arithmetic  31 us (5%)
  between operations  16.8 us (3%)
  matrix products  6.84 us (1%)
    pallas_call x8, Pallas kernels, blocked(): pl.pallas_call(body, grid_spec=pltpu.PrefetchScalarGridSpec(num_scalar_pr...  120 us
    all_gather x1, waiting for transfers between devices, local(): gathered = lax.all_gather(seed, AXES, axis=0)  113 us
    ppermute x50, waiting for transfers between devices, swap(): return lax.ppermute(value, AXES, [(i, i ^ mask) for i in range(self.count)])  106 us
    pallas_call x10, Pallas kernels, run_point(): pl.pallas_call(body, grid_spec=pltpu.PrefetchScalarGridSpec(num_scalar_pr...  45.1 us
    ppermute x50, starting transfers between devices, swap(): return lax.ppermute(value, AXES, [(i, i ^ mask) for i in range(self.count)])  42.4 us
    pallas_call x2, Pallas kernels, run_back(): pl.pallas_call(partial(back_kernel, m), grid=(1,), in_specs=[pl.BlockSpec...  39.1 us
    pallas_call x2, Pallas kernels, call(): pl.pallas_call(kernel, out_shape=outs, in_specs=[pl.BlockSpec(memory_spac...  24.2 us
    pallas_call x1, Pallas kernels, run_shared(): pl.pallas_call(shared_kernel, grid=(total // BLOCK,), in_specs=[pl.BlockS...  18.3 us
  transfers between devices with their start and end apart: 52, of which 21 were waited for; matrix products, arithmetic and copies ran while one was open for 9% of the time, Pallas kernels for 34%

profile of v2, /device:TPU:0, one launch (start us, length us, event | category | flops | bytes accessed | tf_op | source)
XLA Modules:
  0.0 642.5 jit_solution(5568841155702021135)
XLA Ops:
  17.0 11.7 %shard_map.390 = (f32[4096,128]{1,0:T(8,128)}, bf16[512,1024]{1,0:T(8,128)(2,1)}, f32[2,16,8,128]{3,2,1,0:T(8,128)}) custom-call(s32[2,256]{1,0:T(2,128)} %copy-done.54, bf16[512,1024]{1,0:T(8,128)(2,1)} %bitcast.233, f32[1,1024]{1,0:T(1,128)} %bitcast.279, f32[16,8,128]{2,1,0:T(8,128)} %bitcast.243, f32[16,8,128]{2,1,0:T(8,128)} %bitcast.256), custom_call_target="tpu_custom_call" | custom-call | flops 13799999488 | bytes 39600000 | tf_op jit(solution)/shard_map/pallas_call | solution.py:709
  29.7 3.0 collective-permute-start
  32.8 4.9 collective-permute-done
  38.9 1.6 collective-permute-start.1
  40.4 11.0 %collective-permute-done.1 = f32[2,17,8,128]{3,2,1,0:T(8,128)S(1)} collective-permute-done((f32[2,17,8,128]{3,2,1,0:T(8,128)S(1)}, f32[2,17,8,128]{3,2,1,0:T(8,128)S(1)}, u32[]{:S(2)}, u32[]{:S(2)}) %collective-permute-start.1) | collective-permute-done | bytes 139296 | tf_op jit(solution)/shard_map/ppermute | solution.py:52
  53.7 7.7 %collective-permute-done.2 = f32[2,17,8,128]{3,2,1,0:T(8,128)S(1)} collective-permute-done((f32[2,17,8,128]{3,2,1,0:T(8,128)S(1)}, f32[2,17,8,128]{3,2,1,0:T(8,128)S(1)}, u32[]{:S(2)}, u32[]{:S(2)}) %collective-permute-start.2) | collective-permute-done | bytes 139296 | tf_op jit(solution)/shard_map/ppermute | solution.py:52
  62.1 12.5 %shard_map.391 = (f32[512,1024]{1,0:T(8,128)}, bf16[512,1024]{1,0:T(8,128)(2,1)}) custom-call(s32[2,256]{1,0:T(2,128)} %copy-done.54, f32[4096,128]{1,0:T(8,128)} %get-tuple-element.149.normed_ref, f32[2,16,8,128]{3,2,1,0:T(8,128)} %add_select_fusion.2.start_ref, f32[16,8,128]{2,1,0:T(8,128)} %bitcast.244, f32[16,8,128]{2,1,0:T(8,128)} %bitcast.257, ...), custom_call_target="tpu_custom_call" | custom-call | flops 13799999488 | bytes 39600000 | tf_op jit(solution)/shard_map/pallas_call | solution.py:709
  74.6 5.2 convolution_add_fusion.gate_ref
  79.8 2.1 copy-done.6
  83.9 112.7 %all-gather.5.cloned.1.call-done = bf16[14592,1024]{1,0:T(8,128)(2,1)} async-done(((bf16[456,1024]{1,0:T(8,128)(2,1)}), bf16[14592,1024]{1,0:T(8,128)(2,1)}) %all-gather.5.cloned.1.call-update) | async-done | bytes 29884432 | tf_op jit(solution)/shard_map/all_gather | solution.py:1064
  201.8 1.6 broadcast_6_refs_8__refs_6__refs_7_.2.refs_8_.refs_6_.refs_7_
  203.4 11.9 %shard_map.392 = (f32[512,1024]{1,0:T(8,128)}, f32[512,1024]{1,0:T(8,128)}, f32[512,1024]{1,0:T(8,128)}, bf16[512,1024]{1,0:T(8,128)(2,1)}, f32[512,1024]{1,0:T(8,128)}) custom-call(s32[2]{0:T(128)} %get-tuple-element.146.piece, f32[1,1024]{1,0:T(1,128)} %reshape.302.before.refs_6_, bf16[512,1024]{1,0:T(8,128)(2,1)} %get-tuple-element.152.refs_0_.refs_1_, ...), custom_call_target="tpu_custom_call" | custom-call | flops 230000001024 | bytes 660000000 | tf_op jit(solution)/shard_map/pallas_call | solution.py:625
  215.3 11.9 %shard_map.393 = (f32[512,1024]{1,0:T(8,128)}, f32[512,1024]{1,0:T(8,128)}, f32[512,1024]{1,0:T(8,128)}, bf16[512,1024]{1,0:T(8,128)(2,1)}, f32[512,1024]{1,0:T(8,128)}) custom-call(s32[2]{0:T(128)} %get-tuple-element.147.piece, f32[1,1024]{1,0:T(1,128)} %reshape.297.before.refs_6_, bf16[512,1024]{1,0:T(8,128)(2,1)} %get-tuple-element.152.refs_0_.refs_1_, ...), custom_call_target="tpu_custom_call" | custom-call | flops 230000001024 | bytes 660000000 | tf_op jit(solution)/shard_map/pallas_call | solution.py:625
  227.1 5.7 shard_map.394
  232.8 10.0 %shard_map.395 = (f32[512,2048]{1,0:T(8,128)}, bf16[512,2048]{1,0:T(8,128)(2,1)}, bf16[2,1,2048,512]{3,2,1,0:T(8,128)(2,1)}) custom-call(s32[2]{0:T(128)} %get-tuple-element.147.piece, f32[1,2048]{1,0:T(1,128)} %bitcast.269, bf16[512,1024]{1,0:T(8,128)(2,1)} %get-tuple-element.155.refs_0_, bf16[512,1024]{1,0:T(8,128)(2,1)} %bitcast.228, ...), custom_call_target="tpu_custom_call" | custom-call | flops 230000001024 | bytes 660000000 | tf_op jit(solution)/shard_map/pallas_call | solution.py:625
  243.1 10.4 %shard_map.396 = (f32[512,2048]{1,0:T(8,128)}, bf16[512,2048]{1,0:T(8,128)(2,1)}, bf16[2,1,2048,512]{3,2,1,0:T(8,128)(2,1)}) custom-call(s32[2]{0:T(128)} %get-tuple-element.146.piece, bf16[512,2048]{1,0:T(8,128)(2,1)} %get-tuple-element.156.before.refs_5_, bf16[512,1024]{1,0:T(8,128)(2,1)} %get-tuple-element.155.refs_0_, bf16[512,1024]{1,0:T(8,128)(2,1)} %bitcast.229, ...), custom_call_target="tpu_custom_call" | custom-call | flops 230000001024 | bytes 660000000 | tf_op jit(solution)/shard_map/pallas_call | solution.py:625
  253.5 4.1 shard_map.397
  257.6 1.5 collective-permute-start.4
  259.7 21.4 %shard_map.398 = (bf16[2,1,2048,512]{3,2,1,0:T(8,128)(2,1)}, f32[1,2048]{1,0:T(1,128)}, f32[512,1024]{1,0:T(8,128)}, f32[512,1024]{1,0:T(8,128)}) custom-call(s32[2]{0:T(128)} %get-tuple-element.147.piece, f32[8,128]{1,0:T(8,128)} %get-tuple-element.160.before, bf16[512,1024]{1,0:T(8,128)(2,1)} %get-tuple-element.155.refs_0_, bf16[512,1024]{1,0:T(8,128)(2,1)} %bitcast.230, ...), custom_call_target="tpu_custom_call" | custom-call | flops 230000001024 | bytes 660000000 | tf_op jit(solution)/shard_map/pallas_call | solution.py:625
  281.2 2.1 collective-permute-done.4.refs_3_.refs_2_.refs_27_
  284.4 3.6 shard_map.399
  288.6 1.5 collective-permute-start.7
  290.1 20.5 %shard_map.400 = (bf16[2,1,2048,512]{3,2,1,0:T(8,128)(2,1)}, f32[1,2048]{1,0:T(1,128)}, f32[512,1024]{1,0:T(8,128)}, f32[512,1024]{1,0:T(8,128)}) custom-call(s32[2]{0:T(128)} %get-tuple-element.146.piece, f32[8,128]{1,0:T(8,128)} %get-tuple-element.166.before, bf16[512,1024]{1,0:T(8,128)(2,1)} %get-tuple-element.155.refs_0_, bf16[512,1024]{1,0:T(8,128)(2,1)} %bitcast.231, ...), custom_call_target="tpu_custom_call" | custom-call | flops 230000001024 | bytes 660000000 | tf_op jit(solution)/shard_map/pallas_call | solution.py:625
  310.6 5.2 shard_map.401
  315.8 10.5 %shard_map.402 = (bf16[512,1024]{1,0:T(8,128)(2,1)}, f32[512,1024]{1,0:T(8,128)}, bf16[512,2048]{1,0:T(8,128)(2,1)}, f32[8,1024]{1,0:T(8,128)}, f32[8,1024]{1,0:T(8,128)}, /*index=5*/f32[8,2048]{1,0:T(8,128)}) custom-call(f32[8,128]{1,0:T(8,128)} %get-tuple-element.173.before, f32[512,2176]{1,0:T(8,128)} %copy-done.6, ...), custom_call_target="tpu_custom_call" | custom-call | flops 1150000000 | bytes 3300000 | tf_op jit(solution)/shard_map/pallas_call | solution.py:543
  326.3 5.0 shard_map.403.before
  333.4 1.5 collective-permute-start.9
  335.5 4.9 shard_map.404.before
  340.4 17.1 %shard_map.405 = (bf16[2,3,1024,512]{3,2,1,0:T(8,128)(2,1)}, f32[1,1024]{1,0:T(1,128)}, f32[1,1024]{1,0:T(1,128)}, f32[512,1024]{1,0:T(8,128)}, f32[512,1024]{1,0:T(8,128)}, /*index=5*/f32[4,128,128]{2,1,0:T(8,128)}) custom-call(s32[2]{0:T(128)} %get-tuple-element.147.piece, bf16[2,1,512,1024]{3,2,1,0:T(8,128)(2,1)} %shard_map.404.before, ...), custom_call_target="tpu_custom_call" | custom-call | flops 1150000000 | bytes 3300000 | tf_op jit(solution)/shard_map/pallas_call | solution.py:625
  360.4 5.3 shard_map.406
  366.3 1.5 collective-permute-start.15
  369.8 17.3 %shard_map.407 = (bf16[2,3,1024,512]{3,2,1,0:T(8,128)(2,1)}, f32[1,1024]{1,0:T(1,128)}, f32[1,1024]{1,0:T(1,128)}, f32[512,1024]{1,0:T(8,128)}, f32[512,1024]{1,0:T(8,128)}, /*index=5*/f32[4,128,128]{2,1,0:T(8,128)}) custom-call(s32[2]{0:T(128)} %get-tuple-element.146.piece, f32[8,128]{1,0:T(8,128)} %get-tuple-element.190.before, ...), custom_call_target="tpu_custom_call" | custom-call | flops 230000001024 | bytes 660000000 | tf_op jit(solution)/shard_map/pallas_call | solution.py:625
  387.1 4.3 collective-permute-done.16.refs_14_.refs_12_.refs_16_
  391.4 6.8 %shard_map.408 = (bf16[3,2,2,2,64,512]{5,4,3,2,1,0:T(8,128)(2,1)}, bf16[3,2,2,2,64,512]{5,4,3,2,1,0:T(8,128)(2,1)}, bf16[1,2,2,32,1024]{4,3,2,1,0:T(8,128)(2,1)}...) custom-call(s32[8]{0:T(128)} %stack.155.p, ...), custom_call_target="tpu_custom_call" | custom-call | flops 1150000000 | bytes 3300000 | tf_op jit(solution)/shard_map/pallas_call | solution.py:911
  399.2 1.5 collective-permute-start.18
  402.7 18.3 %shard_map.409 = (f32[4096,128]{1,0:T(8,128)}, f32[2,16,8,128]{3,2,1,0:T(8,128)}, bf16[512,128]{1,0:T(8,128)(2,1)}, f32[8,128]{1,0:T(8,128)}) custom-call(f32[8,128]{1,0:T(8,128)} %get-tuple-element.202.before, s32[2,256]{1,0:T(2,128)} %copy-done.54, f32[4,128,128]{2,1,0:T(8,128)} %get-tuple-element.203.gp0_ref, f32[4,128,128]{2,1,0:T(8,128)} %get-tuple-element.204.gp1_ref, ...), custom_call_target="tpu_custom_call" | custom-call | flops 230000001024 | bytes 660000000 | tf_op jit(solution)/shard_map/pallas_call | solution.py:213
  421.7 1.6 collective-permute-done.20.refs_13_.refs_18_.refs_17_.refs_23_
  423.3 3.5 shard_map.410
  429.5 1.5 collective-permute-start.21
  431.9 26.9 %collective-permute-done.21 = f32[2,17,8,128]{3,2,1,0:T(8,128)S(1)} collective-permute-done((f32[2,17,8,128]{3,2,1,0:T(8,128)S(1)}, f32[2,17,8,128]{3,2,1,0:T(8,128)S(1)}, u32[]{:S(2)}, u32[]{:S(2)}) %collective-permute-start.21) | collective-permute-done | bytes 139296 | tf_op jit(solution)/shard_map/ppermute | solution.py:52
  460.3 5.7 collective-permute-done.22
  466.6 3.6 collective-permute-done.34
  470.2 1.5 collective-permute-start.23
  472.4 5.4 collective-permute-done.23
  480.4 4.5 shard_map.411
  487.0 19.5 %shard_map.412 = (f32[256,1024]{1,0:T(8,128)}, f32[16,8,128]{2,1,0:T(8,128)}, f32[16,8,128]{2,1,0:T(8,128)}, f32[16,8,128]{2,1,0:T(8,128)}, f32[8,128]{1,0:T(8,1...) custom-call(f32[8,128]{1,0:T(8,128)} %get-tuple-element.216.before, s32[2,256]{1,0:T(2,128)} %copy-done.54, ...), custom_call_target="tpu_custom_call" | custom-call | flops 230000001024 | bytes 660000000 | tf_op jit(solution)/shard_map/pallas_call | solution.py:325
  507.8 2.0 collective-permute-start.27
  511.3 1.6 collective-permute-done.27.refs_6_.refs_12_
  513.6 5.4 shard_map.413
  520.5 1.7 collective-permute-start.32
  525.9 19.5 %shard_map.414 = (f32[256,1024]{1,0:T(8,128)}, f32[16,8,128]{2,1,0:T(8,128)}, f32[16,8,128]{2,1,0:T(8,128)}, f32[16,8,128]{2,1,0:T(8,128)}, f32[8,128]{1,0:T(8,1...) custom-call(f32[8,128]{1,0:T(8,128)} %get-tuple-element.228.before, s32[2,256]{1,0:T(2,128)} %copy-done.54, ...), custom_call_target="tpu_custom_call" | custom-call | flops 230000001024 | bytes 660000000 | tf_op jit(solution)/shard_map/pallas_call | solution.py:325
  546.1 8.7 %collective-permute-done.37 = bf16[1,1,1,1,1,32,128]{6,5,4,3,2,1,0:T(8,128)(2,1)} collective-permute-done((bf16[1,1,1,1,1,32,128]{6,5,4,3,2,1,0:T(8,128)(2,1)}, bf16[1,1,1,1,1,32,128]{6,5,4,3,2,1,0:T(8,128)(2,1)}, u32[]{:S(2)}, u32[]{:S(2)}) %collective-permute-start.37) | collective-permute-done | bytes 8224 | tf_op jit(solution)/shard_map/ppermute | solution.py:52
  557.4 3.3 shard_map.415
  576.3 2.9 shard_map.420
  580.4 3.1 shard_map.419
  583.5 2.2 collective-permute-done.39
  587.5 5.3 collective-permute-done.40
  595.9 3.1 collective-permute-start.41
  600.5 3.3 shard_map.417
  604.0 4.2 collective-permute-done.41
  609.1 1.5 pad_maximum_fusion
  612.1 6.6 %collective-permute-done.42 = bf16[1024,128]{1,0:T(8,128)(2,1)S(1)} collective-permute-done((bf16[1024,128]{1,0:T(8,128)(2,1)S(1)}, bf16[1024,128]{1,0:T(8,128)(2,1)S(1)}, u32[]{:S(2)}, u32[]{:S(2)}) %collective-permute-start.42) | collective-permute-done | bytes 262176 | tf_op jit(solution)/shard_map/ppermute | solution.py:52
  625.6 3.4 shard_map.418
  629.0 6.3 shard_map.416
  (396 shorter events, 90.1 us)
Async XLA Ops:
  7.2 189.4 %all-gather.5.cloned.1.call-start = ((), (), s32[]{:S(2)}) async-start(), calls=%async_computation | async-start | bytes 30818304 | tf_op jit(solution)/shard_map/all_gather | solution.py:1064
  13.5 615.5 %all-gather.7.cloned.1.call-start = ((), (), s32[]{:S(2)}) async-start(), calls=%async_computation.1 | async-start | bytes 4325376 | tf_op jit(solution)/shard_map/all_gather | solution.py:1238
  17.0 35.0 %copy-start.66 = (f32[2,128]{1,0:T(2,128)S(1)}, f32[2,128]{1,0:T(2,128)}, u32[]{:S(2)}) copy-start(f32[2,128]{1,0:T(2,128)} %gain_ref.1) | copy-start | bytes 3076
  28.7 24.0 %copy-start.44 = (f32[1024,16]{0,1:T(8,128)S(1)}, f32[1024,16]{0,1:T(8,128)}, u32[]{:S(2)}) copy-start(f32[1024,16]{0,1:T(8,128)} %param.32) | copy-start | bytes 196612
  29.7 8.0 %collective-permute-start = (f32[2,17,8,128]{3,2,1,0:T(8,128)S(1)}, f32[2,17,8,128]{3,2,1,0:T(8,128)S(1)}, u32[]{:S(2)}, u32[]{:S(2)}) collective-permute-start(f32[2,17,8,128]{3,2,1,0:T(8,128)S(1)} %pad_maximum_fusion.5), channel_id=1, source_target_pairs={{0,1},{1,0},{2,3},{3,2},{4,5},{5,4},{6,7},{7,6},{8,9},{9,8},{10,11... | collective-permute-start | bytes 417800 | tf_op jit(solution)/shard_map/ppermute | solution.py:52
  32.8 41.8 %copy-start.8 = (f32[16,8,128]{2,1,0:T(8,128)}, f32[16,8,128]{2,1,0:T(8,128)S(1)}, u32[]{:S(2)}) copy-start(f32[16,8,128]{2,1,0:T(8,128)S(1)} %get-tuple-element.298) | copy-start | bytes 196612
  32.8 41.8 %copy-start.10 = (f32[16,8,128]{2,1,0:T(8,128)}, f32[16,8,128]{2,1,0:T(8,128)S(1)}, u32[]{:S(2)}) copy-start(f32[16,8,128]{2,1,0:T(8,128)S(1)} %get-tuple-element.297) | copy-start | bytes 196612
  38.9 12.6 %collective-permute-start.1 = (f32[2,17,8,128]{3,2,1,0:T(8,128)S(1)}, f32[2,17,8,128]{3,2,1,0:T(8,128)S(1)}, u32[]{:S(2)}, u32[]{:S(2)}) collective-permute-start(f32[2,17,8,128]{3,2,1,0:T(8,128)S(1)} %pad_maximum_fusion.8), channel_id=1, source_target_pairs={{0,2},{1,3},{2,0},{3,1},{4,6},{5,7},{6,4},{7,5},{8,10},{9,11},{10,... | collective-permute-start | bytes 417800 | tf_op jit(solution)/shard_map/ppermute | solution.py:52
  51.5 9.8 %collective-permute-start.2 = (f32[2,17,8,128]{3,2,1,0:T(8,128)S(1)}, f32[2,17,8,128]{3,2,1,0:T(8,128)S(1)}, u32[]{:S(2)}, u32[]{:S(2)}) collective-permute-start(f32[2,17,8,128]{3,2,1,0:T(8,128)S(1)} %pad_maximum_fusion.9), channel_id=1, source_target_pairs={{0,4},{1,5},{2,6},{3,7},{4,0},{5,1},{6,2},{7,3},{8,12},{9,13},{10,... | collective-permute-start | bytes 417800 | tf_op jit(solution)/shard_map/ppermute | solution.py:52
  82.7 113.9 %copy-start.38 = (bf16[512,128]{1,0:T(8,128)(2,1)}, bf16[512,128]{1,0:T(8,128)(2,1)S(1)}, u32[]{:S(2)}) copy-start(bf16[512,128]{1,0:T(8,128)(2,1)S(1)} %get-tuple-element.258.key_ref) | copy-start | bytes 393220
  82.7 120.7 %copy-start.17 = (f32[512,128]{1,0:T(8,128)}, f32[512,128]{1,0:T(8,128)S(1)}, u32[]{:S(2)}) copy-start(f32[512,128]{1,0:T(8,128)S(1)} %get-tuple-element.259.shared_ref) | copy-start | bytes 786436
  82.7 113.9 %copy-start.39 = (bf16[512,128]{1,0:T(8,128)(2,1)}, bf16[512,128]{1,0:T(8,128)(2,1)S(1)}, u32[]{:S(2)}) copy-start(bf16[512,128]{1,0:T(8,128)(2,1)S(1)} %add_convert_fusion.4.query_ref) | copy-start | bytes 393220
  242.9 10.7 %collective-permute-start.3 = (bf16[2,1,2,2,2,2,128,512]{7,6,5,4,3,2,1,0:T(8,128)(2,1)}, bf16[2,1,2,2,2,2,128,512]{7,6,5,4,3,2,1,0:T(8,128)(2,1)}, u32[]{:S(2)}, u32[]{:S(2)}) collective-permute-start(bf16[2,1,2,2,2,2,128,512]{7,6,5,4,3,2,1,0:T(8,128)(2,1)} %bitcast.277), channel_id=1, source_target_pairs={{0,8},{1,9},{2,10},{3,11},{4,12},{5,13},{6,14},{7,15},{8,0},{9,1},... | collective-permute-start | bytes 12582920 | tf_op jit(solution)/shard_map/ppermute | solution.py:52
  257.6 25.6 %collective-permute-start.4 = (bf16[1,2,2,2,128,512]{5,4,3,2,1,0:T(8,128)(2,1)}, bf16[1,2,2,2,128,512]{5,4,3,2,1,0:T(8,128)(2,1)}, u32[]{:S(2)}, u32[]{:S(2)}) collective-permute-start(bf16[1,2,2,2,128,512]{5,4,3,2,1,0:T(8,128)(2,1)} %get-tuple-element.159), channel_id=1, source_target_pairs={{0,16},{1,17},{2,18},{3,19},{4,20},{5,21},{6,22},{7,23},{8,24},{9,... | collective-permute-start | bytes 3145736 | tf_op jit(solution)/shard_map/ppermute | solution.py:52
  259.1 25.3 %collective-permute-start.5 = (bf16[1,2,2,2,128,512]{5,4,3,2,1,0:T(8,128)(2,1)}, bf16[1,2,2,2,128,512]{5,4,3,2,1,0:T(8,128)(2,1)}, u32[]{:S(2)}, u32[]{:S(2)}) collective-permute-start(bf16[1,2,2,2,128,512]{5,4,3,2,1,0:T(8,128)(2,1)} %get-tuple-element.163), channel_id=1, source_target_pairs={{0,1},{1,0},{2,3},{3,2},{4,5},{5,4},{6,7},{7,6},{8,9},{9,8},{10,11... | collective-permute-start | bytes 3145736 | tf_op jit(solution)/shard_map/ppermute | solution.py:52
  281.1 29.5 %collective-permute-start.8 = (bf16[2,1,2,2,2,2,128,512]{7,6,5,4,3,2,1,0:T(8,128)(2,1)}, bf16[2,1,2,2,2,2,128,512]{7,6,5,4,3,2,1,0:T(8,128)(2,1)}, u32[]{:S(2)}, u32[]{:S(2)}) collective-permute-start(bf16[2,1,2,2,2,2,128,512]{7,6,5,4,3,2,1,0:T(8,128)(2,1)} %bitcast.276), channel_id=1, source_target_pairs={{0,8},{1,9},{2,10},{3,11},{4,12},{5,13},{6,14},{7,15},{8,0},{9,1},... | collective-permute-start | bytes 12582920 | tf_op jit(solution)/shard_map/ppermute | solution.py:52
  288.0 22.6 %collective-permute-start.6 = (bf16[1,2,2,128,512]{4,3,2,1,0:T(8,128)(2,1)}, bf16[1,2,2,128,512]{4,3,2,1,0:T(8,128)(2,1)}, u32[]{:S(2)}, u32[]{:S(2)}) collective-permute-start(bf16[1,2,2,128,512]{4,3,2,1,0:T(8,128)(2,1)} %get-tuple-element.164), channel_id=1, source_target_pairs={{0,1},{1,0},{2,3},{3,2},{4,5},{5,4},{6,7},{7,6},{8,9},{9,8},{10,11... | collective-permute-start | bytes 1572872 | tf_op jit(solution)/shard_map/ppermute | solution.py:52
  288.6 22.0 %collective-permute-start.7 = (bf16[1,2,2,128,512]{4,3,2,1,0:T(8,128)(2,1)}, bf16[1,2,2,128,512]{4,3,2,1,0:T(8,128)(2,1)}, u32[]{:S(2)}, u32[]{:S(2)}) collective-permute-start(bf16[1,2,2,128,512]{4,3,2,1,0:T(8,128)(2,1)} %get-tuple-element.165), channel_id=1, source_target_pairs={{0,16},{1,17},{2,18},{3,19},{4,20},{5,21},{6,22},{7,23},{8,24},{9,... | collective-permute-start | bytes 1572872 | tf_op jit(solution)/shard_map/ppermute | solution.py:52
  331.3 27.4 %collective-permute-start.12 = (bf16[2,1,2,2,2,2,32,1024]{7,6,5,4,3,2,1,0:T(8,128)(2,1)}, bf16[2,1,2,2,2,2,32,1024]{7,6,5,4,3,2,1,0:T(8,128)(2,1)S(1)}, u32[]{:S(2)}, u32[]{:S(2)}) collective-permute-start(bf16[2,1,2,2,2,2,32,1024]{7,6,5,4,3,2,1,0:T(8,128)(2,1)} %bitcast.224), channel_id=1, source_target_pairs={{0,8},{1,9},{2,10},{3,11},{4,12},{5,13},{6,14},{7,15},{8,0},{9,1},... | collective-permute-start | bytes 6291464 | tf_op jit(solution)/shard_map/ppermute | solution.py:52
  331.4 27.3 %collective-permute-start.10 = (bf16[1,2,2,2,128,512]{5,4,3,2,1,0:T(8,128)(2,1)}, bf16[1,2,2,2,128,512]{5,4,3,2,1,0:T(8,128)(2,1)S(1)}, u32[]{:S(2)}, u32[]{:S(2)}) collective-permute-start(bf16[1,2,2,2,128,512]{5,4,3,2,1,0:T(8,128)(2,1)} %get-tuple-element.188), channel_id=1, source_target_pairs={{0,16},{1,17},{2,18},{3,19},{4,20},{5,21},{6,22},{7,23},{8,24},{9,... | collective-permute-start | bytes 3145736 | tf_op jit(solution)/shard_map/ppermute | solution.py:52
  332.0 26.7 %collective-permute-start.11 = (bf16[1,2,2,2,128,512]{5,4,3,2,1,0:T(8,128)(2,1)}, bf16[1,2,2,2,128,512]{5,4,3,2,1,0:T(8,128)(2,1)}, u32[]{:S(2)}, u32[]{:S(2)}) collective-permute-start(bf16[1,2,2,2,128,512]{5,4,3,2,1,0:T(8,128)(2,1)} %get-tuple-element.189), channel_id=1, source_target_pairs={{0,1},{1,0},{2,3},{3,2},{4,5},{5,4},{6,7},{7,6},{8,9},{9,8},{10,11... | collective-permute-start | bytes 3145736 | tf_op jit(solution)/shard_map/ppermute | solution.py:52
  333.4 25.2 %collective-permute-start.9 = (bf16[1,2,128,1024]{3,2,1,0:T(8,128)(2,1)}, bf16[1,2,128,1024]{3,2,1,0:T(8,128)(2,1)}, u32[]{:S(2)}, u32[]{:S(2)}) collective-permute-start(bf16[1,2,128,1024]{3,2,1,0:T(8,128)(2,1)} %get-tuple-element.187), channel_id=1, source_target_pairs={{0,4},{1,5},{2,6},{3,7},{4,0},{5,1},{6,2},{7,3},{8,12},{9,13},{10,... | collective-permute-start | bytes 1572872 | tf_op jit(solution)/shard_map/ppermute | solution.py:52
  357.5 33.9 %collective-permute-start.13 = (bf16[2,3,2,2,2,2,64,512]{7,6,5,4,3,2,1,0:T(8,128)(2,1)}, bf16[2,3,2,2,2,2,64,512]{7,6,5,4,3,2,1,0:T(8,128)(2,1)}, u32[]{:S(2)}, u32[]{:S(2)}) collective-permute-start(bf16[2,3,2,2,2,2,64,512]{7,6,5,4,3,2,1,0:T(8,128)(2,1)} %bitcast.274), channel_id=1, source_target_pairs={{0,8},{1,9},{2,10},{3,11},{4,12},{5,13},{6,14},{7,15},{8,0},{9,1},... | collective-permute-start | bytes 18874376 | tf_op jit(solution)/shard_map/ppermute | solution.py:52
  365.6 21.4 %collective-permute-start.14 = (bf16[1,2,2,2,32,1024]{5,4,3,2,1,0:T(8,128)(2,1)}, bf16[1,2,2,2,32,1024]{5,4,3,2,1,0:T(8,128)(2,1)}, u32[]{:S(2)}, u32[]{:S(2)}) collective-permute-start(bf16[1,2,2,2,32,1024]{5,4,3,2,1,0:T(8,128)(2,1)} %get-tuple-element.198), channel_id=1, source_target_pairs={{0,16},{1,17},{2,18},{3,19},{4,20},{5,21},{6,22},{7,23},{8,24},{9,... | collective-permute-start | bytes 1572872 | tf_op jit(solution)/shard_map/ppermute | solution.py:52
  366.3 20.8 %collective-permute-start.15 = (bf16[1,2,2,2,32,1024]{5,4,3,2,1,0:T(8,128)(2,1)}, bf16[1,2,2,2,32,1024]{5,4,3,2,1,0:T(8,128)(2,1)}, u32[]{:S(2)}, u32[]{:S(2)}) collective-permute-start(bf16[1,2,2,2,32,1024]{5,4,3,2,1,0:T(8,128)(2,1)} %get-tuple-element.199), channel_id=1, source_target_pairs={{0,1},{1,0},{2,3},{3,2},{4,5},{5,4},{6,7},{7,6},{8,9},{9,8},{10,11... | collective-permute-start | bytes 1572872 | tf_op jit(solution)/shard_map/ppermute | solution.py:52
  367.7 23.7 %collective-permute-start.16 = (bf16[1,2,2,128,512]{4,3,2,1,0:T(8,128)(2,1)}, bf16[1,2,2,128,512]{4,3,2,1,0:T(8,128)(2,1)}, u32[]{:S(2)}, u32[]{:S(2)}) collective-permute-start(bf16[1,2,2,128,512]{4,3,2,1,0:T(8,128)(2,1)} %get-tuple-element.200), channel_id=1, source_target_pairs={{0,1},{1,0},{2,3},{3,2},{4,5},{5,4},{6,7},{7,6},{8,9},{9,8},{10,11... | collective-permute-start | bytes 1572872 | tf_op jit(solution)/shard_map/ppermute | solution.py:52
  368.3 23.1 %collective-permute-start.17 = (bf16[1,2,2,128,512]{4,3,2,1,0:T(8,128)(2,1)}, bf16[1,2,2,128,512]{4,3,2,1,0:T(8,128)(2,1)}, u32[]{:S(2)}, u32[]{:S(2)}) collective-permute-start(bf16[1,2,2,128,512]{4,3,2,1,0:T(8,128)(2,1)} %get-tuple-element.201), channel_id=1, source_target_pairs={{0,16},{1,17},{2,18},{3,19},{4,20},{5,21},{6,22},{7,23},{8,24},{9,... | collective-permute-start | bytes 1572872 | tf_op jit(solution)/shard_map/ppermute | solution.py:52
  387.0 124.2 %collective-permute-start.29 = (bf16[1,128,1024]{2,1,0:T(8,128)(2,1)}, bf16[1,128,1024]{2,1,0:T(8,128)(2,1)}, u32[]{:S(2)}, u32[]{:S(2)}) collective-permute-start(bf16[1,128,1024]{2,1,0:T(8,128)(2,1)} %get-tuple-element.225), channel_id=1, source_target_pairs={{0,2},{1,3},{2,0},{3,1},{4,6},{5,7},{6,4},{7,5},{8,10},{9,11},{10,... | collective-permute-start | bytes 786440 | tf_op jit(solution)/shard_map/ppermute | solution.py:52
  398.2 25.1 %collective-permute-start.20 = (bf16[1,2,128,1024]{3,2,1,0:T(8,128)(2,1)}, bf16[1,2,128,1024]{3,2,1,0:T(8,128)(2,1)}, u32[]{:S(2)}, u32[]{:S(2)}) collective-permute-start(bf16[1,2,128,1024]{3,2,1,0:T(8,128)(2,1)} %get-tuple-element.211), channel_id=1, source_target_pairs={{0,4},{1,5},{2,6},{3,7},{4,0},{5,1},{6,2},{7,3},{8,12},{9,13},{10,... | collective-permute-start | bytes 1572872 | tf_op jit(solution)/shard_map/ppermute | solution.py:52
  399.2 21.8 %collective-permute-start.18 = (bf16[1,2,2,32,1024]{4,3,2,1,0:T(8,128)(2,1)}, bf16[1,2,2,32,1024]{4,3,2,1,0:T(8,128)(2,1)}, u32[]{:S(2)}, u32[]{:S(2)}) collective-permute-start(bf16[1,2,2,32,1024]{4,3,2,1,0:T(8,128)(2,1)} %get-tuple-element.209), channel_id=1, source_target_pairs={{0,1},{1,0},{2,3},{3,2},{4,5},{5,4},{6,7},{7,6},{8,9},{9,8},{10,11... | collective-permute-start | bytes 786440 | tf_op jit(solution)/shard_map/ppermute | solution.py:52
  400.7 21.0 %collective-permute-start.19 = (bf16[1,2,2,32,1024]{4,3,2,1,0:T(8,128)(2,1)}, bf16[1,2,2,32,1024]{4,3,2,1,0:T(8,128)(2,1)}, u32[]{:S(2)}, u32[]{:S(2)}) collective-permute-start(bf16[1,2,2,32,1024]{4,3,2,1,0:T(8,128)(2,1)} %get-tuple-element.210), channel_id=1, source_target_pairs={{0,16},{1,17},{2,18},{3,19},{4,20},{5,21},{6,22},{7,23},{8,24},{9,... | collective-permute-start | bytes 786440 | tf_op jit(solution)/shard_map/ppermute | solution.py:52
  401.2 77.9 %collective-permute-start.24 = (bf16[3,2,2,2,64,512]{5,4,3,2,1,0:T(8,128)(2,1)}, bf16[3,2,2,2,64,512]{5,4,3,2,1,0:T(8,128)(2,1)}, u32[]{:S(2)}, u32[]{:S(2)}) collective-permute-start(bf16[3,2,2,2,64,512]{5,4,3,2,1,0:T(8,128)(2,1)} %get-tuple-element.213), channel_id=1, source_target_pairs={{0,16},{1,17},{2,18},{3,19},{4,20},{5,21},{6,22},{7,23},{8,24},{9,... | collective-permute-start | bytes 4718600 | tf_op jit(solution)/shard_map/ppermute | solution.py:52
  421.0 58.1 %collective-permute-start.25 = (bf16[3,2,2,2,64,512]{5,4,3,2,1,0:T(8,128)(2,1)}, bf16[3,2,2,2,64,512]{5,4,3,2,1,0:T(8,128)(2,1)S(1)}, u32[]{:S(2)}, u32[]{:S(2)}) collective-permute-start(bf16[3,2,2,2,64,512]{5,4,3,2,1,0:T(8,128)(2,1)} %get-tuple-element.214), channel_id=1, source_target_pairs={{0,1},{1,0},{2,3},{3,2},{4,5},{5,4},{6,7},{7,6},{8,9},{9,8},{10,11... | collective-permute-start | bytes 4718600 | tf_op jit(solution)/shard_map/ppermute | solution.py:52
  426.9 32.0 %copy-start.58 = (f32[2]{0:T(128)S(1)}, f32[2]{0:T(128)}, u32[]{:S(2)}) copy-start(f32[2]{0:T(128)} %copy-done.57) | copy-start | bytes 28
  426.9 32.1 %copy-start.9 = (f32[16,8,128]{2,1,0:T(8,128)S(1)}, f32[16,8,128]{2,1,0:T(8,128)}, u32[]{:S(2)}) copy-start(f32[16,8,128]{2,1,0:T(8,128)} %copy-done.8) | copy-start | bytes 196612
  426.9 39.7 %copy-start.11 = (f32[16,8,128]{2,1,0:T(8,128)S(1)}, f32[16,8,128]{2,1,0:T(8,128)}, u32[]{:S(2)}) copy-start(f32[16,8,128]{2,1,0:T(8,128)} %copy-done.10) | copy-start | bytes 196612
  429.5 29.4 %collective-permute-start.21 = (f32[2,17,8,128]{3,2,1,0:T(8,128)S(1)}, f32[2,17,8,128]{3,2,1,0:T(8,128)S(1)}, u32[]{:S(2)}, u32[]{:S(2)}) collective-permute-start(f32[2,17,8,128]{3,2,1,0:T(8,128)S(1)} %pad_maximum_fusion.4), channel_id=1, source_target_pairs={{0,1},{1,0},{2,3},{3,2},{4,5},{5,4},{6,7},{7,6},{8,9},{9,8},{10,11... | collective-permute-start | bytes 417800 | tf_op jit(solution)/shard_map/ppermute | solution.py:52
  430.9 47.6 %collective-permute-start.26 = (bf16[1,2,32,2048]{3,2,1,0:T(8,128)(2,1)}, bf16[1,2,32,2048]{3,2,1,0:T(8,128)(2,1)S(1)}, u32[]{:S(2)}, u32[]{:S(2)}) collective-permute-start(bf16[1,2,32,2048]{3,2,1,0:T(8,128)(2,1)} %get-tuple-element.215), channel_id=1, source_target_pairs={{0,4},{1,5},{2,6},{3,7},{4,0},{5,1},{6,2},{7,3},{8,12},{9,13},{10,... | collective-permute-start | bytes 786440 | tf_op jit(solution)/shard_map/ppermute | solution.py:52
  458.9 1.3 collective-permute-start.33
  460.2 5.7 collective-permute-start.22
  465.9 4.3 collective-permute-start.34
  470.2 7.6 %collective-permute-start.23 = (f32[2,17,8,128]{3,2,1,0:T(8,128)S(1)}, f32[2,17,8,128]{3,2,1,0:T(8,128)S(1)}, u32[]{:S(2)}, u32[]{:S(2)}) collective-permute-start(f32[2,17,8,128]{3,2,1,0:T(8,128)S(1)} %pad_maximum_fusion.11), channel_id=1, source_target_pairs={{0,4},{1,5},{2,6},{3,7},{4,0},{5,1},{6,2},{7,3},{8,12},{9,13},{10,... | collective-permute-start | bytes 417800 | tf_op jit(solution)/shard_map/ppermute | solution.py:52
  477.8 33.5 %collective-permute-start.28 = (bf16[1,128,1024]{2,1,0:T(8,128)(2,1)}, bf16[1,128,1024]{2,1,0:T(8,128)(2,1)}, u32[]{:S(2)}, u32[]{:S(2)}) collective-permute-start(bf16[1,128,1024]{2,1,0:T(8,128)(2,1)} %get-tuple-element.224), channel_id=1, source_target_pairs={{0,2},{1,3},{2,0},{3,1},{4,6},{5,7},{6,4},{7,5},{8,10},{9,11},{10,... | collective-permute-start | bytes 786440 | tf_op jit(solution)/shard_map/ppermute | solution.py:52
  478.6 29.2 %collective-permute-start.35 = (bf16[1,1,2,2,1,32,128]{6,5,4,3,2,1,0:T(8,128)(2,1)}, bf16[1,1,2,2,1,32,128]{6,5,4,3,2,1,0:T(8,128)(2,1)}, u32[]{:S(2)}, u32[]{:S(2)}) collective-permute-start(bf16[1,1,2,2,1,32,128]{6,5,4,3,2,1,0:T(8,128)(2,1)} %dynamic-slice_convert_fusion.2), channel_id=1, source_target_pairs={{0,1},{1,0},{2,3},{3,2},{4,5},{5,4},{6,7},{7,6},{8,9},{9,8},{10,11... | collective-permute-start | bytes 98312 | tf_op jit(solution)/shard_map/ppermute | solution.py:52
  484.9 28.0 %collective-permute-start.30 = (bf16[3,2,2,64,512]{4,3,2,1,0:T(8,128)(2,1)}, bf16[3,2,2,64,512]{4,3,2,1,0:T(8,128)(2,1)}, u32[]{:S(2)}, u32[]{:S(2)}) collective-permute-start(bf16[3,2,2,64,512]{4,3,2,1,0:T(8,128)(2,1)} %get-tuple-element.226), channel_id=1, source_target_pairs={{0,1},{1,0},{2,3},{3,2},{4,5},{5,4},{6,7},{7,6},{8,9},{9,8},{10,11... | collective-permute-start | bytes 2359304 | tf_op jit(solution)/shard_map/ppermute | solution.py:52
  486.3 26.6 %collective-permute-start.31 = (bf16[3,2,2,64,512]{4,3,2,1,0:T(8,128)(2,1)}, bf16[3,2,2,64,512]{4,3,2,1,0:T(8,128)(2,1)}, u32[]{:S(2)}, u32[]{:S(2)}) collective-permute-start(bf16[3,2,2,64,512]{4,3,2,1,0:T(8,128)(2,1)} %get-tuple-element.227), channel_id=1, source_target_pairs={{0,16},{1,17},{2,18},{3,19},{4,20},{5,21},{6,22},{7,23},{8,24},{9,... | collective-permute-start | bytes 2359304 | tf_op jit(solution)/shard_map/ppermute | solution.py:52
  487.0 22.8 %copy-start.20 = (f32[1,1,2,2,2,32,128]{6,5,4,3,2,1,0:T(8,128)S(1)}, f32[1,1,2,2,2,32,128]{6,5,4,3,2,1,0:T(8,128)}, u32[]{:S(2)}) copy-start(f32[1,1,2,2,2,32,128]{6,5,4,3,2,1,0:T(8,128)} %copy-done.19) | copy-start | bytes 393220
  507.8 5.2 collective-permute-start.27
  511.2 12.1 %collective-permute-start.36 = (bf16[1,1,2,1,1,32,128]{6,5,4,3,2,1,0:T(8,128)(2,1)S(1)}, bf16[1,1,2,1,1,32,128]{6,5,4,3,2,1,0:T(8,128)(2,1)S(1)}, u32[]{:S(2)}, u32[]{:S(2)}) collective-permute-start(bf16[1,1,2,1,1,32,128]{6,5,4,3,2,1,0:T(8,128)(2,1)S(1)} %dynamic-slice_convert_fusion.3), channel_id=1, source_target_pairs={{0,2},{1,3},{2,0},{3,1},{4,6},{5,7},{6,4},{7,5},{8,10},{9,11},{10,... | collective-permute-start | bytes 49160 | tf_op jit(solution)/shard_map/ppermute | solution.py:52
  519.0 36.5 %collective-permute-start.48 = (bf16[1,128,1024]{2,1,0:T(8,128)(2,1)}, bf16[1,128,1024]{2,1,0:T(8,128)(2,1)}, u32[]{:S(2)}, u32[]{:S(2)}) collective-permute-start(bf16[1,128,1024]{2,1,0:T(8,128)(2,1)} %get-tuple-element.255.own_ref), channel_id=1, source_target_pairs={{0,16},{1,17},{2,18},{3,19},{4,20},{5,21},{6,22},{7,23},{8,24},{9,... | collective-permute-start | bytes 786440 | tf_op jit(solution)/shard_map/ppermute | solution.py:52
  520.5 36.8 %collective-permute-start.32 = (bf16[3,2,64,1024]{3,2,1,0:T(8,128)(2,1)}, bf16[3,2,64,1024]{3,2,1,0:T(8,128)(2,1)}, u32[]{:S(2)}, u32[]{:S(2)}) collective-permute-start(bf16[3,2,64,1024]{3,2,1,0:T(8,128)(2,1)} %get-tuple-element.230), channel_id=1, source_target_pairs={{0,4},{1,5},{2,6},{3,7},{4,0},{5,1},{6,2},{7,3},{8,12},{9,13},{10,... | collective-permute-start | bytes 2359304 | tf_op jit(solution)/shard_map/ppermute | solution.py:52
  524.6 30.2 %collective-permute-start.37 = (bf16[1,1,1,1,1,32,128]{6,5,4,3,2,1,0:T(8,128)(2,1)}, bf16[1,1,1,1,1,32,128]{6,5,4,3,2,1,0:T(8,128)(2,1)}, u32[]{:S(2)}, u32[]{:S(2)}) collective-permute-start(bf16[1,1,1,1,1,32,128]{6,5,4,3,2,1,0:T(8,128)(2,1)} %dynamic-slice_convert_fusion.4), channel_id=1, source_target_pairs={{0,4},{1,5},{2,6},{3,7},{4,0},{5,1},{6,2},{7,3},{8,12},{9,13},{10,... | collective-permute-start | bytes 24584 | tf_op jit(solution)/shard_map/ppermute | solution.py:52
  525.9 29.7 %copy-start.29 = (bf16[1,128,1024]{2,1,0:T(8,128)(2,1)S(1)}, bf16[1,128,1024]{2,1,0:T(8,128)(2,1)}, u32[]{:S(2)}) copy-start(bf16[1,128,1024]{2,1,0:T(8,128)(2,1)} %get-tuple-element.255.own_ref) | copy-start | bytes 786436
  545.4 11.2 %collective-permute-start.46 = (bf16[1,128,1024]{2,1,0:T(8,128)(2,1)S(1)}, bf16[1,128,1024]{2,1,0:T(8,128)(2,1)S(1)}, u32[]{:S(2)}, u32[]{:S(2)}) collective-permute-start(bf16[1,128,1024]{2,1,0:T(8,128)(2,1)S(1)} %copy-done.28), channel_id=1, source_target_pairs={{0,16},{1,17},{2,18},{3,19},{4,20},{5,21},{6,22},{7,23},{8,24},{9,... | collective-permute-start | bytes 786440 | tf_op jit(solution)/shard_map/ppermute | solution.py:52
  556.6 19.8 %collective-permute-start.49 = (bf16[2,1,128,1024]{3,2,1,0:T(8,128)(2,1)S(1)}, bf16[2,1,128,1024]{3,2,1,0:T(8,128)(2,1)}, u32[]{:S(2)}, u32[]{:S(2)}) collective-permute-start(bf16[2,1,128,1024]{3,2,1,0:T(8,128)(2,1)S(1)} %pad_maximum_fusion.3), channel_id=1, source_target_pairs={{0,8},{1,9},{2,10},{3,11},{4,12},{5,13},{6,14},{7,15},{8,0},{9,1},... | collective-permute-start | bytes 1572872 | tf_op jit(solution)/shard_map/ppermute | solution.py:52
  556.7 23.6 %collective-permute-start.47 = (bf16[2,1,128,1024]{3,2,1,0:T(8,128)(2,1)S(1)}, bf16[2,1,128,1024]{3,2,1,0:T(8,128)(2,1)}, u32[]{:S(2)}, u32[]{:S(2)}) collective-permute-start(bf16[2,1,128,1024]{3,2,1,0:T(8,128)(2,1)S(1)} %pad_maximum_fusion.2), channel_id=1, source_target_pairs={{0,8},{1,9},{2,10},{3,11},{4,12},{5,13},{6,14},{7,15},{8,0},{9,1},... | collective-permute-start | bytes 1572872 | tf_op jit(solution)/shard_map/ppermute | solution.py:52
  566.7 33.1 %collective-permute-start.43 = (bf16[3,64,1024]{2,1,0:T(8,128)(2,1)}, bf16[3,64,1024]{2,1,0:T(8,128)(2,1)S(1)}, u32[]{:S(2)}, u32[]{:S(2)}) collective-permute-start(bf16[3,64,1024]{2,1,0:T(8,128)(2,1)} %get-tuple-element.249), channel_id=1, source_target_pairs={{0,2},{1,3},{2,0},{3,1},{4,6},{5,7},{6,4},{7,5},{8,10},{9,11},{10,... | collective-permute-start | bytes 1179656 | tf_op jit(solution)/shard_map/ppermute | solution.py:52
  576.2 3.1 collective-permute-start.38
  579.4 6.3 collective-permute-start.39
  585.8 7.1 %collective-permute-start.40 = (bf16[640,128]{1,0:T(8,128)(2,1)S(1)}, bf16[640,128]{1,0:T(8,128)(2,1)S(1)}, u32[]{:S(2)}, u32[]{:S(2)}) collective-permute-start(bf16[640,128]{1,0:T(8,128)(2,1)S(1)} %pad_maximum_fusion.6), channel_id=1, source_target_pairs={{0,1},{1,0},{2,3},{3,2},{4,5},{5,4},{6,7},{7,6},{8,9},{9,8},{10,11... | collective-permute-start | bytes 491528 | tf_op jit(solution)/shard_map/ppermute | solution.py:52
  595.9 12.3 %collective-permute-start.41 = (bf16[768,128]{1,0:T(8,128)(2,1)}, bf16[768,128]{1,0:T(8,128)(2,1)S(1)}, u32[]{:S(2)}, u32[]{:S(2)}) collective-permute-start(bf16[768,128]{1,0:T(8,128)(2,1)} %constant_dynamic-update-slice_fusion.8), channel_id=1, source_target_pairs={{0,2},{1,3},{2,0},{3,1},{4,6},{5,7},{6,4},{7,5},{8,10},{9,11},{10,... | collective-permute-start | bytes 589832 | tf_op jit(solution)/shard_map/ppermute | solution.py:52
  603.9 8.1 %collective-permute-start.44 = (bf16[3,64,1024]{2,1,0:T(8,128)(2,1)}, bf16[3,64,1024]{2,1,0:T(8,128)(2,1)S(1)}, u32[]{:S(2)}, u32[]{:S(2)}) collective-permute-start(bf16[3,64,1024]{2,1,0:T(8,128)(2,1)} %get-tuple-element.250.own_ref), channel_id=1, source_target_pairs={{0,16},{1,17},{2,18},{3,19},{4,20},{5,21},{6,22},{7,23},{8,24},{9,... | collective-permute-start | bytes 1179656 | tf_op jit(solution)/shard_map/ppermute | solution.py:52
  609.1 9.7 %collective-permute-start.42 = (bf16[1024,128]{1,0:T(8,128)(2,1)S(1)}, bf16[1024,128]{1,0:T(8,128)(2,1)S(1)}, u32[]{:S(2)}, u32[]{:S(2)}) collective-permute-start(bf16[1024,128]{1,0:T(8,128)(2,1)S(1)} %get-tuple-element.271), channel_id=1, source_target_pairs={{0,4},{1,5},{2,6},{3,7},{4,0},{5,1},{6,2},{7,3},{8,12},{9,13},{10,... | collective-permute-start | bytes 786440 | tf_op jit(solution)/shard_map/ppermute | solution.py:52
  612.0 13.5 %collective-permute-start.45 = (bf16[2,3,64,1024]{3,2,1,0:T(8,128)(2,1)S(1)}, bf16[2,3,64,1024]{3,2,1,0:T(8,128)(2,1)}, u32[]{:S(2)}, u32[]{:S(2)}) collective-permute-start(bf16[2,3,64,1024]{3,2,1,0:T(8,128)(2,1)S(1)} %pad_maximum_fusion.1), channel_id=1, source_target_pairs={{0,8},{1,9},{2,10},{3,11},{4,12},{5,13},{6,14},{7,15},{8,0},{9,1},... | collective-permute-start | bytes 2359304 | tf_op jit(solution)/shard_map/ppermute | solution.py:52
  (61 other events, 507.7 us)
Sparse Core Ops, SparseCore 0:
  13.6 182.9 all-gather.4
  546.3 62.9 all-gather.6

commit v3 on v2

--- a/solution.py
+++ b/solution.py
@@ -386,7 +386,7 @@
 
 
 def value_kernel(
-    piece, normed_ref, mixed_ref, probs_ref, wv_ref, wr_ref, wb_ref, bv_ref, br_ref, sum_ref,
+    piece, normed_ref, mixed_ref, probs_ref, wv_ref, wr_ref, wb_ref, bv_ref, br_ref,
     value_ref, reset_ref, attended_ref, gated_ref, out_ref,
 ):
     value_pre = dot_nt(normed_ref[...], flat(wv_ref)) + bv_ref[...]
@@ -401,7 +401,7 @@
     reset_ref[...] = reset_pre
     gated = (reset_pre * sigmoid(reset_pre) * attended).astype(BF16)
     gated_ref[...] = gated
-    add_to(out_ref, dot_nn(gated, flat(wb_ref)), sum_ref)
+    add_to(out_ref, dot_nn(gated, flat(wb_ref)))
 
 
 def value_back_kernel(
@@ -446,9 +446,10 @@
 
 
 def outer_kernel(
-    piece, ffn_ref, grad_ref, wi_ref, wo_ref, pre_ref, activ_ref, sum_o_ref, sum_f_ref,
-    di_ref, sum_i_ref, out_ref, ffn_out,
+    piece, ffn_ref, grad_ref, wi_ref, wo_ref, pre_ref, activ_ref, *rest
 ):
+    *sums, di_ref, sum_i_ref, out_ref, ffn_out = rest
+    sum_o_ref, sum_f_ref = sums if sums else (None, None)
     wi = flat(wi_ref)
     wo = flat(wo_ref)
     add_to(out_ref, dot_nn(activ_ref[...], wo), sum_o_ref)
@@ -584,8 +585,8 @@
 
 
 class Pieces:
-    def __init__(self, gathered, which, tensor, part_f, part_v):
-        self.gathered, self.which, self.tensor = gathered, which, tensor
+    def __init__(self, gathered, outer, which, tensor, part_f, part_v):
+        self.gathered, self.outer, self.which, self.tensor = gathered, outer, which, tensor
         self.part_f, self.part_v = part_f, part_v
         self.width = gathered.shape[-1]
 
@@ -608,10 +609,10 @@
 
     @property
     def w_out(self):
-        return self.spec(self.part_f, self.part_f)
+        return self.spec(self.part_f, 0)
 
     def v(self, k):
-        return self.spec(self.part_v, 2 * self.part_f + k * self.part_v)
+        return self.spec(self.part_v, self.part_f + k * self.part_v)
 
 
 def flat(ref):
@@ -643,7 +644,7 @@
     return full, cols, line, grads
 
 
-def run_value(pieces, token, normed, mixed, probs, bv, br, before):
+def run_value(pieces, token, normed, mixed, probs, bv, br):
     total, width = normed.shape
     units, block = pieces.units(pieces.part_v), pieces.block(pieces.part_v)
     full, cols, line, grads = block_specs(total, width, block, 3)
@@ -651,14 +652,14 @@
     g = pieces.gathered
     return blocked(
         value_kernel, 200, pieces, units // block, token,
-        [full, full, pairs, pieces.v(0), pieces.v(1), pieces.v(2), line, line, full],
+        [full, full, pairs, pieces.v(0), pieces.v(1), pieces.v(2), line, line],
         [cols, cols, cols, cols, full],
         [shape_of(total, units)] * 3 + [shape_of(total, units, dtype=BF16), shape_of(total, width)],
-        normed, mixed, probs, g, g, g, bv, br, before,
-    )
-
-
-def run_value_back(pieces, micros, token, grad, normed, mixed, probs, kept):
+        normed, mixed, probs, g, g, g, bv, br,
+    )
+
+
+def run_value_back(pieces, k, micros, token, grad, normed, mixed, probs, kept):
     total, width = normed.shape
     units, block = pieces.units(pieces.part_v), pieces.block(pieces.part_v)
     full, cols, line, grads = block_specs(total, width, block, 3)
@@ -668,7 +669,7 @@
         value_back_kernel, micros, pieces, units // block, token,
         [
             pl.BlockSpec((total, width), lambda i, p: (0, 1)), full, full, pairs,
-            pieces.v(0), pieces.v(1), pieces.v(2), cols, cols, cols, cols,
+            pieces.v(0), pieces.v(1), pieces.v(2), *[pl.BlockSpec((total, block), lambda i, p: (0, k * (units // block) + i))] * 4,
         ],
         [grads, line, line, full, full, pairs],
         [shape_of(2, 3, units, width // 2, dtype=BF16)]
@@ -692,16 +693,16 @@
     )
 
 
-def run_outer(pieces, token, ffn, grad, pre, activ, before_out, before_ffn):
+def run_outer(pieces, token, ffn, grad, pre, activ, *before):
     total, width = ffn.shape
     units, block = pieces.units(pieces.part_f), pieces.block(pieces.part_f)
     full, cols, line, grads = block_specs(total, width, block, 1)
     return blocked(
         outer_kernel, 200, pieces, units // block, token,
-        [full, full, pieces.w_in, pieces.w_out, cols, cols, full, full],
+        [full, full, pieces.w_in, pieces.w_out, cols, cols, *[full] * len(before)],
         [grads, line, full, full],
         [shape_of(2, 1, units, width // 2, dtype=BF16), shape_of(1, units), shape_of(total, width), shape_of(total, width)],
-        ffn, grad, pieces.gathered, pieces.gathered, pre, activ, before_out, before_ffn,
+        ffn, grad, pieces.gathered, pieces.outer, pre, activ, *before,
     )
 
 
@@ -820,7 +821,7 @@
     return v.astype(F32)
 
 
-def point(grid, gates, *sums):
+def point(grid, gates, *sums, behind=None):
     for r in sums:
         r.take()
     outs, tasks = [], []
@@ -836,6 +837,11 @@
             outs.append((*shapes[0][:-1], 2 * shapes[0][-1]))
         else:
             outs.extend(shapes)
+    pair = [
+        k for k in range(len(sums) - 1)
+        if 0 < len(sums[k].orders[0][0]) <= sums[k].step < sums[k].steps
+        and sums[k].step == sums[k + 1].step and sums[k].low.shape == sums[k + 1].low.shape
+    ]
     sel = grid.sel
     fits = all(len(r.dims) <= 4 and r.low.shape[-2] % 32 == 0 for r in sums)
     if fits:
@@ -850,14 +856,26 @@
             v = sides.pop(0)
             values.append(v if v.shape == shape else jnp.concatenate([v, sides.pop(0)], axis=-1))
         token = after(jnp.zeros((8, 128), F32), [g[(0,) * g.ndim] for g in gates])
-    done = []
-    for r in sums:
+    if behind is not None:
+        values, behind = lax.optimization_barrier((values, behind))
+    done, skip = [], False
+    for k, r in enumerate(sums):
+        if skip:
+            skip = False
+            continue
         if r.step == r.steps:
             done.append(values.pop(0))
+        elif k in pair:
+            both = grid.swap(jnp.concatenate(values[:2]), r.masks[0])
+            n = values[0].shape[0]
+            r.raw, sums[k + 1].raw = [both[:n]], [both[n:]]
+            values, skip = values[2:], True
         else:
             n = 2 if r.step < len(r.orders[0][0]) else 1
             r.start(values[:n])
             values = values[n:]
+    if behind is not None:
+        return token, behind
     return (token, *done) if done else token
 
 
@@ -948,6 +966,7 @@
 
 def place_kernel(turned, bits, own_ref, x_ref, c_ref, *outs):
     swap_c, swap_x = bits[0] == 1, bits[1] == 1
+    outs[-1][...] = jnp.zeros((8, 128), F32)
     for k, turn in enumerate(turned):
         rows = []
         for own, other in ((own_ref[k], x_ref[k]), (c_ref[0, k], c_ref[1, k])):
@@ -975,50 +994,117 @@
             pl.pallas_call(
                 partial(place_kernel, turns),
                 in_specs=[pl.BlockSpec(memory_space=pltpu.SMEM)] + [pl.BlockSpec(memory_space=pltpu.VMEM)] * 3,
-                out_specs=[pl.BlockSpec(memory_space=pltpu.VMEM)] * lead,
-                out_shape=[shape_of(*((width, 4 * units) if t else (4 * units, width))) for t in turns],
+                out_specs=[pl.BlockSpec(memory_space=pltpu.VMEM)] * (lead + 1),
+                out_shape=[shape_of(*((width, 4 * units) if t else (4 * units, width))) for t in turns] + [shape_of(8, 128)],
                 cost_estimate=cost(5),
             )(jnp.stack([grid.bit(grid.core), grid.bit(grid.xs[0])]).astype(jnp.int32), part, from_x, from_c)
         )
     return results
 
 
-def join_kernel(left_ref, right_ref, out_ref):
+def pack_kernel(
+    bits, before, eta0, eta1, one0, one1, two0, two1, omega0, omega1, gain0, gain1, gates_ref, shared_ref, ffn_ref, out_sum_ref,
+    v0, v1, r0, r1, i0, i1, packed_ref, rows,
+):
+    heads = eta0.shape[0]
+    n = heads * 8
+    for k, (a, b) in enumerate(((eta0, eta1), (one0, one1), (two0, two1))):
+        rows[k * n : (k + 1) * n] = (a[...] + b[...]).reshape(n, 128)
+    at = 3 * n
+
+    def line(v, at):
+        for j in range(v.shape[-1] // 128):
+            rows[at + j : at + j + 1] = v[:, j * 128 : (j + 1) * 128]
+        return at + v.shape[-1] // 128
+
+    total = lambda v: jnp.sum(v, axis=0, keepdims=True)
+    at = line(total(gain0[...] + gain1[...]), at)
+    rows[at : at + 8] = omega0[...] + omega1[...]
+    at = line(total(gates_ref[...]), at + 8)
+    rows[at : at + 1] = shared_ref[3:4]
+    rows[at + 1 : at + 4] = shared_ref[0:3]
+    at = line(total(ffn_ref[...]), at + 4)
+    at = line(total(out_sum_ref[...]), at)
+    core, x = bits[0], bits[1]
+    tensor = i0.shape[-1] // 256
+    for low, high in ((v0, v1), (r0, r1)):
+        for k, ref in enumerate((low, high)):
+            for t in range(tensor):
+                own, other = (ref[:, (q * tensor + t) * 64 : (q * tensor + t + 1) * 64] for q in (0, 1))
+                row = jnp.where(
+                    x == 0, jnp.concatenate([own, other], axis=1), jnp.concatenate([other, own], axis=1)
+                )
+                rows[pl.ds(at + 2 * t + (core ^ k), 1), :] = row
+        at += 2 * tensor
+    for k, ref in enumerate((i0, i1)):
+        for q in (0, 1):
+            for t in range(tensor):
+                row = ref[:, (q * tensor + t) * 128 : (q * tensor + t + 1) * 128]
+                rows[pl.ds(at + 4 * t + 2 * (core ^ k) + (x ^ q), 1), :] = row
+    at += 4 * tensor
+    rows[at:] = jnp.zeros((rows.shape[0] - at, 128), F32)
+    packed_ref[...] = rows[...].astype(BF16)
+
+
+def run_pack(bits, token, sums, count):
+    vmem = pl.BlockSpec(memory_space=pltpu.VMEM)
+    return pl.pallas_call(
+        pack_kernel,
+        in_specs=[pl.BlockSpec(memory_space=pltpu.SMEM), pl.BlockSpec(memory_space=pl.ANY)] + [vmem] * len(sums),
+        out_specs=vmem,
+        out_shape=shape_of(count, 128, dtype=BF16),
+        scratch_shapes=[pltpu.VMEM((count, 128), F32)],
+        cost_estimate=cost(4),
+    )(bits, token, *sums)
+
+
+def join_kernel(place, left_ref, right_ref, out_ref):
     n = left_ref.shape[1]
     out_ref[:, :n] = left_ref[...].astype(F32)
-    out_ref[:, n:] = right_ref[...].astype(F32)
-
-
-def join(left, right):
+    part = right_ref.shape[1]
+    count = out_ref.shape[0] // part
+    for k in range(count):
+        v = right_ref[place[pl.program_id(0) * count + k]]
+        out_ref[k * part : (k + 1) * part, n:] = v.astype(F32)
+
+
+def join(place, left, right):
     rows, n = left.shape
     block = 256
     return pl.pallas_call(
         join_kernel,
-        grid=(rows // block,),
-        in_specs=[pl.BlockSpec((block, n), lambda i: (i, 0)), pl.BlockSpec((block, right.shape[1]), lambda i: (i, 0))],
-        out_specs=pl.BlockSpec((block, n + right.shape[1]), lambda i: (i, 0)),
-        out_shape=shape_of(rows, n + right.shape[1]),
+        grid_spec=pltpu.PrefetchScalarGridSpec(
+            num_scalar_prefetch=1,
+            grid=(rows // block,),
+            in_specs=[pl.BlockSpec((block, n), lambda i, p: (i, 0)), pl.BlockSpec(right.shape, lambda i, p: (0, 0, 0))],
+            out_specs=pl.BlockSpec((block, n + right.shape[2]), lambda i, p: (i, 0)),
+        ),
+        out_shape=shape_of(rows, n + right.shape[2]),
         cost_estimate=cost(5),
-    )(left, right)
-
-
-def sum_flat(grid, v, part):
-    held = v.reshape(-1, 128)
-    n = held.shape[0]
-    parts = part.astype(BF16)
+    )(place, left, right)
+
+
+def sum_flat(grid, packed, hold, last_hold):
+    held = packed.astype(F32)
     masks = [grid.core, *grid.xs, *grid.tensor]
     for mask in masks:
-        low = held.astype(BF16)
-        got = grid.swap(jnp.concatenate([low, parts]), mask)
-        held = low.astype(F32) + got[:n].astype(F32)
-        parts = jnp.concatenate([parts, got[n:]])
-    parts = parts.reshape(*[2] * len(masks), *part.shape)
-    order = masks[::-1]
-    for axis, mask in enumerate(order):
-        parts = jnp.where(grid.bit(mask) == 1, jnp.flip(parts, axis), parts)
-    want = [*grid.xs[::-1], grid.core, *grid.tensor[::-1]]
-    parts = parts.transpose(*[order.index(m) for m in want], len(order), len(order) + 1)
-    return held.reshape(-1), parts.reshape(-1, part.shape[-1])
+        if mask == masks[-1]:
+            held = held + last_hold
+        low = packed if mask == masks[0] else held.astype(BF16)
+        held = low.astype(F32) + grid.swap(low, mask).astype(F32)
+        if mask == masks[0]:
+            held = held + hold
+    return held.reshape(-1)
+
+
+def every_part(grid, part):
+    parts = part
+    masks = [grid.core, *grid.xs, *grid.tensor]
+    for mask in masks:
+        parts = jnp.concatenate([parts, grid.swap(parts, mask)])
+    devices = jnp.arange(grid.count) ^ grid.index
+    place = sum(((devices // mask) % 2) << k for k, mask in enumerate(masks)).astype(jnp.int32)
+    return parts.reshape(grid.count, *part.shape), place
 
 
 def padded(v, size):
@@ -1057,16 +1143,17 @@
     bias = jnp.zeros((8, width), BF16).at[0, : bias.size].set(bias)
     seed = jnp.concatenate(
         [
-            own(w_in, half_f, 1).T, own(w_out, half_f, 0), own(w_value, half_v, 1).T,
-            own(w_reset, half_v, 1).T, own(w_branch, half_v, 0), bias,
+            own(w_in, half_f, 1).T, own(w_value, half_v, 1).T, own(w_reset, half_v, 1).T, own(w_branch, half_v, 0),
+            bias,
         ]
     )
     gathered = lax.all_gather(seed, AXES, axis=0)
+    gathered_out = lax.all_gather(own(w_out, half_f, 0), AXES, axis=0)
     which = [
         jnp.stack([(x_at ^ r) * 2 + c for r in range(n_x)]).astype(jnp.int32) for c in (core, 1 - core)
     ]
-    pieces = [Pieces(gathered, w, n_tensor, part_f, part_v) for w in which]
-    table = gathered[:, 2 * part_f + 3 * part_v].astype(F32).reshape(2 * n_x, n_tensor, width)
+    pieces = [Pieces(gathered, gathered_out, w, n_tensor, part_f, part_v) for w in which]
+    table = gathered[:, part_f + 3 * part_v].astype(F32).reshape(2 * n_x, n_tensor, width)
     tables = [jnp.stack([lax.dynamic_index_in_dim(table, w[r], 0, False) for r in range(n_x)]) for w in which]
     bias_v = [t[..., :part_v].reshape(1, -1) for t in tables]
     bias_r = [t[..., part_v : 2 * part_v].reshape(1, -1) for t in tables]
@@ -1131,11 +1218,9 @@
     probs = jax.nn.softmax(scores, axis=-1)
     probs_low = probs.astype(BF16)
 
-    sums_b = jnp.zeros((total, width), F32)
-    kept = [None, None]
-    for k in (0, 1):
-        *kept[k], sums_b = run_value(pieces[k], bias_v[k], normed_low, mixed_low, probs_low, bias_v[k], bias_r[k], sums_b)
-    branch = sums_b
+    both = Pieces(gathered, gathered_out, jnp.concatenate(which), n_tensor, part_f, part_v)
+    bias_v, bias_r = jnp.concatenate(bias_v, axis=1), jnp.concatenate(bias_r, axis=1)
+    *kept, branch = run_value(both, bias_v, normed_low, mixed_low, probs_low, bias_v, bias_r)
     mixed_out, ffn_low = run_middle(gate_pre, branch, source_low, ffn_gain)
     grad_low = cotangent.reshape(total, width)
 
@@ -1144,11 +1229,12 @@
     r_out = Reduce(grid, inner[1][2], dims, still)
     inner[0] = run_inner(pieces[0], inner[1][1], ffn_low, grad_low, bias_i[0])
     r_out.add_low(inner[0][2])
-    token = point(grid, [], r_out)
-    feed_out = jnp.zeros((total, width), F32)
+    token, gathered_out = point(grid, [], r_out, behind=gathered_out)
+    for p in pieces:
+        p.outer = gathered_out
     sum_in = [None, None]
     d_high, sum_in[1], feed_out, grad_ffn = run_outer(
-        pieces[1], token, ffn_low, grad_low, inner[1][0], inner[1][1], feed_out, feed_out
+        pieces[1], token, ffn_low, grad_low, inner[1][0], inner[1][1]
     )
     r_in = Reduce(grid, d_high, dims, still)
     token = point(grid, [sum_in[1]], r_out)
@@ -1183,12 +1269,14 @@
         token = sum_gates
 
     def run_vb(k, token):
-        return run_value_back(pieces[k], 200 if k == 0 else 1, token, grad_gates_low, normed_low, mixed_low, probs_low, kept[k])
+        return run_value_back(
+            pieces[k], k, 200 if k == 0 else 1, token, grad_gates_low, normed_low, mixed_low, probs_low, kept
+        )
 
     back = [None, None]
     back[1] = run_vb(1, token)
     r_v = Reduce(grid, back[1][0], dims, still)
-    token = point(grid, [back[1][1]], r_out, r_in, r_gates)
+    token = point(grid, [back[1][1], *r_out.raw], r_in, r_gates)
     back[0] = run_vb(0, token)
     r_v.add_low(back[0][0])
     token = point(grid, [back[0][1]], r_v, r_gates, r_in)
@@ -1196,7 +1284,7 @@
         token, flags, back[0][5], back[1][5], probs, query, key, shared, shared_pre, qk_gain, grad_gates_low, w_gates,
         back[0][3], back[1][3], blended, decay, tell,
     )
-    token = point(grid, [left], r_gates, r_in)
+    token = point(grid, [left, *r_in.raw], r_gates)
     left = left + token[0, 0]
     d_shared = dot_over_rows(mixed_low, grad_shared_low + token[0, 0].astype(BF16))
     d_shared = d_shared.reshape(*[2] * len(bits), -1, d_shared.shape[-1])
@@ -1210,7 +1298,7 @@
     t_first, *t_rest = grid.tensor
     for mask in [grid.core, *grid.xs, t_first]:
         d_shared = fold(d_shared, mask)
-    token = point(grid, [right], r_v, r_gates)
+    token = point(grid, [right], r_v, r_gates, r_in, r_out)
     d_shared = fold(d_shared + token[0, 0], t_rest[0])
     column = shape_of(8, 128)
     results = []
@@ -1232,42 +1320,51 @@
     done_in = finish(grid, [token], r_in, *done[1:2])
     done_out = finish(grid, [token], r_out, *done[2:])
     token_v = point(grid, [results[-1][1]], r_v)
-    done_v = finish(grid, [token_v], r_v)
+    token_w, *done_v = ends(point(grid, [token_v], r_v))
+    done_v = finish(grid, [token_w], r_v, *done_v)
     grad_w_out, grad_w_in = share_and_place(grid, [done_out, done_in], [(False,), (True,)], None)
-    (grad_w_out,), (grad_w_in,) = grad_w_out, grad_w_in
+    grad_w_out, grad_w_in = grad_w_out[0], grad_w_in[0]
     grad_w_gates = lax.all_gather(
         done_gates.reshape(width // grid.count, 2 * width), AXES, axis=0, tiled=True
     )
 
     z = token_v[0, 0]
-    spread_in = lambda k: in_place(back[0][k] + z, back[1][k] + z)
-    early = [
-        jnp.concatenate([jnp.sum(sum_gates + z, axis=0), sums_shared[3] + z]), sums_shared[:2].reshape(-1) + z,
-        sums_shared[2] + z, jnp.sum(sum_ffn_gain + z, axis=0), jnp.sum(sum_out + z, axis=0),
-        spread_in(2), spread_in(1), in_place(sum_in[0] + z, sum_in[1] + z),
-    ]
-    sum_eta, sum_one, sum_two, sum_omega, sum_norm_gain = (
-        sum(r[k] + z for r in results) for k in range(1, 6)
-    )
-    late = [
-        sum_eta.reshape(-1), sum_one.reshape(-1), sum_two.reshape(-1), jnp.sum(sum_norm_gain, axis=0), sum_omega.reshape(-1)
-    ]
-
-    def cut_like(v, parts):
+    part = d_shared.reshape(width // grid.count, -1) + token_w[0, 0]
+    sizes_late = [heads * width] * 3 + [width, width]
+    sizes_early = [2 * width + 128, 256, 128, width, width, units_v * n_tensor, units_v * n_tensor, units_f * n_tensor]
+    count = -(-sum(sizes_late + sizes_early) // 2048) * 16
+    if (part_v, part_f, n_x) == (64, 128, 2):
+        by_kind = [r[k] for k in range(1, 4) for r in results]
+        packed = run_pack(
+            jnp.stack([core, x_at]).astype(jnp.int32), token_v,
+            [
+                *by_kind, *[r[4] for r in results], *[r[5] for r in results], sum_gates, sums_shared, sum_ffn_gain, sum_out,
+                back[0][2], back[1][2], back[0][1], back[1][1], *sum_in,
+            ],
+            count,
+        )
+    else:
+        spread_in = lambda k: in_place(back[0][k] + z, back[1][k] + z)
+        both = [sum(r[k] + z for r in results) for k in range(1, 6)]
+        small = [
+            *[v.reshape(-1) for v in both[:3]], jnp.sum(both[4], axis=0), both[3].reshape(-1), jnp.sum(sum_gates + z, axis=0),
+            sums_shared[3] + z, sums_shared[:2].reshape(-1) + z, sums_shared[2] + z, jnp.sum(sum_ffn_gain + z, axis=0),
+            jnp.sum(sum_out + z, axis=0), spread_in(2), spread_in(1), in_place(sum_in[0] + z, sum_in[1] + z),
+        ]
+        packed = padded(jnp.concatenate(small), count * 128).reshape(-1, 128).astype(BF16)
+
+    def cut_like(v, sizes):
         out, first = [], 0
-        for p in parts:
-            out.append(v[first : first + p.size])
-            first += p.size
+        for n in sizes:
+            out.append(v[first : first + n])
+            first += n
         return out
 
-    small = padded(jnp.concatenate(early), 128)
-    summed, d_shared = sum_flat(
-        grid, padded(jnp.concatenate([jnp.concatenate(late), small]), 2048), d_shared.reshape(width // grid.count, -1)
-    )
-    grad_w_gates = join(grad_w_gates, d_shared)
-    last = cut_like(summed, late)
-    cut = cut_like(summed[sum(p.size for p in late) :], early)
-    ((grad_w_branch, grad_w_reset, grad_w_value),) = share_and_place(grid, [done_v], [(False, True, True)], None)
+    ((grad_w_branch, grad_w_reset, grad_w_value, *placed),) = share_and_place(grid, [done_v], [(False, True, True)], None)
+    summed = sum_flat(grid, packed, token_w[0, 0], placed[0][0, 0] if placed else 0.0)
+    parts, place = every_part(grid, part.astype(BF16))
+    grad_w_gates = join(place, grad_w_gates, parts)
+    last, cut = cut_like(summed, sizes_late), cut_like(summed[sum(sizes_late) :], sizes_early)
     untile = lambda v: v.reshape(heads, width).T
     eta, one, two = (untile(v) for v in last[:3])
     mine = lambda v, n: lax.dynamic_slice_in_dim(v, rank * n, n, 0)

time: 653 us -> 601 us (0.920)
  waiting for transfers between devices: 219 us -> 178 us
  starting transfers between devices: 42.5 us -> 56 us
  other arithmetic: 31 us -> 24.3 us
    all_gather x1, waiting for transfers between devices: 113 us -> 76.7 us  [local(): gathered = lax.all_gather(seed, AXES, axis=0)]
    ppermute x50 -> x54, waiting for transfers between devices: 106 us -> 75.2 us  [swap(): return lax.ppermute(value, AXES, [(i, i ^ mask) for i in range(self.count)])]
    all_gather x0 -> x1, waiting for transfers between devices: none -> 26.2 us  [local(): gathered_out = lax.all_gather(own(w_out, half_f, 0), AXES, axis=0)]
    ppermute x50 -> x54, starting transfers between devices: 42.4 us -> 55.9 us  [swap(): return lax.ppermute(value, AXES, [(i, i ^ mask) for i in range(self.count)])]
    pallas_call x8 -> x7, Pallas kernels: 120 us -> 111 us  [blocked(): pl.pallas_call(body, grid_spec=pltpu.PrefetchScalarGridSpec(num_scalar_pr...]
    unnamed x179 -> x121, local copies, waits for them, and re-layouts: 17.6 us -> 12.5 us
  transfers between devices with their start and end apart: 52 -> 57, of which waited for: 21 -> 21; matrix products, arithmetic and copies ran while one was open for 9% -> 8% of each run, Pallas kernels for 34% -> 42%
where the time goes in v3:
time: 601 us; the launch traced here: 597 us
  Pallas kernels  284 us (47%)
  waiting for transfers between devices  178 us (30%)
  starting transfers between devices  56 us (9%)
  local copies, waits for them, and re-layouts  31.4 us (5%)
  other arithmetic  24.3 us (4%)
  between operations  15.8 us (3%)
  matrix products  6.85 us (1%)
    pallas_call x7, Pallas kernels, blocked(): pl.pallas_call(body, grid_spec=pltpu.PrefetchScalarGridSpec(num_scalar_pr...  111 us
    all_gather x1, waiting for transfers between devices, local(): gathered = lax.all_gather(seed, AXES, axis=0)  76.7 us
    ppermute x54, waiting for transfers between devices, swap(): return lax.ppermute(value, AXES, [(i, i ^ mask) for i in range(self.count)])  75.2 us
    ppermute x54, starting transfers between devices, swap(): return lax.ppermute(value, AXES, [(i, i ^ mask) for i in range(self.count)])  55.9 us
    pallas_call x10, Pallas kernels, run_point(): pl.pallas_call(body, grid_spec=pltpu.PrefetchScalarGridSpec(num_scalar_pr...  46.8 us
    pallas_call x2, Pallas kernels, run_back(): pl.pallas_call(partial(back_kernel, m), grid=(1,), in_specs=[pl.BlockSpec...  39.2 us
    all_gather x1, waiting for transfers between devices, local(): gathered_out = lax.all_gather(own(w_out, half_f, 0), AXES, axis=0)  26.2 us
    pallas_call x2, Pallas kernels, call(): pl.pallas_call(kernel, out_shape=outs, in_specs=[pl.BlockSpec(memory_spac...  24.4 us
  transfers between devices with their start and end apart: 57, of which 21 were waited for; matrix products, arithmetic and copies ran while one was open for 8% of the time, Pallas kernels for 42%

profile of v3, /device:TPU:0, one launch (start us, length us, event | category | flops | bytes accessed | tf_op | source)
XLA Modules:
  0.0 596.8 jit_solution(13177210872990591362)
XLA Ops:
  15.5 11.7 %shard_map.390 = (f32[4096,128]{1,0:T(8,128)}, bf16[512,1024]{1,0:T(8,128)(2,1)}, f32[2,16,8,128]{3,2,1,0:T(8,128)}) custom-call(s32[2,256]{1,0:T(2,128)} %copy-done.38, bf16[512,1024]{1,0:T(8,128)(2,1)} %bitcast.193, f32[1,1024]{1,0:T(1,128)} %bitcast.238, f32[16,8,128]{2,1,0:T(8,128)} %bitcast.201, f32[16,8,128]{2,1,0:T(8,128)} %bitcast.215), custom_call_target="tpu_custom_call" | custom-call | flops 13799999488 | bytes 39600000 | tf_op jit(solution)/shard_map/pallas_call | solution.py:710
  28.8 3.0 collective-permute-start
  31.8 1.7 constant_dynamic-slice_fusion
  33.6 1.9 collective-permute-done
  36.6 1.9 collective-permute-start.1
  38.4 6.2 %collective-permute-done.1 = f32[2,17,8,128]{3,2,1,0:T(8,128)S(1)} collective-permute-done((f32[2,17,8,128]{3,2,1,0:T(8,128)S(1)}, f32[2,17,8,128]{3,2,1,0:T(8,128)S(1)}, u32[]{:S(2)}, u32[]{:S(2)}) %collective-permute-start.1) | collective-permute-done | bytes 139296 | tf_op jit(solution)/shard_map/ppermute | solution.py:52
  44.7 2.3 collective-permute-start.2
  48.6 7.0 %collective-permute-done.2 = f32[2,17,8,128]{3,2,1,0:T(8,128)S(1)} collective-permute-done((f32[2,17,8,128]{3,2,1,0:T(8,128)S(1)}, f32[2,17,8,128]{3,2,1,0:T(8,128)S(1)}, u32[]{:S(2)}, u32[]{:S(2)}) %collective-permute-start.2) | collective-permute-done | bytes 139296 | tf_op jit(solution)/shard_map/ppermute | solution.py:52
  56.3 12.7 %shard_map.391 = (f32[512,1024]{1,0:T(8,128)}, bf16[512,1024]{1,0:T(8,128)(2,1)}) custom-call(s32[2,256]{1,0:T(2,128)} %copy-done.38, f32[4096,128]{1,0:T(8,128)} %get-tuple-element.151.normed_ref, f32[2,16,8,128]{3,2,1,0:T(8,128)} %add_select_fusion.2.start_ref, f32[16,8,128]{2,1,0:T(8,128)} %bitcast.202, f32[16,8,128]{2,1,0:T(8,128)} %bitcast.216, ...), custom_call_target="tpu_custom_call" | custom-call | flops 13799999488 | bytes 39600000 | tf_op jit(solution)/shard_map/pallas_call | solution.py:710
  69.1 5.2 convolution_add_fusion.gate_ref
  74.3 2.1 copy-done.5
  78.3 76.7 %all-gather.7.cloned.1.call-done = bf16[10496,1024]{1,0:T(8,128)(2,1)} async-done(((bf16[328,1024]{1,0:T(8,128)(2,1)}), bf16[10496,1024]{1,0:T(8,128)(2,1)}) %all-gather.7.cloned.1.call-update) | async-done | bytes 21495824 | tf_op jit(solution)/shard_map/all_gather | solution.py:1150
  159.1 17.2 %shard_map.392 = (f32[512,2048]{1,0:T(8,128)}, f32[512,2048]{1,0:T(8,128)}, f32[512,2048]{1,0:T(8,128)}, bf16[512,2048]{1,0:T(8,128)(2,1)}, f32[512,1024]{1,0:T(8,128)}) custom-call(s32[4]{0:T(128)} %pad_add_fusion.4.piece, f32[1,2048]{1,0:T(1,128)} %pad_maximum_fusion.20.before.refs_6_, bf16[512,1024]{1,0:T(8,128)(2,1)} %get-tuple-element.154.refs_0_.refs_1_, ...), custom_call_target="tpu_custom_call" | custom-call | flops 230000001024 | bytes 660000000 | tf_op jit(solution)/shard_map/pallas_call | solution.py:626
  176.3 5.7 shard_map.393
  182.0 10.0 %shard_map.394 = (f32[512,2048]{1,0:T(8,128)}, bf16[512,2048]{1,0:T(8,128)(2,1)}, bf16[2,1,2048,512]{3,2,1,0:T(8,128)(2,1)}) custom-call(s32[2]{0:T(128)} %copy-done.42, f32[1,2048]{1,0:T(1,128)} %bitcast.225, bf16[512,1024]{1,0:T(8,128)(2,1)} %get-tuple-element.156.refs_0_, bf16[512,1024]{1,0:T(8,128)(2,1)} %bitcast.188, bf16[32,328,1024]{2,1,0:T(8,128)(2,1)} %bitcast.175, ...), custom_call_target="tpu_custom_call" | custom-call | flops 230000001024 | bytes 660000000 | tf_op jit(solution)/shard_map/pallas_call | solution.py:626
  192.2 9.9 %shard_map.395 = (f32[512,2048]{1,0:T(8,128)}, bf16[512,2048]{1,0:T(8,128)(2,1)}, bf16[2,1,2048,512]{3,2,1,0:T(8,128)(2,1)}) custom-call(s32[2]{0:T(128)} %copy-done.46, bf16[512,2048]{1,0:T(8,128)(2,1)} %get-tuple-element.157.before.refs_5_, bf16[512,1024]{1,0:T(8,128)(2,1)} %get-tuple-element.156.refs_0_, bf16[512,1024]{1,0:T(8,128)(2,1)} %bitcast.189, ...), custom_call_target="tpu_custom_call" | custom-call | flops 230000001024 | bytes 660000000 | tf_op jit(solution)/shard_map/pallas_call | solution.py:626
  202.2 5.3 shard_map.396
  207.5 26.2 %all-gather.9.cloned.1.call-done = bf16[4096,1024]{1,0:T(8,128)(2,1)} async-done(((bf16[128,1024]{1,0:T(8,128)(2,1)}), bf16[4096,1024]{1,0:T(8,128)(2,1)}) %all-gather.9.cloned.1.call-update) | async-done | bytes 8388624 | tf_op jit(solution)/shard_map/all_gather | solution.py:1151
  235.7 19.0 %shard_map.397 = (bf16[2,1,2048,512]{3,2,1,0:T(8,128)(2,1)}, f32[1,2048]{1,0:T(1,128)}, f32[512,1024]{1,0:T(8,128)}, f32[512,1024]{1,0:T(8,128)}) custom-call(s32[2]{0:T(128)} %copy-done.42, f32[8,128]{1,0:T(8,128)} %get-tuple-element.163.before, bf16[512,1024]{1,0:T(8,128)(2,1)} %get-tuple-element.156.refs_0_, bf16[512,1024]{1,0:T(8,128)(2,1)} %bitcast.190, ...), custom_call_target="tpu_custom_call" | custom-call | flops 230000001024 | bytes 660000000 | tf_op jit(solution)/shard_map/pallas_call | solution.py:626
  254.8 4.5 collective-permute-done.4.refs_3_.refs_2_.refs_29_.refs_27_
  260.5 3.7 shard_map.398
  266.3 20.6 %shard_map.399 = (bf16[2,1,2048,512]{3,2,1,0:T(8,128)(2,1)}, f32[1,2048]{1,0:T(1,128)}, f32[512,1024]{1,0:T(8,128)}, f32[512,1024]{1,0:T(8,128)}) custom-call(s32[2]{0:T(128)} %copy-done.46, f32[8,128]{1,0:T(8,128)} %get-tuple-element.170.before, bf16[512,1024]{1,0:T(8,128)(2,1)} %get-tuple-element.156.refs_0_, bf16[512,1024]{1,0:T(8,128)(2,1)} %bitcast.191, ...), custom_call_target="tpu_custom_call" | custom-call | flops 230000001024 | bytes 660000000 | tf_op jit(solution)/shard_map/pallas_call | solution.py:626
  287.0 5.2 shard_map.400
  292.2 10.5 %shard_map.401 = (bf16[512,1024]{1,0:T(8,128)(2,1)}, f32[512,1024]{1,0:T(8,128)}, bf16[512,2048]{1,0:T(8,128)(2,1)}, f32[8,1024]{1,0:T(8,128)}, f32[8,1024]{1,0:T(8,128)}, /*index=5*/f32[8,2048]{1,0:T(8,128)}) custom-call(f32[8,128]{1,0:T(8,128)} %get-tuple-element.177.before, f32[512,2176]{1,0:T(8,128)} %copy-done.5, ...), custom_call_target="tpu_custom_call" | custom-call | flops 1150000000 | bytes 3300000 | tf_op jit(solution)/shard_map/pallas_call | solution.py:544
  302.7 4.9 shard_map.402.before
  309.6 1.9 collective-permute-start.9
  313.3 4.9 shard_map.403.before
  318.1 17.3 %shard_map.404 = (bf16[2,3,1024,512]{3,2,1,0:T(8,128)(2,1)}, f32[1,1024]{1,0:T(1,128)}, f32[1,1024]{1,0:T(1,128)}, f32[512,1024]{1,0:T(8,128)}, f32[512,1024]{1,0:T(8,128)}, /*index=5*/f32[4,128,128]{2,1,0:T(8,128)}) custom-call(s32[2]{0:T(128)} %copy-done.42, bf16[2,1,512,1024]{3,2,1,0:T(8,128)(2,1)} %shard_map.403.before, ...), custom_call_target="tpu_custom_call" | custom-call | flops 1150000000 | bytes 3300000 | tf_op jit(solution)/shard_map/pallas_call | solution.py:626
  337.6 5.0 shard_map.405
  346.7 17.2 %shard_map.406 = (bf16[2,3,1024,512]{3,2,1,0:T(8,128)(2,1)}, f32[1,1024]{1,0:T(1,128)}, f32[1,1024]{1,0:T(1,128)}, f32[512,1024]{1,0:T(8,128)}, f32[512,1024]{1,0:T(8,128)}, /*index=5*/f32[4,128,128]{2,1,0:T(8,128)}) custom-call(s32[2]{0:T(128)} %copy-done.46, f32[8,128]{1,0:T(8,128)} %get-tuple-element.194.before, ...), custom_call_target="tpu_custom_call" | custom-call | flops 230000001024 | bytes 660000000 | tf_op jit(solution)/shard_map/pallas_call | solution.py:626
  363.9 4.6 collective-permute-done.16.refs_14_.refs_20_.refs_16_
  368.5 6.6 %shard_map.407 = (bf16[3,2,2,2,64,512]{5,4,3,2,1,0:T(8,128)(2,1)}, bf16[3,2,2,2,64,512]{5,4,3,2,1,0:T(8,128)(2,1)}, bf16[1,2,2,32,1024]{4,3,2,1,0:T(8,128)(2,1)}...) custom-call(s32[8]{0:T(128)} %stack.135.p, ...), custom_call_target="tpu_custom_call" | custom-call | flops 1150000000 | bytes 3300000 | tf_op jit(solution)/shard_map/pallas_call | solution.py:929
  380.3 18.3 %shard_map.408 = (f32[4096,128]{1,0:T(8,128)}, f32[2,16,8,128]{3,2,1,0:T(8,128)}, bf16[512,128]{1,0:T(8,128)(2,1)}, f32[8,128]{1,0:T(8,128)}) custom-call(f32[8,128]{1,0:T(8,128)} %get-tuple-element.202.before, s32[2,256]{1,0:T(2,128)} %copy-done.38, f32[4,128,128]{2,1,0:T(8,128)} %get-tuple-element.203.gp0_ref, f32[4,128,128]{2,1,0:T(8,128)} %get-tuple-element.204.gp1_ref, ...), custom_call_target="tpu_custom_call" | custom-call | flops 230000001024 | bytes 660000000 | tf_op jit(solution)/shard_map/pallas_call | solution.py:213
  398.7 1.9 collective-permute-done.18.refs_1_.refs_21_.refs_26_.refs_17_.refs_23_
  400.6 2.9 shard_map.409
  408.2 12.2 %collective-permute-done.21 = f32[2,17,8,128]{3,2,1,0:T(8,128)S(1)} collective-permute-done((f32[2,17,8,128]{3,2,1,0:T(8,128)S(1)}, f32[2,17,8,128]{3,2,1,0:T(8,128)S(1)}, u32[]{:S(2)}, u32[]{:S(2)}) %collective-permute-start.21) | collective-permute-done | bytes 139296 | tf_op jit(solution)/shard_map/ppermute | solution.py:52
  424.2 2.2 collective-permute-done.22
  426.5 1.6 collective-permute-start.23
  429.7 4.3 collective-permute-done.23
  435.4 5.8 shard_map.410
  441.3 1.9 pad_maximum_fusion.2
  445.2 2.0 collective-permute-start.27
  449.7 19.7 %shard_map.411 = (f32[256,1024]{1,0:T(8,128)}, f32[16,8,128]{2,1,0:T(8,128)}, f32[16,8,128]{2,1,0:T(8,128)}, f32[16,8,128]{2,1,0:T(8,128)}, f32[8,128]{1,0:T(8,1...) custom-call(f32[8,128]{1,0:T(8,128)} %get-tuple-element.216.before, s32[2,256]{1,0:T(2,128)} %copy-done.38, ...), custom_call_target="tpu_custom_call" | custom-call | flops 230000001024 | bytes 660000000 | tf_op jit(solution)/shard_map/pallas_call | solution.py:325
  469.4 1.9 fusion.43
  471.3 5.5 shard_map.412
  476.8 2.5 collective-permute-start.31
  479.3 19.5 %shard_map.413 = (f32[256,1024]{1,0:T(8,128)}, f32[16,8,128]{2,1,0:T(8,128)}, f32[16,8,128]{2,1,0:T(8,128)}, f32[16,8,128]{2,1,0:T(8,128)}, f32[8,128]{1,0:T(8,1...) custom-call(f32[8,128]{1,0:T(8,128)} %get-tuple-element.228.before, s32[2,256]{1,0:T(2,128)} %copy-done.38, ...), custom_call_target="tpu_custom_call" | custom-call | flops 230000001024 | bytes 660000000 | tf_op jit(solution)/shard_map/pallas_call | solution.py:325
  504.0 2.4 collective-permute-done.52.x_ref
  506.6 2.7 collective-permute-done.50.x_ref
  509.4 2.9 collective-permute-done.31.refs_5_.refs_10_.refs_11_
  512.3 3.2 shard_map.414
  516.8 1.9 shard_map.415
  518.7 3.0 shard_map.420
  522.5 3.1 shard_map.419
  527.6 1.8 collective-permute-done.33.refs_6_.refs_12_
  530.1 3.5 shard_map.416
  535.6 1.8 collective-permute-start.37
  538.4 1.8 collective-permute-start.46
  540.2 12.3 %collective-permute-done.46 = bf16[64,128]{1,0:T(8,128)(2,1)S(1)} collective-permute-done((bf16[64,128]{1,0:T(8,128)(2,1)S(1)}, bf16[64,128]{1,0:T(8,128)(2,1)S(1)}, u32[]{:S(2)}, u32[]{:S(2)}) %collective-permute-start.46) | collective-permute-done | bytes 16416 | tf_op jit(solution)/shard_map/ppermute | solution.py:52
  560.7 2.5 collective-permute-start.49
  563.2 1.6 collective-permute-start.36
  564.8 3.4 shard_map.417
  573.0 4.4 collective-permute-done.39
  583.1 6.9 %shard_map.418 = f32[1024,2176]{1,0:T(8,128)} custom-call(s32[32]{0:T(128)} %fusion.34.place, bf16[1024,2048]{1,0:T(8,128)(2,1)} %bitcast.234, bf16[32,32,128]{2,1,0:T(8,128)(2,1)} %bitcast.230), custom_call_target="tpu_custom_call" | custom-call | flops 5750000128 | bytes 16500000 | tf_op jit(solution)/shard_map/pallas_call | solution.py:1074
  (314 shorter events, 86.9 us)
Async XLA Ops:
  7.2 147.8 %all-gather.7.cloned.1.call-start = ((), (), s32[]{:S(2)}) async-start(), calls=%async_computation | async-start | bytes 22167552 | tf_op jit(solution)/shard_map/all_gather | solution.py:1150
  12.4 221.3 %all-gather.9.cloned.1.call-start = ((), (), s32[]{:S(2)}) async-start(), calls=%async_computation.1 | async-start | bytes 8650752 | tf_op jit(solution)/shard_map/all_gather | solution.py:1151
  13.3 33.7 %copy-start.42 = (s32[2]{0:T(128)}, s32[2]{0:T(128)S(1)}, u32[]{:S(2)}) copy-start(s32[2]{0:T(128)S(1)} %get-tuple-element.149.piece) | copy-start | bytes 28
  13.3 33.7 %copy-start.46 = (s32[2]{0:T(128)}, s32[2]{0:T(128)S(1)}, u32[]{:S(2)}) copy-start(s32[2]{0:T(128)S(1)} %get-tuple-element.148.piece) | copy-start | bytes 28
  28.8 6.7 %collective-permute-start = (f32[2,17,8,128]{3,2,1,0:T(8,128)S(1)}, f32[2,17,8,128]{3,2,1,0:T(8,128)S(1)}, u32[]{:S(2)}, u32[]{:S(2)}) collective-permute-start(f32[2,17,8,128]{3,2,1,0:T(8,128)S(1)} %pad_maximum_fusion.6), channel_id=1, source_target_pairs={{0,1},{1,0},{2,3},{3,2},{4,5},{5,4},{6,7},{7,6},{8,9},{9,8},{10,11... | collective-permute-start | bytes 417800 | tf_op jit(solution)/shard_map/ppermute | solution.py:52
  33.5 549.6 %all-gather.11.cloned.1.call-start = ((), (), s32[]{:S(2)}) async-start(), calls=%async_computation.2 | async-start | bytes 4325376 | tf_op jit(solution)/shard_map/all_gather | solution.py:1327
  33.6 35.4 %copy-start.7 = (f32[16,8,128]{2,1,0:T(8,128)}, f32[16,8,128]{2,1,0:T(8,128)S(1)}, u32[]{:S(2)}) copy-start(f32[16,8,128]{2,1,0:T(8,128)S(1)} %get-tuple-element.298) | copy-start | bytes 196612
  33.6 35.4 %copy-start.9 = (f32[16,8,128]{2,1,0:T(8,128)}, f32[16,8,128]{2,1,0:T(8,128)S(1)}, u32[]{:S(2)}) copy-start(f32[16,8,128]{2,1,0:T(8,128)S(1)} %get-tuple-element.297) | copy-start | bytes 196612
  36.6 8.0 %collective-permute-start.1 = (f32[2,17,8,128]{3,2,1,0:T(8,128)S(1)}, f32[2,17,8,128]{3,2,1,0:T(8,128)S(1)}, u32[]{:S(2)}, u32[]{:S(2)}) collective-permute-start(f32[2,17,8,128]{3,2,1,0:T(8,128)S(1)} %pad_maximum_fusion.7), channel_id=1, source_target_pairs={{0,2},{1,3},{2,0},{3,1},{4,6},{5,7},{6,4},{7,5},{8,10},{9,11},{10,... | collective-permute-start | bytes 417800 | tf_op jit(solution)/shard_map/ppermute | solution.py:52
  44.7 10.9 %collective-permute-start.2 = (f32[2,17,8,128]{3,2,1,0:T(8,128)S(1)}, f32[2,17,8,128]{3,2,1,0:T(8,128)S(1)}, u32[]{:S(2)}, u32[]{:S(2)}) collective-permute-start(f32[2,17,8,128]{3,2,1,0:T(8,128)S(1)} %pad_maximum_fusion.8), channel_id=1, source_target_pairs={{0,4},{1,5},{2,6},{3,7},{4,0},{5,1},{6,2},{7,3},{8,12},{9,13},{10,... | collective-permute-start | bytes 417800 | tf_op jit(solution)/shard_map/ppermute | solution.py:52
  77.1 78.0 %copy-start.31 = (bf16[512,128]{1,0:T(8,128)(2,1)}, bf16[512,128]{1,0:T(8,128)(2,1)S(1)}, u32[]{:S(2)}) copy-start(bf16[512,128]{1,0:T(8,128)(2,1)S(1)} %get-tuple-element.262.key_ref) | copy-start | bytes 393220
  77.1 99.2 %copy-start.16 = (f32[512,128]{1,0:T(8,128)}, f32[512,128]{1,0:T(8,128)S(1)}, u32[]{:S(2)}) copy-start(f32[512,128]{1,0:T(8,128)S(1)} %get-tuple-element.263.shared_ref) | copy-start | bytes 786436
  77.2 77.9 %copy-start.32 = (bf16[512,128]{1,0:T(8,128)(2,1)}, bf16[512,128]{1,0:T(8,128)(2,1)S(1)}, u32[]{:S(2)}) copy-start(bf16[512,128]{1,0:T(8,128)(2,1)S(1)} %add_convert_fusion.4.query_ref) | copy-start | bytes 393220
  192.0 10.2 %collective-permute-start.3 = (bf16[2,1,2,2,2,2,128,512]{7,6,5,4,3,2,1,0:T(8,128)(2,1)}, bf16[2,1,2,2,2,2,128,512]{7,6,5,4,3,2,1,0:T(8,128)(2,1)}, u32[]{:S(2)}, u32[]{:S(2)}) collective-permute-start(bf16[2,1,2,2,2,2,128,512]{7,6,5,4,3,2,1,0:T(8,128)(2,1)} %bitcast.236), channel_id=1, source_target_pairs={{0,8},{1,9},{2,10},{3,11},{4,12},{5,13},{6,14},{7,15},{8,0},{9,1},... | collective-permute-start | bytes 12582920 | tf_op jit(solution)/shard_map/ppermute | solution.py:52
  233.7 25.6 %collective-permute-start.4 = (bf16[1,2,2,2,128,512]{5,4,3,2,1,0:T(8,128)(2,1)}, bf16[1,2,2,2,128,512]{5,4,3,2,1,0:T(8,128)(2,1)}, u32[]{:S(2)}, u32[]{:S(2)}) collective-permute-start(bf16[1,2,2,2,128,512]{5,4,3,2,1,0:T(8,128)(2,1)} %get-tuple-element.162), channel_id=1, source_target_pairs={{0,16},{1,17},{2,18},{3,19},{4,20},{5,21},{6,22},{7,23},{8,24},{9,... | collective-permute-start | bytes 3145736 | tf_op jit(solution)/shard_map/ppermute | solution.py:52
  235.1 25.4 %collective-permute-start.5 = (bf16[1,2,2,2,128,512]{5,4,3,2,1,0:T(8,128)(2,1)}, bf16[1,2,2,2,128,512]{5,4,3,2,1,0:T(8,128)(2,1)}, u32[]{:S(2)}, u32[]{:S(2)}) collective-permute-start(bf16[1,2,2,2,128,512]{5,4,3,2,1,0:T(8,128)(2,1)} %get-tuple-element.167), channel_id=1, source_target_pairs={{0,1},{1,0},{2,3},{3,2},{4,5},{5,4},{6,7},{7,6},{8,9},{9,8},{10,11... | collective-permute-start | bytes 3145736 | tf_op jit(solution)/shard_map/ppermute | solution.py:52
  254.7 32.3 %collective-permute-start.8 = (bf16[2,1,2,2,2,2,128,512]{7,6,5,4,3,2,1,0:T(8,128)(2,1)}, bf16[2,1,2,2,2,2,128,512]{7,6,5,4,3,2,1,0:T(8,128)(2,1)}, u32[]{:S(2)}, u32[]{:S(2)}) collective-permute-start(bf16[2,1,2,2,2,2,128,512]{7,6,5,4,3,2,1,0:T(8,128)(2,1)} %bitcast.235), channel_id=1, source_target_pairs={{0,8},{1,9},{2,10},{3,11},{4,12},{5,13},{6,14},{7,15},{8,0},{9,1},... | collective-permute-start | bytes 12582920 | tf_op jit(solution)/shard_map/ppermute | solution.py:52
  264.2 22.8 %collective-permute-start.6 = (bf16[1,2,2,128,512]{4,3,2,1,0:T(8,128)(2,1)}, bf16[1,2,2,128,512]{4,3,2,1,0:T(8,128)(2,1)}, u32[]{:S(2)}, u32[]{:S(2)}) collective-permute-start(bf16[1,2,2,128,512]{4,3,2,1,0:T(8,128)(2,1)} %get-tuple-element.168), channel_id=1, source_target_pairs={{0,1},{1,0},{2,3},{3,2},{4,5},{5,4},{6,7},{7,6},{8,9},{9,8},{10,11... | collective-permute-start | bytes 1572872 | tf_op jit(solution)/shard_map/ppermute | solution.py:52
  264.9 22.1 %collective-permute-start.7 = (bf16[1,2,2,128,512]{4,3,2,1,0:T(8,128)(2,1)}, bf16[1,2,2,128,512]{4,3,2,1,0:T(8,128)(2,1)}, u32[]{:S(2)}, u32[]{:S(2)}) collective-permute-start(bf16[1,2,2,128,512]{4,3,2,1,0:T(8,128)(2,1)} %get-tuple-element.169), channel_id=1, source_target_pairs={{0,16},{1,17},{2,18},{3,19},{4,20},{5,21},{6,22},{7,23},{8,24},{9,... | collective-permute-start | bytes 1572872 | tf_op jit(solution)/shard_map/ppermute | solution.py:52
  307.6 28.2 %collective-permute-start.12 = (bf16[2,1,2,2,2,2,32,1024]{7,6,5,4,3,2,1,0:T(8,128)(2,1)}, bf16[2,1,2,2,2,2,32,1024]{7,6,5,4,3,2,1,0:T(8,128)(2,1)S(1)}, u32[]{:S(2)}, u32[]{:S(2)}) collective-permute-start(bf16[2,1,2,2,2,2,32,1024]{7,6,5,4,3,2,1,0:T(8,128)(2,1)} %bitcast.185), channel_id=1, source_target_pairs={{0,8},{1,9},{2,10},{3,11},{4,12},{5,13},{6,14},{7,15},{8,0},{9,1},... | collective-permute-start | bytes 6291464 | tf_op jit(solution)/shard_map/ppermute | solution.py:52
  307.6 28.2 %collective-permute-start.10 = (bf16[1,2,2,2,128,512]{5,4,3,2,1,0:T(8,128)(2,1)}, bf16[1,2,2,2,128,512]{5,4,3,2,1,0:T(8,128)(2,1)S(1)}, u32[]{:S(2)}, u32[]{:S(2)}) collective-permute-start(bf16[1,2,2,2,128,512]{5,4,3,2,1,0:T(8,128)(2,1)} %get-tuple-element.192), channel_id=1, source_target_pairs={{0,16},{1,17},{2,18},{3,19},{4,20},{5,21},{6,22},{7,23},{8,24},{9,... | collective-permute-start | bytes 3145736 | tf_op jit(solution)/shard_map/ppermute | solution.py:52
  308.2 27.7 %collective-permute-start.11 = (bf16[1,2,2,2,128,512]{5,4,3,2,1,0:T(8,128)(2,1)}, bf16[1,2,2,2,128,512]{5,4,3,2,1,0:T(8,128)(2,1)}, u32[]{:S(2)}, u32[]{:S(2)}) collective-permute-start(bf16[1,2,2,2,128,512]{5,4,3,2,1,0:T(8,128)(2,1)} %get-tuple-element.193), channel_id=1, source_target_pairs={{0,1},{1,0},{2,3},{3,2},{4,5},{5,4},{6,7},{7,6},{8,9},{9,8},{10,11... | collective-permute-start | bytes 3145736 | tf_op jit(solution)/shard_map/ppermute | solution.py:52
  309.6 26.2 %collective-permute-start.9 = (bf16[1,2,128,1024]{3,2,1,0:T(8,128)(2,1)}, bf16[1,2,128,1024]{3,2,1,0:T(8,128)(2,1)}, u32[]{:S(2)}, u32[]{:S(2)}) collective-permute-start(bf16[1,2,128,1024]{3,2,1,0:T(8,128)(2,1)} %get-tuple-element.191), channel_id=1, source_target_pairs={{0,4},{1,5},{2,6},{3,7},{4,0},{5,1},{6,2},{7,3},{8,12},{9,13},{10,... | collective-permute-start | bytes 1572872 | tf_op jit(solution)/shard_map/ppermute | solution.py:52
  335.4 33.1 %collective-permute-start.13 = (bf16[2,3,2,2,2,2,64,512]{7,6,5,4,3,2,1,0:T(8,128)(2,1)}, bf16[2,3,2,2,2,2,64,512]{7,6,5,4,3,2,1,0:T(8,128)(2,1)}, u32[]{:S(2)}, u32[]{:S(2)}) collective-permute-start(bf16[2,3,2,2,2,2,64,512]{7,6,5,4,3,2,1,0:T(8,128)(2,1)} %bitcast.233), channel_id=1, source_target_pairs={{0,8},{1,9},{2,10},{3,11},{4,12},{5,13},{6,14},{7,15},{8,0},{9,1},... | collective-permute-start | bytes 18874376 | tf_op jit(solution)/shard_map/ppermute | solution.py:52
  342.6 21.3 %collective-permute-start.14 = (bf16[1,2,2,2,32,1024]{5,4,3,2,1,0:T(8,128)(2,1)}, bf16[1,2,2,2,32,1024]{5,4,3,2,1,0:T(8,128)(2,1)}, u32[]{:S(2)}, u32[]{:S(2)}) collective-permute-start(bf16[1,2,2,2,32,1024]{5,4,3,2,1,0:T(8,128)(2,1)} %get-tuple-element.198), channel_id=1, source_target_pairs={{0,16},{1,17},{2,18},{3,19},{4,20},{5,21},{6,22},{7,23},{8,24},{9,... | collective-permute-start | bytes 1572872 | tf_op jit(solution)/shard_map/ppermute | solution.py:52
  343.3 20.6 %collective-permute-start.15 = (bf16[1,2,2,2,32,1024]{5,4,3,2,1,0:T(8,128)(2,1)}, bf16[1,2,2,2,32,1024]{5,4,3,2,1,0:T(8,128)(2,1)}, u32[]{:S(2)}, u32[]{:S(2)}) collective-permute-start(bf16[1,2,2,2,32,1024]{5,4,3,2,1,0:T(8,128)(2,1)} %get-tuple-element.199), channel_id=1, source_target_pairs={{0,1},{1,0},{2,3},{3,2},{4,5},{5,4},{6,7},{7,6},{8,9},{9,8},{10,11... | collective-permute-start | bytes 1572872 | tf_op jit(solution)/shard_map/ppermute | solution.py:52
  344.7 23.8 %collective-permute-start.16 = (bf16[1,2,2,128,512]{4,3,2,1,0:T(8,128)(2,1)}, bf16[1,2,2,128,512]{4,3,2,1,0:T(8,128)(2,1)}, u32[]{:S(2)}, u32[]{:S(2)}) collective-permute-start(bf16[1,2,2,128,512]{4,3,2,1,0:T(8,128)(2,1)} %get-tuple-element.200), channel_id=1, source_target_pairs={{0,1},{1,0},{2,3},{3,2},{4,5},{5,4},{6,7},{7,6},{8,9},{9,8},{10,11... | collective-permute-start | bytes 1572872 | tf_op jit(solution)/shard_map/ppermute | solution.py:52
  345.3 23.3 %collective-permute-start.17 = (bf16[1,2,2,128,512]{4,3,2,1,0:T(8,128)(2,1)}, bf16[1,2,2,128,512]{4,3,2,1,0:T(8,128)(2,1)}, u32[]{:S(2)}, u32[]{:S(2)}) collective-permute-start(bf16[1,2,2,128,512]{4,3,2,1,0:T(8,128)(2,1)} %get-tuple-element.201), channel_id=1, source_target_pairs={{0,16},{1,17},{2,18},{3,19},{4,20},{5,21},{6,22},{7,23},{8,24},{9,... | collective-permute-start | bytes 1572872 | tf_op jit(solution)/shard_map/ppermute | solution.py:52
  375.2 25.4 %collective-permute-start.18 = (bf16[1,2,128,1024]{3,2,1,0:T(8,128)(2,1)}, bf16[1,2,128,1024]{3,2,1,0:T(8,128)(2,1)}, u32[]{:S(2)}, u32[]{:S(2)}) collective-permute-start(bf16[1,2,128,1024]{3,2,1,0:T(8,128)(2,1)} %get-tuple-element.209), channel_id=1, source_target_pairs={{0,4},{1,5},{2,6},{3,7},{4,0},{5,1},{6,2},{7,3},{8,12},{9,13},{10,... | collective-permute-start | bytes 1572872 | tf_op jit(solution)/shard_map/ppermute | solution.py:52
  376.2 22.4 %collective-permute-start.19 = (bf16[1,2,2,32,1024]{4,3,2,1,0:T(8,128)(2,1)}, bf16[1,2,2,32,1024]{4,3,2,1,0:T(8,128)(2,1)}, u32[]{:S(2)}, u32[]{:S(2)}) collective-permute-start(bf16[1,2,2,32,1024]{4,3,2,1,0:T(8,128)(2,1)} %get-tuple-element.210), channel_id=1, source_target_pairs={{0,1},{1,0},{2,3},{3,2},{4,5},{5,4},{6,7},{7,6},{8,9},{9,8},{10,11... | collective-permute-start | bytes 786440 | tf_op jit(solution)/shard_map/ppermute | solution.py:52
  377.7 20.9 %collective-permute-start.20 = (bf16[1,2,2,32,1024]{4,3,2,1,0:T(8,128)(2,1)}, bf16[1,2,2,32,1024]{4,3,2,1,0:T(8,128)(2,1)}, u32[]{:S(2)}, u32[]{:S(2)}) collective-permute-start(bf16[1,2,2,32,1024]{4,3,2,1,0:T(8,128)(2,1)} %get-tuple-element.211), channel_id=1, source_target_pairs={{0,16},{1,17},{2,18},{3,19},{4,20},{5,21},{6,22},{7,23},{8,24},{9,... | collective-permute-start | bytes 786440 | tf_op jit(solution)/shard_map/ppermute | solution.py:52
  378.3 56.4 %collective-permute-start.24 = (bf16[3,2,2,2,64,512]{5,4,3,2,1,0:T(8,128)(2,1)}, bf16[3,2,2,2,64,512]{5,4,3,2,1,0:T(8,128)(2,1)}, u32[]{:S(2)}, u32[]{:S(2)}) collective-permute-start(bf16[3,2,2,2,64,512]{5,4,3,2,1,0:T(8,128)(2,1)} %get-tuple-element.213), channel_id=1, source_target_pairs={{0,16},{1,17},{2,18},{3,19},{4,20},{5,21},{6,22},{7,23},{8,24},{9,... | collective-permute-start | bytes 4718600 | tf_op jit(solution)/shard_map/ppermute | solution.py:52
  379.7 55.0 %collective-permute-start.25 = (bf16[3,2,2,2,64,512]{5,4,3,2,1,0:T(8,128)(2,1)}, bf16[3,2,2,2,64,512]{5,4,3,2,1,0:T(8,128)(2,1)}, u32[]{:S(2)}, u32[]{:S(2)}) collective-permute-start(bf16[3,2,2,2,64,512]{5,4,3,2,1,0:T(8,128)(2,1)} %get-tuple-element.214), channel_id=1, source_target_pairs={{0,1},{1,0},{2,3},{3,2},{4,5},{5,4},{6,7},{7,6},{8,9},{9,8},{10,11... | collective-permute-start | bytes 4718600 | tf_op jit(solution)/shard_map/ppermute | solution.py:52
  406.0 14.4 %collective-permute-start.21 = (f32[2,17,8,128]{3,2,1,0:T(8,128)S(1)}, f32[2,17,8,128]{3,2,1,0:T(8,128)S(1)}, u32[]{:S(2)}, u32[]{:S(2)}) collective-permute-start(f32[2,17,8,128]{3,2,1,0:T(8,128)S(1)} %pad_maximum_fusion.5), channel_id=1, source_target_pairs={{0,1},{1,0},{2,3},{3,2},{4,5},{5,4},{6,7},{7,6},{8,9},{9,8},{10,11... | collective-permute-start | bytes 417800 | tf_op jit(solution)/shard_map/ppermute | solution.py:52
  407.6 27.1 %collective-permute-start.26 = (bf16[1,2,32,2048]{3,2,1,0:T(8,128)(2,1)}, bf16[1,2,32,2048]{3,2,1,0:T(8,128)(2,1)S(1)}, u32[]{:S(2)}, u32[]{:S(2)}) collective-permute-start(bf16[1,2,32,2048]{3,2,1,0:T(8,128)(2,1)} %get-tuple-element.215), channel_id=1, source_target_pairs={{0,4},{1,5},{2,6},{3,7},{4,0},{5,1},{6,2},{7,3},{8,12},{9,13},{10,... | collective-permute-start | bytes 786440 | tf_op jit(solution)/shard_map/ppermute | solution.py:52
  408.2 14.5 %collective-permute-start.40 = (bf16[2,1,2,2,2,32,128]{6,5,4,3,2,1,0:T(8,128)(2,1)S(1)}, bf16[2,1,2,2,2,32,128]{6,5,4,3,2,1,0:T(8,128)(2,1)S(1)}, u32[]{:S(2)}, u32[]{:S(2)}) collective-permute-start(bf16[2,1,2,2,2,32,128]{6,5,4,3,2,1,0:T(8,128)(2,1)S(1)} %dynamic-slice_convert_fusion), channel_id=1, source_target_pairs={{0,8},{1,9},{2,10},{3,11},{4,12},{5,13},{6,14},{7,15},{8,0},{9,1},... | collective-permute-start | bytes 393224 | tf_op jit(solution)/shard_map/ppermute | solution.py:52
  421.3 5.1 collective-permute-start.22
  422.7 5.4 collective-permute-start.41
  426.5 7.5 %collective-permute-start.23 = (f32[2,17,8,128]{3,2,1,0:T(8,128)S(1)}, f32[2,17,8,128]{3,2,1,0:T(8,128)S(1)}, u32[]{:S(2)}, u32[]{:S(2)}) collective-permute-start(f32[2,17,8,128]{3,2,1,0:T(8,128)S(1)} %pad_maximum_fusion.10), channel_id=1, source_target_pairs={{0,4},{1,5},{2,6},{3,7},{4,0},{5,1},{6,2},{7,3},{8,12},{9,13},{10,... | collective-permute-start | bytes 417800 | tf_op jit(solution)/shard_map/ppermute | solution.py:52
  428.2 20.2 %collective-permute-start.42 = (bf16[1,1,2,2,1,32,128]{6,5,4,3,2,1,0:T(8,128)(2,1)S(1)}, bf16[1,1,2,2,1,32,128]{6,5,4,3,2,1,0:T(8,128)(2,1)S(1)}, u32[]{:S(2)}, u32[]{:S(2)}) collective-permute-start(bf16[1,1,2,2,1,32,128]{6,5,4,3,2,1,0:T(8,128)(2,1)S(1)} %dynamic-slice_convert_fusion.2), channel_id=1, source_target_pairs={{0,1},{1,0},{2,3},{3,2},{4,5},{5,4},{6,7},{7,6},{8,9},{9,8},{10,11... | collective-permute-start | bytes 98312 | tf_op jit(solution)/shard_map/ppermute | solution.py:52
  443.1 26.3 %collective-permute-start.28 = (bf16[2,128,1024]{2,1,0:T(8,128)(2,1)}, bf16[2,128,1024]{2,1,0:T(8,128)(2,1)}, u32[]{:S(2)}, u32[]{:S(2)}) collective-permute-start(bf16[2,128,1024]{2,1,0:T(8,128)(2,1)} %pad_maximum_fusion.2), channel_id=1, source_target_pairs={{0,2},{1,3},{2,0},{3,1},{4,6},{5,7},{6,4},{7,5},{8,10},{9,11},{10,... | collective-permute-start | bytes 1572872 | tf_op jit(solution)/shard_map/ppermute | solution.py:52
  443.1 28.1 %collective-permute-start.29 = (bf16[3,2,2,64,512]{4,3,2,1,0:T(8,128)(2,1)}, bf16[3,2,2,64,512]{4,3,2,1,0:T(8,128)(2,1)}, u32[]{:S(2)}, u32[]{:S(2)}) collective-permute-start(bf16[3,2,2,64,512]{4,3,2,1,0:T(8,128)(2,1)} %get-tuple-element.226), channel_id=1, source_target_pairs={{0,1},{1,0},{2,3},{3,2},{4,5},{5,4},{6,7},{7,6},{8,9},{9,8},{10,11... | collective-permute-start | bytes 2359304 | tf_op jit(solution)/shard_map/ppermute | solution.py:52
  444.6 26.7 %collective-permute-start.30 = (bf16[3,2,2,64,512]{4,3,2,1,0:T(8,128)(2,1)}, bf16[3,2,2,64,512]{4,3,2,1,0:T(8,128)(2,1)}, u32[]{:S(2)}, u32[]{:S(2)}) collective-permute-start(bf16[3,2,2,64,512]{4,3,2,1,0:T(8,128)(2,1)} %get-tuple-element.227), channel_id=1, source_target_pairs={{0,16},{1,17},{2,18},{3,19},{4,20},{5,21},{6,22},{7,23},{8,24},{9,... | collective-permute-start | bytes 2359304 | tf_op jit(solution)/shard_map/ppermute | solution.py:52
  445.2 26.1 %collective-permute-start.27 = (bf16[1,32,2048]{2,1,0:T(8,128)(2,1)}, bf16[1,32,2048]{2,1,0:T(8,128)(2,1)}, u32[]{:S(2)}, u32[]{:S(2)}) collective-permute-start(bf16[1,32,2048]{2,1,0:T(8,128)(2,1)} %get-tuple-element.223), channel_id=1, source_target_pairs={{0,2},{1,3},{2,0},{3,1},{4,6},{5,7},{6,4},{7,5},{8,10},{9,11},{10,... | collective-permute-start | bytes 393224 | tf_op jit(solution)/shard_map/ppermute | solution.py:52
  449.7 52.4 %collective-permute-start.43 = (bf16[1,1,2,1,1,32,128]{6,5,4,3,2,1,0:T(8,128)(2,1)}, bf16[1,1,2,1,1,32,128]{6,5,4,3,2,1,0:T(8,128)(2,1)}, u32[]{:S(2)}, u32[]{:S(2)}) collective-permute-start(bf16[1,1,2,1,1,32,128]{6,5,4,3,2,1,0:T(8,128)(2,1)} %dynamic-slice_convert_fusion.3), channel_id=1, source_target_pairs={{0,2},{1,3},{2,0},{3,1},{4,6},{5,7},{6,4},{7,5},{8,10},{9,11},{10,... | collective-permute-start | bytes 49160 | tf_op jit(solution)/shard_map/ppermute | solution.py:52
  476.8 35.5 %collective-permute-start.31 = (bf16[3,2,64,1024]{3,2,1,0:T(8,128)(2,1)}, bf16[3,2,64,1024]{3,2,1,0:T(8,128)(2,1)}, u32[]{:S(2)}, u32[]{:S(2)}) collective-permute-start(bf16[3,2,64,1024]{3,2,1,0:T(8,128)(2,1)} %get-tuple-element.230), channel_id=1, source_target_pairs={{0,4},{1,5},{2,6},{3,7},{4,0},{5,1},{6,2},{7,3},{8,12},{9,13},{10,... | collective-permute-start | bytes 2359304 | tf_op jit(solution)/shard_map/ppermute | solution.py:52
  500.1 6.4 %collective-permute-start.52 = (bf16[1,128,1024]{2,1,0:T(8,128)(2,1)S(1)}, bf16[1,128,1024]{2,1,0:T(8,128)(2,1)S(1)}, u32[]{:S(2)}, u32[]{:S(2)}) collective-permute-start(bf16[1,128,1024]{2,1,0:T(8,128)(2,1)S(1)} %copy-done.20), channel_id=1, source_target_pairs={{0,16},{1,17},{2,18},{3,19},{4,20},{5,21},{6,22},{7,23},{8,24},{9,... | collective-permute-start | bytes 786440 | tf_op jit(solution)/shard_map/ppermute | solution.py:52
  501.5 7.7 %collective-permute-start.50 = (bf16[1,128,1024]{2,1,0:T(8,128)(2,1)S(1)}, bf16[1,128,1024]{2,1,0:T(8,128)(2,1)S(1)}, u32[]{:S(2)}, u32[]{:S(2)}) collective-permute-start(bf16[1,128,1024]{2,1,0:T(8,128)(2,1)S(1)} %copy-done.19), channel_id=1, source_target_pairs={{0,16},{1,17},{2,18},{3,19},{4,20},{5,21},{6,22},{7,23},{8,24},{9,... | collective-permute-start | bytes 786440 | tf_op jit(solution)/shard_map/ppermute | solution.py:52
  503.5 31.3 %collective-permute-start.44 = (bf16[1,1,1,1,1,32,128]{6,5,4,3,2,1,0:T(8,128)(2,1)S(1)}, bf16[1,1,1,1,1,32,128]{6,5,4,3,2,1,0:T(8,128)(2,1)S(1)}, u32[]{:S(2)}, u32[]{:S(2)}) collective-permute-start(bf16[1,1,1,1,1,32,128]{6,5,4,3,2,1,0:T(8,128)(2,1)S(1)} %dynamic-slice_convert_fusion.4), channel_id=1, source_target_pairs={{0,4},{1,5},{2,6},{3,7},{4,0},{5,1},{6,2},{7,3},{8,12},{9,13},{10,... | collective-permute-start | bytes 24584 | tf_op jit(solution)/shard_map/ppermute | solution.py:52
  506.5 12.2 %collective-permute-start.53 = (bf16[2,1,128,1024]{3,2,1,0:T(8,128)(2,1)S(1)}, bf16[2,1,128,1024]{3,2,1,0:T(8,128)(2,1)}, u32[]{:S(2)}, u32[]{:S(2)}) collective-permute-start(bf16[2,1,128,1024]{3,2,1,0:T(8,128)(2,1)S(1)} %pad_maximum_fusion.4), channel_id=1, source_target_pairs={{0,8},{1,9},{2,10},{3,11},{4,12},{5,13},{6,14},{7,15},{8,0},{9,1},... | collective-permute-start | bytes 1572872 | tf_op jit(solution)/shard_map/ppermute | solution.py:52
  509.3 12.4 %collective-permute-start.51 = (bf16[2,1,128,1024]{3,2,1,0:T(8,128)(2,1)S(1)}, bf16[2,1,128,1024]{3,2,1,0:T(8,128)(2,1)S(1)}, u32[]{:S(2)}, u32[]{:S(2)}) collective-permute-start(bf16[2,1,128,1024]{3,2,1,0:T(8,128)(2,1)S(1)} %pad_maximum_fusion.3), channel_id=1, source_target_pairs={{0,8},{1,9},{2,10},{3,11},{4,12},{5,13},{6,14},{7,15},{8,0},{9,1},... | collective-permute-start | bytes 1572872 | tf_op jit(solution)/shard_map/ppermute | solution.py:52
  515.5 13.8 %collective-permute-start.33 = (bf16[3,64,1024]{2,1,0:T(8,128)(2,1)}, bf16[3,64,1024]{2,1,0:T(8,128)(2,1)S(1)}, u32[]{:S(2)}, u32[]{:S(2)}) collective-permute-start(bf16[3,64,1024]{2,1,0:T(8,128)(2,1)} %get-tuple-element.247), channel_id=1, source_target_pairs={{0,2},{1,3},{2,0},{3,1},{4,6},{5,7},{6,4},{7,5},{8,10},{9,11},{10,... | collective-permute-start | bytes 1179656 | tf_op jit(solution)/shard_map/ppermute | solution.py:52
  518.7 18.7 %collective-permute-start.32 = (bf16[512,128]{1,0:T(8,128)(2,1)}, bf16[512,128]{1,0:T(8,128)(2,1)S(1)}, u32[]{:S(2)}, u32[]{:S(2)}) collective-permute-start(bf16[512,128]{1,0:T(8,128)(2,1)} %shard_map.415), channel_id=1, source_target_pairs={{0,8},{1,9},{2,10},{3,11},{4,12},{5,13},{6,14},{7,15},{8,0},{9,1},... | collective-permute-start | bytes 393224 | tf_op jit(solution)/shard_map/ppermute | solution.py:52
  535.5 2.9 collective-permute-start.45
  535.6 18.4 %collective-permute-start.37 = (bf16[3,64,1024]{2,1,0:T(8,128)(2,1)}, bf16[3,64,1024]{2,1,0:T(8,128)(2,1)S(1)}, u32[]{:S(2)}, u32[]{:S(2)}) collective-permute-start(bf16[3,64,1024]{2,1,0:T(8,128)(2,1)} %get-tuple-element.249.own_ref), channel_id=1, source_target_pairs={{0,16},{1,17},{2,18},{3,19},{4,20},{5,21},{6,22},{7,23},{8,24},{9,... | collective-permute-start | bytes 1179656 | tf_op jit(solution)/shard_map/ppermute | solution.py:52
  538.1 19.8 %collective-permute-start.34 = (bf16[512,128]{1,0:T(8,128)(2,1)S(1)}, bf16[512,128]{1,0:T(8,128)(2,1)S(1)}, u32[]{:S(2)}, u32[]{:S(2)}) collective-permute-start(bf16[512,128]{1,0:T(8,128)(2,1)S(1)} %add_convert_fusion.3), channel_id=1, source_target_pairs={{0,16},{1,17},{2,18},{3,19},{4,20},{5,21},{6,22},{7,23},{8,24},{9,... | collective-permute-start | bytes 393224 | tf_op jit(solution)/shard_map/ppermute | solution.py:52
  538.4 14.0 %collective-permute-start.46 = (bf16[64,128]{1,0:T(8,128)(2,1)S(1)}, bf16[64,128]{1,0:T(8,128)(2,1)S(1)}, u32[]{:S(2)}, u32[]{:S(2)}) collective-permute-start(bf16[64,128]{1,0:T(8,128)(2,1)S(1)} %pad_maximum_fusion.13), channel_id=1, source_target_pairs={{0,16},{1,17},{2,18},{3,19},{4,20},{5,21},{6,22},{7,23},{8,24},{9,... | collective-permute-start | bytes 49160 | tf_op jit(solution)/shard_map/ppermute | solution.py:52
  552.5 3.9 collective-permute-start.47
  555.2 9.6 %collective-permute-start.38 = (bf16[2,3,64,1024]{3,2,1,0:T(8,128)(2,1)S(1)}, bf16[2,3,64,1024]{3,2,1,0:T(8,128)(2,1)}, u32[]{:S(2)}, u32[]{:S(2)}) collective-permute-start(bf16[2,3,64,1024]{3,2,1,0:T(8,128)(2,1)S(1)} %pad_maximum_fusion.1), channel_id=1, source_target_pairs={{0,8},{1,9},{2,10},{3,11},{4,12},{5,13},{6,14},{7,15},{8,0},{9,1},... | collective-permute-start | bytes 2359304 | tf_op jit(solution)/shard_map/ppermute | solution.py:52
  556.4 4.3 collective-permute-start.48
  557.9 5.2 collective-permute-start.35
  560.7 12.3 %collective-permute-start.49 = (bf16[512,128]{1,0:T(8,128)(2,1)S(1)}, bf16[512,128]{1,0:T(8,128)(2,1)S(1)}, u32[]{:S(2)}, u32[]{:S(2)}) collective-permute-start(bf16[512,128]{1,0:T(8,128)(2,1)S(1)} %get-tuple-element.288), channel_id=1, source_target_pairs={{0,4},{1,5},{2,6},{3,7},{4,0},{5,1},{6,2},{7,3},{8,12},{9,13},{10,... | collective-permute-start | bytes 393224 | tf_op jit(solution)/shard_map/ppermute | solution.py:52
  563.2 6.2 %collective-permute-start.36 = (bf16[512,128]{1,0:T(8,128)(2,1)S(1)}, bf16[512,128]{1,0:T(8,128)(2,1)S(1)}, u32[]{:S(2)}, u32[]{:S(2)}) collective-permute-start(bf16[512,128]{1,0:T(8,128)(2,1)S(1)} %add_convert_fusion.1), channel_id=1, source_target_pairs={{0,2},{1,3},{2,0},{3,1},{4,6},{5,7},{6,4},{7,5},{8,10},{9,11},{10,... | collective-permute-start | bytes 393224 | tf_op jit(solution)/shard_map/ppermute | solution.py:52
  570.1 7.3 %collective-permute-start.39 = (bf16[512,128]{1,0:T(8,128)(2,1)S(1)}, bf16[512,128]{1,0:T(8,128)(2,1)S(1)}, u32[]{:S(2)}, u32[]{:S(2)}) collective-permute-start(bf16[512,128]{1,0:T(8,128)(2,1)S(1)} %add_convert_fusion), channel_id=1, source_target_pairs={{0,4},{1,5},{2,6},{3,7},{4,0},{5,1},{6,2},{7,3},{8,12},{9,13},{10,... | collective-permute-start | bytes 393224 | tf_op jit(solution)/shard_map/ppermute | solution.py:52
  (46 other events, 426.6 us)
Sparse Core Ops, SparseCore 0:
  12.5 142.4 all-gather.6
  158.0 75.5 all-gather.8
  479.4 72.6 all-gather.10

commit v4 on v3

--- a/solution.py
+++ b/solution.py
@@ -460,7 +460,7 @@
     add_to(ffn_out, dot_nn(grad, wi), sum_f_ref)
 
 
-UNITS = 512
+UNITS = 1024
 
 
 def cost(micros):
@@ -753,7 +753,7 @@
         self.labels = ["side", "lead", *self.dims, "u", "h"]
         xs, (lo, *hi) = grid.xs[::-1], grid.tensor
         self.orders = [[*xs, lo], [lo, *xs]], hi[::-1]
-        self.step = -1
+        self.step, self.pair = -1, None
         self.high = self.view(high)
         self.raw = [grid.swap(self.high, grid.core)]
 
@@ -780,8 +780,12 @@
                 self.left[s] = [d for d in self.left[s] if d != self.masks[s]]
                 if len(self.raw) == 2:
                     self.sides[s].append(Term(self.raw[s], ["lead", *self.left[s], "u", "h"], {}))
+                elif self.pair is None:
+                    self.sides[s].append(Term(self.raw[0], ["lead", *self.left[s], "u", "hh"], {"hh": s}))
                 else:
-                    self.sides[s].append(Term(self.raw[0], ["lead", *self.left[s], "u", "hh"], {"hh": s}))
+                    names = ["pair", "lead", *self.left[s], "u", "hh"]
+                    self.sides[s].append(Term(self.raw[0], names, {"pair": self.pair, "hh": s}))
+            self.pair = None
         self.step += 1
 
     def wanted(self):
@@ -842,10 +846,23 @@
         if 0 < len(sums[k].orders[0][0]) <= sums[k].step < sums[k].steps
         and sums[k].step == sums[k + 1].step and sums[k].low.shape == sums[k + 1].low.shape
     ]
+    joined_outs, ranks, k = [], [], 0
+    for n, r in enumerate(sums):
+        if n - 1 in pair:
+            continue
+        if n in pair:
+            joined_outs.append((2, *outs[k]))
+            ranks.append(True)
+            k += 2
+        else:
+            m = 1 if r.step >= len(r.orders[0][0]) else 2
+            joined_outs.extend(outs[k : k + m])
+            ranks.extend([False] * m)
+            k += m
     sel = grid.sel
     fits = all(len(r.dims) <= 4 and r.low.shape[-2] % 32 == 0 for r in sums)
     if fits:
-        *values, token = run_point(grid, gates, tasks, outs, sel)
+        *values, token = run_point(grid, gates, tasks, joined_outs, ranks, sel)
     else:
         values = []
         sides = [
@@ -855,6 +872,9 @@
         for shape in outs:
             v = sides.pop(0)
             values.append(v if v.shape == shape else jnp.concatenate([v, sides.pop(0)], axis=-1))
+        for n in pair:
+            first = sum(1 if r.step >= len(r.orders[0][0]) else 2 for r in sums[:n]) - sum(m < n for m in pair)
+            values[first : first + 2] = [jnp.stack(values[first : first + 2])]
         token = after(jnp.zeros((8, 128), F32), [g[(0,) * g.ndim] for g in gates])
     if behind is not None:
         values, behind = lax.optimization_barrier((values, behind))
@@ -866,10 +886,10 @@
         if r.step == r.steps:
             done.append(values.pop(0))
         elif k in pair:
-            both = grid.swap(jnp.concatenate(values[:2]), r.masks[0])
-            n = values[0].shape[0]
-            r.raw, sums[k + 1].raw = [both[:n]], [both[n:]]
-            values, skip = values[2:], True
+            both = grid.swap(values[0], r.masks[0])
+            r.raw, r.pair = [both], 0
+            sums[k + 1].raw, sums[k + 1].pair = [both], 1
+            values, skip = values[1:], True
         else:
             n = 2 if r.step < len(r.orders[0][0]) else 1
             r.start(values[:n])
@@ -879,7 +899,7 @@
     return (token, *done) if done else token
 
 
-def run_point(grid, gates, tasks, outs, sel):
+def run_point(grid, gates, tasks, outs, ranks, sel):
     parts = 2
     arrays, specs, layout = [], [], []
     for r, terms, extra, left in tasks:
@@ -915,15 +935,16 @@
         refs = refs[len(gates) :]
         ins, results = refs[: len(arrays)], refs[len(arrays) :]
         queue = list(layout)
-        for ref in results[:-1]:
-            first = 0
-            while first < ref.shape[-1]:
-                mine = queue.pop(0)
-                total = ins[mine[0]][...].astype(F32)
-                for k in mine[1:]:
-                    total = total + ins[k][...].astype(F32)
-                ref[..., first : first + total.shape[-1]] = total.astype(BF16)
-                first += total.shape[-1]
+        for ref, rank in zip(results[:-1], ranks):
+            for ref in [ref.at[k] for k in (0, 1)] if rank else [ref]:
+                first = 0
+                while first < ref.shape[-1]:
+                    mine = queue.pop(0)
+                    total = ins[mine[0]][...].astype(F32)
+                    for k in mine[1:]:
+                        total = total + ins[k][...].astype(F32)
+                    ref[..., first : first + total.shape[-1]] = total.astype(BF16)
+                    first += total.shape[-1]
         results[-1][...] = jnp.zeros((8, 128), F32)
 
     return pl.pallas_call(
@@ -1058,7 +1079,8 @@
     )(bits, token, *sums)
 
 
-def join_kernel(place, left_ref, right_ref, out_ref):
+def join_kernel(place, left_ref, right_ref, out_ref, token_ref):
+    token_ref[...] = jnp.zeros((8, 128), F32)
     n = left_ref.shape[1]
     out_ref[:, :n] = left_ref[...].astype(F32)
     part = right_ref.shape[1]
@@ -1077,34 +1099,40 @@
             num_scalar_prefetch=1,
             grid=(rows // block,),
             in_specs=[pl.BlockSpec((block, n), lambda i, p: (i, 0)), pl.BlockSpec(right.shape, lambda i, p: (0, 0, 0))],
-            out_specs=pl.BlockSpec((block, n + right.shape[2]), lambda i, p: (i, 0)),
+            out_specs=[
+                pl.BlockSpec((block, n + right.shape[2]), lambda i, p: (i, 0)), pl.BlockSpec((8, 128), lambda i, p: (0, 0))
+            ],
         ),
-        out_shape=shape_of(rows, n + right.shape[2]),
-        cost_estimate=cost(5),
+        out_shape=[shape_of(rows, n + right.shape[2]), shape_of(8, 128)],
+        cost_estimate=cost(50),
     )(place, left, right)
 
 
-def sum_flat(grid, packed, hold, last_hold):
+def sum_flat(grid, packed, hold, last_hold, end_hold):
     held = packed.astype(F32)
-    masks = [grid.core, *grid.xs, *grid.tensor]
+    masks = [grid.core, *grid.tensor, *grid.xs]
     for mask in masks:
         if mask == masks[-1]:
-            held = held + last_hold
+            held = tied(held, last_hold)
         low = packed if mask == masks[0] else held.astype(BF16)
         held = low.astype(F32) + grid.swap(low, mask).astype(F32)
         if mask == masks[0]:
-            held = held + hold
-    return held.reshape(-1)
+            held = tied(held, hold)
+    return tied(held, end_hold).reshape(-1)
 
 
 def every_part(grid, part):
     parts = part
-    masks = [grid.core, *grid.xs, *grid.tensor]
+    masks = [grid.core, *grid.tensor, *grid.xs]
     for mask in masks:
         parts = jnp.concatenate([parts, grid.swap(parts, mask)])
     devices = jnp.arange(grid.count) ^ grid.index
     place = sum(((devices // mask) % 2) << k for k, mask in enumerate(masks)).astype(jnp.int32)
     return parts.reshape(grid.count, *part.shape), place
+
+
+def tied(v, token):
+    return (v.reshape(-1, 8, 128) + token.astype(v.dtype)).reshape(v.shape)
 
 
 def padded(v, size):
@@ -1285,8 +1313,8 @@
         back[0][3], back[1][3], blended, decay, tell,
     )
     token = point(grid, [left, *r_in.raw], r_gates)
-    left = left + token[0, 0]
-    d_shared = dot_over_rows(mixed_low, grad_shared_low + token[0, 0].astype(BF16))
+    left = left + token
+    d_shared = dot_over_rows(mixed_low, tied(grad_shared_low, token))
     d_shared = d_shared.reshape(*[2] * len(bits), -1, d_shared.shape[-1])
 
     def fold(v, mask):
@@ -1299,7 +1327,7 @@
     for mask in [grid.core, *grid.xs, t_first]:
         d_shared = fold(d_shared, mask)
     token = point(grid, [right], r_v, r_gates, r_in, r_out)
-    d_shared = fold(d_shared + token[0, 0], t_rest[0])
+    d_shared = fold(tied(d_shared, token) if d_shared.shape[-2] % 8 == 0 else d_shared, t_rest[0])
     column = shape_of(8, 128)
     results = []
     for m in range(micros):
@@ -1313,7 +1341,7 @@
         )
         if m == 0:
             token, *done = ends(point(grid, [results[0][1]], r_gates, r_in, r_out, r_v))
-            d_shared = d_shared + token[0, 0]
+            d_shared = tied(d_shared, token) if d_shared.shape[-2] % 8 == 0 else d_shared
             for mask in t_rest[1:]:
                 d_shared = fold(d_shared, mask)
     done_gates = finish(grid, [token], r_gates, *done[:1])
@@ -1329,7 +1357,8 @@
     )
 
     z = token_v[0, 0]
-    part = d_shared.reshape(width // grid.count, -1) + token_w[0, 0]
+    part = d_shared.reshape(width // grid.count, -1)
+    part = tied(part, token_w) if part.shape[0] % 8 == 0 else part
     sizes_late = [heads * width] * 3 + [width, width]
     sizes_early = [2 * width + 128, 256, 128, width, width, units_v * n_tensor, units_v * n_tensor, units_f * n_tensor]
     count = -(-sum(sizes_late + sizes_early) // 2048) * 16
@@ -1361,9 +1390,9 @@
         return out
 
     ((grad_w_branch, grad_w_reset, grad_w_value, *placed),) = share_and_place(grid, [done_v], [(False, True, True)], None)
-    summed = sum_flat(grid, packed, token_w[0, 0], placed[0][0, 0] if placed else 0.0)
     parts, place = every_part(grid, part.astype(BF16))
-    grad_w_gates = join(place, grad_w_gates, parts)
+    grad_w_gates, token_j = join(place, grad_w_gates, parts)
+    summed = sum_flat(grid, packed, token_w, placed[0] if placed else token_w, token_j)
     last, cut = cut_like(summed, sizes_late), cut_like(summed[sum(sizes_late) :], sizes_early)
     untile = lambda v: v.reshape(heads, width).T
     eta, one, two = (untile(v) for v in last[:3])

time: 601 us -> 596 us (level); the launches traced: 597 us -> 585 us
    slice x6 -> x0, local copies, waits for them, and re-layouts: 7.88 us -> none  [the longest x1 1.86 us: point(): r.raw, sums[k + 1].raw = ([both[:n]], [both[n:]])]
    ppermute x54, waiting for transfers between devices: 75.2 us -> 67.7 us  [swap(): return lax.ppermute(value, AXES, [(i, i ^ mask) for i in range(self.count)])]
    unnamed x121 -> x124, local copies, waits for them, and re-layouts: 12.5 us -> 14 us
  transfers between devices with their start and end apart: 57 -> 57, of which waited for: 21 -> 19; matrix products, arithmetic and copies ran while one was open for 8% -> 7% of each run, Pallas kernels for 42% -> 43%
where the time goes in v4:
time: 596 us; the launch traced here: 585 us
  Pallas kernels  280 us (47%)
  waiting for transfers between devices  172 us (29%)
  starting transfers between devices  58.7 us (10%)
  local copies, waits for them, and re-layouts  28 us (5%)
  other arithmetic  23.9 us (4%)
  between operations  15.5 us (3%)
  matrix products  6.78 us (1%)
    pallas_call x7, Pallas kernels, blocked(): pl.pallas_call(body, grid_spec=pltpu.PrefetchScalarGridSpec(num_scalar_pr...  109 us
    all_gather x1, waiting for transfers between devices, local(): gathered = lax.all_gather(seed, AXES, axis=0)  76.9 us
    ppermute x54, waiting for transfers between devices, swap(): return lax.ppermute(value, AXES, [(i, i ^ mask) for i in range(self.count)])  67.7 us
    ppermute x54, starting transfers between devices, swap(): return lax.ppermute(value, AXES, [(i, i ^ mask) for i in range(self.count)])  58.6 us
    pallas_call x10, Pallas kernels, run_point(): pl.pallas_call(body, grid_spec=pltpu.PrefetchScalarGridSpec(num_scalar_pr...  45.4 us
    pallas_call x2, Pallas kernels, run_back(): pl.pallas_call(partial(back_kernel, m), grid=(1,), in_specs=[pl.BlockSpec...  39 us
    all_gather x1, waiting for transfers between devices, local(): gathered_out = lax.all_gather(own(w_out, half_f, 0), AXES, axis=0)  27.4 us
    pallas_call x2, Pallas kernels, call(): pl.pallas_call(kernel, out_shape=outs, in_specs=[pl.BlockSpec(memory_spac...  24.2 us
  transfers between devices with their start and end apart: 57, of which 19 were waited for; matrix products, arithmetic and copies ran while one was open for 7% of the time, Pallas kernels for 43%

profile of v4, /device:TPU:0, one launch (start us, length us, event | category | flops | bytes accessed | tf_op | source)
XLA Modules:
  0.0 585.3 jit_solution(6217325710434788169)
XLA Ops:
  15.4 11.7 %shard_map.390 = (f32[4096,128]{1,0:T(8,128)}, bf16[512,1024]{1,0:T(8,128)(2,1)}, f32[2,16,8,128]{3,2,1,0:T(8,128)}) custom-call(s32[2,256]{1,0:T(2,128)} %copy-done.37, bf16[512,1024]{1,0:T(8,128)(2,1)} %bitcast.236, f32[1,1024]{1,0:T(1,128)} %bitcast.284, f32[16,8,128]{2,1,0:T(8,128)} %bitcast.244, f32[16,8,128]{2,1,0:T(8,128)} %bitcast.261), custom_call_target="tpu_custom_call" | custom-call | flops 13799999488 | bytes 39600000 | tf_op jit(solution)/shard_map/pallas_call | solution.py:710
  28.7 3.0 collective-permute-start
  31.7 1.7 constant_dynamic-slice_fusion
  33.5 1.9 collective-permute-done
  36.5 1.9 collective-permute-start.1
  38.4 6.2 %collective-permute-done.1 = f32[2,17,8,128]{3,2,1,0:T(8,128)S(1)} collective-permute-done((f32[2,17,8,128]{3,2,1,0:T(8,128)S(1)}, f32[2,17,8,128]{3,2,1,0:T(8,128)S(1)}, u32[]{:S(2)}, u32[]{:S(2)}) %collective-permute-start.1) | collective-permute-done | bytes 139296 | tf_op jit(solution)/shard_map/ppermute | solution.py:52
  44.7 2.3 collective-permute-start.2
  48.6 7.1 %collective-permute-done.2 = f32[2,17,8,128]{3,2,1,0:T(8,128)S(1)} collective-permute-done((f32[2,17,8,128]{3,2,1,0:T(8,128)S(1)}, f32[2,17,8,128]{3,2,1,0:T(8,128)S(1)}, u32[]{:S(2)}, u32[]{:S(2)}) %collective-permute-start.2) | collective-permute-done | bytes 139296 | tf_op jit(solution)/shard_map/ppermute | solution.py:52
  56.3 12.5 %shard_map.391 = (f32[512,1024]{1,0:T(8,128)}, bf16[512,1024]{1,0:T(8,128)(2,1)}) custom-call(s32[2,256]{1,0:T(2,128)} %copy-done.37, f32[4096,128]{1,0:T(8,128)} %get-tuple-element.152.normed_ref, f32[2,16,8,128]{3,2,1,0:T(8,128)} %add_select_fusion.2.start_ref, f32[16,8,128]{2,1,0:T(8,128)} %bitcast.245, f32[16,8,128]{2,1,0:T(8,128)} %bitcast.262, ...), custom_call_target="tpu_custom_call" | custom-call | flops 13799999488 | bytes 39600000 | tf_op jit(solution)/shard_map/pallas_call | solution.py:710
  68.9 5.2 convolution_add_fusion.gate_ref
  74.1 2.1 copy-done.4
  78.2 76.9 %all-gather.7.cloned.1.call-done = bf16[10496,1024]{1,0:T(8,128)(2,1)} async-done(((bf16[328,1024]{1,0:T(8,128)(2,1)}), bf16[10496,1024]{1,0:T(8,128)(2,1)}) %all-gather.7.cloned.1.call-update) | async-done | bytes 21495824 | tf_op jit(solution)/shard_map/all_gather | solution.py:1178
  159.2 17.2 %shard_map.392 = (f32[512,2048]{1,0:T(8,128)}, f32[512,2048]{1,0:T(8,128)}, f32[512,2048]{1,0:T(8,128)}, bf16[512,2048]{1,0:T(8,128)(2,1)}, f32[512,1024]{1,0:T(8,128)}) custom-call(s32[4]{0:T(128)} %pad_add_fusion.4.piece, f32[1,2048]{1,0:T(1,128)} %pad_maximum_fusion.19.before.refs_6_, bf16[512,1024]{1,0:T(8,128)(2,1)} %get-tuple-element.155.refs_0_.refs_1_, ...), custom_call_target="tpu_custom_call" | custom-call | flops 230000001024 | bytes 660000000 | tf_op jit(solution)/shard_map/pallas_call | solution.py:626
  176.3 5.7 shard_map.393
  182.1 9.6 %shard_map.394 = (f32[512,2048]{1,0:T(8,128)}, bf16[512,2048]{1,0:T(8,128)(2,1)}, bf16[2,1,2048,512]{3,2,1,0:T(8,128)(2,1)}) custom-call(s32[2]{0:T(128)} %copy-done.42, f32[1,2048]{1,0:T(1,128)} %bitcast.271, bf16[512,1024]{1,0:T(8,128)(2,1)} %get-tuple-element.157.refs_0_, bf16[512,1024]{1,0:T(8,128)(2,1)} %bitcast.231, bf16[32,328,1024]{2,1,0:T(8,128)(2,1)} %bitcast.218, ...), custom_call_target="tpu_custom_call" | custom-call | flops 230000001024 | bytes 660000000 | tf_op jit(solution)/shard_map/pallas_call | solution.py:626
  191.9 9.6 %shard_map.395 = (f32[512,2048]{1,0:T(8,128)}, bf16[512,2048]{1,0:T(8,128)(2,1)}, bf16[2,1,2048,512]{3,2,1,0:T(8,128)(2,1)}) custom-call(s32[2]{0:T(128)} %copy-done.46, bf16[512,2048]{1,0:T(8,128)(2,1)} %get-tuple-element.158.before.refs_5_, bf16[512,1024]{1,0:T(8,128)(2,1)} %get-tuple-element.157.refs_0_, bf16[512,1024]{1,0:T(8,128)(2,1)} %bitcast.232, ...), custom_call_target="tpu_custom_call" | custom-call | flops 230000001024 | bytes 660000000 | tf_op jit(solution)/shard_map/pallas_call | solution.py:626
  201.5 4.6 shard_map.396
  206.1 27.4 %all-gather.9.cloned.1.call-done = bf16[4096,1024]{1,0:T(8,128)(2,1)} async-done(((bf16[128,1024]{1,0:T(8,128)(2,1)}), bf16[4096,1024]{1,0:T(8,128)(2,1)}) %all-gather.9.cloned.1.call-update) | async-done | bytes 8388624 | tf_op jit(solution)/shard_map/all_gather | solution.py:1179
  235.6 18.4 %shard_map.397 = (bf16[2,1,2048,512]{3,2,1,0:T(8,128)(2,1)}, f32[1,2048]{1,0:T(1,128)}, f32[512,1024]{1,0:T(8,128)}, f32[512,1024]{1,0:T(8,128)}) custom-call(s32[2]{0:T(128)} %copy-done.42, f32[8,128]{1,0:T(8,128)} %get-tuple-element.164.before, bf16[512,1024]{1,0:T(8,128)(2,1)} %get-tuple-element.157.refs_0_, bf16[512,1024]{1,0:T(8,128)(2,1)} %bitcast.233, ...), custom_call_target="tpu_custom_call" | custom-call | flops 230000001024 | bytes 660000000 | tf_op jit(solution)/shard_map/pallas_call | solution.py:626
  254.0 5.2 collective-permute-done.4.refs_3_.refs_2_.refs_29_.refs_27_
  260.4 3.5 shard_map.398
  266.0 19.4 %shard_map.399 = (bf16[2,1,2048,512]{3,2,1,0:T(8,128)(2,1)}, f32[1,2048]{1,0:T(1,128)}, f32[512,1024]{1,0:T(8,128)}, f32[512,1024]{1,0:T(8,128)}) custom-call(s32[2]{0:T(128)} %copy-done.46, f32[8,128]{1,0:T(8,128)} %get-tuple-element.171.before, bf16[512,1024]{1,0:T(8,128)(2,1)} %get-tuple-element.157.refs_0_, bf16[512,1024]{1,0:T(8,128)(2,1)} %bitcast.234, ...), custom_call_target="tpu_custom_call" | custom-call | flops 230000001024 | bytes 660000000 | tf_op jit(solution)/shard_map/pallas_call | solution.py:626
  285.5 5.1 shard_map.400
  290.6 10.6 %shard_map.401 = (bf16[512,1024]{1,0:T(8,128)(2,1)}, f32[512,1024]{1,0:T(8,128)}, bf16[512,2048]{1,0:T(8,128)(2,1)}, f32[8,1024]{1,0:T(8,128)}, f32[8,1024]{1,0:T(8,128)}, /*index=5*/f32[8,2048]{1,0:T(8,128)}) custom-call(f32[8,128]{1,0:T(8,128)} %get-tuple-element.178.before, f32[512,2176]{1,0:T(8,128)} %copy-done.4, ...), custom_call_target="tpu_custom_call" | custom-call | flops 1150000000 | bytes 3300000 | tf_op jit(solution)/shard_map/pallas_call | solution.py:544
  301.3 4.9 shard_map.402.before
  308.2 1.9 collective-permute-start.9
  311.8 2.3 copy.58
  314.1 4.9 shard_map.403.before
  319.0 17.3 %shard_map.404 = (bf16[2,3,1024,512]{3,2,1,0:T(8,128)(2,1)}, f32[1,1024]{1,0:T(1,128)}, f32[1,1024]{1,0:T(1,128)}, f32[512,1024]{1,0:T(8,128)}, f32[512,1024]{1,0:T(8,128)}, /*index=5*/f32[4,128,128]{2,1,0:T(8,128)}) custom-call(s32[2]{0:T(128)} %copy-done.42, bf16[2,1,512,1024]{3,2,1,0:T(8,128)(2,1)} %shard_map.403.before, ...), custom_call_target="tpu_custom_call" | custom-call | flops 1150000000 | bytes 3300000 | tf_op jit(solution)/shard_map/pallas_call | solution.py:626
  338.1 4.5 shard_map.405
  346.8 17.4 %shard_map.406 = (bf16[2,3,1024,512]{3,2,1,0:T(8,128)(2,1)}, f32[1,1024]{1,0:T(1,128)}, f32[1,1024]{1,0:T(1,128)}, f32[512,1024]{1,0:T(8,128)}, f32[512,1024]{1,0:T(8,128)}, /*index=5*/f32[4,128,128]{2,1,0:T(8,128)}) custom-call(s32[2]{0:T(128)} %copy-done.46, f32[8,128]{1,0:T(8,128)} %get-tuple-element.195.before, ...), custom_call_target="tpu_custom_call" | custom-call | flops 230000001024 | bytes 660000000 | tf_op jit(solution)/shard_map/pallas_call | solution.py:626
  364.2 4.7 collective-permute-done.16.refs_14_.refs_20_.refs_16_
  368.9 6.6 %shard_map.407 = (bf16[3,2,2,2,64,512]{5,4,3,2,1,0:T(8,128)(2,1)}, bf16[3,2,2,2,64,512]{5,4,3,2,1,0:T(8,128)(2,1)}, bf16[1,2,2,32,1024]{4,3,2,1,0:T(8,128)(2,1)}...) custom-call(s32[8]{0:T(128)} %stack.135.p, ...), custom_call_target="tpu_custom_call" | custom-call | flops 1150000000 | bytes 3300000 | tf_op jit(solution)/shard_map/pallas_call | solution.py:950
  380.7 18.3 %shard_map.408 = (f32[4096,128]{1,0:T(8,128)}, f32[2,16,8,128]{3,2,1,0:T(8,128)}, bf16[512,128]{1,0:T(8,128)(2,1)}, f32[8,128]{1,0:T(8,128)}) custom-call(f32[8,128]{1,0:T(8,128)} %get-tuple-element.203.before, s32[2,256]{1,0:T(2,128)} %copy-done.37, f32[4,128,128]{2,1,0:T(8,128)} %get-tuple-element.204.gp0_ref, f32[4,128,128]{2,1,0:T(8,128)} %get-tuple-element.205.gp1_ref, ...), custom_call_target="tpu_custom_call" | custom-call | flops 230000001024 | bytes 660000000 | tf_op jit(solution)/shard_map/pallas_call | solution.py:213
  399.1 2.2 collective-permute-done.18.refs_1_.refs_21_.refs_26_.refs_17_.refs_23_
  401.3 2.9 shard_map.409
  407.8 13.1 %collective-permute-done.21 = f32[2,17,8,128]{3,2,1,0:T(8,128)S(1)} collective-permute-done((f32[2,17,8,128]{3,2,1,0:T(8,128)S(1)}, f32[2,17,8,128]{3,2,1,0:T(8,128)S(1)}, u32[]{:S(2)}, u32[]{:S(2)}) %collective-permute-start.21) | collective-permute-done | bytes 139296 | tf_op jit(solution)/shard_map/ppermute | solution.py:52
  421.1 1.6 collective-permute-start.22
  424.2 2.0 collective-permute-done.22
  426.2 2.0 collective-permute-start.23
  428.3 1.6 collective-permute-start.42
  429.8 3.9 collective-permute-done.23
  435.2 5.8 shard_map.410
  443.2 1.9 collective-permute-start.27
  446.6 19.5 %shard_map.411 = (f32[256,1024]{1,0:T(8,128)}, f32[16,8,128]{2,1,0:T(8,128)}, f32[16,8,128]{2,1,0:T(8,128)}, f32[16,8,128]{2,1,0:T(8,128)}, f32[8,128]{1,0:T(8,1...) custom-call(f32[8,128]{1,0:T(8,128)} %get-tuple-element.217.before, s32[2,256]{1,0:T(2,128)} %copy-done.37, ...), custom_call_target="tpu_custom_call" | custom-call | flops 230000001024 | bytes 660000000 | tf_op jit(solution)/shard_map/pallas_call | solution.py:325
  466.1 5.8 shard_map.412
  474.0 2.4 collective-permute-start.31
  476.4 19.5 %shard_map.413 = (f32[256,1024]{1,0:T(8,128)}, f32[16,8,128]{2,1,0:T(8,128)}, f32[16,8,128]{2,1,0:T(8,128)}, f32[16,8,128]{2,1,0:T(8,128)}, f32[8,128]{1,0:T(8,1...) custom-call(f32[8,128]{1,0:T(8,128)} %get-tuple-element.228.before, s32[2,256]{1,0:T(2,128)} %copy-done.37, ...), custom_call_target="tpu_custom_call" | custom-call | flops 230000001024 | bytes 660000000 | tf_op jit(solution)/shard_map/pallas_call | solution.py:325
  500.0 8.8 %collective-permute-done.31.refs_5_.refs_10_.refs_11_ = bf16[3,2,64,1024]{3,2,1,0:T(8,128)(2,1)} collective-permute-done((bf16[3,2,64,1024]{3,2,1,0:T(8,128)(2,1)}, bf16[3,2,64,1024]{3,2,1,0:T(8,128)(2,1)}, u32[]{:S(2)}, u32[]{:S(2)}) %collective-permute-start.31) | collective-permute-done | bytes 786464 | tf_op jit(solution)/shard_map/ppermute | solution.py:52
  508.8 3.2 shard_map.414
  514.2 1.9 shard_map.415
  517.0 2.9 shard_map.420
  520.7 3.1 shard_map.419
  526.6 3.3 shard_map.416
  532.9 1.8 collective-permute-start.46
  534.7 3.5 collective-permute-done.46
  538.2 2.0 collective-permute-start.47
  540.2 1.9 collective-permute-done.47
  542.2 4.0 collective-permute-start.48
  547.5 1.6 collective-permute-done.48
  551.8 2.3 collective-permute-done.49
  555.3 2.9 collective-permute-start.36
  558.2 3.4 shard_map.417
  564.4 6.9 %shard_map.418 = (f32[1024,2176]{1,0:T(8,128)}, f32[8,128]{1,0:T(8,128)}) custom-call(s32[32]{0:T(128)} %fusion.40.place, bf16[1024,2048]{1,0:T(8,128)(2,1)} %bitcast.280, bf16[32,32,128]{2,1,0:T(8,128)(2,1)} %bitcast.276), custom_call_target="tpu_custom_call" | custom-call | flops 57500000256 | bytes 165000000 | tf_op jit(solution)/shard_map/pallas_call | solution.py:1096
  (313 shorter events, 80.2 us)
Async XLA Ops:
  7.2 147.9 %all-gather.7.cloned.1.call-start = ((), (), s32[]{:S(2)}) async-start(), calls=%async_computation | async-start | bytes 22167552 | tf_op jit(solution)/shard_map/all_gather | solution.py:1178
  12.4 221.1 %all-gather.9.cloned.1.call-start = ((), (), s32[]{:S(2)}) async-start(), calls=%async_computation.1 | async-start | bytes 8650752 | tf_op jit(solution)/shard_map/all_gather | solution.py:1179
  13.3 33.7 %copy-start.42 = (s32[2]{0:T(128)}, s32[2]{0:T(128)S(1)}, u32[]{:S(2)}) copy-start(s32[2]{0:T(128)S(1)} %get-tuple-element.150.piece) | copy-start | bytes 28
  13.3 33.7 %copy-start.46 = (s32[2]{0:T(128)}, s32[2]{0:T(128)S(1)}, u32[]{:S(2)}) copy-start(s32[2]{0:T(128)S(1)} %get-tuple-element.149.piece) | copy-start | bytes 28
  28.7 6.7 %collective-permute-start = (f32[2,17,8,128]{3,2,1,0:T(8,128)S(1)}, f32[2,17,8,128]{3,2,1,0:T(8,128)S(1)}, u32[]{:S(2)}, u32[]{:S(2)}) collective-permute-start(f32[2,17,8,128]{3,2,1,0:T(8,128)S(1)} %pad_maximum_fusion.5), channel_id=1, source_target_pairs={{0,1},{1,0},{2,3},{3,2},{4,5},{5,4},{6,7},{7,6},{8,9},{9,8},{10,11... | collective-permute-start | bytes 417800 | tf_op jit(solution)/shard_map/ppermute | solution.py:52
  33.4 531.0 %all-gather.11.cloned.1.call-start = ((), (), s32[]{:S(2)}) async-start(), calls=%async_computation.2 | async-start | bytes 4325376 | tf_op jit(solution)/shard_map/all_gather | solution.py:1355
  33.5 35.3 %copy-start.7 = (f32[16,8,128]{2,1,0:T(8,128)}, f32[16,8,128]{2,1,0:T(8,128)S(1)}, u32[]{:S(2)}) copy-start(f32[16,8,128]{2,1,0:T(8,128)S(1)} %get-tuple-element.296) | copy-start | bytes 196612
  33.5 35.3 %copy-start.9 = (f32[16,8,128]{2,1,0:T(8,128)}, f32[16,8,128]{2,1,0:T(8,128)S(1)}, u32[]{:S(2)}) copy-start(f32[16,8,128]{2,1,0:T(8,128)S(1)} %get-tuple-element.295) | copy-start | bytes 196612
  36.5 8.1 %collective-permute-start.1 = (f32[2,17,8,128]{3,2,1,0:T(8,128)S(1)}, f32[2,17,8,128]{3,2,1,0:T(8,128)S(1)}, u32[]{:S(2)}, u32[]{:S(2)}) collective-permute-start(f32[2,17,8,128]{3,2,1,0:T(8,128)S(1)} %pad_maximum_fusion.6), channel_id=1, source_target_pairs={{0,2},{1,3},{2,0},{3,1},{4,6},{5,7},{6,4},{7,5},{8,10},{9,11},{10,... | collective-permute-start | bytes 417800 | tf_op jit(solution)/shard_map/ppermute | solution.py:52
  44.7 11.0 %collective-permute-start.2 = (f32[2,17,8,128]{3,2,1,0:T(8,128)S(1)}, f32[2,17,8,128]{3,2,1,0:T(8,128)S(1)}, u32[]{:S(2)}, u32[]{:S(2)}) collective-permute-start(f32[2,17,8,128]{3,2,1,0:T(8,128)S(1)} %pad_maximum_fusion.7), channel_id=1, source_target_pairs={{0,4},{1,5},{2,6},{3,7},{4,0},{5,1},{6,2},{7,3},{8,12},{9,13},{10,... | collective-permute-start | bytes 417800 | tf_op jit(solution)/shard_map/ppermute | solution.py:52
  76.9 78.2 %copy-start.29 = (bf16[512,128]{1,0:T(8,128)(2,1)}, bf16[512,128]{1,0:T(8,128)(2,1)S(1)}, u32[]{:S(2)}) copy-start(bf16[512,128]{1,0:T(8,128)(2,1)S(1)} %get-tuple-element.264.key_ref) | copy-start | bytes 393220
  76.9 99.4 %copy-start.16 = (f32[512,128]{1,0:T(8,128)}, f32[512,128]{1,0:T(8,128)S(1)}, u32[]{:S(2)}) copy-start(f32[512,128]{1,0:T(8,128)S(1)} %get-tuple-element.265.shared_ref) | copy-start | bytes 786436
  77.0 78.1 %copy-start.30 = (bf16[512,128]{1,0:T(8,128)(2,1)}, bf16[512,128]{1,0:T(8,128)(2,1)S(1)}, u32[]{:S(2)}) copy-start(bf16[512,128]{1,0:T(8,128)(2,1)S(1)} %add_convert_fusion.2.query_ref) | copy-start | bytes 393220
  191.6 9.9 %collective-permute-start.3 = (bf16[2,1,2,2,2,2,128,512]{7,6,5,4,3,2,1,0:T(8,128)(2,1)}, bf16[2,1,2,2,2,2,128,512]{7,6,5,4,3,2,1,0:T(8,128)(2,1)}, u32[]{:S(2)}, u32[]{:S(2)}) collective-permute-start(bf16[2,1,2,2,2,2,128,512]{7,6,5,4,3,2,1,0:T(8,128)(2,1)} %bitcast.282), channel_id=1, source_target_pairs={{0,8},{1,9},{2,10},{3,11},{4,12},{5,13},{6,14},{7,15},{8,0},{9,1},... | collective-permute-start | bytes 12582920 | tf_op jit(solution)/shard_map/ppermute | solution.py:52
  233.6 25.6 %collective-permute-start.4 = (bf16[1,2,2,2,128,512]{5,4,3,2,1,0:T(8,128)(2,1)}, bf16[1,2,2,2,128,512]{5,4,3,2,1,0:T(8,128)(2,1)}, u32[]{:S(2)}, u32[]{:S(2)}) collective-permute-start(bf16[1,2,2,2,128,512]{5,4,3,2,1,0:T(8,128)(2,1)} %get-tuple-element.163), channel_id=1, source_target_pairs={{0,16},{1,17},{2,18},{3,19},{4,20},{5,21},{6,22},{7,23},{8,24},{9,... | collective-permute-start | bytes 3145736 | tf_op jit(solution)/shard_map/ppermute | solution.py:52
  235.0 25.4 %collective-permute-start.5 = (bf16[1,2,2,2,128,512]{5,4,3,2,1,0:T(8,128)(2,1)}, bf16[1,2,2,2,128,512]{5,4,3,2,1,0:T(8,128)(2,1)}, u32[]{:S(2)}, u32[]{:S(2)}) collective-permute-start(bf16[1,2,2,2,128,512]{5,4,3,2,1,0:T(8,128)(2,1)} %get-tuple-element.168), channel_id=1, source_target_pairs={{0,1},{1,0},{2,3},{3,2},{4,5},{5,4},{6,7},{7,6},{8,9},{9,8},{10,11... | collective-permute-start | bytes 3145736 | tf_op jit(solution)/shard_map/ppermute | solution.py:52
  254.0 31.5 %collective-permute-start.8 = (bf16[2,1,2,2,2,2,128,512]{7,6,5,4,3,2,1,0:T(8,128)(2,1)}, bf16[2,1,2,2,2,2,128,512]{7,6,5,4,3,2,1,0:T(8,128)(2,1)}, u32[]{:S(2)}, u32[]{:S(2)}) collective-permute-start(bf16[2,1,2,2,2,2,128,512]{7,6,5,4,3,2,1,0:T(8,128)(2,1)} %bitcast.281), channel_id=1, source_target_pairs={{0,8},{1,9},{2,10},{3,11},{4,12},{5,13},{6,14},{7,15},{8,0},{9,1},... | collective-permute-start | bytes 12582920 | tf_op jit(solution)/shard_map/ppermute | solution.py:52
  263.9 21.6 %collective-permute-start.6 = (bf16[1,2,2,128,512]{4,3,2,1,0:T(8,128)(2,1)}, bf16[1,2,2,128,512]{4,3,2,1,0:T(8,128)(2,1)}, u32[]{:S(2)}, u32[]{:S(2)}) collective-permute-start(bf16[1,2,2,128,512]{4,3,2,1,0:T(8,128)(2,1)} %get-tuple-element.169), channel_id=1, source_target_pairs={{0,1},{1,0},{2,3},{3,2},{4,5},{5,4},{6,7},{7,6},{8,9},{9,8},{10,11... | collective-permute-start | bytes 1572872 | tf_op jit(solution)/shard_map/ppermute | solution.py:52
  264.5 20.9 %collective-permute-start.7 = (bf16[1,2,2,128,512]{4,3,2,1,0:T(8,128)(2,1)}, bf16[1,2,2,128,512]{4,3,2,1,0:T(8,128)(2,1)}, u32[]{:S(2)}, u32[]{:S(2)}) collective-permute-start(bf16[1,2,2,128,512]{4,3,2,1,0:T(8,128)(2,1)} %get-tuple-element.170), channel_id=1, source_target_pairs={{0,16},{1,17},{2,18},{3,19},{4,20},{5,21},{6,22},{7,23},{8,24},{9,... | collective-permute-start | bytes 1572872 | tf_op jit(solution)/shard_map/ppermute | solution.py:52
  306.2 30.3 %collective-permute-start.12 = (bf16[2,1,2,2,2,2,32,1024]{7,6,5,4,3,2,1,0:T(8,128)(2,1)}, bf16[2,1,2,2,2,2,32,1024]{7,6,5,4,3,2,1,0:T(8,128)(2,1)S(1)}, u32[]{:S(2)}, u32[]{:S(2)}) collective-permute-start(bf16[2,1,2,2,2,2,32,1024]{7,6,5,4,3,2,1,0:T(8,128)(2,1)} %bitcast.229), channel_id=1, source_target_pairs={{0,8},{1,9},{2,10},{3,11},{4,12},{5,13},{6,14},{7,15},{8,0},{9,1},... | collective-permute-start | bytes 6291464 | tf_op jit(solution)/shard_map/ppermute | solution.py:52
  306.2 30.2 %collective-permute-start.10 = (bf16[1,2,2,2,128,512]{5,4,3,2,1,0:T(8,128)(2,1)}, bf16[1,2,2,2,128,512]{5,4,3,2,1,0:T(8,128)(2,1)S(1)}, u32[]{:S(2)}, u32[]{:S(2)}) collective-permute-start(bf16[1,2,2,2,128,512]{5,4,3,2,1,0:T(8,128)(2,1)} %get-tuple-element.193), channel_id=1, source_target_pairs={{0,16},{1,17},{2,18},{3,19},{4,20},{5,21},{6,22},{7,23},{8,24},{9,... | collective-permute-start | bytes 3145736 | tf_op jit(solution)/shard_map/ppermute | solution.py:52
  306.7 29.7 %collective-permute-start.11 = (bf16[1,2,2,2,128,512]{5,4,3,2,1,0:T(8,128)(2,1)}, bf16[1,2,2,2,128,512]{5,4,3,2,1,0:T(8,128)(2,1)}, u32[]{:S(2)}, u32[]{:S(2)}) collective-permute-start(bf16[1,2,2,2,128,512]{5,4,3,2,1,0:T(8,128)(2,1)} %get-tuple-element.194), channel_id=1, source_target_pairs={{0,1},{1,0},{2,3},{3,2},{4,5},{5,4},{6,7},{7,6},{8,9},{9,8},{10,11... | collective-permute-start | bytes 3145736 | tf_op jit(solution)/shard_map/ppermute | solution.py:52
  308.2 28.2 %collective-permute-start.9 = (bf16[1,2,128,1024]{3,2,1,0:T(8,128)(2,1)}, bf16[1,2,128,1024]{3,2,1,0:T(8,128)(2,1)}, u32[]{:S(2)}, u32[]{:S(2)}) collective-permute-start(bf16[1,2,128,1024]{3,2,1,0:T(8,128)(2,1)} %get-tuple-element.192), channel_id=1, source_target_pairs={{0,4},{1,5},{2,6},{3,7},{4,0},{5,1},{6,2},{7,3},{8,12},{9,13},{10,... | collective-permute-start | bytes 1572872 | tf_op jit(solution)/shard_map/ppermute | solution.py:52
  336.3 32.6 %collective-permute-start.13 = (bf16[2,3,2,2,2,2,64,512]{7,6,5,4,3,2,1,0:T(8,128)(2,1)}, bf16[2,3,2,2,2,2,64,512]{7,6,5,4,3,2,1,0:T(8,128)(2,1)}, u32[]{:S(2)}, u32[]{:S(2)}) collective-permute-start(bf16[2,3,2,2,2,2,64,512]{7,6,5,4,3,2,1,0:T(8,128)(2,1)} %bitcast.279), channel_id=1, source_target_pairs={{0,8},{1,9},{2,10},{3,11},{4,12},{5,13},{6,14},{7,15},{8,0},{9,1},... | collective-permute-start | bytes 18874376 | tf_op jit(solution)/shard_map/ppermute | solution.py:52
  342.7 21.5 %collective-permute-start.14 = (bf16[1,2,2,2,32,1024]{5,4,3,2,1,0:T(8,128)(2,1)}, bf16[1,2,2,2,32,1024]{5,4,3,2,1,0:T(8,128)(2,1)}, u32[]{:S(2)}, u32[]{:S(2)}) collective-permute-start(bf16[1,2,2,2,32,1024]{5,4,3,2,1,0:T(8,128)(2,1)} %get-tuple-element.199), channel_id=1, source_target_pairs={{0,16},{1,17},{2,18},{3,19},{4,20},{5,21},{6,22},{7,23},{8,24},{9,... | collective-permute-start | bytes 1572872 | tf_op jit(solution)/shard_map/ppermute | solution.py:52
  343.3 20.8 %collective-permute-start.15 = (bf16[1,2,2,2,32,1024]{5,4,3,2,1,0:T(8,128)(2,1)}, bf16[1,2,2,2,32,1024]{5,4,3,2,1,0:T(8,128)(2,1)}, u32[]{:S(2)}, u32[]{:S(2)}) collective-permute-start(bf16[1,2,2,2,32,1024]{5,4,3,2,1,0:T(8,128)(2,1)} %get-tuple-element.200), channel_id=1, source_target_pairs={{0,1},{1,0},{2,3},{3,2},{4,5},{5,4},{6,7},{7,6},{8,9},{9,8},{10,11... | collective-permute-start | bytes 1572872 | tf_op jit(solution)/shard_map/ppermute | solution.py:52
  344.8 24.1 %collective-permute-start.16 = (bf16[1,2,2,128,512]{4,3,2,1,0:T(8,128)(2,1)}, bf16[1,2,2,128,512]{4,3,2,1,0:T(8,128)(2,1)}, u32[]{:S(2)}, u32[]{:S(2)}) collective-permute-start(bf16[1,2,2,128,512]{4,3,2,1,0:T(8,128)(2,1)} %get-tuple-element.201), channel_id=1, source_target_pairs={{0,1},{1,0},{2,3},{3,2},{4,5},{5,4},{6,7},{7,6},{8,9},{9,8},{10,11... | collective-permute-start | bytes 1572872 | tf_op jit(solution)/shard_map/ppermute | solution.py:52
  345.4 23.6 %collective-permute-start.17 = (bf16[1,2,2,128,512]{4,3,2,1,0:T(8,128)(2,1)}, bf16[1,2,2,128,512]{4,3,2,1,0:T(8,128)(2,1)}, u32[]{:S(2)}, u32[]{:S(2)}) collective-permute-start(bf16[1,2,2,128,512]{4,3,2,1,0:T(8,128)(2,1)} %get-tuple-element.202), channel_id=1, source_target_pairs={{0,16},{1,17},{2,18},{3,19},{4,20},{5,21},{6,22},{7,23},{8,24},{9,... | collective-permute-start | bytes 1572872 | tf_op jit(solution)/shard_map/ppermute | solution.py:52
  375.6 25.7 %collective-permute-start.18 = (bf16[1,2,128,1024]{3,2,1,0:T(8,128)(2,1)}, bf16[1,2,128,1024]{3,2,1,0:T(8,128)(2,1)}, u32[]{:S(2)}, u32[]{:S(2)}) collective-permute-start(bf16[1,2,128,1024]{3,2,1,0:T(8,128)(2,1)} %get-tuple-element.210), channel_id=1, source_target_pairs={{0,4},{1,5},{2,6},{3,7},{4,0},{5,1},{6,2},{7,3},{8,12},{9,13},{10,... | collective-permute-start | bytes 1572872 | tf_op jit(solution)/shard_map/ppermute | solution.py:52
  376.7 22.4 %collective-permute-start.19 = (bf16[1,2,2,32,1024]{4,3,2,1,0:T(8,128)(2,1)}, bf16[1,2,2,32,1024]{4,3,2,1,0:T(8,128)(2,1)}, u32[]{:S(2)}, u32[]{:S(2)}) collective-permute-start(bf16[1,2,2,32,1024]{4,3,2,1,0:T(8,128)(2,1)} %get-tuple-element.211), channel_id=1, source_target_pairs={{0,1},{1,0},{2,3},{3,2},{4,5},{5,4},{6,7},{7,6},{8,9},{9,8},{10,11... | collective-permute-start | bytes 786440 | tf_op jit(solution)/shard_map/ppermute | solution.py:52
  378.1 20.9 %collective-permute-start.20 = (bf16[1,2,2,32,1024]{4,3,2,1,0:T(8,128)(2,1)}, bf16[1,2,2,32,1024]{4,3,2,1,0:T(8,128)(2,1)}, u32[]{:S(2)}, u32[]{:S(2)}) collective-permute-start(bf16[1,2,2,32,1024]{4,3,2,1,0:T(8,128)(2,1)} %get-tuple-element.212), channel_id=1, source_target_pairs={{0,16},{1,17},{2,18},{3,19},{4,20},{5,21},{6,22},{7,23},{8,24},{9,... | collective-permute-start | bytes 786440 | tf_op jit(solution)/shard_map/ppermute | solution.py:52
  378.7 55.8 %collective-permute-start.24 = (bf16[3,2,2,2,64,512]{5,4,3,2,1,0:T(8,128)(2,1)}, bf16[3,2,2,2,64,512]{5,4,3,2,1,0:T(8,128)(2,1)}, u32[]{:S(2)}, u32[]{:S(2)}) collective-permute-start(bf16[3,2,2,2,64,512]{5,4,3,2,1,0:T(8,128)(2,1)} %get-tuple-element.214), channel_id=1, source_target_pairs={{0,16},{1,17},{2,18},{3,19},{4,20},{5,21},{6,22},{7,23},{8,24},{9,... | collective-permute-start | bytes 4718600 | tf_op jit(solution)/shard_map/ppermute | solution.py:52
  380.1 54.3 %collective-permute-start.25 = (bf16[3,2,2,2,64,512]{5,4,3,2,1,0:T(8,128)(2,1)}, bf16[3,2,2,2,64,512]{5,4,3,2,1,0:T(8,128)(2,1)}, u32[]{:S(2)}, u32[]{:S(2)}) collective-permute-start(bf16[3,2,2,2,64,512]{5,4,3,2,1,0:T(8,128)(2,1)} %get-tuple-element.215), channel_id=1, source_target_pairs={{0,1},{1,0},{2,3},{3,2},{4,5},{5,4},{6,7},{7,6},{8,9},{9,8},{10,11... | collective-permute-start | bytes 4718600 | tf_op jit(solution)/shard_map/ppermute | solution.py:52
  405.7 15.2 %collective-permute-start.21 = (f32[2,17,8,128]{3,2,1,0:T(8,128)S(1)}, f32[2,17,8,128]{3,2,1,0:T(8,128)S(1)}, u32[]{:S(2)}, u32[]{:S(2)}) collective-permute-start(f32[2,17,8,128]{3,2,1,0:T(8,128)S(1)} %pad_maximum_fusion.4), channel_id=1, source_target_pairs={{0,1},{1,0},{2,3},{3,2},{4,5},{5,4},{6,7},{7,6},{8,9},{9,8},{10,11... | collective-permute-start | bytes 417800 | tf_op jit(solution)/shard_map/ppermute | solution.py:52
  407.2 27.3 %collective-permute-start.26 = (bf16[1,2,32,2048]{3,2,1,0:T(8,128)(2,1)}, bf16[1,2,32,2048]{3,2,1,0:T(8,128)(2,1)S(1)}, u32[]{:S(2)}, u32[]{:S(2)}) collective-permute-start(bf16[1,2,32,2048]{3,2,1,0:T(8,128)(2,1)} %get-tuple-element.216), channel_id=1, source_target_pairs={{0,4},{1,5},{2,6},{3,7},{4,0},{5,1},{6,2},{7,3},{8,12},{9,13},{10,... | collective-permute-start | bytes 786440 | tf_op jit(solution)/shard_map/ppermute | solution.py:52
  407.7 14.9 %collective-permute-start.40 = (bf16[2,1,2,2,2,32,128]{6,5,4,3,2,1,0:T(8,128)(2,1)S(1)}, bf16[2,1,2,2,2,32,128]{6,5,4,3,2,1,0:T(8,128)(2,1)S(1)}, u32[]{:S(2)}, u32[]{:S(2)}) collective-permute-start(bf16[2,1,2,2,2,32,128]{6,5,4,3,2,1,0:T(8,128)(2,1)S(1)} %dynamic-slice_convert_fusion), channel_id=1, source_target_pairs={{0,8},{1,9},{2,10},{3,11},{4,12},{5,13},{6,14},{7,15},{8,0},{9,1},... | collective-permute-start | bytes 393224 | tf_op jit(solution)/shard_map/ppermute | solution.py:52
  421.1 5.1 collective-permute-start.22
  422.7 5.5 collective-permute-start.41
  426.2 7.5 %collective-permute-start.23 = (f32[2,17,8,128]{3,2,1,0:T(8,128)S(1)}, f32[2,17,8,128]{3,2,1,0:T(8,128)S(1)}, u32[]{:S(2)}, u32[]{:S(2)}) collective-permute-start(f32[2,17,8,128]{3,2,1,0:T(8,128)S(1)} %pad_maximum_fusion.9), channel_id=1, source_target_pairs={{0,4},{1,5},{2,6},{3,7},{4,0},{5,1},{6,2},{7,3},{8,12},{9,13},{10,... | collective-permute-start | bytes 417800 | tf_op jit(solution)/shard_map/ppermute | solution.py:52
  428.3 16.9 %collective-permute-start.42 = (bf16[1,1,2,2,1,32,128]{6,5,4,3,2,1,0:T(8,128)(2,1)S(1)}, bf16[1,1,2,2,1,32,128]{6,5,4,3,2,1,0:T(8,128)(2,1)S(1)}, u32[]{:S(2)}, u32[]{:S(2)}) collective-permute-start(bf16[1,1,2,2,1,32,128]{6,5,4,3,2,1,0:T(8,128)(2,1)S(1)} %dynamic-slice_convert_fusion.2), channel_id=1, source_target_pairs={{0,1},{1,0},{2,3},{3,2},{4,5},{5,4},{6,7},{7,6},{8,9},{9,8},{10,11... | collective-permute-start | bytes 98312 | tf_op jit(solution)/shard_map/ppermute | solution.py:52
  441.0 25.1 %collective-permute-start.29 = (bf16[3,2,2,64,512]{4,3,2,1,0:T(8,128)(2,1)}, bf16[3,2,2,64,512]{4,3,2,1,0:T(8,128)(2,1)}, u32[]{:S(2)}, u32[]{:S(2)}) collective-permute-start(bf16[3,2,2,64,512]{4,3,2,1,0:T(8,128)(2,1)} %get-tuple-element.226), channel_id=1, source_target_pairs={{0,1},{1,0},{2,3},{3,2},{4,5},{5,4},{6,7},{7,6},{8,9},{9,8},{10,11... | collective-permute-start | bytes 2359304 | tf_op jit(solution)/shard_map/ppermute | solution.py:52
  442.5 23.6 %collective-permute-start.30 = (bf16[3,2,2,64,512]{4,3,2,1,0:T(8,128)(2,1)}, bf16[3,2,2,64,512]{4,3,2,1,0:T(8,128)(2,1)}, u32[]{:S(2)}, u32[]{:S(2)}) collective-permute-start(bf16[3,2,2,64,512]{4,3,2,1,0:T(8,128)(2,1)} %get-tuple-element.227), channel_id=1, source_target_pairs={{0,16},{1,17},{2,18},{3,19},{4,20},{5,21},{6,22},{7,23},{8,24},{9,... | collective-permute-start | bytes 2359304 | tf_op jit(solution)/shard_map/ppermute | solution.py:52
  443.1 23.0 %collective-permute-start.28 = (bf16[2,1,128,1024]{3,2,1,0:T(8,128)(2,1)}, bf16[2,1,128,1024]{3,2,1,0:T(8,128)(2,1)}, u32[]{:S(2)}, u32[]{:S(2)}) collective-permute-start(bf16[2,1,128,1024]{3,2,1,0:T(8,128)(2,1)} %get-tuple-element.225), channel_id=1, source_target_pairs={{0,2},{1,3},{2,0},{3,1},{4,6},{5,7},{6,4},{7,5},{8,10},{9,11},{10,... | collective-permute-start | bytes 1572872 | tf_op jit(solution)/shard_map/ppermute | solution.py:52
  443.2 22.9 %collective-permute-start.27 = (bf16[1,32,2048]{2,1,0:T(8,128)(2,1)}, bf16[1,32,2048]{2,1,0:T(8,128)(2,1)}, u32[]{:S(2)}, u32[]{:S(2)}) collective-permute-start(bf16[1,32,2048]{2,1,0:T(8,128)(2,1)} %get-tuple-element.224), channel_id=1, source_target_pairs={{0,2},{1,3},{2,0},{3,1},{4,6},{5,7},{6,4},{7,5},{8,10},{9,11},{10,... | collective-permute-start | bytes 393224 | tf_op jit(solution)/shard_map/ppermute | solution.py:52
  446.4 49.5 %collective-permute-start.43 = (bf16[1,1,2,1,1,32,128]{6,5,4,3,2,1,0:T(8,128)(2,1)}, bf16[1,1,2,1,1,32,128]{6,5,4,3,2,1,0:T(8,128)(2,1)}, u32[]{:S(2)}, u32[]{:S(2)}) collective-permute-start(bf16[1,1,2,1,1,32,128]{6,5,4,3,2,1,0:T(8,128)(2,1)} %dynamic-slice_convert_fusion.3), channel_id=1, source_target_pairs={{0,2},{1,3},{2,0},{3,1},{4,6},{5,7},{6,4},{7,5},{8,10},{9,11},{10,... | collective-permute-start | bytes 49160 | tf_op jit(solution)/shard_map/ppermute | solution.py:52
  471.9 25.5 %collective-permute-start.52 = (bf16[1,128,1024]{2,1,0:T(8,128)(2,1)}, bf16[1,128,1024]{2,1,0:T(8,128)(2,1)}, u32[]{:S(2)}, u32[]{:S(2)}) collective-permute-start(bf16[1,128,1024]{2,1,0:T(8,128)(2,1)} %get-tuple-element.260.own_ref), channel_id=1, source_target_pairs={{0,16},{1,17},{2,18},{3,19},{4,20},{5,21},{6,22},{7,23},{8,24},{9,... | collective-permute-start | bytes 786440 | tf_op jit(solution)/shard_map/ppermute | solution.py:52
  473.4 25.1 %collective-permute-start.50 = (bf16[1,128,1024]{2,1,0:T(8,128)(2,1)}, bf16[1,128,1024]{2,1,0:T(8,128)(2,1)}, u32[]{:S(2)}, u32[]{:S(2)}) collective-permute-start(bf16[1,128,1024]{2,1,0:T(8,128)(2,1)} %get-tuple-element.258.own_ref), channel_id=1, source_target_pairs={{0,16},{1,17},{2,18},{3,19},{4,20},{5,21},{6,22},{7,23},{8,24},{9,... | collective-permute-start | bytes 786440 | tf_op jit(solution)/shard_map/ppermute | solution.py:52
  474.0 34.8 %collective-permute-start.31 = (bf16[3,2,64,1024]{3,2,1,0:T(8,128)(2,1)}, bf16[3,2,64,1024]{3,2,1,0:T(8,128)(2,1)}, u32[]{:S(2)}, u32[]{:S(2)}) collective-permute-start(bf16[3,2,64,1024]{3,2,1,0:T(8,128)(2,1)} %get-tuple-element.230), channel_id=1, source_target_pairs={{0,4},{1,5},{2,6},{3,7},{4,0},{5,1},{6,2},{7,3},{8,12},{9,13},{10,... | collective-permute-start | bytes 2359304 | tf_op jit(solution)/shard_map/ppermute | solution.py:52
  496.7 33.3 %collective-permute-start.44 = (bf16[1,1,1,1,1,32,128]{6,5,4,3,2,1,0:T(8,128)(2,1)S(1)}, bf16[1,1,1,1,1,32,128]{6,5,4,3,2,1,0:T(8,128)(2,1)S(1)}, u32[]{:S(2)}, u32[]{:S(2)}) collective-permute-start(bf16[1,1,1,1,1,32,128]{6,5,4,3,2,1,0:T(8,128)(2,1)S(1)} %dynamic-slice_convert_fusion.4), channel_id=1, source_target_pairs={{0,4},{1,5},{2,6},{3,7},{4,0},{5,1},{6,2},{7,3},{8,12},{9,13},{10,... | collective-permute-start | bytes 24584 | tf_op jit(solution)/shard_map/ppermute | solution.py:52
  498.4 17.8 %collective-permute-start.53 = (bf16[2,1,128,1024]{3,2,1,0:T(8,128)(2,1)S(1)}, bf16[2,1,128,1024]{3,2,1,0:T(8,128)(2,1)S(1)}, u32[]{:S(2)}, u32[]{:S(2)}) collective-permute-start(bf16[2,1,128,1024]{3,2,1,0:T(8,128)(2,1)S(1)} %pad_maximum_fusion.3), channel_id=1, source_target_pairs={{0,8},{1,9},{2,10},{3,11},{4,12},{5,13},{6,14},{7,15},{8,0},{9,1},... | collective-permute-start | bytes 1572872 | tf_op jit(solution)/shard_map/ppermute | solution.py:52
  499.5 20.5 %collective-permute-start.51 = (bf16[2,1,128,1024]{3,2,1,0:T(8,128)(2,1)S(1)}, bf16[2,1,128,1024]{3,2,1,0:T(8,128)(2,1)S(1)}, u32[]{:S(2)}, u32[]{:S(2)}) collective-permute-start(bf16[2,1,128,1024]{3,2,1,0:T(8,128)(2,1)S(1)} %pad_maximum_fusion.2), channel_id=1, source_target_pairs={{0,8},{1,9},{2,10},{3,11},{4,12},{5,13},{6,14},{7,15},{8,0},{9,1},... | collective-permute-start | bytes 1572872 | tf_op jit(solution)/shard_map/ppermute | solution.py:52
  512.0 13.9 %collective-permute-start.33 = (bf16[3,64,1024]{2,1,0:T(8,128)(2,1)}, bf16[3,64,1024]{2,1,0:T(8,128)(2,1)S(1)}, u32[]{:S(2)}, u32[]{:S(2)}) collective-permute-start(bf16[3,64,1024]{2,1,0:T(8,128)(2,1)} %get-tuple-element.247), channel_id=1, source_target_pairs={{0,2},{1,3},{2,0},{3,1},{4,6},{5,7},{6,4},{7,5},{8,10},{9,11},{10,... | collective-permute-start | bytes 1179656 | tf_op jit(solution)/shard_map/ppermute | solution.py:52
  516.2 15.7 %collective-permute-start.32 = (bf16[512,128]{1,0:T(8,128)(2,1)}, bf16[512,128]{1,0:T(8,128)(2,1)S(1)}, u32[]{:S(2)}, u32[]{:S(2)}) collective-permute-start(bf16[512,128]{1,0:T(8,128)(2,1)} %shard_map.415), channel_id=1, source_target_pairs={{0,8},{1,9},{2,10},{3,11},{4,12},{5,13},{6,14},{7,15},{8,0},{9,1},... | collective-permute-start | bytes 393224 | tf_op jit(solution)/shard_map/ppermute | solution.py:52
  530.7 2.2 collective-permute-start.45
  531.2 15.0 %collective-permute-start.37 = (bf16[3,64,1024]{2,1,0:T(8,128)(2,1)}, bf16[3,64,1024]{2,1,0:T(8,128)(2,1)S(1)}, u32[]{:S(2)}, u32[]{:S(2)}) collective-permute-start(bf16[3,64,1024]{2,1,0:T(8,128)(2,1)} %get-tuple-element.249.own_ref), channel_id=1, source_target_pairs={{0,16},{1,17},{2,18},{3,19},{4,20},{5,21},{6,22},{7,23},{8,24},{9,... | collective-permute-start | bytes 1179656 | tf_op jit(solution)/shard_map/ppermute | solution.py:52
  532.6 17.6 %collective-permute-start.34 = (bf16[512,128]{1,0:T(8,128)(2,1)S(1)}, bf16[512,128]{1,0:T(8,128)(2,1)S(1)}, u32[]{:S(2)}, u32[]{:S(2)}) collective-permute-start(bf16[512,128]{1,0:T(8,128)(2,1)S(1)} %fusion.7), channel_id=1, source_target_pairs={{0,1},{1,0},{2,3},{3,2},{4,5},{5,4},{6,7},{7,6},{8,9},{9,8},{10,11... | collective-permute-start | bytes 393224 | tf_op jit(solution)/shard_map/ppermute | solution.py:52
  532.9 5.4 collective-permute-start.46
  538.2 3.9 collective-permute-start.47
  542.2 6.9 %collective-permute-start.48 = (bf16[256,128]{1,0:T(8,128)(2,1)S(1)}, bf16[256,128]{1,0:T(8,128)(2,1)S(1)}, u32[]{:S(2)}, u32[]{:S(2)}) collective-permute-start(bf16[256,128]{1,0:T(8,128)(2,1)S(1)} %pad_maximum_fusion.10), channel_id=1, source_target_pairs={{0,4},{1,5},{2,6},{3,7},{4,0},{5,1},{6,2},{7,3},{8,12},{9,13},{10,... | collective-permute-start | bytes 196616 | tf_op jit(solution)/shard_map/ppermute | solution.py:52
  547.4 10.8 %collective-permute-start.38 = (bf16[2,3,64,1024]{3,2,1,0:T(8,128)(2,1)S(1)}, bf16[2,3,64,1024]{3,2,1,0:T(8,128)(2,1)}, u32[]{:S(2)}, u32[]{:S(2)}) collective-permute-start(bf16[2,3,64,1024]{3,2,1,0:T(8,128)(2,1)S(1)} %pad_maximum_fusion.1), channel_id=1, source_target_pairs={{0,8},{1,9},{2,10},{3,11},{4,12},{5,13},{6,14},{7,15},{8,0},{9,1},... | collective-permute-start | bytes 2359304 | tf_op jit(solution)/shard_map/ppermute | solution.py:52
  549.1 5.0 collective-permute-start.49
  550.2 5.0 collective-permute-start.35
  555.3 7.3 %collective-permute-start.36 = (bf16[512,128]{1,0:T(8,128)(2,1)S(1)}, bf16[512,128]{1,0:T(8,128)(2,1)S(1)}, u32[]{:S(2)}, u32[]{:S(2)}) collective-permute-start(bf16[512,128]{1,0:T(8,128)(2,1)S(1)} %add_convert_fusion), channel_id=1, source_target_pairs={{0,4},{1,5},{2,6},{3,7},{4,0},{5,1},{6,2},{7,3},{8,12},{9,13},{10,... | collective-permute-start | bytes 393224 | tf_op jit(solution)/shard_map/ppermute | solution.py:52
  563.4 8.0 %collective-permute-start.39 = (bf16[512,128]{1,0:T(8,128)(2,1)S(1)}, bf16[512,128]{1,0:T(8,128)(2,1)S(1)}, u32[]{:S(2)}, u32[]{:S(2)}) collective-permute-start(bf16[512,128]{1,0:T(8,128)(2,1)S(1)} %fusion.6), channel_id=1, source_target_pairs={{0,16},{1,17},{2,18},{3,19},{4,20},{5,21},{6,22},{7,23},{8,24},{9,... | collective-permute-start | bytes 393224 | tf_op jit(solution)/shard_map/ppermute | solution.py:52
  (47 other events, 434.9 us)
Sparse Core Ops, SparseCore 0:
  12.5 142.5 all-gather.6
  158.1 75.4 all-gather.8
  476.5 66.4 all-gather.10

commit v5 on v4

--- a/solution.py
+++ b/solution.py
@@ -460,7 +460,7 @@
     add_to(ffn_out, dot_nn(grad, wi), sum_f_ref)
 
 
-UNITS = 1024
+UNITS = 512
 
 
 def cost(micros):

time: 596 us -> 591 us (level); the launches traced: 585 us -> 587 us
  transfers between devices with their start and end apart: 57 -> 57, of which waited for: 19 -> 19; matrix products, arithmetic and copies ran while one was open for 7% -> 7% of each run, Pallas kernels for 43% -> 44%
where the time goes in v5:
time: 591 us; the launch traced here: 587 us
  Pallas kernels  284 us (48%)
  waiting for transfers between devices  170 us (29%)
  starting transfers between devices  58.5 us (10%)
  local copies, waits for them, and re-layouts  28 us (5%)
  other arithmetic  23.9 us (4%)
  between operations  15.3 us (3%)
  matrix products  6.78 us (1%)
    pallas_call x7, Pallas kernels, blocked(): pl.pallas_call(body, grid_spec=pltpu.PrefetchScalarGridSpec(num_scalar_pr...  112 us
    all_gather x1, waiting for transfers between devices, local(): gathered = lax.all_gather(seed, AXES, axis=0)  76.8 us
    ppermute x54, waiting for transfers between devices, swap(): return lax.ppermute(value, AXES, [(i, i ^ mask) for i in range(self.count)])  67.2 us
    ppermute x54, starting transfers between devices, swap(): return lax.ppermute(value, AXES, [(i, i ^ mask) for i in range(self.count)])  58.4 us
    pallas_call x10, Pallas kernels, run_point(): pl.pallas_call(body, grid_spec=pltpu.PrefetchScalarGridSpec(num_scalar_pr...  46.3 us
    pallas_call x2, Pallas kernels, run_back(): pl.pallas_call(partial(back_kernel, m), grid=(1,), in_specs=[pl.BlockSpec...  39 us
    all_gather x1, waiting for transfers between devices, local(): gathered_out = lax.all_gather(own(w_out, half_f, 0), AXES, axis=0)  26.1 us
    pallas_call x2, Pallas kernels, call(): pl.pallas_call(kernel, out_shape=outs, in_specs=[pl.BlockSpec(memory_spac...  24.4 us
  transfers between devices with their start and end apart: 57, of which 19 were waited for; matrix products, arithmetic and copies ran while one was open for 7% of the time, Pallas kernels for 44%

profile of v5, /device:TPU:0, one launch (start us, length us, event | category | flops | bytes accessed | tf_op | source)
XLA Modules:
  0.0 586.6 jit_solution(1208056485272959377)
XLA Ops:
  15.4 11.7 %shard_map.390 = (f32[4096,128]{1,0:T(8,128)}, bf16[512,1024]{1,0:T(8,128)(2,1)}, f32[2,16,8,128]{3,2,1,0:T(8,128)}) custom-call(s32[2,256]{1,0:T(2,128)} %copy-done.37, bf16[512,1024]{1,0:T(8,128)(2,1)} %bitcast.236, f32[1,1024]{1,0:T(1,128)} %bitcast.284, f32[16,8,128]{2,1,0:T(8,128)} %bitcast.244, f32[16,8,128]{2,1,0:T(8,128)} %bitcast.261), custom_call_target="tpu_custom_call" | custom-call | flops 13799999488 | bytes 39600000 | tf_op jit(solution)/shard_map/pallas_call | solution.py:710
  28.7 3.0 collective-permute-start
  31.7 1.7 constant_dynamic-slice_fusion
  33.5 1.9 collective-permute-done
  36.5 1.9 collective-permute-start.1
  38.4 6.2 %collective-permute-done.1 = f32[2,17,8,128]{3,2,1,0:T(8,128)S(1)} collective-permute-done((f32[2,17,8,128]{3,2,1,0:T(8,128)S(1)}, f32[2,17,8,128]{3,2,1,0:T(8,128)S(1)}, u32[]{:S(2)}, u32[]{:S(2)}) %collective-permute-start.1) | collective-permute-done | bytes 139296 | tf_op jit(solution)/shard_map/ppermute | solution.py:52
  44.7 2.3 collective-permute-start.2
  48.6 7.1 %collective-permute-done.2 = f32[2,17,8,128]{3,2,1,0:T(8,128)S(1)} collective-permute-done((f32[2,17,8,128]{3,2,1,0:T(8,128)S(1)}, f32[2,17,8,128]{3,2,1,0:T(8,128)S(1)}, u32[]{:S(2)}, u32[]{:S(2)}) %collective-permute-start.2) | collective-permute-done | bytes 139296 | tf_op jit(solution)/shard_map/ppermute | solution.py:52
  56.3 12.7 %shard_map.391 = (f32[512,1024]{1,0:T(8,128)}, bf16[512,1024]{1,0:T(8,128)(2,1)}) custom-call(s32[2,256]{1,0:T(2,128)} %copy-done.37, f32[4096,128]{1,0:T(8,128)} %get-tuple-element.152.normed_ref, f32[2,16,8,128]{3,2,1,0:T(8,128)} %add_select_fusion.2.start_ref, f32[16,8,128]{2,1,0:T(8,128)} %bitcast.245, f32[16,8,128]{2,1,0:T(8,128)} %bitcast.262, ...), custom_call_target="tpu_custom_call" | custom-call | flops 13799999488 | bytes 39600000 | tf_op jit(solution)/shard_map/pallas_call | solution.py:710
  69.1 5.2 convolution_add_fusion.gate_ref
  74.3 2.1 copy-done.4
  78.3 76.8 %all-gather.7.cloned.1.call-done = bf16[10496,1024]{1,0:T(8,128)(2,1)} async-done(((bf16[328,1024]{1,0:T(8,128)(2,1)}), bf16[10496,1024]{1,0:T(8,128)(2,1)}) %all-gather.7.cloned.1.call-update) | async-done | bytes 21495824 | tf_op jit(solution)/shard_map/all_gather | solution.py:1178
  159.2 17.2 %shard_map.392 = (f32[512,2048]{1,0:T(8,128)}, f32[512,2048]{1,0:T(8,128)}, f32[512,2048]{1,0:T(8,128)}, bf16[512,2048]{1,0:T(8,128)(2,1)}, f32[512,1024]{1,0:T(8,128)}) custom-call(s32[4]{0:T(128)} %pad_add_fusion.4.piece, f32[1,2048]{1,0:T(1,128)} %pad_maximum_fusion.19.before.refs_6_, bf16[512,1024]{1,0:T(8,128)(2,1)} %get-tuple-element.155.refs_0_.refs_1_, ...), custom_call_target="tpu_custom_call" | custom-call | flops 230000001024 | bytes 660000000 | tf_op jit(solution)/shard_map/pallas_call | solution.py:626
  176.3 5.7 shard_map.393
  182.1 10.0 %shard_map.394 = (f32[512,2048]{1,0:T(8,128)}, bf16[512,2048]{1,0:T(8,128)(2,1)}, bf16[2,1,2048,512]{3,2,1,0:T(8,128)(2,1)}) custom-call(s32[2]{0:T(128)} %copy-done.42, f32[1,2048]{1,0:T(1,128)} %bitcast.271, bf16[512,1024]{1,0:T(8,128)(2,1)} %get-tuple-element.157.refs_0_, bf16[512,1024]{1,0:T(8,128)(2,1)} %bitcast.231, bf16[32,328,1024]{2,1,0:T(8,128)(2,1)} %bitcast.218, ...), custom_call_target="tpu_custom_call" | custom-call | flops 230000001024 | bytes 660000000 | tf_op jit(solution)/shard_map/pallas_call | solution.py:626
  192.3 9.9 %shard_map.395 = (f32[512,2048]{1,0:T(8,128)}, bf16[512,2048]{1,0:T(8,128)(2,1)}, bf16[2,1,2048,512]{3,2,1,0:T(8,128)(2,1)}) custom-call(s32[2]{0:T(128)} %copy-done.46, bf16[512,2048]{1,0:T(8,128)(2,1)} %get-tuple-element.158.before.refs_5_, bf16[512,1024]{1,0:T(8,128)(2,1)} %get-tuple-element.157.refs_0_, bf16[512,1024]{1,0:T(8,128)(2,1)} %bitcast.232, ...), custom_call_target="tpu_custom_call" | custom-call | flops 230000001024 | bytes 660000000 | tf_op jit(solution)/shard_map/pallas_call | solution.py:626
  202.3 5.3 shard_map.396
  207.6 26.1 %all-gather.9.cloned.1.call-done = bf16[4096,1024]{1,0:T(8,128)(2,1)} async-done(((bf16[128,1024]{1,0:T(8,128)(2,1)}), bf16[4096,1024]{1,0:T(8,128)(2,1)}) %all-gather.9.cloned.1.call-update) | async-done | bytes 8388624 | tf_op jit(solution)/shard_map/all_gather | solution.py:1179
  235.7 19.0 %shard_map.397 = (bf16[2,1,2048,512]{3,2,1,0:T(8,128)(2,1)}, f32[1,2048]{1,0:T(1,128)}, f32[512,1024]{1,0:T(8,128)}, f32[512,1024]{1,0:T(8,128)}) custom-call(s32[2]{0:T(128)} %copy-done.42, f32[8,128]{1,0:T(8,128)} %get-tuple-element.164.before, bf16[512,1024]{1,0:T(8,128)(2,1)} %get-tuple-element.157.refs_0_, bf16[512,1024]{1,0:T(8,128)(2,1)} %bitcast.233, ...), custom_call_target="tpu_custom_call" | custom-call | flops 230000001024 | bytes 660000000 | tf_op jit(solution)/shard_map/pallas_call | solution.py:626
  254.8 4.5 collective-permute-done.4.refs_3_.refs_2_.refs_29_.refs_27_
  260.5 3.8 shard_map.398
  266.4 20.6 %shard_map.399 = (bf16[2,1,2048,512]{3,2,1,0:T(8,128)(2,1)}, f32[1,2048]{1,0:T(1,128)}, f32[512,1024]{1,0:T(8,128)}, f32[512,1024]{1,0:T(8,128)}) custom-call(s32[2]{0:T(128)} %copy-done.46, f32[8,128]{1,0:T(8,128)} %get-tuple-element.171.before, bf16[512,1024]{1,0:T(8,128)(2,1)} %get-tuple-element.157.refs_0_, bf16[512,1024]{1,0:T(8,128)(2,1)} %bitcast.234, ...), custom_call_target="tpu_custom_call" | custom-call | flops 230000001024 | bytes 660000000 | tf_op jit(solution)/shard_map/pallas_call | solution.py:626
  287.0 5.1 shard_map.400
  292.1 10.5 %shard_map.401 = (bf16[512,1024]{1,0:T(8,128)(2,1)}, f32[512,1024]{1,0:T(8,128)}, bf16[512,2048]{1,0:T(8,128)(2,1)}, f32[8,1024]{1,0:T(8,128)}, f32[8,1024]{1,0:T(8,128)}, /*index=5*/f32[8,2048]{1,0:T(8,128)}) custom-call(f32[8,128]{1,0:T(8,128)} %get-tuple-element.178.before, f32[512,2176]{1,0:T(8,128)} %copy-done.4, ...), custom_call_target="tpu_custom_call" | custom-call | flops 1150000000 | bytes 3300000 | tf_op jit(solution)/shard_map/pallas_call | solution.py:544
  302.6 4.9 shard_map.402.before
  309.5 1.9 collective-permute-start.9
  313.1 2.3 copy.58
  315.4 4.9 shard_map.403.before
  320.3 17.7 %shard_map.404 = (bf16[2,3,1024,512]{3,2,1,0:T(8,128)(2,1)}, f32[1,1024]{1,0:T(1,128)}, f32[1,1024]{1,0:T(1,128)}, f32[512,1024]{1,0:T(8,128)}, f32[512,1024]{1,0:T(8,128)}, /*index=5*/f32[4,128,128]{2,1,0:T(8,128)}) custom-call(s32[2]{0:T(128)} %copy-done.42, bf16[2,1,512,1024]{3,2,1,0:T(8,128)(2,1)} %shard_map.403.before, ...), custom_call_target="tpu_custom_call" | custom-call | flops 1150000000 | bytes 3300000 | tf_op jit(solution)/shard_map/pallas_call | solution.py:626
  339.9 4.5 shard_map.405
  348.5 17.2 %shard_map.406 = (bf16[2,3,1024,512]{3,2,1,0:T(8,128)(2,1)}, f32[1,1024]{1,0:T(1,128)}, f32[1,1024]{1,0:T(1,128)}, f32[512,1024]{1,0:T(8,128)}, f32[512,1024]{1,0:T(8,128)}, /*index=5*/f32[4,128,128]{2,1,0:T(8,128)}) custom-call(s32[2]{0:T(128)} %copy-done.46, f32[8,128]{1,0:T(8,128)} %get-tuple-element.195.before, ...), custom_call_target="tpu_custom_call" | custom-call | flops 230000001024 | bytes 660000000 | tf_op jit(solution)/shard_map/pallas_call | solution.py:626
  365.7 4.9 collective-permute-done.16.refs_14_.refs_20_.refs_16_
  370.7 6.6 %shard_map.407 = (bf16[3,2,2,2,64,512]{5,4,3,2,1,0:T(8,128)(2,1)}, bf16[3,2,2,2,64,512]{5,4,3,2,1,0:T(8,128)(2,1)}, bf16[1,2,2,32,1024]{4,3,2,1,0:T(8,128)(2,1)}...) custom-call(s32[8]{0:T(128)} %stack.135.p, ...), custom_call_target="tpu_custom_call" | custom-call | flops 1150000000 | bytes 3300000 | tf_op jit(solution)/shard_map/pallas_call | solution.py:950
  382.4 18.5 %shard_map.408 = (f32[4096,128]{1,0:T(8,128)}, f32[2,16,8,128]{3,2,1,0:T(8,128)}, bf16[512,128]{1,0:T(8,128)(2,1)}, f32[8,128]{1,0:T(8,128)}) custom-call(f32[8,128]{1,0:T(8,128)} %get-tuple-element.203.before, s32[2,256]{1,0:T(2,128)} %copy-done.37, f32[4,128,128]{2,1,0:T(8,128)} %get-tuple-element.204.gp0_ref, f32[4,128,128]{2,1,0:T(8,128)} %get-tuple-element.205.gp1_ref, ...), custom_call_target="tpu_custom_call" | custom-call | flops 230000001024 | bytes 660000000 | tf_op jit(solution)/shard_map/pallas_call | solution.py:213
  401.0 2.1 collective-permute-done.18.refs_1_.refs_21_.refs_26_.refs_17_.refs_23_
  403.0 2.9 shard_map.409
  407.4 1.5 collective-permute-start.21
  409.5 13.1 %collective-permute-done.21 = f32[2,17,8,128]{3,2,1,0:T(8,128)S(1)} collective-permute-done((f32[2,17,8,128]{3,2,1,0:T(8,128)S(1)}, f32[2,17,8,128]{3,2,1,0:T(8,128)S(1)}, u32[]{:S(2)}, u32[]{:S(2)}) %collective-permute-start.21) | collective-permute-done | bytes 139296 | tf_op jit(solution)/shard_map/ppermute | solution.py:52
  422.8 1.6 collective-permute-start.22
  425.9 2.0 collective-permute-done.22
  428.0 2.0 collective-permute-start.23
  431.5 3.9 collective-permute-done.23
  436.9 5.8 shard_map.410
  445.0 1.9 collective-permute-start.27
  448.3 19.5 %shard_map.411 = (f32[256,1024]{1,0:T(8,128)}, f32[16,8,128]{2,1,0:T(8,128)}, f32[16,8,128]{2,1,0:T(8,128)}, f32[16,8,128]{2,1,0:T(8,128)}, f32[8,128]{1,0:T(8,1...) custom-call(f32[8,128]{1,0:T(8,128)} %get-tuple-element.217.before, s32[2,256]{1,0:T(2,128)} %copy-done.37, ...), custom_call_target="tpu_custom_call" | custom-call | flops 230000001024 | bytes 660000000 | tf_op jit(solution)/shard_map/pallas_call | solution.py:325
  467.9 5.5 shard_map.412
  475.5 2.3 collective-permute-start.31
  477.9 19.5 %shard_map.413 = (f32[256,1024]{1,0:T(8,128)}, f32[16,8,128]{2,1,0:T(8,128)}, f32[16,8,128]{2,1,0:T(8,128)}, f32[16,8,128]{2,1,0:T(8,128)}, f32[8,128]{1,0:T(8,1...) custom-call(f32[8,128]{1,0:T(8,128)} %get-tuple-element.228.before, s32[2,256]{1,0:T(2,128)} %copy-done.37, ...), custom_call_target="tpu_custom_call" | custom-call | flops 230000001024 | bytes 660000000 | tf_op jit(solution)/shard_map/pallas_call | solution.py:325
  501.5 8.8 %collective-permute-done.31.refs_5_.refs_10_.refs_11_ = bf16[3,2,64,1024]{3,2,1,0:T(8,128)(2,1)} collective-permute-done((bf16[3,2,64,1024]{3,2,1,0:T(8,128)(2,1)}, bf16[3,2,64,1024]{3,2,1,0:T(8,128)(2,1)}, u32[]{:S(2)}, u32[]{:S(2)}) %collective-permute-start.31) | collective-permute-done | bytes 786464 | tf_op jit(solution)/shard_map/ppermute | solution.py:52
  510.3 3.2 shard_map.414
  515.7 1.9 shard_map.415
  518.4 2.9 shard_map.420
  522.2 3.1 shard_map.419
  528.1 3.5 shard_map.416
  534.6 1.8 collective-permute-start.46
  536.4 3.5 collective-permute-done.46
  539.9 2.0 collective-permute-start.47
  541.9 1.9 collective-permute-done.47
  543.8 3.9 collective-permute-start.48
  549.1 1.6 collective-permute-done.48
  553.5 2.2 collective-permute-done.49
  556.9 2.9 collective-permute-start.36
  559.8 3.4 shard_map.417
  565.9 6.9 %shard_map.418 = (f32[1024,2176]{1,0:T(8,128)}, f32[8,128]{1,0:T(8,128)}) custom-call(s32[32]{0:T(128)} %fusion.40.place, bf16[1024,2048]{1,0:T(8,128)(2,1)} %bitcast.280, bf16[32,32,128]{2,1,0:T(8,128)(2,1)} %bitcast.276), custom_call_target="tpu_custom_call" | custom-call | flops 57500000256 | bytes 165000000 | tf_op jit(solution)/shard_map/pallas_call | solution.py:1096
  (313 shorter events, 80.3 us)
Async XLA Ops:
  7.2 147.9 %all-gather.7.cloned.1.call-start = ((), (), s32[]{:S(2)}) async-start(), calls=%async_computation | async-start | bytes 22167552 | tf_op jit(solution)/shard_map/all_gather | solution.py:1178
  12.4 221.3 %all-gather.9.cloned.1.call-start = ((), (), s32[]{:S(2)}) async-start(), calls=%async_computation.1 | async-start | bytes 8650752 | tf_op jit(solution)/shard_map/all_gather | solution.py:1179
  13.3 33.7 %copy-start.42 = (s32[2]{0:T(128)}, s32[2]{0:T(128)S(1)}, u32[]{:S(2)}) copy-start(s32[2]{0:T(128)S(1)} %get-tuple-element.150.piece) | copy-start | bytes 28
  13.3 33.7 %copy-start.46 = (s32[2]{0:T(128)}, s32[2]{0:T(128)S(1)}, u32[]{:S(2)}) copy-start(s32[2]{0:T(128)S(1)} %get-tuple-element.149.piece) | copy-start | bytes 28
  28.7 6.7 %collective-permute-start = (f32[2,17,8,128]{3,2,1,0:T(8,128)S(1)}, f32[2,17,8,128]{3,2,1,0:T(8,128)S(1)}, u32[]{:S(2)}, u32[]{:S(2)}) collective-permute-start(f32[2,17,8,128]{3,2,1,0:T(8,128)S(1)} %pad_maximum_fusion.5), channel_id=1, source_target_pairs={{0,1},{1,0},{2,3},{3,2},{4,5},{5,4},{6,7},{7,6},{8,9},{9,8},{10,11... | collective-permute-start | bytes 417800 | tf_op jit(solution)/shard_map/ppermute | solution.py:52
  33.4 532.5 %all-gather.11.cloned.1.call-start = ((), (), s32[]{:S(2)}) async-start(), calls=%async_computation.2 | async-start | bytes 4325376 | tf_op jit(solution)/shard_map/all_gather | solution.py:1355
  33.5 35.5 %copy-start.7 = (f32[16,8,128]{2,1,0:T(8,128)}, f32[16,8,128]{2,1,0:T(8,128)S(1)}, u32[]{:S(2)}) copy-start(f32[16,8,128]{2,1,0:T(8,128)S(1)} %get-tuple-element.296) | copy-start | bytes 196612
  33.5 35.5 %copy-start.9 = (f32[16,8,128]{2,1,0:T(8,128)}, f32[16,8,128]{2,1,0:T(8,128)S(1)}, u32[]{:S(2)}) copy-start(f32[16,8,128]{2,1,0:T(8,128)S(1)} %get-tuple-element.295) | copy-start | bytes 196612
  36.5 8.1 %collective-permute-start.1 = (f32[2,17,8,128]{3,2,1,0:T(8,128)S(1)}, f32[2,17,8,128]{3,2,1,0:T(8,128)S(1)}, u32[]{:S(2)}, u32[]{:S(2)}) collective-permute-start(f32[2,17,8,128]{3,2,1,0:T(8,128)S(1)} %pad_maximum_fusion.6), channel_id=1, source_target_pairs={{0,2},{1,3},{2,0},{3,1},{4,6},{5,7},{6,4},{7,5},{8,10},{9,11},{10,... | collective-permute-start | bytes 417800 | tf_op jit(solution)/shard_map/ppermute | solution.py:52
  44.7 11.0 %collective-permute-start.2 = (f32[2,17,8,128]{3,2,1,0:T(8,128)S(1)}, f32[2,17,8,128]{3,2,1,0:T(8,128)S(1)}, u32[]{:S(2)}, u32[]{:S(2)}) collective-permute-start(f32[2,17,8,128]{3,2,1,0:T(8,128)S(1)} %pad_maximum_fusion.7), channel_id=1, source_target_pairs={{0,4},{1,5},{2,6},{3,7},{4,0},{5,1},{6,2},{7,3},{8,12},{9,13},{10,... | collective-permute-start | bytes 417800 | tf_op jit(solution)/shard_map/ppermute | solution.py:52
  77.1 78.0 %copy-start.29 = (bf16[512,128]{1,0:T(8,128)(2,1)}, bf16[512,128]{1,0:T(8,128)(2,1)S(1)}, u32[]{:S(2)}) copy-start(bf16[512,128]{1,0:T(8,128)(2,1)S(1)} %get-tuple-element.264.key_ref) | copy-start | bytes 393220
  77.1 99.2 %copy-start.16 = (f32[512,128]{1,0:T(8,128)}, f32[512,128]{1,0:T(8,128)S(1)}, u32[]{:S(2)}) copy-start(f32[512,128]{1,0:T(8,128)S(1)} %get-tuple-element.265.shared_ref) | copy-start | bytes 786436
  77.2 77.9 %copy-start.30 = (bf16[512,128]{1,0:T(8,128)(2,1)}, bf16[512,128]{1,0:T(8,128)(2,1)S(1)}, u32[]{:S(2)}) copy-start(bf16[512,128]{1,0:T(8,128)(2,1)S(1)} %add_convert_fusion.2.query_ref) | copy-start | bytes 393220
  192.0 10.2 %collective-permute-start.3 = (bf16[2,1,2,2,2,2,128,512]{7,6,5,4,3,2,1,0:T(8,128)(2,1)}, bf16[2,1,2,2,2,2,128,512]{7,6,5,4,3,2,1,0:T(8,128)(2,1)}, u32[]{:S(2)}, u32[]{:S(2)}) collective-permute-start(bf16[2,1,2,2,2,2,128,512]{7,6,5,4,3,2,1,0:T(8,128)(2,1)} %bitcast.282), channel_id=1, source_target_pairs={{0,8},{1,9},{2,10},{3,11},{4,12},{5,13},{6,14},{7,15},{8,0},{9,1},... | collective-permute-start | bytes 12582920 | tf_op jit(solution)/shard_map/ppermute | solution.py:52
  233.7 25.6 %collective-permute-start.4 = (bf16[1,2,2,2,128,512]{5,4,3,2,1,0:T(8,128)(2,1)}, bf16[1,2,2,2,128,512]{5,4,3,2,1,0:T(8,128)(2,1)}, u32[]{:S(2)}, u32[]{:S(2)}) collective-permute-start(bf16[1,2,2,2,128,512]{5,4,3,2,1,0:T(8,128)(2,1)} %get-tuple-element.163), channel_id=1, source_target_pairs={{0,16},{1,17},{2,18},{3,19},{4,20},{5,21},{6,22},{7,23},{8,24},{9,... | collective-permute-start | bytes 3145736 | tf_op jit(solution)/shard_map/ppermute | solution.py:52
  235.1 25.4 %collective-permute-start.5 = (bf16[1,2,2,2,128,512]{5,4,3,2,1,0:T(8,128)(2,1)}, bf16[1,2,2,2,128,512]{5,4,3,2,1,0:T(8,128)(2,1)}, u32[]{:S(2)}, u32[]{:S(2)}) collective-permute-start(bf16[1,2,2,2,128,512]{5,4,3,2,1,0:T(8,128)(2,1)} %get-tuple-element.168), channel_id=1, source_target_pairs={{0,1},{1,0},{2,3},{3,2},{4,5},{5,4},{6,7},{7,6},{8,9},{9,8},{10,11... | collective-permute-start | bytes 3145736 | tf_op jit(solution)/shard_map/ppermute | solution.py:52
  254.7 32.3 %collective-permute-start.8 = (bf16[2,1,2,2,2,2,128,512]{7,6,5,4,3,2,1,0:T(8,128)(2,1)}, bf16[2,1,2,2,2,2,128,512]{7,6,5,4,3,2,1,0:T(8,128)(2,1)}, u32[]{:S(2)}, u32[]{:S(2)}) collective-permute-start(bf16[2,1,2,2,2,2,128,512]{7,6,5,4,3,2,1,0:T(8,128)(2,1)} %bitcast.281), channel_id=1, source_target_pairs={{0,8},{1,9},{2,10},{3,11},{4,12},{5,13},{6,14},{7,15},{8,0},{9,1},... | collective-permute-start | bytes 12582920 | tf_op jit(solution)/shard_map/ppermute | solution.py:52
  264.2 22.7 %collective-permute-start.6 = (bf16[1,2,2,128,512]{4,3,2,1,0:T(8,128)(2,1)}, bf16[1,2,2,128,512]{4,3,2,1,0:T(8,128)(2,1)}, u32[]{:S(2)}, u32[]{:S(2)}) collective-permute-start(bf16[1,2,2,128,512]{4,3,2,1,0:T(8,128)(2,1)} %get-tuple-element.169), channel_id=1, source_target_pairs={{0,1},{1,0},{2,3},{3,2},{4,5},{5,4},{6,7},{7,6},{8,9},{9,8},{10,11... | collective-permute-start | bytes 1572872 | tf_op jit(solution)/shard_map/ppermute | solution.py:52
  264.9 22.1 %collective-permute-start.7 = (bf16[1,2,2,128,512]{4,3,2,1,0:T(8,128)(2,1)}, bf16[1,2,2,128,512]{4,3,2,1,0:T(8,128)(2,1)}, u32[]{:S(2)}, u32[]{:S(2)}) collective-permute-start(bf16[1,2,2,128,512]{4,3,2,1,0:T(8,128)(2,1)} %get-tuple-element.170), channel_id=1, source_target_pairs={{0,16},{1,17},{2,18},{3,19},{4,20},{5,21},{6,22},{7,23},{8,24},{9,... | collective-permute-start | bytes 1572872 | tf_op jit(solution)/shard_map/ppermute | solution.py:52
  307.5 30.7 %collective-permute-start.12 = (bf16[2,1,2,2,2,2,32,1024]{7,6,5,4,3,2,1,0:T(8,128)(2,1)}, bf16[2,1,2,2,2,2,32,1024]{7,6,5,4,3,2,1,0:T(8,128)(2,1)S(1)}, u32[]{:S(2)}, u32[]{:S(2)}) collective-permute-start(bf16[2,1,2,2,2,2,32,1024]{7,6,5,4,3,2,1,0:T(8,128)(2,1)} %bitcast.229), channel_id=1, source_target_pairs={{0,8},{1,9},{2,10},{3,11},{4,12},{5,13},{6,14},{7,15},{8,0},{9,1},... | collective-permute-start | bytes 6291464 | tf_op jit(solution)/shard_map/ppermute | solution.py:52
  307.5 30.6 %collective-permute-start.10 = (bf16[1,2,2,2,128,512]{5,4,3,2,1,0:T(8,128)(2,1)}, bf16[1,2,2,2,128,512]{5,4,3,2,1,0:T(8,128)(2,1)S(1)}, u32[]{:S(2)}, u32[]{:S(2)}) collective-permute-start(bf16[1,2,2,2,128,512]{5,4,3,2,1,0:T(8,128)(2,1)} %get-tuple-element.193), channel_id=1, source_target_pairs={{0,16},{1,17},{2,18},{3,19},{4,20},{5,21},{6,22},{7,23},{8,24},{9,... | collective-permute-start | bytes 3145736 | tf_op jit(solution)/shard_map/ppermute | solution.py:52
  308.1 30.1 %collective-permute-start.11 = (bf16[1,2,2,2,128,512]{5,4,3,2,1,0:T(8,128)(2,1)}, bf16[1,2,2,2,128,512]{5,4,3,2,1,0:T(8,128)(2,1)}, u32[]{:S(2)}, u32[]{:S(2)}) collective-permute-start(bf16[1,2,2,2,128,512]{5,4,3,2,1,0:T(8,128)(2,1)} %get-tuple-element.194), channel_id=1, source_target_pairs={{0,1},{1,0},{2,3},{3,2},{4,5},{5,4},{6,7},{7,6},{8,9},{9,8},{10,11... | collective-permute-start | bytes 3145736 | tf_op jit(solution)/shard_map/ppermute | solution.py:52
  309.5 28.6 %collective-permute-start.9 = (bf16[1,2,128,1024]{3,2,1,0:T(8,128)(2,1)}, bf16[1,2,128,1024]{3,2,1,0:T(8,128)(2,1)}, u32[]{:S(2)}, u32[]{:S(2)}) collective-permute-start(bf16[1,2,128,1024]{3,2,1,0:T(8,128)(2,1)} %get-tuple-element.192), channel_id=1, source_target_pairs={{0,4},{1,5},{2,6},{3,7},{4,0},{5,1},{6,2},{7,3},{8,12},{9,13},{10,... | collective-permute-start | bytes 1572872 | tf_op jit(solution)/shard_map/ppermute | solution.py:52
  338.0 32.6 %collective-permute-start.13 = (bf16[2,3,2,2,2,2,64,512]{7,6,5,4,3,2,1,0:T(8,128)(2,1)}, bf16[2,3,2,2,2,2,64,512]{7,6,5,4,3,2,1,0:T(8,128)(2,1)}, u32[]{:S(2)}, u32[]{:S(2)}) collective-permute-start(bf16[2,3,2,2,2,2,64,512]{7,6,5,4,3,2,1,0:T(8,128)(2,1)} %bitcast.279), channel_id=1, source_target_pairs={{0,8},{1,9},{2,10},{3,11},{4,12},{5,13},{6,14},{7,15},{8,0},{9,1},... | collective-permute-start | bytes 18874376 | tf_op jit(solution)/shard_map/ppermute | solution.py:52
  344.4 21.3 %collective-permute-start.14 = (bf16[1,2,2,2,32,1024]{5,4,3,2,1,0:T(8,128)(2,1)}, bf16[1,2,2,2,32,1024]{5,4,3,2,1,0:T(8,128)(2,1)}, u32[]{:S(2)}, u32[]{:S(2)}) collective-permute-start(bf16[1,2,2,2,32,1024]{5,4,3,2,1,0:T(8,128)(2,1)} %get-tuple-element.199), channel_id=1, source_target_pairs={{0,16},{1,17},{2,18},{3,19},{4,20},{5,21},{6,22},{7,23},{8,24},{9,... | collective-permute-start | bytes 1572872 | tf_op jit(solution)/shard_map/ppermute | solution.py:52
  345.1 20.6 %collective-permute-start.15 = (bf16[1,2,2,2,32,1024]{5,4,3,2,1,0:T(8,128)(2,1)}, bf16[1,2,2,2,32,1024]{5,4,3,2,1,0:T(8,128)(2,1)}, u32[]{:S(2)}, u32[]{:S(2)}) collective-permute-start(bf16[1,2,2,2,32,1024]{5,4,3,2,1,0:T(8,128)(2,1)} %get-tuple-element.200), channel_id=1, source_target_pairs={{0,1},{1,0},{2,3},{3,2},{4,5},{5,4},{6,7},{7,6},{8,9},{9,8},{10,11... | collective-permute-start | bytes 1572872 | tf_op jit(solution)/shard_map/ppermute | solution.py:52
  346.6 24.1 %collective-permute-start.16 = (bf16[1,2,2,128,512]{4,3,2,1,0:T(8,128)(2,1)}, bf16[1,2,2,128,512]{4,3,2,1,0:T(8,128)(2,1)}, u32[]{:S(2)}, u32[]{:S(2)}) collective-permute-start(bf16[1,2,2,128,512]{4,3,2,1,0:T(8,128)(2,1)} %get-tuple-element.201), channel_id=1, source_target_pairs={{0,1},{1,0},{2,3},{3,2},{4,5},{5,4},{6,7},{7,6},{8,9},{9,8},{10,11... | collective-permute-start | bytes 1572872 | tf_op jit(solution)/shard_map/ppermute | solution.py:52
  347.1 23.6 %collective-permute-start.17 = (bf16[1,2,2,128,512]{4,3,2,1,0:T(8,128)(2,1)}, bf16[1,2,2,128,512]{4,3,2,1,0:T(8,128)(2,1)}, u32[]{:S(2)}, u32[]{:S(2)}) collective-permute-start(bf16[1,2,2,128,512]{4,3,2,1,0:T(8,128)(2,1)} %get-tuple-element.202), channel_id=1, source_target_pairs={{0,16},{1,17},{2,18},{3,19},{4,20},{5,21},{6,22},{7,23},{8,24},{9,... | collective-permute-start | bytes 1572872 | tf_op jit(solution)/shard_map/ppermute | solution.py:52
  377.3 25.7 %collective-permute-start.18 = (bf16[1,2,128,1024]{3,2,1,0:T(8,128)(2,1)}, bf16[1,2,128,1024]{3,2,1,0:T(8,128)(2,1)}, u32[]{:S(2)}, u32[]{:S(2)}) collective-permute-start(bf16[1,2,128,1024]{3,2,1,0:T(8,128)(2,1)} %get-tuple-element.210), channel_id=1, source_target_pairs={{0,4},{1,5},{2,6},{3,7},{4,0},{5,1},{6,2},{7,3},{8,12},{9,13},{10,... | collective-permute-start | bytes 1572872 | tf_op jit(solution)/shard_map/ppermute | solution.py:52
  378.4 22.6 %collective-permute-start.19 = (bf16[1,2,2,32,1024]{4,3,2,1,0:T(8,128)(2,1)}, bf16[1,2,2,32,1024]{4,3,2,1,0:T(8,128)(2,1)}, u32[]{:S(2)}, u32[]{:S(2)}) collective-permute-start(bf16[1,2,2,32,1024]{4,3,2,1,0:T(8,128)(2,1)} %get-tuple-element.211), channel_id=1, source_target_pairs={{0,1},{1,0},{2,3},{3,2},{4,5},{5,4},{6,7},{7,6},{8,9},{9,8},{10,11... | collective-permute-start | bytes 786440 | tf_op jit(solution)/shard_map/ppermute | solution.py:52
  379.9 21.1 %collective-permute-start.20 = (bf16[1,2,2,32,1024]{4,3,2,1,0:T(8,128)(2,1)}, bf16[1,2,2,32,1024]{4,3,2,1,0:T(8,128)(2,1)}, u32[]{:S(2)}, u32[]{:S(2)}) collective-permute-start(bf16[1,2,2,32,1024]{4,3,2,1,0:T(8,128)(2,1)} %get-tuple-element.212), channel_id=1, source_target_pairs={{0,16},{1,17},{2,18},{3,19},{4,20},{5,21},{6,22},{7,23},{8,24},{9,... | collective-permute-start | bytes 786440 | tf_op jit(solution)/shard_map/ppermute | solution.py:52
  380.4 55.8 %collective-permute-start.24 = (bf16[3,2,2,2,64,512]{5,4,3,2,1,0:T(8,128)(2,1)}, bf16[3,2,2,2,64,512]{5,4,3,2,1,0:T(8,128)(2,1)}, u32[]{:S(2)}, u32[]{:S(2)}) collective-permute-start(bf16[3,2,2,2,64,512]{5,4,3,2,1,0:T(8,128)(2,1)} %get-tuple-element.214), channel_id=1, source_target_pairs={{0,16},{1,17},{2,18},{3,19},{4,20},{5,21},{6,22},{7,23},{8,24},{9,... | collective-permute-start | bytes 4718600 | tf_op jit(solution)/shard_map/ppermute | solution.py:52
  381.9 54.3 %collective-permute-start.25 = (bf16[3,2,2,2,64,512]{5,4,3,2,1,0:T(8,128)(2,1)}, bf16[3,2,2,2,64,512]{5,4,3,2,1,0:T(8,128)(2,1)}, u32[]{:S(2)}, u32[]{:S(2)}) collective-permute-start(bf16[3,2,2,2,64,512]{5,4,3,2,1,0:T(8,128)(2,1)} %get-tuple-element.215), channel_id=1, source_target_pairs={{0,1},{1,0},{2,3},{3,2},{4,5},{5,4},{6,7},{7,6},{8,9},{9,8},{10,11... | collective-permute-start | bytes 4718600 | tf_op jit(solution)/shard_map/ppermute | solution.py:52
  407.4 15.2 %collective-permute-start.21 = (f32[2,17,8,128]{3,2,1,0:T(8,128)S(1)}, f32[2,17,8,128]{3,2,1,0:T(8,128)S(1)}, u32[]{:S(2)}, u32[]{:S(2)}) collective-permute-start(f32[2,17,8,128]{3,2,1,0:T(8,128)S(1)} %pad_maximum_fusion.4), channel_id=1, source_target_pairs={{0,1},{1,0},{2,3},{3,2},{4,5},{5,4},{6,7},{7,6},{8,9},{9,8},{10,11... | collective-permute-start | bytes 417800 | tf_op jit(solution)/shard_map/ppermute | solution.py:52
  408.9 27.3 %collective-permute-start.26 = (bf16[1,2,32,2048]{3,2,1,0:T(8,128)(2,1)}, bf16[1,2,32,2048]{3,2,1,0:T(8,128)(2,1)S(1)}, u32[]{:S(2)}, u32[]{:S(2)}) collective-permute-start(bf16[1,2,32,2048]{3,2,1,0:T(8,128)(2,1)} %get-tuple-element.216), channel_id=1, source_target_pairs={{0,4},{1,5},{2,6},{3,7},{4,0},{5,1},{6,2},{7,3},{8,12},{9,13},{10,... | collective-permute-start | bytes 786440 | tf_op jit(solution)/shard_map/ppermute | solution.py:52
  409.4 14.9 %collective-permute-start.40 = (bf16[2,1,2,2,2,32,128]{6,5,4,3,2,1,0:T(8,128)(2,1)S(1)}, bf16[2,1,2,2,2,32,128]{6,5,4,3,2,1,0:T(8,128)(2,1)S(1)}, u32[]{:S(2)}, u32[]{:S(2)}) collective-permute-start(bf16[2,1,2,2,2,32,128]{6,5,4,3,2,1,0:T(8,128)(2,1)S(1)} %dynamic-slice_convert_fusion), channel_id=1, source_target_pairs={{0,8},{1,9},{2,10},{3,11},{4,12},{5,13},{6,14},{7,15},{8,0},{9,1},... | collective-permute-start | bytes 393224 | tf_op jit(solution)/shard_map/ppermute | solution.py:52
  422.8 5.1 collective-permute-start.22
  424.4 5.5 collective-permute-start.41
  428.0 7.5 %collective-permute-start.23 = (f32[2,17,8,128]{3,2,1,0:T(8,128)S(1)}, f32[2,17,8,128]{3,2,1,0:T(8,128)S(1)}, u32[]{:S(2)}, u32[]{:S(2)}) collective-permute-start(f32[2,17,8,128]{3,2,1,0:T(8,128)S(1)} %pad_maximum_fusion.9), channel_id=1, source_target_pairs={{0,4},{1,5},{2,6},{3,7},{4,0},{5,1},{6,2},{7,3},{8,12},{9,13},{10,... | collective-permute-start | bytes 417800 | tf_op jit(solution)/shard_map/ppermute | solution.py:52
  430.0 16.9 %collective-permute-start.42 = (bf16[1,1,2,2,1,32,128]{6,5,4,3,2,1,0:T(8,128)(2,1)S(1)}, bf16[1,1,2,2,1,32,128]{6,5,4,3,2,1,0:T(8,128)(2,1)S(1)}, u32[]{:S(2)}, u32[]{:S(2)}) collective-permute-start(bf16[1,1,2,2,1,32,128]{6,5,4,3,2,1,0:T(8,128)(2,1)S(1)} %dynamic-slice_convert_fusion.2), channel_id=1, source_target_pairs={{0,1},{1,0},{2,3},{3,2},{4,5},{5,4},{6,7},{7,6},{8,9},{9,8},{10,11... | collective-permute-start | bytes 98312 | tf_op jit(solution)/shard_map/ppermute | solution.py:52
  442.7 25.2 %collective-permute-start.29 = (bf16[3,2,2,64,512]{4,3,2,1,0:T(8,128)(2,1)}, bf16[3,2,2,64,512]{4,3,2,1,0:T(8,128)(2,1)}, u32[]{:S(2)}, u32[]{:S(2)}) collective-permute-start(bf16[3,2,2,64,512]{4,3,2,1,0:T(8,128)(2,1)} %get-tuple-element.226), channel_id=1, source_target_pairs={{0,1},{1,0},{2,3},{3,2},{4,5},{5,4},{6,7},{7,6},{8,9},{9,8},{10,11... | collective-permute-start | bytes 2359304 | tf_op jit(solution)/shard_map/ppermute | solution.py:52
  444.2 23.6 %collective-permute-start.30 = (bf16[3,2,2,64,512]{4,3,2,1,0:T(8,128)(2,1)}, bf16[3,2,2,64,512]{4,3,2,1,0:T(8,128)(2,1)}, u32[]{:S(2)}, u32[]{:S(2)}) collective-permute-start(bf16[3,2,2,64,512]{4,3,2,1,0:T(8,128)(2,1)} %get-tuple-element.227), channel_id=1, source_target_pairs={{0,16},{1,17},{2,18},{3,19},{4,20},{5,21},{6,22},{7,23},{8,24},{9,... | collective-permute-start | bytes 2359304 | tf_op jit(solution)/shard_map/ppermute | solution.py:52
  444.8 23.0 %collective-permute-start.28 = (bf16[2,1,128,1024]{3,2,1,0:T(8,128)(2,1)}, bf16[2,1,128,1024]{3,2,1,0:T(8,128)(2,1)}, u32[]{:S(2)}, u32[]{:S(2)}) collective-permute-start(bf16[2,1,128,1024]{3,2,1,0:T(8,128)(2,1)} %get-tuple-element.225), channel_id=1, source_target_pairs={{0,2},{1,3},{2,0},{3,1},{4,6},{5,7},{6,4},{7,5},{8,10},{9,11},{10,... | collective-permute-start | bytes 1572872 | tf_op jit(solution)/shard_map/ppermute | solution.py:52
  445.0 22.9 %collective-permute-start.27 = (bf16[1,32,2048]{2,1,0:T(8,128)(2,1)}, bf16[1,32,2048]{2,1,0:T(8,128)(2,1)}, u32[]{:S(2)}, u32[]{:S(2)}) collective-permute-start(bf16[1,32,2048]{2,1,0:T(8,128)(2,1)} %get-tuple-element.224), channel_id=1, source_target_pairs={{0,2},{1,3},{2,0},{3,1},{4,6},{5,7},{6,4},{7,5},{8,10},{9,11},{10,... | collective-permute-start | bytes 393224 | tf_op jit(solution)/shard_map/ppermute | solution.py:52
  448.2 49.2 %collective-permute-start.43 = (bf16[1,1,2,1,1,32,128]{6,5,4,3,2,1,0:T(8,128)(2,1)}, bf16[1,1,2,1,1,32,128]{6,5,4,3,2,1,0:T(8,128)(2,1)}, u32[]{:S(2)}, u32[]{:S(2)}) collective-permute-start(bf16[1,1,2,1,1,32,128]{6,5,4,3,2,1,0:T(8,128)(2,1)} %dynamic-slice_convert_fusion.3), channel_id=1, source_target_pairs={{0,2},{1,3},{2,0},{3,1},{4,6},{5,7},{6,4},{7,5},{8,10},{9,11},{10,... | collective-permute-start | bytes 49160 | tf_op jit(solution)/shard_map/ppermute | solution.py:52
  473.4 25.5 %collective-permute-start.52 = (bf16[1,128,1024]{2,1,0:T(8,128)(2,1)}, bf16[1,128,1024]{2,1,0:T(8,128)(2,1)}, u32[]{:S(2)}, u32[]{:S(2)}) collective-permute-start(bf16[1,128,1024]{2,1,0:T(8,128)(2,1)} %get-tuple-element.260.own_ref), channel_id=1, source_target_pairs={{0,16},{1,17},{2,18},{3,19},{4,20},{5,21},{6,22},{7,23},{8,24},{9,... | collective-permute-start | bytes 786440 | tf_op jit(solution)/shard_map/ppermute | solution.py:52
  474.9 25.1 %collective-permute-start.50 = (bf16[1,128,1024]{2,1,0:T(8,128)(2,1)}, bf16[1,128,1024]{2,1,0:T(8,128)(2,1)}, u32[]{:S(2)}, u32[]{:S(2)}) collective-permute-start(bf16[1,128,1024]{2,1,0:T(8,128)(2,1)} %get-tuple-element.258.own_ref), channel_id=1, source_target_pairs={{0,16},{1,17},{2,18},{3,19},{4,20},{5,21},{6,22},{7,23},{8,24},{9,... | collective-permute-start | bytes 786440 | tf_op jit(solution)/shard_map/ppermute | solution.py:52
  475.5 34.8 %collective-permute-start.31 = (bf16[3,2,64,1024]{3,2,1,0:T(8,128)(2,1)}, bf16[3,2,64,1024]{3,2,1,0:T(8,128)(2,1)}, u32[]{:S(2)}, u32[]{:S(2)}) collective-permute-start(bf16[3,2,64,1024]{3,2,1,0:T(8,128)(2,1)} %get-tuple-element.230), channel_id=1, source_target_pairs={{0,4},{1,5},{2,6},{3,7},{4,0},{5,1},{6,2},{7,3},{8,12},{9,13},{10,... | collective-permute-start | bytes 2359304 | tf_op jit(solution)/shard_map/ppermute | solution.py:52
  498.2 33.5 %collective-permute-start.44 = (bf16[1,1,1,1,1,32,128]{6,5,4,3,2,1,0:T(8,128)(2,1)S(1)}, bf16[1,1,1,1,1,32,128]{6,5,4,3,2,1,0:T(8,128)(2,1)S(1)}, u32[]{:S(2)}, u32[]{:S(2)}) collective-permute-start(bf16[1,1,1,1,1,32,128]{6,5,4,3,2,1,0:T(8,128)(2,1)S(1)} %dynamic-slice_convert_fusion.4), channel_id=1, source_target_pairs={{0,4},{1,5},{2,6},{3,7},{4,0},{5,1},{6,2},{7,3},{8,12},{9,13},{10,... | collective-permute-start | bytes 24584 | tf_op jit(solution)/shard_map/ppermute | solution.py:52
  499.9 17.8 %collective-permute-start.53 = (bf16[2,1,128,1024]{3,2,1,0:T(8,128)(2,1)S(1)}, bf16[2,1,128,1024]{3,2,1,0:T(8,128)(2,1)S(1)}, u32[]{:S(2)}, u32[]{:S(2)}) collective-permute-start(bf16[2,1,128,1024]{3,2,1,0:T(8,128)(2,1)S(1)} %pad_maximum_fusion.3), channel_id=1, source_target_pairs={{0,8},{1,9},{2,10},{3,11},{4,12},{5,13},{6,14},{7,15},{8,0},{9,1},... | collective-permute-start | bytes 1572872 | tf_op jit(solution)/shard_map/ppermute | solution.py:52
  501.0 20.4 %collective-permute-start.51 = (bf16[2,1,128,1024]{3,2,1,0:T(8,128)(2,1)S(1)}, bf16[2,1,128,1024]{3,2,1,0:T(8,128)(2,1)S(1)}, u32[]{:S(2)}, u32[]{:S(2)}) collective-permute-start(bf16[2,1,128,1024]{3,2,1,0:T(8,128)(2,1)S(1)} %pad_maximum_fusion.2), channel_id=1, source_target_pairs={{0,8},{1,9},{2,10},{3,11},{4,12},{5,13},{6,14},{7,15},{8,0},{9,1},... | collective-permute-start | bytes 1572872 | tf_op jit(solution)/shard_map/ppermute | solution.py:52
  513.5 13.9 %collective-permute-start.33 = (bf16[3,64,1024]{2,1,0:T(8,128)(2,1)}, bf16[3,64,1024]{2,1,0:T(8,128)(2,1)S(1)}, u32[]{:S(2)}, u32[]{:S(2)}) collective-permute-start(bf16[3,64,1024]{2,1,0:T(8,128)(2,1)} %get-tuple-element.247), channel_id=1, source_target_pairs={{0,2},{1,3},{2,0},{3,1},{4,6},{5,7},{6,4},{7,5},{8,10},{9,11},{10,... | collective-permute-start | bytes 1179656 | tf_op jit(solution)/shard_map/ppermute | solution.py:52
  517.6 15.9 %collective-permute-start.32 = (bf16[512,128]{1,0:T(8,128)(2,1)}, bf16[512,128]{1,0:T(8,128)(2,1)S(1)}, u32[]{:S(2)}, u32[]{:S(2)}) collective-permute-start(bf16[512,128]{1,0:T(8,128)(2,1)} %shard_map.415), channel_id=1, source_target_pairs={{0,8},{1,9},{2,10},{3,11},{4,12},{5,13},{6,14},{7,15},{8,0},{9,1},... | collective-permute-start | bytes 393224 | tf_op jit(solution)/shard_map/ppermute | solution.py:52
  532.4 2.2 collective-permute-start.45
  532.8 14.9 %collective-permute-start.37 = (bf16[3,64,1024]{2,1,0:T(8,128)(2,1)}, bf16[3,64,1024]{2,1,0:T(8,128)(2,1)S(1)}, u32[]{:S(2)}, u32[]{:S(2)}) collective-permute-start(bf16[3,64,1024]{2,1,0:T(8,128)(2,1)} %get-tuple-element.249.own_ref), channel_id=1, source_target_pairs={{0,16},{1,17},{2,18},{3,19},{4,20},{5,21},{6,22},{7,23},{8,24},{9,... | collective-permute-start | bytes 1179656 | tf_op jit(solution)/shard_map/ppermute | solution.py:52
  534.3 17.5 %collective-permute-start.34 = (bf16[512,128]{1,0:T(8,128)(2,1)S(1)}, bf16[512,128]{1,0:T(8,128)(2,1)S(1)}, u32[]{:S(2)}, u32[]{:S(2)}) collective-permute-start(bf16[512,128]{1,0:T(8,128)(2,1)S(1)} %fusion.7), channel_id=1, source_target_pairs={{0,1},{1,0},{2,3},{3,2},{4,5},{5,4},{6,7},{7,6},{8,9},{9,8},{10,11... | collective-permute-start | bytes 393224 | tf_op jit(solution)/shard_map/ppermute | solution.py:52
  534.6 5.3 collective-permute-start.46
  539.9 3.9 collective-permute-start.47
  543.8 6.8 %collective-permute-start.48 = (bf16[256,128]{1,0:T(8,128)(2,1)S(1)}, bf16[256,128]{1,0:T(8,128)(2,1)S(1)}, u32[]{:S(2)}, u32[]{:S(2)}) collective-permute-start(bf16[256,128]{1,0:T(8,128)(2,1)S(1)} %pad_maximum_fusion.10), channel_id=1, source_target_pairs={{0,4},{1,5},{2,6},{3,7},{4,0},{5,1},{6,2},{7,3},{8,12},{9,13},{10,... | collective-permute-start | bytes 196616 | tf_op jit(solution)/shard_map/ppermute | solution.py:52
  549.0 10.9 %collective-permute-start.38 = (bf16[2,3,64,1024]{3,2,1,0:T(8,128)(2,1)S(1)}, bf16[2,3,64,1024]{3,2,1,0:T(8,128)(2,1)}, u32[]{:S(2)}, u32[]{:S(2)}) collective-permute-start(bf16[2,3,64,1024]{3,2,1,0:T(8,128)(2,1)S(1)} %pad_maximum_fusion.1), channel_id=1, source_target_pairs={{0,8},{1,9},{2,10},{3,11},{4,12},{5,13},{6,14},{7,15},{8,0},{9,1},... | collective-permute-start | bytes 2359304 | tf_op jit(solution)/shard_map/ppermute | solution.py:52
  550.7 5.0 collective-permute-start.49
  551.9 5.0 collective-permute-start.35
  556.9 7.3 %collective-permute-start.36 = (bf16[512,128]{1,0:T(8,128)(2,1)S(1)}, bf16[512,128]{1,0:T(8,128)(2,1)S(1)}, u32[]{:S(2)}, u32[]{:S(2)}) collective-permute-start(bf16[512,128]{1,0:T(8,128)(2,1)S(1)} %add_convert_fusion), channel_id=1, source_target_pairs={{0,4},{1,5},{2,6},{3,7},{4,0},{5,1},{6,2},{7,3},{8,12},{9,13},{10,... | collective-permute-start | bytes 393224 | tf_op jit(solution)/shard_map/ppermute | solution.py:52
  565.0 7.9 %collective-permute-start.39 = (bf16[512,128]{1,0:T(8,128)(2,1)S(1)}, bf16[512,128]{1,0:T(8,128)(2,1)S(1)}, u32[]{:S(2)}, u32[]{:S(2)}) collective-permute-start(bf16[512,128]{1,0:T(8,128)(2,1)S(1)} %fusion.6), channel_id=1, source_target_pairs={{0,16},{1,17},{2,18},{3,19},{4,20},{5,21},{6,22},{7,23},{8,24},{9,... | collective-permute-start | bytes 393224 | tf_op jit(solution)/shard_map/ppermute | solution.py:52
  (47 other events, 435.5 us)
Sparse Core Ops, SparseCore 0:
  12.5 142.5 all-gather.6
  158.1 75.5 all-gather.8
  477.9 66.4 all-gather.10

commit v6 on v5

--- a/solution.py
+++ b/solution.py
@@ -1018,7 +1018,7 @@
                 out_specs=[pl.BlockSpec(memory_space=pltpu.VMEM)] * (lead + 1),
                 out_shape=[shape_of(*((width, 4 * units) if t else (4 * units, width))) for t in turns] + [shape_of(8, 128)],
                 cost_estimate=cost(5),
-            )(jnp.stack([grid.bit(grid.core), grid.bit(grid.xs[0])]).astype(jnp.int32), part, from_x, from_c)
+            )(grid.turns, part, from_x, from_c)
         )
     return results
 
@@ -1126,9 +1126,7 @@
     masks = [grid.core, *grid.tensor, *grid.xs]
     for mask in masks:
         parts = jnp.concatenate([parts, grid.swap(parts, mask)])
-    devices = jnp.arange(grid.count) ^ grid.index
-    place = sum(((devices // mask) % 2) << k for k, mask in enumerate(masks)).astype(jnp.int32)
-    return parts.reshape(grid.count, *part.shape), place
+    return parts.reshape(grid.count, *part.shape), grid.place
 
 
 def tied(v, token):
@@ -1202,7 +1200,14 @@
     flags = jnp.where(offsets[None] == 0, 1, resets).astype(jnp.int32)
     sel = jnp.stack([grid.bit(m) ^ i for m in [*grid.tensor, *grid.xs] for i in (0, 1)]).astype(jnp.int32)
     places = [jnp.stack([2 * x + c for x in range(n_x)]).astype(jnp.int32) for c in (core, 1 - core)]
-    flags, grid.sel, places, which = lax.optimization_barrier((flags, sel, places, which))
+    devices = jnp.arange(grid.count) ^ grid.index
+    place = sum(
+        ((devices // mask) % 2) << k for k, mask in enumerate([grid.core, *grid.tensor, *grid.xs])
+    ).astype(jnp.int32)
+    turns = jnp.stack([core, x_at % 2]).astype(jnp.int32)
+    flags, grid.sel, places, which, grid.place, grid.turns = lax.optimization_barrier(
+        (flags, sel, places, which, place, turns)
+    )
     for p, w in zip(pieces, which):
         p.which = w
     tile = lambda a: a.T.reshape(heads, 8, 128)
@@ -1365,7 +1370,7 @@
     if (part_v, part_f, n_x) == (64, 128, 2):
         by_kind = [r[k] for k in range(1, 4) for r in results]
         packed = run_pack(
-            jnp.stack([core, x_at]).astype(jnp.int32), token_v,
+            grid.turns, token_v,
             [
                 *by_kind, *[r[4] for r in results], *[r[5] for r in results], sum_gates, sums_shared, sum_ffn_gain, sum_out,
                 back[0][2], back[1][2], back[0][1], back[1][1], *sum_in,

time: 591 us -> 588 us (level)
  no operation moved by 1% of the time
where the time goes in v6:
time: 588 us; the launch traced here: 584 us
  Pallas kernels  284 us (48%)
  waiting for transfers between devices  168 us (29%)
  starting transfers between devices  58.5 us (10%)
  local copies, waits for them, and re-layouts  28 us (5%)
  other arithmetic  23.3 us (4%)
  between operations  15.3 us (3%)
  matrix products  6.91 us (1%)
    pallas_call x7, Pallas kernels, blocked(): pl.pallas_call(body, grid_spec=pltpu.PrefetchScalarGridSpec(num_scalar_pr...  112 us
    all_gather x1, waiting for transfers between devices, local(): gathered = lax.all_gather(seed, AXES, axis=0)  74.6 us
    ppermute x54, waiting for transfers between devices, swap(): return lax.ppermute(value, AXES, [(i, i ^ mask) for i in range(self.count)])  67.5 us
    ppermute x54, starting transfers between devices, swap(): return lax.ppermute(value, AXES, [(i, i ^ mask) for i in range(self.count)])  58.4 us
    pallas_call x10, Pallas kernels, run_point(): pl.pallas_call(body, grid_spec=pltpu.PrefetchScalarGridSpec(num_scalar_pr...  45.9 us
    pallas_call x2, Pallas kernels, run_back(): pl.pallas_call(partial(back_kernel, m), grid=(1,), in_specs=[pl.BlockSpec...  39.2 us
    all_gather x1, waiting for transfers between devices, local(): gathered_out = lax.all_gather(own(w_out, half_f, 0), AXES, axis=0)  26.2 us
    pallas_call x2, Pallas kernels, call(): pl.pallas_call(kernel, out_shape=outs, in_specs=[pl.BlockSpec(memory_spac...  24.4 us
  transfers between devices with their start and end apart: 57, of which 19 were waited for; matrix products, arithmetic and copies ran while one was open for 7% of the time, Pallas kernels for 44%

profile of v6, /device:TPU:0, one launch (start us, length us, event | category | flops | bytes accessed | tf_op | source)
XLA Modules:
  0.0 584.0 jit_solution(10351865937746849396)
XLA Ops:
  16.6 11.7 %shard_map.390 = (f32[4096,128]{1,0:T(8,128)}, bf16[512,1024]{1,0:T(8,128)(2,1)}, f32[2,16,8,128]{3,2,1,0:T(8,128)}) custom-call(s32[2,256]{1,0:T(2,128)} %copy-done.37, bf16[512,1024]{1,0:T(8,128)(2,1)} %bitcast.236, f32[1,1024]{1,0:T(1,128)} %bitcast.284, f32[16,8,128]{2,1,0:T(8,128)} %bitcast.244, f32[16,8,128]{2,1,0:T(8,128)} %bitcast.261), custom_call_target="tpu_custom_call" | custom-call | flops 13799999488 | bytes 39600000 | tf_op jit(solution)/shard_map/pallas_call | solution.py:710
  29.9 3.0 collective-permute-start
  32.9 1.7 constant_dynamic-slice_fusion
  34.7 1.9 collective-permute-done
  37.7 1.9 collective-permute-start.1
  39.6 5.1 collective-permute-done.1
  44.7 2.3 collective-permute-start.2
  48.6 8.4 %collective-permute-done.2 = f32[2,17,8,128]{3,2,1,0:T(8,128)S(1)} collective-permute-done((f32[2,17,8,128]{3,2,1,0:T(8,128)S(1)}, f32[2,17,8,128]{3,2,1,0:T(8,128)S(1)}, u32[]{:S(2)}, u32[]{:S(2)}) %collective-permute-start.2) | collective-permute-done | bytes 139296 | tf_op jit(solution)/shard_map/ppermute | solution.py:52
  57.8 12.7 %shard_map.391 = (f32[512,1024]{1,0:T(8,128)}, bf16[512,1024]{1,0:T(8,128)(2,1)}) custom-call(s32[2,256]{1,0:T(2,128)} %copy-done.37, f32[4096,128]{1,0:T(8,128)} %get-tuple-element.154.normed_ref, f32[2,16,8,128]{3,2,1,0:T(8,128)} %add_select_fusion.2.start_ref, f32[16,8,128]{2,1,0:T(8,128)} %bitcast.245, f32[16,8,128]{2,1,0:T(8,128)} %bitcast.262, ...), custom_call_target="tpu_custom_call" | custom-call | flops 13799999488 | bytes 39600000 | tf_op jit(solution)/shard_map/pallas_call | solution.py:710
  70.5 5.3 convolution_add_fusion.gate_ref
  75.8 2.1 copy-done.4
  79.9 74.6 %all-gather.7.cloned.1.call-done = bf16[10496,1024]{1,0:T(8,128)(2,1)} async-done(((bf16[328,1024]{1,0:T(8,128)(2,1)}), bf16[10496,1024]{1,0:T(8,128)(2,1)}) %all-gather.7.cloned.1.call-update) | async-done | bytes 21495824 | tf_op jit(solution)/shard_map/all_gather | solution.py:1176
  158.5 17.2 %shard_map.392 = (f32[512,2048]{1,0:T(8,128)}, f32[512,2048]{1,0:T(8,128)}, f32[512,2048]{1,0:T(8,128)}, bf16[512,2048]{1,0:T(8,128)(2,1)}, f32[512,1024]{1,0:T(8,128)}) custom-call(s32[4]{0:T(128)} %pad_add_fusion.5.piece, f32[1,2048]{1,0:T(1,128)} %pad_maximum_fusion.19.before.refs_6_, bf16[512,1024]{1,0:T(8,128)(2,1)} %get-tuple-element.157.refs_0_.refs_1_, ...), custom_call_target="tpu_custom_call" | custom-call | flops 230000001024 | bytes 660000000 | tf_op jit(solution)/shard_map/pallas_call | solution.py:626
  175.7 5.7 shard_map.393
  181.4 10.0 %shard_map.394 = (f32[512,2048]{1,0:T(8,128)}, bf16[512,2048]{1,0:T(8,128)(2,1)}, bf16[2,1,2048,512]{3,2,1,0:T(8,128)(2,1)}) custom-call(s32[2]{0:T(128)} %copy-done.42, f32[1,2048]{1,0:T(1,128)} %bitcast.271, bf16[512,1024]{1,0:T(8,128)(2,1)} %get-tuple-element.159.refs_0_, bf16[512,1024]{1,0:T(8,128)(2,1)} %bitcast.231, bf16[32,328,1024]{2,1,0:T(8,128)(2,1)} %bitcast.218, ...), custom_call_target="tpu_custom_call" | custom-call | flops 230000001024 | bytes 660000000 | tf_op jit(solution)/shard_map/pallas_call | solution.py:626
  191.7 9.9 %shard_map.395 = (f32[512,2048]{1,0:T(8,128)}, bf16[512,2048]{1,0:T(8,128)(2,1)}, bf16[2,1,2048,512]{3,2,1,0:T(8,128)(2,1)}) custom-call(s32[2]{0:T(128)} %copy-done.46, bf16[512,2048]{1,0:T(8,128)(2,1)} %get-tuple-element.160.before.refs_5_, bf16[512,1024]{1,0:T(8,128)(2,1)} %get-tuple-element.159.refs_0_, bf16[512,1024]{1,0:T(8,128)(2,1)} %bitcast.232, ...), custom_call_target="tpu_custom_call" | custom-call | flops 230000001024 | bytes 660000000 | tf_op jit(solution)/shard_map/pallas_call | solution.py:626
  201.6 5.2 shard_map.396
  206.8 26.2 %all-gather.9.cloned.1.call-done = bf16[4096,1024]{1,0:T(8,128)(2,1)} async-done(((bf16[128,1024]{1,0:T(8,128)(2,1)}), bf16[4096,1024]{1,0:T(8,128)(2,1)}) %all-gather.9.cloned.1.call-update) | async-done | bytes 8388624 | tf_op jit(solution)/shard_map/all_gather | solution.py:1177
  235.0 19.0 %shard_map.397 = (bf16[2,1,2048,512]{3,2,1,0:T(8,128)(2,1)}, f32[1,2048]{1,0:T(1,128)}, f32[512,1024]{1,0:T(8,128)}, f32[512,1024]{1,0:T(8,128)}) custom-call(s32[2]{0:T(128)} %copy-done.42, f32[8,128]{1,0:T(8,128)} %get-tuple-element.166.before, bf16[512,1024]{1,0:T(8,128)(2,1)} %get-tuple-element.159.refs_0_, bf16[512,1024]{1,0:T(8,128)(2,1)} %bitcast.233, ...), custom_call_target="tpu_custom_call" | custom-call | flops 230000001024 | bytes 660000000 | tf_op jit(solution)/shard_map/pallas_call | solution.py:626
  254.0 4.5 collective-permute-done.4.refs_3_.refs_2_.refs_29_.refs_27_
  259.7 3.8 shard_map.398
  265.6 20.6 %shard_map.399 = (bf16[2,1,2048,512]{3,2,1,0:T(8,128)(2,1)}, f32[1,2048]{1,0:T(1,128)}, f32[512,1024]{1,0:T(8,128)}, f32[512,1024]{1,0:T(8,128)}) custom-call(s32[2]{0:T(128)} %copy-done.46, f32[8,128]{1,0:T(8,128)} %get-tuple-element.173.before, bf16[512,1024]{1,0:T(8,128)(2,1)} %get-tuple-element.159.refs_0_, bf16[512,1024]{1,0:T(8,128)(2,1)} %bitcast.234, ...), custom_call_target="tpu_custom_call" | custom-call | flops 230000001024 | bytes 660000000 | tf_op jit(solution)/shard_map/pallas_call | solution.py:626
  286.2 5.1 shard_map.400
  291.4 10.5 %shard_map.401 = (bf16[512,1024]{1,0:T(8,128)(2,1)}, f32[512,1024]{1,0:T(8,128)}, bf16[512,2048]{1,0:T(8,128)(2,1)}, f32[8,1024]{1,0:T(8,128)}, f32[8,1024]{1,0:T(8,128)}, /*index=5*/f32[8,2048]{1,0:T(8,128)}) custom-call(f32[8,128]{1,0:T(8,128)} %get-tuple-element.180.before, f32[512,2176]{1,0:T(8,128)} %copy-done.4, ...), custom_call_target="tpu_custom_call" | custom-call | flops 1150000000 | bytes 3300000 | tf_op jit(solution)/shard_map/pallas_call | solution.py:544
  301.8 4.9 shard_map.402.before
  308.7 1.9 collective-permute-start.9
  310.6 2.3 copy.58
  312.9 4.9 shard_map.403.before
  317.9 17.7 %shard_map.404 = (bf16[2,3,1024,512]{3,2,1,0:T(8,128)(2,1)}, f32[1,1024]{1,0:T(1,128)}, f32[1,1024]{1,0:T(1,128)}, f32[512,1024]{1,0:T(8,128)}, f32[512,1024]{1,0:T(8,128)}, /*index=5*/f32[4,128,128]{2,1,0:T(8,128)}) custom-call(s32[2]{0:T(128)} %copy-done.42, bf16[2,1,512,1024]{3,2,1,0:T(8,128)(2,1)} %shard_map.403.before, ...), custom_call_target="tpu_custom_call" | custom-call | flops 1150000000 | bytes 3300000 | tf_op jit(solution)/shard_map/pallas_call | solution.py:626
  337.4 4.5 shard_map.405
  346.0 17.2 %shard_map.406 = (bf16[2,3,1024,512]{3,2,1,0:T(8,128)(2,1)}, f32[1,1024]{1,0:T(1,128)}, f32[1,1024]{1,0:T(1,128)}, f32[512,1024]{1,0:T(8,128)}, f32[512,1024]{1,0:T(8,128)}, /*index=5*/f32[4,128,128]{2,1,0:T(8,128)}) custom-call(s32[2]{0:T(128)} %copy-done.46, f32[8,128]{1,0:T(8,128)} %get-tuple-element.197.before, ...), custom_call_target="tpu_custom_call" | custom-call | flops 230000001024 | bytes 660000000 | tf_op jit(solution)/shard_map/pallas_call | solution.py:626
  363.2 4.9 collective-permute-done.16.refs_14_.refs_20_.refs_16_
  368.2 6.6 %shard_map.407 = (bf16[3,2,2,2,64,512]{5,4,3,2,1,0:T(8,128)(2,1)}, bf16[3,2,2,2,64,512]{5,4,3,2,1,0:T(8,128)(2,1)}, bf16[1,2,2,32,1024]{4,3,2,1,0:T(8,128)(2,1)}...) custom-call(s32[8]{0:T(128)} %stack.124.p, ...), custom_call_target="tpu_custom_call" | custom-call | flops 1150000000 | bytes 3300000 | tf_op jit(solution)/shard_map/pallas_call | solution.py:950
  379.9 18.3 %shard_map.408 = (f32[4096,128]{1,0:T(8,128)}, f32[2,16,8,128]{3,2,1,0:T(8,128)}, bf16[512,128]{1,0:T(8,128)(2,1)}, f32[8,128]{1,0:T(8,128)}) custom-call(f32[8,128]{1,0:T(8,128)} %get-tuple-element.205.before, s32[2,256]{1,0:T(2,128)} %copy-done.37, f32[4,128,128]{2,1,0:T(8,128)} %get-tuple-element.206.gp0_ref, f32[4,128,128]{2,1,0:T(8,128)} %get-tuple-element.207.gp1_ref, ...), custom_call_target="tpu_custom_call" | custom-call | flops 230000001024 | bytes 660000000 | tf_op jit(solution)/shard_map/pallas_call | solution.py:213
  398.3 2.2 collective-permute-done.18.refs_1_.refs_21_.refs_26_.refs_17_.refs_23_
  400.5 2.9 shard_map.409
  407.0 13.1 %collective-permute-done.21 = f32[2,17,8,128]{3,2,1,0:T(8,128)S(1)} collective-permute-done((f32[2,17,8,128]{3,2,1,0:T(8,128)S(1)}, f32[2,17,8,128]{3,2,1,0:T(8,128)S(1)}, u32[]{:S(2)}, u32[]{:S(2)}) %collective-permute-start.21) | collective-permute-done | bytes 139296 | tf_op jit(solution)/shard_map/ppermute | solution.py:52
  420.3 1.6 collective-permute-start.22
  423.4 2.0 collective-permute-done.22
  425.5 2.0 collective-permute-start.23
  429.1 3.9 collective-permute-done.23
  434.4 5.8 shard_map.410
  440.2 1.5 collective-permute-start.29
  442.4 1.9 collective-permute-start.27
  445.8 19.7 %shard_map.411 = (f32[256,1024]{1,0:T(8,128)}, f32[16,8,128]{2,1,0:T(8,128)}, f32[16,8,128]{2,1,0:T(8,128)}, f32[16,8,128]{2,1,0:T(8,128)}, f32[8,128]{1,0:T(8,1...) custom-call(f32[8,128]{1,0:T(8,128)} %get-tuple-element.219.before, s32[2,256]{1,0:T(2,128)} %copy-done.37, ...), custom_call_target="tpu_custom_call" | custom-call | flops 230000001024 | bytes 660000000 | tf_op jit(solution)/shard_map/pallas_call | solution.py:325
  465.5 5.5 shard_map.412
  473.1 2.3 collective-permute-start.31
  475.5 19.5 %shard_map.413 = (f32[256,1024]{1,0:T(8,128)}, f32[16,8,128]{2,1,0:T(8,128)}, f32[16,8,128]{2,1,0:T(8,128)}, f32[16,8,128]{2,1,0:T(8,128)}, f32[8,128]{1,0:T(8,1...) custom-call(f32[8,128]{1,0:T(8,128)} %get-tuple-element.230.before, s32[2,256]{1,0:T(2,128)} %copy-done.37, ...), custom_call_target="tpu_custom_call" | custom-call | flops 230000001024 | bytes 660000000 | tf_op jit(solution)/shard_map/pallas_call | solution.py:325
  499.2 8.8 %collective-permute-done.31.refs_5_.refs_10_.refs_11_ = bf16[3,2,64,1024]{3,2,1,0:T(8,128)(2,1)} collective-permute-done((bf16[3,2,64,1024]{3,2,1,0:T(8,128)(2,1)}, bf16[3,2,64,1024]{3,2,1,0:T(8,128)(2,1)}, u32[]{:S(2)}, u32[]{:S(2)}) %collective-permute-start.31) | collective-permute-done | bytes 786464 | tf_op jit(solution)/shard_map/ppermute | solution.py:52
  508.0 3.2 shard_map.414
  513.3 1.9 shard_map.415
  516.1 2.9 shard_map.420
  519.8 3.1 shard_map.419
  525.8 3.3 shard_map.416
  532.0 1.6 collective-permute-start.46
  533.6 3.5 collective-permute-done.46
  537.1 2.3 collective-permute-start.47
  539.4 1.9 collective-permute-done.47
  541.3 3.9 collective-permute-start.48
  546.6 1.6 collective-permute-done.48
  551.0 2.3 collective-permute-done.49
  554.4 2.9 collective-permute-start.36
  557.3 3.4 shard_map.417
  563.4 6.9 %shard_map.418 = (f32[1024,2176]{1,0:T(8,128)}, f32[8,128]{1,0:T(8,128)}) custom-call(s32[32]{0:T(128)} %fusion.40.place, bf16[1024,2048]{1,0:T(8,128)(2,1)} %bitcast.280, bf16[32,32,128]{2,1,0:T(8,128)(2,1)} %bitcast.276), custom_call_target="tpu_custom_call" | custom-call | flops 57500000256 | bytes 165000000 | tf_op jit(solution)/shard_map/pallas_call | solution.py:1096
  (312 shorter events, 79.6 us)
Async XLA Ops:
  7.2 147.2 %all-gather.7.cloned.1.call-start = ((), (), s32[]{:S(2)}) async-start(), calls=%async_computation | async-start | bytes 22167552 | tf_op jit(solution)/shard_map/all_gather | solution.py:1176
  12.4 220.5 %all-gather.9.cloned.1.call-start = ((), (), s32[]{:S(2)}) async-start(), calls=%async_computation.1 | async-start | bytes 8650752 | tf_op jit(solution)/shard_map/all_gather | solution.py:1177
  15.1 32.0 %copy-start.42 = (s32[2]{0:T(128)}, s32[2]{0:T(128)S(1)}, u32[]{:S(2)}) copy-start(s32[2]{0:T(128)S(1)} %get-tuple-element.152.piece) | copy-start | bytes 28
  15.1 32.0 %copy-start.46 = (s32[2]{0:T(128)}, s32[2]{0:T(128)S(1)}, u32[]{:S(2)}) copy-start(s32[2]{0:T(128)S(1)} %get-tuple-element.151.piece) | copy-start | bytes 28
  29.9 6.7 %collective-permute-start = (f32[2,17,8,128]{3,2,1,0:T(8,128)S(1)}, f32[2,17,8,128]{3,2,1,0:T(8,128)S(1)}, u32[]{:S(2)}, u32[]{:S(2)}) collective-permute-start(f32[2,17,8,128]{3,2,1,0:T(8,128)S(1)} %pad_maximum_fusion.5), channel_id=1, source_target_pairs={{0,1},{1,0},{2,3},{3,2},{4,5},{5,4},{6,7},{7,6},{8,9},{9,8},{10,11... | collective-permute-start | bytes 417800 | tf_op jit(solution)/shard_map/ppermute | solution.py:52
  34.6 528.8 %all-gather.11.cloned.1.call-start = ((), (), s32[]{:S(2)}) async-start(), calls=%async_computation.2 | async-start | bytes 4325376 | tf_op jit(solution)/shard_map/all_gather | solution.py:1360
  34.7 35.7 %copy-start.7 = (f32[16,8,128]{2,1,0:T(8,128)}, f32[16,8,128]{2,1,0:T(8,128)S(1)}, u32[]{:S(2)}) copy-start(f32[16,8,128]{2,1,0:T(8,128)S(1)} %get-tuple-element.300) | copy-start | bytes 196612
  34.7 35.7 %copy-start.9 = (f32[16,8,128]{2,1,0:T(8,128)}, f32[16,8,128]{2,1,0:T(8,128)S(1)}, u32[]{:S(2)}) copy-start(f32[16,8,128]{2,1,0:T(8,128)S(1)} %get-tuple-element.299) | copy-start | bytes 196612
  37.7 7.0 %collective-permute-start.1 = (f32[2,17,8,128]{3,2,1,0:T(8,128)S(1)}, f32[2,17,8,128]{3,2,1,0:T(8,128)S(1)}, u32[]{:S(2)}, u32[]{:S(2)}) collective-permute-start(f32[2,17,8,128]{3,2,1,0:T(8,128)S(1)} %pad_maximum_fusion.6), channel_id=1, source_target_pairs={{0,2},{1,3},{2,0},{3,1},{4,6},{5,7},{6,4},{7,5},{8,10},{9,11},{10,... | collective-permute-start | bytes 417800 | tf_op jit(solution)/shard_map/ppermute | solution.py:52
  44.7 12.3 %collective-permute-start.2 = (f32[2,17,8,128]{3,2,1,0:T(8,128)S(1)}, f32[2,17,8,128]{3,2,1,0:T(8,128)S(1)}, u32[]{:S(2)}, u32[]{:S(2)}) collective-permute-start(f32[2,17,8,128]{3,2,1,0:T(8,128)S(1)} %pad_maximum_fusion.7), channel_id=1, source_target_pairs={{0,4},{1,5},{2,6},{3,7},{4,0},{5,1},{6,2},{7,3},{8,12},{9,13},{10,... | collective-permute-start | bytes 417800 | tf_op jit(solution)/shard_map/ppermute | solution.py:52
  78.6 75.8 %copy-start.29 = (bf16[512,128]{1,0:T(8,128)(2,1)}, bf16[512,128]{1,0:T(8,128)(2,1)S(1)}, u32[]{:S(2)}) copy-start(bf16[512,128]{1,0:T(8,128)(2,1)S(1)} %get-tuple-element.268.key_ref) | copy-start | bytes 393220
  78.6 97.0 %copy-start.16 = (f32[512,128]{1,0:T(8,128)}, f32[512,128]{1,0:T(8,128)S(1)}, u32[]{:S(2)}) copy-start(f32[512,128]{1,0:T(8,128)S(1)} %get-tuple-element.269.shared_ref) | copy-start | bytes 786436
  78.7 75.8 %copy-start.30 = (bf16[512,128]{1,0:T(8,128)(2,1)}, bf16[512,128]{1,0:T(8,128)(2,1)S(1)}, u32[]{:S(2)}) copy-start(bf16[512,128]{1,0:T(8,128)(2,1)S(1)} %add_convert_fusion.2.query_ref) | copy-start | bytes 393220
  191.4 10.2 %collective-permute-start.3 = (bf16[2,1,2,2,2,2,128,512]{7,6,5,4,3,2,1,0:T(8,128)(2,1)}, bf16[2,1,2,2,2,2,128,512]{7,6,5,4,3,2,1,0:T(8,128)(2,1)}, u32[]{:S(2)}, u32[]{:S(2)}) collective-permute-start(bf16[2,1,2,2,2,2,128,512]{7,6,5,4,3,2,1,0:T(8,128)(2,1)} %bitcast.282), channel_id=1, source_target_pairs={{0,8},{1,9},{2,10},{3,11},{4,12},{5,13},{6,14},{7,15},{8,0},{9,1},... | collective-permute-start | bytes 12582920 | tf_op jit(solution)/shard_map/ppermute | solution.py:52
  232.9 25.6 %collective-permute-start.4 = (bf16[1,2,2,2,128,512]{5,4,3,2,1,0:T(8,128)(2,1)}, bf16[1,2,2,2,128,512]{5,4,3,2,1,0:T(8,128)(2,1)}, u32[]{:S(2)}, u32[]{:S(2)}) collective-permute-start(bf16[1,2,2,2,128,512]{5,4,3,2,1,0:T(8,128)(2,1)} %get-tuple-element.165), channel_id=1, source_target_pairs={{0,16},{1,17},{2,18},{3,19},{4,20},{5,21},{6,22},{7,23},{8,24},{9,... | collective-permute-start | bytes 3145736 | tf_op jit(solution)/shard_map/ppermute | solution.py:52
  234.3 25.4 %collective-permute-start.5 = (bf16[1,2,2,2,128,512]{5,4,3,2,1,0:T(8,128)(2,1)}, bf16[1,2,2,2,128,512]{5,4,3,2,1,0:T(8,128)(2,1)}, u32[]{:S(2)}, u32[]{:S(2)}) collective-permute-start(bf16[1,2,2,2,128,512]{5,4,3,2,1,0:T(8,128)(2,1)} %get-tuple-element.170), channel_id=1, source_target_pairs={{0,1},{1,0},{2,3},{3,2},{4,5},{5,4},{6,7},{7,6},{8,9},{9,8},{10,11... | collective-permute-start | bytes 3145736 | tf_op jit(solution)/shard_map/ppermute | solution.py:52
  253.9 32.3 %collective-permute-start.8 = (bf16[2,1,2,2,2,2,128,512]{7,6,5,4,3,2,1,0:T(8,128)(2,1)}, bf16[2,1,2,2,2,2,128,512]{7,6,5,4,3,2,1,0:T(8,128)(2,1)}, u32[]{:S(2)}, u32[]{:S(2)}) collective-permute-start(bf16[2,1,2,2,2,2,128,512]{7,6,5,4,3,2,1,0:T(8,128)(2,1)} %bitcast.281), channel_id=1, source_target_pairs={{0,8},{1,9},{2,10},{3,11},{4,12},{5,13},{6,14},{7,15},{8,0},{9,1},... | collective-permute-start | bytes 12582920 | tf_op jit(solution)/shard_map/ppermute | solution.py:52
  263.5 22.8 %collective-permute-start.6 = (bf16[1,2,2,128,512]{4,3,2,1,0:T(8,128)(2,1)}, bf16[1,2,2,128,512]{4,3,2,1,0:T(8,128)(2,1)}, u32[]{:S(2)}, u32[]{:S(2)}) collective-permute-start(bf16[1,2,2,128,512]{4,3,2,1,0:T(8,128)(2,1)} %get-tuple-element.171), channel_id=1, source_target_pairs={{0,1},{1,0},{2,3},{3,2},{4,5},{5,4},{6,7},{7,6},{8,9},{9,8},{10,11... | collective-permute-start | bytes 1572872 | tf_op jit(solution)/shard_map/ppermute | solution.py:52
  264.1 22.1 %collective-permute-start.7 = (bf16[1,2,2,128,512]{4,3,2,1,0:T(8,128)(2,1)}, bf16[1,2,2,128,512]{4,3,2,1,0:T(8,128)(2,1)}, u32[]{:S(2)}, u32[]{:S(2)}) collective-permute-start(bf16[1,2,2,128,512]{4,3,2,1,0:T(8,128)(2,1)} %get-tuple-element.172), channel_id=1, source_target_pairs={{0,16},{1,17},{2,18},{3,19},{4,20},{5,21},{6,22},{7,23},{8,24},{9,... | collective-permute-start | bytes 1572872 | tf_op jit(solution)/shard_map/ppermute | solution.py:52
  306.7 28.9 %collective-permute-start.12 = (bf16[2,1,2,2,2,2,32,1024]{7,6,5,4,3,2,1,0:T(8,128)(2,1)}, bf16[2,1,2,2,2,2,32,1024]{7,6,5,4,3,2,1,0:T(8,128)(2,1)S(1)}, u32[]{:S(2)}, u32[]{:S(2)}) collective-permute-start(bf16[2,1,2,2,2,2,32,1024]{7,6,5,4,3,2,1,0:T(8,128)(2,1)} %bitcast.229), channel_id=1, source_target_pairs={{0,8},{1,9},{2,10},{3,11},{4,12},{5,13},{6,14},{7,15},{8,0},{9,1},... | collective-permute-start | bytes 6291464 | tf_op jit(solution)/shard_map/ppermute | solution.py:52
  306.7 28.9 %collective-permute-start.10 = (bf16[1,2,2,2,128,512]{5,4,3,2,1,0:T(8,128)(2,1)}, bf16[1,2,2,2,128,512]{5,4,3,2,1,0:T(8,128)(2,1)S(1)}, u32[]{:S(2)}, u32[]{:S(2)}) collective-permute-start(bf16[1,2,2,2,128,512]{5,4,3,2,1,0:T(8,128)(2,1)} %get-tuple-element.195), channel_id=1, source_target_pairs={{0,16},{1,17},{2,18},{3,19},{4,20},{5,21},{6,22},{7,23},{8,24},{9,... | collective-permute-start | bytes 3145736 | tf_op jit(solution)/shard_map/ppermute | solution.py:52
  307.3 28.4 %collective-permute-start.11 = (bf16[1,2,2,2,128,512]{5,4,3,2,1,0:T(8,128)(2,1)}, bf16[1,2,2,2,128,512]{5,4,3,2,1,0:T(8,128)(2,1)}, u32[]{:S(2)}, u32[]{:S(2)}) collective-permute-start(bf16[1,2,2,2,128,512]{5,4,3,2,1,0:T(8,128)(2,1)} %get-tuple-element.196), channel_id=1, source_target_pairs={{0,1},{1,0},{2,3},{3,2},{4,5},{5,4},{6,7},{7,6},{8,9},{9,8},{10,11... | collective-permute-start | bytes 3145736 | tf_op jit(solution)/shard_map/ppermute | solution.py:52
  308.7 26.9 %collective-permute-start.9 = (bf16[1,2,128,1024]{3,2,1,0:T(8,128)(2,1)}, bf16[1,2,128,1024]{3,2,1,0:T(8,128)(2,1)}, u32[]{:S(2)}, u32[]{:S(2)}) collective-permute-start(bf16[1,2,128,1024]{3,2,1,0:T(8,128)(2,1)} %get-tuple-element.194), channel_id=1, source_target_pairs={{0,4},{1,5},{2,6},{3,7},{4,0},{5,1},{6,2},{7,3},{8,12},{9,13},{10,... | collective-permute-start | bytes 1572872 | tf_op jit(solution)/shard_map/ppermute | solution.py:52
  335.6 32.6 %collective-permute-start.13 = (bf16[2,3,2,2,2,2,64,512]{7,6,5,4,3,2,1,0:T(8,128)(2,1)}, bf16[2,3,2,2,2,2,64,512]{7,6,5,4,3,2,1,0:T(8,128)(2,1)}, u32[]{:S(2)}, u32[]{:S(2)}) collective-permute-start(bf16[2,3,2,2,2,2,64,512]{7,6,5,4,3,2,1,0:T(8,128)(2,1)} %bitcast.279), channel_id=1, source_target_pairs={{0,8},{1,9},{2,10},{3,11},{4,12},{5,13},{6,14},{7,15},{8,0},{9,1},... | collective-permute-start | bytes 18874376 | tf_op jit(solution)/shard_map/ppermute | solution.py:52
  341.9 21.3 %collective-permute-start.14 = (bf16[1,2,2,2,32,1024]{5,4,3,2,1,0:T(8,128)(2,1)}, bf16[1,2,2,2,32,1024]{5,4,3,2,1,0:T(8,128)(2,1)}, u32[]{:S(2)}, u32[]{:S(2)}) collective-permute-start(bf16[1,2,2,2,32,1024]{5,4,3,2,1,0:T(8,128)(2,1)} %get-tuple-element.201), channel_id=1, source_target_pairs={{0,16},{1,17},{2,18},{3,19},{4,20},{5,21},{6,22},{7,23},{8,24},{9,... | collective-permute-start | bytes 1572872 | tf_op jit(solution)/shard_map/ppermute | solution.py:52
  342.6 20.6 %collective-permute-start.15 = (bf16[1,2,2,2,32,1024]{5,4,3,2,1,0:T(8,128)(2,1)}, bf16[1,2,2,2,32,1024]{5,4,3,2,1,0:T(8,128)(2,1)}, u32[]{:S(2)}, u32[]{:S(2)}) collective-permute-start(bf16[1,2,2,2,32,1024]{5,4,3,2,1,0:T(8,128)(2,1)} %get-tuple-element.202), channel_id=1, source_target_pairs={{0,1},{1,0},{2,3},{3,2},{4,5},{5,4},{6,7},{7,6},{8,9},{9,8},{10,11... | collective-permute-start | bytes 1572872 | tf_op jit(solution)/shard_map/ppermute | solution.py:52
  344.1 24.1 %collective-permute-start.16 = (bf16[1,2,2,128,512]{4,3,2,1,0:T(8,128)(2,1)}, bf16[1,2,2,128,512]{4,3,2,1,0:T(8,128)(2,1)}, u32[]{:S(2)}, u32[]{:S(2)}) collective-permute-start(bf16[1,2,2,128,512]{4,3,2,1,0:T(8,128)(2,1)} %get-tuple-element.203), channel_id=1, source_target_pairs={{0,1},{1,0},{2,3},{3,2},{4,5},{5,4},{6,7},{7,6},{8,9},{9,8},{10,11... | collective-permute-start | bytes 1572872 | tf_op jit(solution)/shard_map/ppermute | solution.py:52
  344.6 23.6 %collective-permute-start.17 = (bf16[1,2,2,128,512]{4,3,2,1,0:T(8,128)(2,1)}, bf16[1,2,2,128,512]{4,3,2,1,0:T(8,128)(2,1)}, u32[]{:S(2)}, u32[]{:S(2)}) collective-permute-start(bf16[1,2,2,128,512]{4,3,2,1,0:T(8,128)(2,1)} %get-tuple-element.204), channel_id=1, source_target_pairs={{0,16},{1,17},{2,18},{3,19},{4,20},{5,21},{6,22},{7,23},{8,24},{9,... | collective-permute-start | bytes 1572872 | tf_op jit(solution)/shard_map/ppermute | solution.py:52
  374.8 25.7 %collective-permute-start.18 = (bf16[1,2,128,1024]{3,2,1,0:T(8,128)(2,1)}, bf16[1,2,128,1024]{3,2,1,0:T(8,128)(2,1)}, u32[]{:S(2)}, u32[]{:S(2)}) collective-permute-start(bf16[1,2,128,1024]{3,2,1,0:T(8,128)(2,1)} %get-tuple-element.212), channel_id=1, source_target_pairs={{0,4},{1,5},{2,6},{3,7},{4,0},{5,1},{6,2},{7,3},{8,12},{9,13},{10,... | collective-permute-start | bytes 1572872 | tf_op jit(solution)/shard_map/ppermute | solution.py:52
  375.9 22.4 %collective-permute-start.19 = (bf16[1,2,2,32,1024]{4,3,2,1,0:T(8,128)(2,1)}, bf16[1,2,2,32,1024]{4,3,2,1,0:T(8,128)(2,1)}, u32[]{:S(2)}, u32[]{:S(2)}) collective-permute-start(bf16[1,2,2,32,1024]{4,3,2,1,0:T(8,128)(2,1)} %get-tuple-element.213), channel_id=1, source_target_pairs={{0,1},{1,0},{2,3},{3,2},{4,5},{5,4},{6,7},{7,6},{8,9},{9,8},{10,11... | collective-permute-start | bytes 786440 | tf_op jit(solution)/shard_map/ppermute | solution.py:52
  377.4 20.9 %collective-permute-start.20 = (bf16[1,2,2,32,1024]{4,3,2,1,0:T(8,128)(2,1)}, bf16[1,2,2,32,1024]{4,3,2,1,0:T(8,128)(2,1)}, u32[]{:S(2)}, u32[]{:S(2)}) collective-permute-start(bf16[1,2,2,32,1024]{4,3,2,1,0:T(8,128)(2,1)} %get-tuple-element.214), channel_id=1, source_target_pairs={{0,16},{1,17},{2,18},{3,19},{4,20},{5,21},{6,22},{7,23},{8,24},{9,... | collective-permute-start | bytes 786440 | tf_op jit(solution)/shard_map/ppermute | solution.py:52
  377.9 55.8 %collective-permute-start.24 = (bf16[3,2,2,2,64,512]{5,4,3,2,1,0:T(8,128)(2,1)}, bf16[3,2,2,2,64,512]{5,4,3,2,1,0:T(8,128)(2,1)}, u32[]{:S(2)}, u32[]{:S(2)}) collective-permute-start(bf16[3,2,2,2,64,512]{5,4,3,2,1,0:T(8,128)(2,1)} %get-tuple-element.216), channel_id=1, source_target_pairs={{0,16},{1,17},{2,18},{3,19},{4,20},{5,21},{6,22},{7,23},{8,24},{9,... | collective-permute-start | bytes 4718600 | tf_op jit(solution)/shard_map/ppermute | solution.py:52
  379.4 54.3 %collective-permute-start.25 = (bf16[3,2,2,2,64,512]{5,4,3,2,1,0:T(8,128)(2,1)}, bf16[3,2,2,2,64,512]{5,4,3,2,1,0:T(8,128)(2,1)}, u32[]{:S(2)}, u32[]{:S(2)}) collective-permute-start(bf16[3,2,2,2,64,512]{5,4,3,2,1,0:T(8,128)(2,1)} %get-tuple-element.217), channel_id=1, source_target_pairs={{0,1},{1,0},{2,3},{3,2},{4,5},{5,4},{6,7},{7,6},{8,9},{9,8},{10,11... | collective-permute-start | bytes 4718600 | tf_op jit(solution)/shard_map/ppermute | solution.py:52
  404.9 15.2 %collective-permute-start.21 = (f32[2,17,8,128]{3,2,1,0:T(8,128)S(1)}, f32[2,17,8,128]{3,2,1,0:T(8,128)S(1)}, u32[]{:S(2)}, u32[]{:S(2)}) collective-permute-start(f32[2,17,8,128]{3,2,1,0:T(8,128)S(1)} %pad_maximum_fusion.4), channel_id=1, source_target_pairs={{0,1},{1,0},{2,3},{3,2},{4,5},{5,4},{6,7},{7,6},{8,9},{9,8},{10,11... | collective-permute-start | bytes 417800 | tf_op jit(solution)/shard_map/ppermute | solution.py:52
  406.4 27.3 %collective-permute-start.26 = (bf16[1,2,32,2048]{3,2,1,0:T(8,128)(2,1)}, bf16[1,2,32,2048]{3,2,1,0:T(8,128)(2,1)S(1)}, u32[]{:S(2)}, u32[]{:S(2)}) collective-permute-start(bf16[1,2,32,2048]{3,2,1,0:T(8,128)(2,1)} %get-tuple-element.218), channel_id=1, source_target_pairs={{0,4},{1,5},{2,6},{3,7},{4,0},{5,1},{6,2},{7,3},{8,12},{9,13},{10,... | collective-permute-start | bytes 786440 | tf_op jit(solution)/shard_map/ppermute | solution.py:52
  406.9 15.0 %collective-permute-start.40 = (bf16[2,1,2,2,2,32,128]{6,5,4,3,2,1,0:T(8,128)(2,1)S(1)}, bf16[2,1,2,2,2,32,128]{6,5,4,3,2,1,0:T(8,128)(2,1)S(1)}, u32[]{:S(2)}, u32[]{:S(2)}) collective-permute-start(bf16[2,1,2,2,2,32,128]{6,5,4,3,2,1,0:T(8,128)(2,1)S(1)} %dynamic-slice_convert_fusion), channel_id=1, source_target_pairs={{0,8},{1,9},{2,10},{3,11},{4,12},{5,13},{6,14},{7,15},{8,0},{9,1},... | collective-permute-start | bytes 393224 | tf_op jit(solution)/shard_map/ppermute | solution.py:52
  420.3 5.1 collective-permute-start.22
  421.9 5.5 collective-permute-start.41
  425.5 7.5 %collective-permute-start.23 = (f32[2,17,8,128]{3,2,1,0:T(8,128)S(1)}, f32[2,17,8,128]{3,2,1,0:T(8,128)S(1)}, u32[]{:S(2)}, u32[]{:S(2)}) collective-permute-start(f32[2,17,8,128]{3,2,1,0:T(8,128)S(1)} %pad_maximum_fusion.9), channel_id=1, source_target_pairs={{0,4},{1,5},{2,6},{3,7},{4,0},{5,1},{6,2},{7,3},{8,12},{9,13},{10,... | collective-permute-start | bytes 417800 | tf_op jit(solution)/shard_map/ppermute | solution.py:52
  427.5 16.9 %collective-permute-start.42 = (bf16[1,1,2,2,1,32,128]{6,5,4,3,2,1,0:T(8,128)(2,1)S(1)}, bf16[1,1,2,2,1,32,128]{6,5,4,3,2,1,0:T(8,128)(2,1)S(1)}, u32[]{:S(2)}, u32[]{:S(2)}) collective-permute-start(bf16[1,1,2,2,1,32,128]{6,5,4,3,2,1,0:T(8,128)(2,1)S(1)} %dynamic-slice_convert_fusion.2), channel_id=1, source_target_pairs={{0,1},{1,0},{2,3},{3,2},{4,5},{5,4},{6,7},{7,6},{8,9},{9,8},{10,11... | collective-permute-start | bytes 98312 | tf_op jit(solution)/shard_map/ppermute | solution.py:52
  440.2 25.3 %collective-permute-start.29 = (bf16[3,2,2,64,512]{4,3,2,1,0:T(8,128)(2,1)}, bf16[3,2,2,64,512]{4,3,2,1,0:T(8,128)(2,1)}, u32[]{:S(2)}, u32[]{:S(2)}) collective-permute-start(bf16[3,2,2,64,512]{4,3,2,1,0:T(8,128)(2,1)} %get-tuple-element.228), channel_id=1, source_target_pairs={{0,1},{1,0},{2,3},{3,2},{4,5},{5,4},{6,7},{7,6},{8,9},{9,8},{10,11... | collective-permute-start | bytes 2359304 | tf_op jit(solution)/shard_map/ppermute | solution.py:52
  441.7 23.8 %collective-permute-start.30 = (bf16[3,2,2,64,512]{4,3,2,1,0:T(8,128)(2,1)}, bf16[3,2,2,64,512]{4,3,2,1,0:T(8,128)(2,1)}, u32[]{:S(2)}, u32[]{:S(2)}) collective-permute-start(bf16[3,2,2,64,512]{4,3,2,1,0:T(8,128)(2,1)} %get-tuple-element.229), channel_id=1, source_target_pairs={{0,16},{1,17},{2,18},{3,19},{4,20},{5,21},{6,22},{7,23},{8,24},{9,... | collective-permute-start | bytes 2359304 | tf_op jit(solution)/shard_map/ppermute | solution.py:52
  442.3 23.2 %collective-permute-start.28 = (bf16[2,1,128,1024]{3,2,1,0:T(8,128)(2,1)}, bf16[2,1,128,1024]{3,2,1,0:T(8,128)(2,1)}, u32[]{:S(2)}, u32[]{:S(2)}) collective-permute-start(bf16[2,1,128,1024]{3,2,1,0:T(8,128)(2,1)} %get-tuple-element.227), channel_id=1, source_target_pairs={{0,2},{1,3},{2,0},{3,1},{4,6},{5,7},{6,4},{7,5},{8,10},{9,11},{10,... | collective-permute-start | bytes 1572872 | tf_op jit(solution)/shard_map/ppermute | solution.py:52
  442.4 23.0 %collective-permute-start.27 = (bf16[1,32,2048]{2,1,0:T(8,128)(2,1)}, bf16[1,32,2048]{2,1,0:T(8,128)(2,1)}, u32[]{:S(2)}, u32[]{:S(2)}) collective-permute-start(bf16[1,32,2048]{2,1,0:T(8,128)(2,1)} %get-tuple-element.226), channel_id=1, source_target_pairs={{0,2},{1,3},{2,0},{3,1},{4,6},{5,7},{6,4},{7,5},{8,10},{9,11},{10,... | collective-permute-start | bytes 393224 | tf_op jit(solution)/shard_map/ppermute | solution.py:52
  445.7 49.4 %collective-permute-start.43 = (bf16[1,1,2,1,1,32,128]{6,5,4,3,2,1,0:T(8,128)(2,1)}, bf16[1,1,2,1,1,32,128]{6,5,4,3,2,1,0:T(8,128)(2,1)}, u32[]{:S(2)}, u32[]{:S(2)}) collective-permute-start(bf16[1,1,2,1,1,32,128]{6,5,4,3,2,1,0:T(8,128)(2,1)} %dynamic-slice_convert_fusion.3), channel_id=1, source_target_pairs={{0,2},{1,3},{2,0},{3,1},{4,6},{5,7},{6,4},{7,5},{8,10},{9,11},{10,... | collective-permute-start | bytes 49160 | tf_op jit(solution)/shard_map/ppermute | solution.py:52
  471.0 25.5 %collective-permute-start.52 = (bf16[1,128,1024]{2,1,0:T(8,128)(2,1)}, bf16[1,128,1024]{2,1,0:T(8,128)(2,1)}, u32[]{:S(2)}, u32[]{:S(2)}) collective-permute-start(bf16[1,128,1024]{2,1,0:T(8,128)(2,1)} %get-tuple-element.264.own_ref), channel_id=1, source_target_pairs={{0,16},{1,17},{2,18},{3,19},{4,20},{5,21},{6,22},{7,23},{8,24},{9,... | collective-permute-start | bytes 786440 | tf_op jit(solution)/shard_map/ppermute | solution.py:52
  472.5 25.1 %collective-permute-start.50 = (bf16[1,128,1024]{2,1,0:T(8,128)(2,1)}, bf16[1,128,1024]{2,1,0:T(8,128)(2,1)}, u32[]{:S(2)}, u32[]{:S(2)}) collective-permute-start(bf16[1,128,1024]{2,1,0:T(8,128)(2,1)} %get-tuple-element.262.own_ref), channel_id=1, source_target_pairs={{0,16},{1,17},{2,18},{3,19},{4,20},{5,21},{6,22},{7,23},{8,24},{9,... | collective-permute-start | bytes 786440 | tf_op jit(solution)/shard_map/ppermute | solution.py:52
  473.1 34.8 %collective-permute-start.31 = (bf16[3,2,64,1024]{3,2,1,0:T(8,128)(2,1)}, bf16[3,2,64,1024]{3,2,1,0:T(8,128)(2,1)}, u32[]{:S(2)}, u32[]{:S(2)}) collective-permute-start(bf16[3,2,64,1024]{3,2,1,0:T(8,128)(2,1)} %get-tuple-element.232), channel_id=1, source_target_pairs={{0,4},{1,5},{2,6},{3,7},{4,0},{5,1},{6,2},{7,3},{8,12},{9,13},{10,... | collective-permute-start | bytes 2359304 | tf_op jit(solution)/shard_map/ppermute | solution.py:52
  495.9 33.3 %collective-permute-start.44 = (bf16[1,1,1,1,1,32,128]{6,5,4,3,2,1,0:T(8,128)(2,1)S(1)}, bf16[1,1,1,1,1,32,128]{6,5,4,3,2,1,0:T(8,128)(2,1)S(1)}, u32[]{:S(2)}, u32[]{:S(2)}) collective-permute-start(bf16[1,1,1,1,1,32,128]{6,5,4,3,2,1,0:T(8,128)(2,1)S(1)} %dynamic-slice_convert_fusion.4), channel_id=1, source_target_pairs={{0,4},{1,5},{2,6},{3,7},{4,0},{5,1},{6,2},{7,3},{8,12},{9,13},{10,... | collective-permute-start | bytes 24584 | tf_op jit(solution)/shard_map/ppermute | solution.py:52
  497.5 17.8 %collective-permute-start.53 = (bf16[2,1,128,1024]{3,2,1,0:T(8,128)(2,1)S(1)}, bf16[2,1,128,1024]{3,2,1,0:T(8,128)(2,1)S(1)}, u32[]{:S(2)}, u32[]{:S(2)}) collective-permute-start(bf16[2,1,128,1024]{3,2,1,0:T(8,128)(2,1)S(1)} %pad_maximum_fusion.3), channel_id=1, source_target_pairs={{0,8},{1,9},{2,10},{3,11},{4,12},{5,13},{6,14},{7,15},{8,0},{9,1},... | collective-permute-start | bytes 1572872 | tf_op jit(solution)/shard_map/ppermute | solution.py:52
  498.6 20.4 %collective-permute-start.51 = (bf16[2,1,128,1024]{3,2,1,0:T(8,128)(2,1)S(1)}, bf16[2,1,128,1024]{3,2,1,0:T(8,128)(2,1)S(1)}, u32[]{:S(2)}, u32[]{:S(2)}) collective-permute-start(bf16[2,1,128,1024]{3,2,1,0:T(8,128)(2,1)S(1)} %pad_maximum_fusion.2), channel_id=1, source_target_pairs={{0,8},{1,9},{2,10},{3,11},{4,12},{5,13},{6,14},{7,15},{8,0},{9,1},... | collective-permute-start | bytes 1572872 | tf_op jit(solution)/shard_map/ppermute | solution.py:52
  511.2 13.9 %collective-permute-start.33 = (bf16[3,64,1024]{2,1,0:T(8,128)(2,1)}, bf16[3,64,1024]{2,1,0:T(8,128)(2,1)S(1)}, u32[]{:S(2)}, u32[]{:S(2)}) collective-permute-start(bf16[3,64,1024]{2,1,0:T(8,128)(2,1)} %get-tuple-element.250), channel_id=1, source_target_pairs={{0,2},{1,3},{2,0},{3,1},{4,6},{5,7},{6,4},{7,5},{8,10},{9,11},{10,... | collective-permute-start | bytes 1179656 | tf_op jit(solution)/shard_map/ppermute | solution.py:52
  515.3 15.5 %collective-permute-start.32 = (bf16[512,128]{1,0:T(8,128)(2,1)}, bf16[512,128]{1,0:T(8,128)(2,1)S(1)}, u32[]{:S(2)}, u32[]{:S(2)}) collective-permute-start(bf16[512,128]{1,0:T(8,128)(2,1)} %shard_map.415), channel_id=1, source_target_pairs={{0,8},{1,9},{2,10},{3,11},{4,12},{5,13},{6,14},{7,15},{8,0},{9,1},... | collective-permute-start | bytes 393224 | tf_op jit(solution)/shard_map/ppermute | solution.py:52
  529.9 2.2 collective-permute-start.45
  530.3 15.0 %collective-permute-start.37 = (bf16[3,64,1024]{2,1,0:T(8,128)(2,1)}, bf16[3,64,1024]{2,1,0:T(8,128)(2,1)S(1)}, u32[]{:S(2)}, u32[]{:S(2)}) collective-permute-start(bf16[3,64,1024]{2,1,0:T(8,128)(2,1)} %get-tuple-element.252.own_ref), channel_id=1, source_target_pairs={{0,16},{1,17},{2,18},{3,19},{4,20},{5,21},{6,22},{7,23},{8,24},{9,... | collective-permute-start | bytes 1179656 | tf_op jit(solution)/shard_map/ppermute | solution.py:52
  531.5 17.8 %collective-permute-start.34 = (bf16[512,128]{1,0:T(8,128)(2,1)S(1)}, bf16[512,128]{1,0:T(8,128)(2,1)S(1)}, u32[]{:S(2)}, u32[]{:S(2)}) collective-permute-start(bf16[512,128]{1,0:T(8,128)(2,1)S(1)} %fusion.7), channel_id=1, source_target_pairs={{0,1},{1,0},{2,3},{3,2},{4,5},{5,4},{6,7},{7,6},{8,9},{9,8},{10,11... | collective-permute-start | bytes 393224 | tf_op jit(solution)/shard_map/ppermute | solution.py:52
  532.0 5.1 collective-permute-start.46
  537.1 4.2 collective-permute-start.47
  541.3 6.9 %collective-permute-start.48 = (bf16[256,128]{1,0:T(8,128)(2,1)S(1)}, bf16[256,128]{1,0:T(8,128)(2,1)S(1)}, u32[]{:S(2)}, u32[]{:S(2)}) collective-permute-start(bf16[256,128]{1,0:T(8,128)(2,1)S(1)} %pad_maximum_fusion.10), channel_id=1, source_target_pairs={{0,4},{1,5},{2,6},{3,7},{4,0},{5,1},{6,2},{7,3},{8,12},{9,13},{10,... | collective-permute-start | bytes 196616 | tf_op jit(solution)/shard_map/ppermute | solution.py:52
  546.5 10.8 %collective-permute-start.38 = (bf16[2,3,64,1024]{3,2,1,0:T(8,128)(2,1)S(1)}, bf16[2,3,64,1024]{3,2,1,0:T(8,128)(2,1)}, u32[]{:S(2)}, u32[]{:S(2)}) collective-permute-start(bf16[2,3,64,1024]{3,2,1,0:T(8,128)(2,1)S(1)} %pad_maximum_fusion.1), channel_id=1, source_target_pairs={{0,8},{1,9},{2,10},{3,11},{4,12},{5,13},{6,14},{7,15},{8,0},{9,1},... | collective-permute-start | bytes 2359304 | tf_op jit(solution)/shard_map/ppermute | solution.py:52
  548.2 5.0 collective-permute-start.49
  549.3 5.0 collective-permute-start.35
  554.4 7.3 %collective-permute-start.36 = (bf16[512,128]{1,0:T(8,128)(2,1)S(1)}, bf16[512,128]{1,0:T(8,128)(2,1)S(1)}, u32[]{:S(2)}, u32[]{:S(2)}) collective-permute-start(bf16[512,128]{1,0:T(8,128)(2,1)S(1)} %add_convert_fusion), channel_id=1, source_target_pairs={{0,4},{1,5},{2,6},{3,7},{4,0},{5,1},{6,2},{7,3},{8,12},{9,13},{10,... | collective-permute-start | bytes 393224 | tf_op jit(solution)/shard_map/ppermute | solution.py:52
  562.5 7.9 %collective-permute-start.39 = (bf16[512,128]{1,0:T(8,128)(2,1)S(1)}, bf16[512,128]{1,0:T(8,128)(2,1)S(1)}, u32[]{:S(2)}, u32[]{:S(2)}) collective-permute-start(bf16[512,128]{1,0:T(8,128)(2,1)S(1)} %fusion.6), channel_id=1, source_target_pairs={{0,16},{1,17},{2,18},{3,19},{4,20},{5,21},{6,22},{7,23},{8,24},{9,... | collective-permute-start | bytes 393224 | tf_op jit(solution)/shard_map/ppermute | solution.py:52
  (47 other events, 437.7 us)
Sparse Core Ops, SparseCore 0:
  12.5 141.8 all-gather.6
  157.4 75.4 all-gather.8
  475.6 66.4 all-gather.10
